TPU v7x, 32 devices: a whole 2x2x4 slice. The times are simulated.
32 devices in a mesh: groups: 2 (over y), strip: 4 (over z), sub: 2 (over x), rep: 2 (over core).
Axes of the slice: x: 2, y: 2, z: 4, core: 2. Of those that a mesh axis runs over, the one named last changes fastest.
Arguments:
- source: bfloat16 [32, 16, 128, 128], P(('groups', 'strip'), 'sub', 'rep'), parts along dimension 0, may hold values from -6 to 6
- target: bfloat16 [32, 16, 128, 128], P(('groups', 'strip'), 'sub', 'rep'), parts along dimension 0, may hold values from -6 to 6
- target_ids: int32 [32, 16, 25], P(('groups', 'strip'), 'sub'), parts along dimension 0, may hold values from 0 to 255, as said below
- out_grad: bfloat16 [32, 16, 25, 128], P(('groups', 'strip'), 'sub'), parts along dimension 0, may hold values from -6 to 6
- w_in: bfloat16 [128, 256], replicated, may hold values from -0.5 to 0.5
- b_in: float32 [256], replicated, may hold values from -4 to 4
- w_out: bfloat16 [256, 128], replicated, may hold values from -0.375 to 0.375
Outputs:
- source_grad: bfloat16 [32, 16, 128, 128], P(('groups', 'strip'), 'sub', 'rep'), parts along dimension 0
- target_grad: bfloat16 [32, 16, 128, 128], P(('groups', 'strip'), 'sub', 'rep'), parts along dimension 0
There are 2 independent parts, one for each index of `groups`. A program takes and returns all parts, laid end to end along the dimension named above; an argument that names none is the same for every part. Nothing has to cross between parts.
Inputs may be any that keep to these rules, and one draw needn't show every extreme that they name: `target_ids`: the targets of source block (i, j) lie within 3 block rows and 3 block columns of it and inside the section; they come in no particular order and may repeat.
All inputs are finite; a program needn't handle non-finite values.
Results may differ from a plain program's by a relative error of at most 0.007.
Values may be sent and summed in bfloat16 or wider, within the bound.
No kernel may reach another device: no remote copies, remote signals or barrier semaphores. Data moves between devices by JAX's collectives and lax.ppermute only.
A program may use at most 64 MiB of HBM per device.

v0:
```python
from functools import partial
import math

import jax
import jax.numpy as jnp
from jax import lax
from jax.sharding import PartitionSpec as P

H = 3


def with_halo(cells, sides, width):
    for axis, dim in sides:
        count = lax.axis_size(axis)
        ends = count - 1
        head = lax.slice_in_dim(cells, 0, width, axis=dim)
        tail = lax.slice_in_dim(cells, cells.shape[dim] - width, cells.shape[dim], axis=dim)
        cells = jnp.concatenate(
            [
                lax.ppermute(tail, axis, [(i, (i + 1) % count) for i in range(ends)]),
                cells,
                lax.ppermute(head, axis, [((i + 1) % count, i) for i in range(ends)]),
            ],
            axis=dim,
        )
    return cells


def shifted(x, axis, by):
    peers = lax.axis_size(axis)
    pairs = [(i, i + by) for i in range(peers) if 0 <= i + by < peers]
    return lax.ppermute(x, axis, pairs)


def decoder_grad(cost_block, grad_block, w_in, b_in, w_out):
    count, picks, pixels = cost_block.shape
    cost_rows = cost_block.reshape(count * picks, pixels)
    hidden_pre = jnp.dot(cost_rows, w_in, preferred_element_type=jnp.float32) + b_in
    grad_hidden = lax.dot_general(
        grad_block.reshape(count * picks, pixels),
        w_out,
        (((1,), (1,)), ((), ())),
        preferred_element_type=jnp.float32,
    )
    _, pullback = jax.vjp(partial(jax.nn.gelu, approximate=True), hidden_pre)
    grad_pre = pullback(grad_hidden)[0].astype(jnp.bfloat16)
    grad_cost = lax.dot_general(
        grad_pre, w_in, (((1,), (1,)), ((), ())), preferred_element_type=jnp.float32
    )
    return grad_cost.astype(jnp.bfloat16).reshape(count, picks, pixels)


def shards(source, target, target_ids, out_grad, w_in, b_in, w_out):
    blk_rows, blk_cols, pix_half, channels = source.shape
    picks = target_ids.shape[2]
    rim_width = H
    num_blocks = blk_rows * blk_cols
    inv_root = 1.0 / math.sqrt(channels)
    strip_at = lax.axis_index("strip")
    sub_at = lax.axis_index("sub")
    total_cols = blk_cols * lax.axis_size("sub")
    ext_rows = blk_rows + 2 * rim_width
    ext_cols = blk_cols + 2 * rim_width
    ext_count = ext_rows * ext_cols
    src_flat = source.reshape(num_blocks, pix_half, channels)
    block_ids = target_ids.reshape(num_blocks, picks)
    local_row = block_ids // total_cols - (strip_at * blk_rows - rim_width)
    local_col = block_ids % total_cols - (sub_at * blk_cols - rim_width)
    ext_index = local_row * ext_cols + local_col
    selector = (
        ext_index[:, :, None] == jnp.arange(ext_count, dtype=jnp.int32)[None, None, :]
    ).astype(jnp.float32)
    padded_target = with_halo(target, (("strip", 0), ("sub", 1)), rim_width)
    target_ext = padded_target.reshape(ext_count, pix_half, channels)
    correlation = jnp.einsum(
        "bpc,epc->bep", src_flat, target_ext, preferred_element_type=jnp.float32
    )
    chosen = jnp.take_along_axis(correlation, ext_index[:, :, None], axis=1)
    costs = (chosen * inv_root).astype(jnp.bfloat16)
    grad_local = out_grad.reshape(num_blocks, picks, out_grad.shape[3])
    cost_whole = lax.all_gather(costs, "rep", axis=2, tiled=True)
    dcost_whole = decoder_grad(cost_whole, grad_local, w_in, b_in, w_out)
    grad_cost = lax.dynamic_slice_in_dim(dcost_whole, lax.axis_index("rep") * pix_half, pix_half, 2)
    pair_weight = jnp.einsum(
        "bke,bkp->bep", selector, grad_cost.astype(jnp.float32), precision=lax.Precision.HIGHEST
    ).astype(jnp.bfloat16)
    source_grad = jnp.einsum(
        "bep,epc->bpc", pair_weight, target_ext, preferred_element_type=jnp.float32
    )
    source_grad = (source_grad * inv_root).astype(jnp.bfloat16).reshape(source.shape)
    partial_sum = jnp.einsum(
        "bep,bpc->epc", pair_weight, src_flat, preferred_element_type=jnp.float32
    )
    partial_sum = partial_sum.reshape(ext_rows, ext_cols, pix_half, channels)
    from_before = shifted(
        partial_sum[:, ext_cols - rim_width :].astype(jnp.bfloat16), "sub", 1
    ).astype(jnp.float32)
    from_after = shifted(partial_sum[:, :rim_width].astype(jnp.bfloat16), "sub", -1).astype(
        jnp.float32
    )
    partial_sum = partial_sum.at[:, rim_width : 2 * rim_width].add(from_before)
    partial_sum = partial_sum.at[:, blk_cols : blk_cols + rim_width].add(from_after)
    middle = partial_sum[:, rim_width : rim_width + blk_cols]
    above = shifted(middle[ext_rows - rim_width :].astype(jnp.bfloat16), "strip", 1).astype(
        jnp.float32
    )
    below = shifted(middle[:rim_width].astype(jnp.bfloat16), "strip", -1).astype(jnp.float32)
    middle = middle.at[rim_width : 2 * rim_width].add(above)
    middle = middle.at[blk_rows : blk_rows + rim_width].add(below)
    owned = middle[rim_width : rim_width + blk_rows]
    target_grad = (owned * inv_root).astype(jnp.bfloat16)
    return (source_grad, target_grad)


def solution(mesh):
    placed = (
        P(("groups", "strip"), "sub", "rep", None),
        P(("groups", "strip"), "sub", "rep", None),
        P(("groups", "strip"), "sub", None),
        P(("groups", "strip"), "sub", None, None),
        P(),
        P(),
        P(),
    )
    return jax.shard_map(
        shards,
        mesh=mesh,
        in_specs=placed,
        out_specs=(
            P(("groups", "strip"), "sub", "rep", None),
            P(("groups", "strip"), "sub", "rep", None),
        ),
        check_vma=False,
    )
```

profile of v0, /device:TPU:0, one launch (start us, length us, event | category | flops | bytes accessed | tf_op | source)
XLA Modules:
  0.0 101.6 jit_solution(12239588834286984082)
XLA Ops:
  0.7 1.3 %fusion.76 = (bf16[3,8,64,128]{3,2,1,0:T(8,128)(2,1)S(1)}, bf16[3,8,64,128]{3,2,1,0:T(8,128)(2,1)S(1)}) fusion(bf16[4,8,64,128]{3,2,1,0:T(8,128)(2,1)} %param.16), kind=kLoop, calls=%fused_computation.100 | loop fusion | bytes 1572864 | tf_op jit(solution)/shard_map/slice | solution.py:16
  1.9 5.0 %collective-permute-start = (bf16[3,8,64,128]{3,2,1,0:T(8,128)(2,1)S(1)}, bf16[3,8,64,128]{3,2,1,0:T(8,128)(2,1)S(1)}, u32[]{:S(2)}, u32[]{:S(2)}) collective-permute-start(bf16[3,8,64,128]{3,2,1,0:T(8,128)(2,1)S(1)} %get-tuple-element.67), channel_id=1, source_target_pairs={{0,4},{4,8},{8,12},{1,5},{5,9},{9,13},{2,6},{6,10},{10,14},{3,7},{... | collective-permute-start | bytes 1179656 | tf_op jit(solution)/shard_map/ppermute | solution.py:20
  6.9 1.4 %collective-permute-start.1 = (bf16[3,8,64,128]{3,2,1,0:T(8,128)(2,1)S(1)}, bf16[3,8,64,128]{3,2,1,0:T(8,128)(2,1)S(1)}, u32[]{:S(2)}, u32[]{:S(2)}) collective-permute-start(bf16[3,8,64,128]{3,2,1,0:T(8,128)(2,1)S(1)} %get-tuple-element.66), channel_id=1, source_target_pairs={{4,0},{8,4},{12,8},{5,1},{9,5},{13,9},{6,2},{10,6},{14,10},{7,3},{... | collective-permute-start | bytes 1179656 | tf_op jit(solution)/shard_map/ppermute | solution.py:22
  8.4 6.9 %collective-permute-done = bf16[3,8,64,128]{3,2,1,0:T(8,128)(2,1)S(1)} collective-permute-done((bf16[3,8,64,128]{3,2,1,0:T(8,128)(2,1)S(1)}, bf16[3,8,64,128]{3,2,1,0:T(8,128)(2,1)S(1)}, u32[]{:S(2)}, u32[]{:S(2)}) %collective-permute-start) | collective-permute-done | bytes 393248 | tf_op jit(solution)/shard_map/ppermute | solution.py:20
  15.4 4.2 %collective-permute-done.1 = bf16[3,8,64,128]{3,2,1,0:T(8,128)(2,1)S(1)} collective-permute-done((bf16[3,8,64,128]{3,2,1,0:T(8,128)(2,1)S(1)}, bf16[3,8,64,128]{3,2,1,0:T(8,128)(2,1)S(1)}, u32[]{:S(2)}, u32[]{:S(2)}) %collective-permute-start.1) | collective-permute-done | bytes 393248 | tf_op jit(solution)/shard_map/ppermute | solution.py:22
  19.6 1.0 %fusion.75 = (bf16[10,3,64,128]{3,2,1,0:T(8,128)(2,1)}, bf16[10,3,64,128]{3,2,1,0:T(8,128)(2,1)}) fusion(bf16[10,8,64,128]{3,2,1,0:T(8,128)(2,1)S(1)} %constant_dynamic-update-slice_fusion), kind=kLoop, calls=%fused_computation.99 | loop fusion | bytes 1966080 | tf_op jit(solution)/shard_map/slice | solution.py:17
  20.6 3.4 %collective-permute-start.2 = (bf16[10,3,64,128]{3,2,1,0:T(8,128)(2,1)}, bf16[10,3,64,128]{3,2,1,0:T(8,128)(2,1)S(1)}, u32[]{:S(2)}, u32[]{:S(2)}) collective-permute-start(bf16[10,3,64,128]{3,2,1,0:T(8,128)(2,1)} %get-tuple-element.64), channel_id=1, source_target_pairs={{0,2},{1,3},{4,6},{5,7},{8,10},{9,11},{12,14},{13,15},{16,18},{17,... | collective-permute-start | bytes 1474568 | tf_op jit(solution)/shard_map/ppermute | solution.py:20
  24.0 1.3 %collective-permute-start.3 = (bf16[10,3,64,128]{3,2,1,0:T(8,128)(2,1)}, bf16[10,3,64,128]{3,2,1,0:T(8,128)(2,1)S(1)}, u32[]{:S(2)}, u32[]{:S(2)}) collective-permute-start(bf16[10,3,64,128]{3,2,1,0:T(8,128)(2,1)} %get-tuple-element.65), channel_id=1, source_target_pairs={{2,0},{3,1},{6,4},{7,5},{10,8},{11,9},{14,12},{15,13},{18,16},{19,... | collective-permute-start | bytes 1474568 | tf_op jit(solution)/shard_map/ppermute | solution.py:22
  25.9 7.8 %collective-permute-done.2 = bf16[10,3,64,128]{3,2,1,0:T(8,128)(2,1)S(1)} collective-permute-done((bf16[10,3,64,128]{3,2,1,0:T(8,128)(2,1)}, bf16[10,3,64,128]{3,2,1,0:T(8,128)(2,1)S(1)}, u32[]{:S(2)}, u32[]{:S(2)}) %collective-permute-start.2) | collective-permute-done | bytes 491552 | tf_op jit(solution)/shard_map/ppermute | solution.py:20
  33.7 4.0 %collective-permute-done.3 = bf16[10,3,64,128]{3,2,1,0:T(8,128)(2,1)S(1)} collective-permute-done((bf16[10,3,64,128]{3,2,1,0:T(8,128)(2,1)}, bf16[10,3,64,128]{3,2,1,0:T(8,128)(2,1)S(1)}, u32[]{:S(2)}, u32[]{:S(2)}) %collective-permute-start.3) | collective-permute-done | bytes 491552 | tf_op jit(solution)/shard_map/ppermute | solution.py:22
  38.0 1.4 %copy-done.1 = bf16[10,14,64,128]{3,2,1,0:T(8,128)(2,1)} copy-done((bf16[10,14,64,128]{3,2,1,0:T(8,128)(2,1)}, bf16[10,14,64,128]{3,2,1,0:T(8,128)(2,1)S(1)}, u32[]{:S(2)}) %copy-start.1) | copy-done | bytes 2293784
  39.4 3.7 %fusion.4 = f32[32,140,64]{1,0,2:T(8,128)} fusion(bf16[140,64,128]{2,1,0:T(8,128)(2,1)S(1)} %bitcast.45, bf16[32,64,128]{2,1,0:T(8,128)(2,1)S(1)} %bitcast.41), kind=kOutput, calls=%fused_computation.7 | convolution fusion | flops 73400320 | bytes 3964928 | tf_op jit(solution)/shard_map/bpc,epc->bep/dot_general | solution.py:75
  43.1 3.3 %copy.49 = f32[32,140,64]{2,0,1:T(8,128)S(1)} copy(f32[32,140,64]{1,0,2:T(8,128)} %fusion.4) | data formatting | bytes 2293760 | tf_op jit(solution)/shard_map/bpc,epc->bep/transpose | solution.py:75
  46.4 9.8 %gather_fusion = f32[800,64]{1,0:T(8,128)S(1)} fusion(f32[32,140,64]{2,0,1:T(8,128)S(1)} %copy.49, s32[800]{0:T(1024)S(1)} %reshape.311), kind=kCustom, calls=%fused_computation | custom fusion | bytes 416000 | tf_op jit(solution)/shard_map/jit(take_along_axis)/gather | solution.py:78
  56.6 0.9 copy.51
  57.5 2.7 %all_gather.3 = bf16[32,25,128]{1,0,2:T(8,128)(2,1)S(1)} all-gather(bf16[32,25,64]{1,0,2:T(8,128)(2,1)S(1)} %copy.51), channel_id=1, replica_groups=mesh['groups'=2,'strip'=4,'sub'=2,'rep'=2] {'rep'}, dimensions={2}, use_global_device_ids=true | all-gather | bytes 307200 | tf_op jit(solution)/shard_map/all_gather | solution.py:81
  60.3 1.9 %reshape.317 = bf16[800,128]{0,1:T(8,128)(2,1)S(1)} reshape(bf16[32,25,128]{1,0,2:T(8,128)(2,1)S(1)} %all_gather.3) | data formatting | bytes 409600 | tf_op jit(solution)/shard_map/reshape | solution.py:37
  62.5 0.7 convolution_convert_fusion.1
  63.4 0.8 convolution_convert_fusion
  64.1 1.5 %convolution_bitcast_fusion = f32[140,64,128]{2,0,1:T(8,128)S(1)} fusion(bf16[32,140,64]{1,2,0:T(8,128)(2,1)S(1)} %convolution_convert_fusion, bf16[32,64,128]{2,1,0:T(8,128)(2,1)S(1)} %bitcast.42), kind=kOutput, calls=%fused_computation.2 | convolution fusion | flops 73400320 | bytes 5685248 | tf_op jit(solution)/shard_map/bep,bpc->epc/dot_general | solution.py:91
  65.6 1.5 %copy.57 = f32[140,64,128]{2,1,0:T(8,128)S(1)} copy(f32[140,64,128]{2,0,1:T(8,128)S(1)} %convolution_bitcast_fusion) | data formatting | bytes 9175040 | tf_op jit(solution)/shard_map/bep,bpc->epc/transpose | solution.py:91
  67.7 1.6 %collective-permute-start.4 = (bf16[10,3,64,128]{3,2,1,0:T(8,128)(2,1)S(1)}, bf16[10,3,64,128]{3,2,1,0:T(8,128)(2,1)S(1)}, u32[]{:S(2)}, u32[]{:S(2)}) collective-permute-start(bf16[10,3,64,128]{3,2,1,0:T(8,128)(2,1)S(1)} %get-tuple-element.63), channel_id=1, source_target_pairs={{0,2},{1,3},{4,6},{5,7},{8,10},{9,11},{12,14},{13,15},{16,18},{17,... | collective-permute-start | bytes 1474568 | tf_op jit(solution)/shard_map/ppermute | solution.py:32
  69.3 1.3 %collective-permute-start.5 = (bf16[10,3,64,128]{3,2,1,0:T(8,128)(2,1)S(1)}, bf16[10,3,64,128]{3,2,1,0:T(8,128)(2,1)S(1)}, u32[]{:S(2)}, u32[]{:S(2)}) collective-permute-start(bf16[10,3,64,128]{3,2,1,0:T(8,128)(2,1)S(1)} %get-tuple-element.62), channel_id=1, source_target_pairs={{2,0},{3,1},{6,4},{7,5},{10,8},{11,9},{14,12},{15,13},{18,16},{19,... | collective-permute-start | bytes 1474568 | tf_op jit(solution)/shard_map/ppermute | solution.py:32
  70.6 9.4 %collective-permute-done.4 = bf16[10,3,64,128]{3,2,1,0:T(8,128)(2,1)S(1)} collective-permute-done((bf16[10,3,64,128]{3,2,1,0:T(8,128)(2,1)S(1)}, bf16[10,3,64,128]{3,2,1,0:T(8,128)(2,1)S(1)}, u32[]{:S(2)}, u32[]{:S(2)}) %collective-permute-start.4) | collective-permute-done | bytes 491552 | tf_op jit(solution)/shard_map/ppermute | solution.py:32
  80.3 3.9 %collective-permute-done.5 = bf16[10,3,64,128]{3,2,1,0:T(8,128)(2,1)S(1)} collective-permute-done((bf16[10,3,64,128]{3,2,1,0:T(8,128)(2,1)S(1)}, bf16[10,3,64,128]{3,2,1,0:T(8,128)(2,1)S(1)}, u32[]{:S(2)}, u32[]{:S(2)}) %collective-permute-start.5) | collective-permute-done | bytes 491552 | tf_op jit(solution)/shard_map/ppermute | solution.py:32
  85.1 3.6 %collective-permute-start.6 = (bf16[3,8,64,128]{3,2,1,0:T(8,128)(2,1)S(1)}, bf16[3,8,64,128]{3,2,1,0:T(8,128)(2,1)S(1)}, u32[]{:S(2)}, u32[]{:S(2)}) collective-permute-start(bf16[3,8,64,128]{3,2,1,0:T(8,128)(2,1)S(1)} %get-tuple-element.61), channel_id=1, source_target_pairs={{0,4},{4,8},{8,12},{1,5},{5,9},{9,13},{2,6},{6,10},{10,14},{3,7},{... | collective-permute-start | bytes 1179656 | tf_op jit(solution)/shard_map/ppermute | solution.py:32
  88.8 1.3 %collective-permute-start.7 = (bf16[3,8,64,128]{3,2,1,0:T(8,128)(2,1)S(1)}, bf16[3,8,64,128]{3,2,1,0:T(8,128)(2,1)S(1)}, u32[]{:S(2)}, u32[]{:S(2)}) collective-permute-start(bf16[3,8,64,128]{3,2,1,0:T(8,128)(2,1)S(1)} %get-tuple-element.60), channel_id=1, source_target_pairs={{4,0},{8,4},{12,8},{5,1},{9,5},{13,9},{6,2},{10,6},{14,10},{7,3},{... | collective-permute-start | bytes 1179656 | tf_op jit(solution)/shard_map/ppermute | solution.py:32
  90.1 2.5 %fusion.13 = bf16[4,8,64,128]{3,1,0,2:T(8,128)(2,1)S(1)} fusion(bf16[140,64,128]{2,1,0:T(8,128)(2,1)S(1)} %bitcast.46, bf16[32,140,64]{1,2,0:T(8,128)(2,1)S(1)} %convolution_convert_fusion), kind=kOutput, calls=%fused_computation.12 | convolution fusion | flops 73924608 | bytes 3391488 | tf_op jit(solution)/shard_map/bep,epc->bpc/dot_general | solution.py:87
  92.6 1.0 copy.58
  93.8 2.5 %collective-permute-done.6 = bf16[3,8,64,128]{3,2,1,0:T(8,128)(2,1)S(1)} collective-permute-done((bf16[3,8,64,128]{3,2,1,0:T(8,128)(2,1)S(1)}, bf16[3,8,64,128]{3,2,1,0:T(8,128)(2,1)S(1)}, u32[]{:S(2)}, u32[]{:S(2)}) %collective-permute-start.6) | collective-permute-done | bytes 393248 | tf_op jit(solution)/shard_map/ppermute | solution.py:32
  96.4 4.0 %collective-permute-done.7 = bf16[3,8,64,128]{3,2,1,0:T(8,128)(2,1)S(1)} collective-permute-done((bf16[3,8,64,128]{3,2,1,0:T(8,128)(2,1)S(1)}, bf16[3,8,64,128]{3,2,1,0:T(8,128)(2,1)S(1)}, u32[]{:S(2)}, u32[]{:S(2)}) %collective-permute-start.7) | collective-permute-done | bytes 393248 | tf_op jit(solution)/shard_map/ppermute | solution.py:32
  100.6 0.9 fusion.16
  (41 shorter events, 3.8 us)
Async XLA Ops:
  0.6 37.3 %copy-start = (bf16[4,8,64,128]{3,2,1,0:T(8,128)(2,1)S(1)}, bf16[4,8,64,128]{3,2,1,0:T(8,128)(2,1)}, u32[]{:S(2)}) copy-start(bf16[4,8,64,128]{3,2,1,0:T(8,128)(2,1)} %param.15) | copy-start | bytes 1572868
  0.6 14.6 %copy-start.3 = (bf16[4,8,64,128]{3,2,1,0:T(8,128)(2,1)S(1)}, bf16[4,8,64,128]{3,2,1,0:T(8,128)(2,1)}, u32[]{:S(2)}) copy-start(bf16[4,8,64,128]{3,2,1,0:T(8,128)(2,1)} %param.16) | copy-start | bytes 1572868
  1.9 13.3 %collective-permute-start = (bf16[3,8,64,128]{3,2,1,0:T(8,128)(2,1)S(1)}, bf16[3,8,64,128]{3,2,1,0:T(8,128)(2,1)S(1)}, u32[]{:S(2)}, u32[]{:S(2)}) collective-permute-start(bf16[3,8,64,128]{3,2,1,0:T(8,128)(2,1)S(1)} %get-tuple-element.67), channel_id=1, source_target_pairs={{0,4},{4,8},{8,12},{1,5},{5,9},{9,13},{2,6},{6,10},{10,14},{3,7},{... | collective-permute-start | bytes 1179656 | tf_op jit(solution)/shard_map/ppermute | solution.py:20
  6.9 18.4 %copy-start.6 = (s32[4,8,25]{2,1,0:T(8,128)S(1)}, s32[4,8,25]{2,1,0:T(8,128)}, u32[]{:S(2)}) copy-start(s32[4,8,25]{2,1,0:T(8,128)} %param.17) | copy-start | bytes 9604
  6.9 18.8 %copy-start.4 = (bf16[4,8,25,128]{3,1,2,0:T(8,128)(2,1)S(1)}, bf16[4,8,25,128]{3,1,2,0:T(8,128)(2,1)}, u32[]{:S(2)}) copy-start(bf16[4,8,25,128]{3,1,2,0:T(8,128)(2,1)} %param.18) | copy-start | bytes 614404
  6.9 12.6 %collective-permute-start.1 = (bf16[3,8,64,128]{3,2,1,0:T(8,128)(2,1)S(1)}, bf16[3,8,64,128]{3,2,1,0:T(8,128)(2,1)S(1)}, u32[]{:S(2)}, u32[]{:S(2)}) collective-permute-start(bf16[3,8,64,128]{3,2,1,0:T(8,128)(2,1)S(1)} %get-tuple-element.66), channel_id=1, source_target_pairs={{4,0},{8,4},{12,8},{5,1},{9,5},{13,9},{6,2},{10,6},{14,10},{7,3},{... | collective-permute-start | bytes 1179656 | tf_op jit(solution)/shard_map/ppermute | solution.py:22
  20.6 13.0 %collective-permute-start.2 = (bf16[10,3,64,128]{3,2,1,0:T(8,128)(2,1)}, bf16[10,3,64,128]{3,2,1,0:T(8,128)(2,1)S(1)}, u32[]{:S(2)}, u32[]{:S(2)}) collective-permute-start(bf16[10,3,64,128]{3,2,1,0:T(8,128)(2,1)} %get-tuple-element.64), channel_id=1, source_target_pairs={{0,2},{1,3},{4,6},{5,7},{8,10},{9,11},{12,14},{13,15},{16,18},{17,... | collective-permute-start | bytes 1474568 | tf_op jit(solution)/shard_map/ppermute | solution.py:20
  24.0 13.7 %collective-permute-start.3 = (bf16[10,3,64,128]{3,2,1,0:T(8,128)(2,1)}, bf16[10,3,64,128]{3,2,1,0:T(8,128)(2,1)S(1)}, u32[]{:S(2)}, u32[]{:S(2)}) collective-permute-start(bf16[10,3,64,128]{3,2,1,0:T(8,128)(2,1)} %get-tuple-element.65), channel_id=1, source_target_pairs={{2,0},{3,1},{6,4},{7,5},{10,8},{11,9},{14,12},{15,13},{18,16},{19,... | collective-permute-start | bytes 1474568 | tf_op jit(solution)/shard_map/ppermute | solution.py:22
  38.0 1.4 %copy-start.1 = (bf16[10,14,64,128]{3,2,1,0:T(8,128)(2,1)}, bf16[10,14,64,128]{3,2,1,0:T(8,128)(2,1)S(1)}, u32[]{:S(2)}) copy-start(bf16[10,14,64,128]{3,2,1,0:T(8,128)(2,1)S(1)} %pad_maximum_fusion) | copy-start | bytes 6881284
  56.3 5.9 %copy-start.5 = (bf16[128,256]{1,0:T(8,128)(2,1)S(1)}, bf16[128,256]{1,0:T(8,128)(2,1)}, u32[]{:S(2)}) copy-start(bf16[128,256]{1,0:T(8,128)(2,1)} %param.19) | copy-start | bytes 196612
  56.3 5.9 %copy-start.7 = (f32[256]{0:T(256)S(1)}, f32[256]{0:T(256)}, u32[]{:S(2)}) copy-start(f32[256]{0:T(256)} %param.20) | copy-start | bytes 3076
  56.6 5.9 %copy-start.8 = (bf16[256,128]{1,0:T(8,128)(2,1)S(1)}, bf16[256,128]{1,0:T(8,128)(2,1)}, u32[]{:S(2)}) copy-start(bf16[256,128]{1,0:T(8,128)(2,1)} %param.21) | copy-start | bytes 196612
  67.7 12.3 %collective-permute-start.4 = (bf16[10,3,64,128]{3,2,1,0:T(8,128)(2,1)S(1)}, bf16[10,3,64,128]{3,2,1,0:T(8,128)(2,1)S(1)}, u32[]{:S(2)}, u32[]{:S(2)}) collective-permute-start(bf16[10,3,64,128]{3,2,1,0:T(8,128)(2,1)S(1)} %get-tuple-element.63), channel_id=1, source_target_pairs={{0,2},{1,3},{4,6},{5,7},{8,10},{9,11},{12,14},{13,15},{16,18},{17,... | collective-permute-start | bytes 1474568 | tf_op jit(solution)/shard_map/ppermute | solution.py:32
  69.3 14.9 %collective-permute-start.5 = (bf16[10,3,64,128]{3,2,1,0:T(8,128)(2,1)S(1)}, bf16[10,3,64,128]{3,2,1,0:T(8,128)(2,1)S(1)}, u32[]{:S(2)}, u32[]{:S(2)}) collective-permute-start(bf16[10,3,64,128]{3,2,1,0:T(8,128)(2,1)S(1)} %get-tuple-element.62), channel_id=1, source_target_pairs={{2,0},{3,1},{6,4},{7,5},{10,8},{11,9},{14,12},{15,13},{18,16},{19,... | collective-permute-start | bytes 1474568 | tf_op jit(solution)/shard_map/ppermute | solution.py:32
  84.5 5.6 %copy-start.2 = (bf16[10,14,64,128]{3,2,1,0:T(8,128)(2,1)S(1)}, bf16[10,14,64,128]{3,2,1,0:T(8,128)(2,1)}, u32[]{:S(2)}) copy-start(bf16[10,14,64,128]{3,2,1,0:T(8,128)(2,1)} %copy-done.1) | copy-start | bytes 6881284
  85.1 11.1 %collective-permute-start.6 = (bf16[3,8,64,128]{3,2,1,0:T(8,128)(2,1)S(1)}, bf16[3,8,64,128]{3,2,1,0:T(8,128)(2,1)S(1)}, u32[]{:S(2)}, u32[]{:S(2)}) collective-permute-start(bf16[3,8,64,128]{3,2,1,0:T(8,128)(2,1)S(1)} %get-tuple-element.61), channel_id=1, source_target_pairs={{0,4},{4,8},{8,12},{1,5},{5,9},{9,13},{2,6},{6,10},{10,14},{3,7},{... | collective-permute-start | bytes 1179656 | tf_op jit(solution)/shard_map/ppermute | solution.py:32
  88.8 11.7 %collective-permute-start.7 = (bf16[3,8,64,128]{3,2,1,0:T(8,128)(2,1)S(1)}, bf16[3,8,64,128]{3,2,1,0:T(8,128)(2,1)S(1)}, u32[]{:S(2)}, u32[]{:S(2)}) collective-permute-start(bf16[3,8,64,128]{3,2,1,0:T(8,128)(2,1)S(1)} %get-tuple-element.60), channel_id=1, source_target_pairs={{4,0},{8,4},{12,8},{5,1},{9,5},{13,9},{6,2},{10,6},{14,10},{7,3},{... | collective-permute-start | bytes 1179656 | tf_op jit(solution)/shard_map/ppermute | solution.py:32
where the time goes:
time: 102 us
  waiting for transfers between devices  42.8 us (42%)
  local copies, waits for them, and re-layouts  23.2 us (23%)
  starting transfers between devices  18.9 us (19%)
  matrix products  9.48 us (9%)
  other arithmetic  3.45 us (3%)
  blocking collectives  2.74 us (3%)
  between operations  1.03 us (1%)
    ppermute x4, waiting for transfers between devices, shifted(): return lax.ppermute(x, axis, pairs)  19.9 us
    ppermute x2, waiting for transfers between devices, with_halo(): lax.ppermute(tail, axis, [(i, (i + 1) % count) for i in range(ends)])  14.7 us
    gather x3, local copies, waits for them, and re-layouts, shards(): chosen = jnp.take_along_axis(correlation, ext_index[:, :, None], axis=1)  9.9 us
    ppermute x2, starting transfers between devices, with_halo(): lax.ppermute(tail, axis, [(i, (i + 1) % count) for i in range(ends)])  8.39 us
    ppermute x2, waiting for transfers between devices, with_halo(): lax.ppermute(head, axis, [((i + 1) % count, i) for i in range(ends)])  8.21 us
    ppermute x4, starting transfers between devices, shifted(): return lax.ppermute(x, axis, pairs)  7.79 us
    dot_general x1, matrix products, shards(): jnp.einsum('bpc,epc->bep', src_flat, target_ext, preferred_element_type=j...  3.7 us
    transpose x1, local copies, waits for them, and re-layouts, shards(): jnp.einsum('bpc,epc->bep', src_flat, target_ext, preferred_element_type=j...  3.35 us
  transfers between devices with their start and end apart: 8, of which 8 were waited for; matrix products, arithmetic and copies ran while one was open for 4% of the time, Pallas kernels for 0%

commit v1 on v0

v1 whole, which is shorter than its diff:
```python
from functools import partial
import math

import jax
import jax.numpy as jnp
from jax import lax
from jax.experimental import pallas as pl
from jax.experimental.pallas import tpu as pltpu
from jax.sharding import PartitionSpec as P

H = 3
LANES = 128
NT = (((1,), (1,)), ((), ()))
TN = (((0,), (0,)), ((), ()))
F32 = jnp.float32
BF16 = jnp.bfloat16


def mate(i, q, n):
    j = i + 1 if (i + q) % 2 == 0 else i - 1
    return j if 0 <= j < n else None


def turns(n):
    return [q for q in (0, 1) if any(mate(i, q, n) is not None for i in range(n))]


def swap(x, qz, qx):
    strips, subs = lax.axis_size("strip"), lax.axis_size("sub")
    pairs = []
    for s in range(strips):
        for u in range(subs):
            t = s if qz is None else mate(s, qz, strips)
            v = u if qx is None else mate(u, qx, subs)
            if t is not None and v is not None:
                pairs.append((s * subs + u, t * subs + v))
    return lax.ppermute(x, ("strip", "sub"), pairs)


def plan(rows, cols):
    zs, xs = turns(lax.axis_size("strip")), turns(lax.axis_size("sub"))
    pieces = [(q, None) for q in zs]
    pieces += [(q, r) for q in zs for r in xs]
    pieces += [(None, r) for r in xs]
    base, at = {(None, None): 0}, rows * cols
    for qz, qx in pieces:
        base[qz, qx] = at
        at += (rows if qz is None else H) * (cols if qx is None else H)
    return pieces, base, at


def facing(q, extent, index):
    return jnp.where((index + q) % 2 == 0, extent - H, 0)


def places(target_ids, base, rows, cols):
    total_cols = cols * lax.axis_size("sub")
    strip_at, sub_at = lax.axis_index("strip"), lax.axis_index("sub")

    def split(d, extent, index):
        side = jnp.where(d < 0, -1, jnp.where(d >= extent, 1, 0))
        inner = jnp.where(side < 0, d + H, jnp.where(side > 0, d - extent, d))
        ahead = jnp.where(index % 2 == 0, 1, -1)
        turn = jnp.where(side == 0, -1, jnp.where(side == ahead, 0, 1))
        return turn, inner

    tz, dr = split(target_ids // total_cols - strip_at * rows, rows, strip_at)
    tx, dc = split(target_ids % total_cols - sub_at * cols, cols, sub_at)
    where_to = jnp.full(target_ids.shape, -1, jnp.int32)
    for (qz, qx), start in base.items():
        here = (tz == (-1 if qz is None else qz)) & (tx == (-1 if qx is None else qx))
        width = cols if qx is None else H
        where_to = jnp.where(here, start + dr * width + dc, where_to)
    return where_to


def widen(dst, at, src_ref, px):
    count = src_ref.shape[0] // px

    def body(i, _):
        dst[pl.ds((at + i) * px, px), :] = src_ref[pl.ds(i * px, px), :].astype(F32)
        return 0

    lax.fori_loop(0, count, body, 0)


def one_hot(x_ref, b, slots, tile):
    group, j = divmod(b, LANES // slots)
    lane = lax.broadcasted_iota(jnp.int32, (1, LANES), 1) // slots
    row = jnp.where(lane == j, x_ref[group : group + 1, :], -1)
    e = lax.broadcasted_iota(jnp.int32, (LANES, LANES), 0) + tile * LANES
    return (e == row).astype(F32).astype(BF16)


def corr_kernel(px, n, ext, starts, slots, *refs):
    k = len(starts)
    src_ref, tgt_refs, x_ref = refs[0], refs[1 : 1 + k], refs[1 + k]
    costs_ref, tgt_t, src_t, s32, t32, corr = refs[2 + k :]
    ext_pad = tgt_t.shape[1]
    channels = src_ref.shape[1]
    inv_root = 1.0 / math.sqrt(channels)
    widen(s32, 0, src_ref, px)
    for start, ref in zip(starts, tgt_refs):
        widen(t32, start, ref, px)

    def clear(i, _):
        t32[pl.ds(i * px, px), :] = jnp.zeros((px, channels), F32)
        return 0

    lax.fori_loop(ext, ext_pad, clear, 0)

    def per_pixel(p, _):
        sp = s32[pl.ds(p, n, stride=px), :].astype(BF16)
        tp = t32[pl.ds(p, ext_pad, stride=px), :].astype(BF16)
        src_t[p] = sp
        tgt_t[p] = tp
        c = lax.dot_general(sp, tp, NT, preferred_element_type=F32) * inv_root
        for t in range(ext_pad // LANES):
            corr[t, pl.ds(p, n, stride=px), :] = c[:, t * LANES : (t + 1) * LANES]
        return 0

    lax.fori_loop(0, px, per_pixel, 0, unroll=4)
    per = LANES // slots
    for g in range(n // per):
        acc = jnp.zeros((px, LANES), F32)
        for j in range(per):
            b = g * per + j
            for t in range(ext_pad // LANES):
                acc += jnp.dot(
                    corr[t, b * px : (b + 1) * px, :].astype(BF16),
                    one_hot(x_ref, b, slots, t),
                    preferred_element_type=F32,
                )
        costs_ref[:, g * LANES : (g + 1) * LANES] = acc.astype(BF16)


def hidden_kernel(og_ref, w_out_ref, gh_ref):
    gh_ref[...] = lax.dot_general(
        w_out_ref[...], og_ref[...], NT, preferred_element_type=F32
    )


def gelu_slope(x):
    c = math.sqrt(2.0 / math.pi)
    x2 = x * x
    th = jnp.tanh(c * (x + 0.044715 * (x2 * x)))
    inner = c * (1.0 + (3.0 * 0.044715) * x2)
    return 0.5 * (1.0 + th) + (0.5 * x) * ((1.0 - th) * (1.0 + th)) * inner


def decoder_kernel(rep_ref, mine_ref, other_ref, gh_ref, wt_ref, b_ref, w_ref, gc_ref, whole):
    px = mine_ref.shape[0]
    rep = rep_ref[0]
    whole[pl.ds(pl.multiple_of(rep * px, px), px), :] = mine_ref[...]
    whole[pl.ds(pl.multiple_of((1 - rep) * px, px), px), :] = other_ref[...]
    w_half = w_ref[pl.ds(pl.multiple_of(rep * px, px), px), :]
    width = 2 * LANES
    for g in range(mine_ref.shape[1] // width):
        cut = slice(g * width, (g + 1) * width)
        pre = jnp.dot(wt_ref[...], whole[:, cut], preferred_element_type=F32) + b_ref[...]
        grad = (gh_ref[:, cut] * gelu_slope(pre)).astype(BF16)
        gc_ref[:, cut] = jnp.dot(w_half, grad, preferred_element_type=F32).astype(BF16)


def grads_kernel(px, n, starts, counts, slots, gc_ref, x_ref, tgt_t, src_t, *refs):
    k = len(starts)
    sg_ref, own_ref, part_refs = refs[0], refs[1], refs[2 : 1 + k]
    pw, s32, part = refs[1 + k :]
    ext_pad = tgt_t.shape[1]
    inv_root = 1.0 / math.sqrt(tgt_t.shape[2])
    tiles = ext_pad // LANES
    per = LANES // slots
    for b in range(n):
        g = b // per
        gc = gc_ref[:, g * LANES : (g + 1) * LANES]
        for t in range(tiles):
            pw[t, b * px : (b + 1) * px, :] = lax.dot_general(
                gc, one_hot(x_ref, b, slots, t), NT, preferred_element_type=F32
            )

    def per_pixel(p, _):
        tp, sp = tgt_t[p], src_t[p]
        sg = jnp.zeros((n, tp.shape[1]), F32)
        for t in range(tiles):
            w = pw[t, pl.ds(p, n, stride=px), :].astype(BF16)
            sg += jnp.dot(
                w, tp[t * LANES : (t + 1) * LANES, :], preferred_element_type=F32
            )
            part[pl.ds(t * LANES * px + p, LANES, stride=px), :] = lax.dot_general(
                w, sp, TN, preferred_element_type=F32
            )
        s32[pl.ds(p, n, stride=px), :] = sg * inv_root
        return 0

    lax.fori_loop(0, px, per_pixel, 0, unroll=4)

    def narrow(dst, src, at, count):
        def body(i, _):
            dst[pl.ds(i * px, px), :] = src[pl.ds((at + i) * px, px), :].astype(dst.dtype)
            return 0

        lax.fori_loop(0, count, body, 0)

    narrow(sg_ref, s32, 0, n)
    for start, count, ref in zip(starts, counts, (own_ref, *part_refs)):
        narrow(ref, part, start, count)


def total_kernel(px, rows, cols, pieces, off_ref, own_ref, *refs):
    parts, tg_ref, acc = refs[: len(pieces)], refs[-2], refs[-1]
    inv_root = 1.0 / math.sqrt(own_ref.shape[1])
    n = rows * cols

    def load(i, _):
        acc[pl.ds(i * px, px), :] = own_ref[pl.ds(i * px, px), :]
        return 0

    lax.fori_loop(0, n, load, 0)
    for (qz, qx), ref in zip(pieces, parts):
        r0 = 0 if qz is None else off_ref[qz]
        c0 = 0 if qx is None else off_ref[2 + qx]
        high = rows if qz is None else H
        wide = cols if qx is None else H

        def add(r, _, r0=r0, c0=c0, wide=wide, ref=ref):
            for c in range(wide):
                at = pl.ds(pl.multiple_of(((r0 + r) * cols + c0 + c) * px, px), px)
                piece = ref[pl.ds(pl.multiple_of((r * wide + c) * px, px), px), :]
                acc[at, :] += piece.astype(F32)
            return 0

        lax.fori_loop(0, high, add, 0)

    def store(i, _):
        tg_ref[pl.ds(i * px, px), :] = (acc[pl.ds(i * px, px), :] * inv_root).astype(BF16)
        return 0

    lax.fori_loop(0, n, store, 0)


VM = pl.BlockSpec(memory_space=pltpu.VMEM)
SM = pl.BlockSpec(memory_space=pltpu.SMEM)


def call(kernel, outs, scratch, args, scalars=0, flops=10**8, moved=4 * 10**6):
    return pl.pallas_call(
        kernel,
        out_shape=[jax.ShapeDtypeStruct(s, d) for s, d in outs],
        in_specs=[SM] * scalars + [VM] * (len(args) - scalars),
        out_specs=[VM] * len(outs),
        scratch_shapes=[pltpu.VMEM(s, d) for s, d in scratch],
        compiler_params=pltpu.CompilerParams(vmem_limit_bytes=60 * 2**20),
        cost_estimate=pl.CostEstimate(flops=flops, bytes_accessed=moved, transcendentals=0),
    )(*args)


def shards(source, target, target_ids, out_grad, w_in, b_in, w_out):
    rows, cols, px, channels = source.shape
    picks = target_ids.shape[2]
    n = rows * cols
    slots = 1 << (picks - 1).bit_length()
    per = LANES // slots
    groups = n // per
    pieces, base, ext = plan(rows, cols)
    ext_pad = -(-ext // LANES) * LANES
    strip_at, sub_at = lax.axis_index("strip"), lax.axis_index("sub")
    rep = lax.axis_index("rep")

    def boundary(x, qz, qx):
        if qz is not None:
            x = lax.dynamic_slice_in_dim(x, facing(qz, rows, strip_at), H, 0)
        if qx is not None:
            x = lax.dynamic_slice_in_dim(x, facing(qx, cols, sub_at), H, 1)
        return x

    halo = [swap(boundary(target, qz, qx), qz, qx) for qz, qx in pieces]
    flat = [h.reshape(-1, channels) for h in halo]
    starts = [0] + [base[q] for q in pieces]
    counts = [n] + [f.shape[0] // px for f in flat]

    place = places(target_ids.reshape(n, picks), base, rows, cols)
    x_ids = jnp.pad(place, ((0, 0), (0, slots - picks)), constant_values=-1).reshape(groups, LANES)
    og = jnp.pad(
        out_grad.reshape(n, picks, out_grad.shape[3]), ((0, 0), (0, slots - picks), (0, 0))
    ).reshape(n * slots, out_grad.shape[3])
    (grad_hidden,) = call(
        hidden_kernel, [((w_out.shape[0], n * slots), F32)], [], (og, w_out)
    )

    src = source.reshape(n * px, channels)
    tgt = target.reshape(n * px, channels)
    costs, tgt_t, src_t = call(
        partial(corr_kernel, px, n, ext, starts, slots),
        [((px, n * slots), BF16), ((px, ext_pad, channels), BF16), ((px, n, channels), BF16)],
        [
            ((n * px, channels), F32),
            ((ext_pad * px, channels), F32),
            ((ext_pad // LANES, n * px, LANES), F32),
        ],
        (src, tgt, *flat, x_ids),
    )
    reps = lax.axis_size("rep")
    other = lax.ppermute(costs, "rep", [(i, reps - 1 - i) for i in range(reps)])
    (gc,) = call(
        decoder_kernel,
        [((px, n * slots), BF16)],
        [((2 * px, n * slots), BF16)],
        (rep.astype(jnp.int32)[None], costs, other, grad_hidden, w_in.T, b_in[:, None], w_in),
        scalars=1,
    )
    sg, own, *parts = call(
        partial(grads_kernel, px, n, starts, counts, slots),
        [((n * px, channels), BF16), ((n * px, channels), F32)]
        + [((c * px, channels), BF16) for c in counts[1:]],
        [
            ((ext_pad // LANES, n * px, LANES), F32),
            ((n * px, channels), F32),
            ((ext_pad * px, channels), F32),
        ],
        (gc, x_ids, tgt_t, src_t),
    )
    back = [swap(part, qz, qx) for part, (qz, qx) in zip(parts, pieces)]
    offs = jnp.stack(
        [facing(q, rows, strip_at) for q in (0, 1)] + [facing(q, cols, sub_at) for q in (0, 1)]
    ).astype(jnp.int32)
    (tg,) = call(
        partial(total_kernel, px, rows, cols, pieces),
        [((n * px, channels), BF16)],
        [((n * px, channels), F32)],
        (offs, own, *back),
        scalars=1,
    )
    return sg.reshape(source.shape), tg.reshape(source.shape)


def solution(mesh):
    cells = P(("groups", "strip"), "sub", "rep", None)
    placed = (
        cells,
        cells,
        P(("groups", "strip"), "sub", None),
        P(("groups", "strip"), "sub", None, None),
        P(),
        P(),
        P(),
    )
    return jax.shard_map(
        shards, mesh=mesh, in_specs=placed, out_specs=(cells, cells), check_vma=False
    )
```

time: 102 us -> 75.3 us (0.74)
  the two profiles are of different devices: /device:TPU:0 before, /device:TPU:12 now
where the time goes in v1:
time: 75.3 us; the launch traced here: 74.9 us
  Pallas kernels  30.3 us (40%)
  waiting for transfers between devices  19.8 us (26%)
  starting transfers between devices  15.3 us (20%)
  local copies, waits for them, and re-layouts  7.86 us (10%)
  between operations  0.9 us (1%)
    pallas_call x5, Pallas kernels, call(): pl.pallas_call(kernel, out_shape=[jax.ShapeDtypeStruct(s, d) for s, d in...  30.3 us
    ppermute x10, waiting for transfers between devices, swap(): return lax.ppermute(x, ('strip', 'sub'), pairs)  19.8 us
    ppermute x10, starting transfers between devices, swap(): return lax.ppermute(x, ('strip', 'sub'), pairs)  15.3 us
    unnamed x35, local copies, waits for them, and re-layouts  3.48 us
  transfers between devices with their start and end apart: 11, of which 4 were waited for; matrix products, arithmetic and copies ran while one was open for 6% of the time, Pallas kernels for 3%

profile of v1, /device:TPU:12, one launch (start us, length us, event | category | flops | bytes accessed | tf_op | source)
XLA Modules:
  0.0 74.9 jit_solution(873835271612615166)
XLA Ops:
  0.7 1.2 %constant_dynamic-slice_fusion.3 = (bf16[3,8,64,128]{3,2,1,0:T(8,128)(2,1)S(1)}, bf16[3,8,64,128]{3,2,1,0:T(8,128)(2,1)S(1)}) fusion(bf16[4,8,64,128]{3,2,1,0:T(8,128)(2,1)} %param.8, s32[]{:T(128)} %select_n.149, s32[]{:T(128)} %select_n.147), kind=kLoop, calls=%fused_computation.40 | loop fusion | bytes 1572872 | tf_op jit(solution)/shard_map/dynamic_slice | solution.py:271
  1.9 3.6 %collective-permute-start.1 = (bf16[3,8,64,128]{3,2,1,0:T(8,128)(2,1)S(1)}, bf16[3,8,64,128]{3,2,1,0:T(8,128)(2,1)S(1)}, u32[]{:S(2)}, u32[]{:S(2)}) collective-permute-start(bf16[3,8,64,128]{3,2,1,0:T(8,128)(2,1)S(1)} %get-tuple-element.24), channel_id=1, source_target_pairs={{4,8},{6,10},{8,4},{10,6},{5,9},{7,11},{9,5},{11,7},{20,24},{22,26... | collective-permute-start | bytes 1179656 | tf_op jit(solution)/shard_map/ppermute | solution.py:37
  5.7 0.9 %constant_dynamic-slice_fusion = bf16[4,3,64,128]{3,2,1,0:T(8,128)(2,1)S(1)} fusion(bf16[4,8,64,128]{3,2,1,0:T(8,128)(2,1)} %param.8, s32[]{:T(128)} %select_n.152), kind=kLoop, calls=%fused_computation.37 | loop fusion | bytes 393220 | tf_op jit(solution)/shard_map/dynamic_slice | solution.py:273
  6.6 1.6 %collective-permute-start.4 = (bf16[4,3,64,128]{3,2,1,0:T(8,128)(2,1)S(1)}, bf16[4,3,64,128]{3,2,1,0:T(8,128)(2,1)S(1)}, u32[]{:S(2)}, u32[]{:S(2)}) collective-permute-start(bf16[4,3,64,128]{3,2,1,0:T(8,128)(2,1)S(1)} %constant_dynamic-slice_fusion), channel_id=1, source_target_pairs={{0,2},{2,0},{4,6},{6,4},{8,10},{10,8},{12,14},{14,12},{1,3},{3,1},... | collective-permute-start | bytes 589832 | tf_op jit(solution)/shard_map/ppermute | solution.py:37
  8.2 2.3 %collective-permute-start.3 = (bf16[3,3,64,128]{3,2,1,0:T(8,128)(2,1)S(1)}, bf16[3,3,64,128]{3,2,1,0:T(8,128)(2,1)S(1)}, u32[]{:S(2)}, u32[]{:S(2)}) collective-permute-start(bf16[3,3,64,128]{3,2,1,0:T(8,128)(2,1)S(1)} %get-tuple-element.22), channel_id=1, source_target_pairs={{4,10},{6,8},{8,6},{10,4},{5,11},{7,9},{9,7},{11,5},{20,26},{22,24... | collective-permute-start | bytes 442376 | tf_op jit(solution)/shard_map/ppermute | solution.py:37
  10.5 0.4 collective-permute-start.2
  11.0 0.7 reshape.51.refs_7_.x_ref
  11.6 8.8 %collective-permute-done.3 = bf16[3,3,64,128]{3,2,1,0:T(8,128)(2,1)S(1)} collective-permute-done((bf16[3,3,64,128]{3,2,1,0:T(8,128)(2,1)S(1)}, bf16[3,3,64,128]{3,2,1,0:T(8,128)(2,1)S(1)}, u32[]{:S(2)}, u32[]{:S(2)}) %collective-permute-start.3) | collective-permute-done | bytes 147488 | tf_op jit(solution)/shard_map/ppermute | solution.py:37
  20.4 1.1 %collective-permute-done.2 = bf16[3,3,64,128]{3,2,1,0:T(8,128)(2,1)S(1)} collective-permute-done((bf16[3,3,64,128]{3,2,1,0:T(8,128)(2,1)S(1)}, bf16[3,3,64,128]{3,2,1,0:T(8,128)(2,1)S(1)}, u32[]{:S(2)}, u32[]{:S(2)}) %collective-permute-start.2) | collective-permute-done | bytes 147488 | tf_op jit(solution)/shard_map/ppermute | solution.py:37
  21.5 0.6 copy-done.12
  22.2 0.1 copy-done.1
  22.4 0.1 copy-done.2
  22.5 9.1 %shard_map.86 = (bf16[64,1024]{1,0:T(8,128)(2,1)}, bf16[64,128,128]{2,1,0:T(8,128)(2,1)}, bf16[64,32,128]{2,1,0:T(8,128)(2,1)}) custom-call(bf16[2048,128]{1,0:T(8,128)(2,1)} %bitcast.41, bf16[2048,128]{1,0:T(8,128)(2,1)} %bitcast.38, bf16[1536,128]{1,0:T(8,128)(2,1)} %bitcast.44, bf16[1536,128]{1,0:T(8,128)(2,1)} %bitcast.43, bf16[576,128]{1,0:T(8,128)(2,1)} %bitcast.48, ...), custom_call_target="tpu_custom_call" | custom-call | flops 100000000 | bytes 4000000 | tf_op jit(solution)/shard_map/pallas_call | solution.py:246
  31.6 0.7 copy.12
  32.3 0.8 %copy.13.b_ref = f32[256,1]{1,0:T(8,128)} copy(f32[256,1]{0,1:T(1,128)S(1)} %bitcast.49) | data formatting | bytes 2048 | tf_op jit(solution)/shard_map/broadcast_in_dim | solution.py:308
  33.2 0.1 copy.14
  33.3 0.7 pad.9.clone
  34.0 2.2 %shard_map.87.gh_ref = f32[256,1024]{1,0:T(8,128)} custom-call(bf16[1024,128]{1,0:T(8,128)(2,1)} %bitcast.39, bf16[256,128]{1,0:T(8,128)(2,1)} %w_out_ref.1), custom_call_target="tpu_custom_call" | custom-call | flops 100000000 | bytes 4000000 | tf_op jit(solution)/shard_map/pallas_call | solution.py:246
  36.2 0.7 copy-done.13
  36.9 3.5 %shard_map.88.gc_ref = bf16[64,1024]{1,0:T(8,128)(2,1)} custom-call(s32[1]{0:T(128)} %bitcast.rep_ref, bf16[64,1024]{1,0:T(8,128)(2,1)} %get-tuple-element.12.mine_ref, bf16[64,1024]{1,0:T(8,128)(2,1)} %copy-done.13, f32[256,1024]{1,0:T(8,128)} %shard_map.87.gh_ref, bf16[256,128]{1,0:T(8,128)(2,1)} %bitcast.45, f32[256,1]{1,0:T(8,128)} %copy.13.b_ref, ...), custom_call_target="tpu_custom_call" | custom-call | flops 100000000 | bytes 4000000 | tf_op jit(solution)/shard_map/pallas_call | solution.py:246
  40.4 12.3 %shard_map.89 = (bf16[2048,128]{1,0:T(8,128)(2,1)}, f32[2048,128]{1,0:T(8,128)}, bf16[1536,128]{1,0:T(8,128)(2,1)}, bf16[1536,128]{1,0:T(8,128)(2,1)}, bf16[576,...) custom-call(bf16[64,1024]{1,0:T(8,128)(2,1)} %shard_map.88.gc_ref, ...), custom_call_target="tpu_custom_call" | custom-call | flops 100000000 | bytes 4000000 | tf_op jit(solution)/shard_map/pallas_call | solution.py:246
  52.7 2.9 %collective-permute-start.7 = (bf16[1536,128]{1,0:T(8,128)(2,1)}, bf16[1536,128]{1,0:T(8,128)(2,1)S(1)}, u32[]{:S(2)}, u32[]{:S(2)}) collective-permute-start(bf16[1536,128]{1,0:T(8,128)(2,1)} %get-tuple-element.18), channel_id=1, source_target_pairs={{4,8},{6,10},{8,4},{10,6},{5,9},{7,11},{9,5},{11,7},{20,24},{22,26... | collective-permute-start | bytes 1179656 | tf_op jit(solution)/shard_map/ppermute | solution.py:37
  55.6 0.6 collective-permute-start.10
  56.2 0.7 collective-permute-start.8
  56.9 3.1 %collective-permute-start.9 = (bf16[576,128]{1,0:T(8,128)(2,1)}, bf16[576,128]{1,0:T(8,128)(2,1)S(1)}, u32[]{:S(2)}, u32[]{:S(2)}) collective-permute-start(bf16[576,128]{1,0:T(8,128)(2,1)} %get-tuple-element.20), channel_id=1, source_target_pairs={{4,10},{6,8},{8,6},{10,4},{5,11},{7,9},{9,7},{11,5},{20,26},{22,24... | collective-permute-start | bytes 442376 | tf_op jit(solution)/shard_map/ppermute | solution.py:37
  60.1 0.7 pad_add_fusion.off_ref
  60.7 8.2 %collective-permute-done.8.refs_2_ = bf16[576,128]{1,0:T(8,128)(2,1)S(1)} collective-permute-done((bf16[576,128]{1,0:T(8,128)(2,1)}, bf16[576,128]{1,0:T(8,128)(2,1)S(1)}, u32[]{:S(2)}, u32[]{:S(2)}) %collective-permute-start.8) | collective-permute-done | bytes 147488 | tf_op jit(solution)/shard_map/ppermute | solution.py:37
  68.9 1.8 %collective-permute-done.9.refs_3_ = bf16[576,128]{1,0:T(8,128)(2,1)S(1)} collective-permute-done((bf16[576,128]{1,0:T(8,128)(2,1)}, bf16[576,128]{1,0:T(8,128)(2,1)S(1)}, u32[]{:S(2)}, u32[]{:S(2)}) %collective-permute-start.9) | collective-permute-done | bytes 147488 | tf_op jit(solution)/shard_map/ppermute | solution.py:37
  70.8 0.6 copy-done.10
  71.5 0.2 copy-done.3
  71.6 0.1 copy-done.4
  71.7 3.2 %shard_map.90 = bf16[2048,128]{1,0:T(8,128)(2,1)} custom-call(s32[4]{0:T(128)} %pad_add_fusion.off_ref, f32[2048,128]{1,0:T(8,128)} %get-tuple-element.16.own_ref, bf16[1536,128]{1,0:T(8,128)(2,1)} %copy-done.3, bf16[1536,128]{1,0:T(8,128)(2,1)} %copy-done.4, bf16[576,128]{1,0:T(8,128)(2,1)} %copy-done.9, bf16[576,128]{1,0:T(8,128)(2,1)} %copy-done.10, ...), custom_call_target="tpu_custom_call" | custom-call | flops 100000000 | bytes 4000000 | tf_op jit(solution)/shard_map/pallas_call | solution.py:246
  (39 shorter events, 0.4 us)
Async XLA Ops:
  0.6 7.5 %copy-start = (bf16[4,8,64,128]{3,2,1,0:T(8,128)(2,1)S(1)}, bf16[4,8,64,128]{3,2,1,0:T(8,128)(2,1)}, u32[]{:S(2)}) copy-start(bf16[4,8,64,128]{3,2,1,0:T(8,128)(2,1)} %param.8) | copy-start | bytes 1572868
  0.6 10.3 %copy-start.14 = (s32[4,8,25]{2,1,0:T(8,128)S(1)}, s32[4,8,25]{2,1,0:T(8,128)}, u32[]{:S(2)}) copy-start(s32[4,8,25]{2,1,0:T(8,128)} %param.9) | copy-start | bytes 9604
  1.9 29.7 %copy-start.5 = (bf16[128,256]{1,0:T(8,128)(2,1)S(1)}, bf16[128,256]{1,0:T(8,128)(2,1)}, u32[]{:S(2)}) copy-start(bf16[128,256]{1,0:T(8,128)(2,1)} %w_ref.1) | copy-start | bytes 196612
  1.9 30.4 %copy-start.15 = (f32[256]{0:T(256)S(1)}, f32[256]{0:T(256)}, u32[]{:S(2)}) copy-start(f32[256]{0:T(256)} %param.12) | copy-start | bytes 3076
  1.9 31.2 %copy-start.6 = (bf16[4,8,25,128]{3,1,2,0:T(8,128)(2,1)S(1)}, bf16[4,8,25,128]{3,1,2,0:T(8,128)(2,1)}, u32[]{:S(2)}) copy-start(bf16[4,8,25,128]{3,1,2,0:T(8,128)(2,1)} %param.10) | copy-start | bytes 614404
  1.9 19.6 %collective-permute-start.1 = (bf16[3,8,64,128]{3,2,1,0:T(8,128)(2,1)S(1)}, bf16[3,8,64,128]{3,2,1,0:T(8,128)(2,1)S(1)}, u32[]{:S(2)}, u32[]{:S(2)}) collective-permute-start(bf16[3,8,64,128]{3,2,1,0:T(8,128)(2,1)S(1)} %get-tuple-element.24), channel_id=1, source_target_pairs={{4,8},{6,10},{8,4},{10,6},{5,9},{7,11},{9,5},{11,7},{20,24},{22,26... | collective-permute-start | bytes 1179656 | tf_op jit(solution)/shard_map/ppermute | solution.py:37
  5.6 15.9 %collective-permute-start = (bf16[3,8,64,128]{3,2,1,0:T(8,128)(2,1)S(1)}, bf16[3,8,64,128]{3,2,1,0:T(8,128)(2,1)S(1)}, u32[]{:S(2)}, u32[]{:S(2)}) collective-permute-start(bf16[3,8,64,128]{3,2,1,0:T(8,128)(2,1)S(1)} %get-tuple-element.25), channel_id=1, source_target_pairs={{0,4},{2,6},{4,0},{6,2},{8,12},{10,14},{12,8},{14,10},{1,5},{3,7},... | collective-permute-start | bytes 1179656 | tf_op jit(solution)/shard_map/ppermute | solution.py:37
  6.6 14.9 %collective-permute-start.4 = (bf16[4,3,64,128]{3,2,1,0:T(8,128)(2,1)S(1)}, bf16[4,3,64,128]{3,2,1,0:T(8,128)(2,1)S(1)}, u32[]{:S(2)}, u32[]{:S(2)}) collective-permute-start(bf16[4,3,64,128]{3,2,1,0:T(8,128)(2,1)S(1)} %constant_dynamic-slice_fusion), channel_id=1, source_target_pairs={{0,2},{2,0},{4,6},{6,4},{8,10},{10,8},{12,14},{14,12},{1,3},{3,1},... | collective-permute-start | bytes 589832 | tf_op jit(solution)/shard_map/ppermute | solution.py:37
  8.2 12.2 %collective-permute-start.3 = (bf16[3,3,64,128]{3,2,1,0:T(8,128)(2,1)S(1)}, bf16[3,3,64,128]{3,2,1,0:T(8,128)(2,1)S(1)}, u32[]{:S(2)}, u32[]{:S(2)}) collective-permute-start(bf16[3,3,64,128]{3,2,1,0:T(8,128)(2,1)S(1)} %get-tuple-element.22), channel_id=1, source_target_pairs={{4,10},{6,8},{8,6},{10,4},{5,11},{7,9},{9,7},{11,5},{20,26},{22,24... | collective-permute-start | bytes 442376 | tf_op jit(solution)/shard_map/ppermute | solution.py:37
  10.5 11.0 %collective-permute-start.2 = (bf16[3,3,64,128]{3,2,1,0:T(8,128)(2,1)S(1)}, bf16[3,3,64,128]{3,2,1,0:T(8,128)(2,1)S(1)}, u32[]{:S(2)}, u32[]{:S(2)}) collective-permute-start(bf16[3,3,64,128]{3,2,1,0:T(8,128)(2,1)S(1)} %get-tuple-element.23), channel_id=1, source_target_pairs={{0,6},{2,4},{4,2},{6,0},{8,14},{10,12},{12,10},{14,8},{1,7},{3,5},... | collective-permute-start | bytes 442376 | tf_op jit(solution)/shard_map/ppermute | solution.py:37
  20.4 1.1 %copy-start.11 = (bf16[3,3,64,128]{3,2,1,0:T(8,128)(2,1)}, bf16[3,3,64,128]{3,2,1,0:T(8,128)(2,1)S(1)}, u32[]{:S(2)}) copy-start(bf16[3,3,64,128]{3,2,1,0:T(8,128)(2,1)S(1)} %collective-permute-done.3) | copy-start | bytes 442372
  21.5 0.7 copy-start.12
  21.5 0.7 copy-start.8
  21.5 0.9 %copy-start.1 = (bf16[3,8,64,128]{3,2,1,0:T(8,128)(2,1)}, bf16[3,8,64,128]{3,2,1,0:T(8,128)(2,1)S(1)}, u32[]{:S(2)}) copy-start(bf16[3,8,64,128]{3,2,1,0:T(8,128)(2,1)S(1)} %collective-permute-done.1) | copy-start | bytes 1179652
  21.5 1.0 %copy-start.2 = (bf16[3,8,64,128]{3,2,1,0:T(8,128)(2,1)}, bf16[3,8,64,128]{3,2,1,0:T(8,128)(2,1)S(1)}, u32[]{:S(2)}) copy-start(bf16[3,8,64,128]{3,2,1,0:T(8,128)(2,1)S(1)} %collective-permute-done) | copy-start | bytes 1179652
  31.6 4.6 %collective-permute-start.5 = (bf16[64,1024]{1,0:T(8,128)(2,1)}, bf16[64,1024]{1,0:T(8,128)(2,1)S(1)}, u32[]{:S(2)}, u32[]{:S(2)}) collective-permute-start(bf16[64,1024]{1,0:T(8,128)(2,1)} %get-tuple-element.12.mine_ref), channel_id=1, source_target_pairs={{0,1},{1,0},{2,3},{3,2},{4,5},{5,4},{6,7},{7,6},{8,9},{9,8},{10,11... | collective-permute-start | bytes 393224 | tf_op jit(solution)/shard_map/ppermute | solution.py:303
  36.2 0.7 copy-start.13
  52.7 18.0 %collective-permute-start.6 = (bf16[1536,128]{1,0:T(8,128)(2,1)}, bf16[1536,128]{1,0:T(8,128)(2,1)S(1)}, u32[]{:S(2)}, u32[]{:S(2)}) collective-permute-start(bf16[1536,128]{1,0:T(8,128)(2,1)} %get-tuple-element.17), channel_id=1, source_target_pairs={{0,4},{2,6},{4,0},{6,2},{8,12},{10,14},{12,8},{14,10},{1,5},{3,7},... | collective-permute-start | bytes 1179656 | tf_op jit(solution)/shard_map/ppermute | solution.py:37
  52.7 18.1 %collective-permute-start.7 = (bf16[1536,128]{1,0:T(8,128)(2,1)}, bf16[1536,128]{1,0:T(8,128)(2,1)S(1)}, u32[]{:S(2)}, u32[]{:S(2)}) collective-permute-start(bf16[1536,128]{1,0:T(8,128)(2,1)} %get-tuple-element.18), channel_id=1, source_target_pairs={{4,8},{6,10},{8,4},{10,6},{5,9},{7,11},{9,5},{11,7},{20,24},{22,26... | collective-permute-start | bytes 1179656 | tf_op jit(solution)/shard_map/ppermute | solution.py:37
  55.6 15.1 %collective-permute-start.10 = (bf16[768,128]{1,0:T(8,128)(2,1)}, bf16[768,128]{1,0:T(8,128)(2,1)S(1)}, u32[]{:S(2)}, u32[]{:S(2)}) collective-permute-start(bf16[768,128]{1,0:T(8,128)(2,1)} %get-tuple-element.21), channel_id=1, source_target_pairs={{0,2},{2,0},{4,6},{6,4},{8,10},{10,8},{12,14},{14,12},{1,3},{3,1},... | collective-permute-start | bytes 589832 | tf_op jit(solution)/shard_map/ppermute | solution.py:37
  56.2 12.7 %collective-permute-start.8 = (bf16[576,128]{1,0:T(8,128)(2,1)}, bf16[576,128]{1,0:T(8,128)(2,1)S(1)}, u32[]{:S(2)}, u32[]{:S(2)}) collective-permute-start(bf16[576,128]{1,0:T(8,128)(2,1)} %get-tuple-element.19), channel_id=1, source_target_pairs={{0,6},{2,4},{4,2},{6,0},{8,14},{10,12},{12,10},{14,8},{1,7},{3,5},... | collective-permute-start | bytes 442376 | tf_op jit(solution)/shard_map/ppermute | solution.py:37
  56.9 13.8 %collective-permute-start.9 = (bf16[576,128]{1,0:T(8,128)(2,1)}, bf16[576,128]{1,0:T(8,128)(2,1)S(1)}, u32[]{:S(2)}, u32[]{:S(2)}) collective-permute-start(bf16[576,128]{1,0:T(8,128)(2,1)} %get-tuple-element.20), channel_id=1, source_target_pairs={{4,10},{6,8},{8,6},{10,4},{5,11},{7,9},{9,7},{11,5},{20,26},{22,24... | collective-permute-start | bytes 442376 | tf_op jit(solution)/shard_map/ppermute | solution.py:37
  68.9 1.9 %copy-start.9 = (bf16[576,128]{1,0:T(8,128)(2,1)}, bf16[576,128]{1,0:T(8,128)(2,1)S(1)}, u32[]{:S(2)}) copy-start(bf16[576,128]{1,0:T(8,128)(2,1)S(1)} %collective-permute-done.8.refs_2_) | copy-start | bytes 442372
  70.7 0.7 copy-start.10
  70.7 0.7 copy-start.7
  70.7 0.9 %copy-start.3 = (bf16[1536,128]{1,0:T(8,128)(2,1)}, bf16[1536,128]{1,0:T(8,128)(2,1)S(1)}, u32[]{:S(2)}) copy-start(bf16[1536,128]{1,0:T(8,128)(2,1)S(1)} %collective-permute-done.6.refs_0_) | copy-start | bytes 1179652
  70.7 1.0 %copy-start.4 = (bf16[1536,128]{1,0:T(8,128)(2,1)}, bf16[1536,128]{1,0:T(8,128)(2,1)S(1)}, u32[]{:S(2)}) copy-start(bf16[1536,128]{1,0:T(8,128)(2,1)S(1)} %collective-permute-done.7.refs_1_) | copy-start | bytes 1179652

commit v2 on v1

v2 whole, which is shorter than its diff:
```python
from functools import partial
import math

import jax
import jax.numpy as jnp
from jax import lax
from jax.experimental import pallas as pl
from jax.experimental.pallas import tpu as pltpu
from jax.sharding import PartitionSpec as P

H = 3
LANES = 128
NT = (((1,), (1,)), ((), ()))
TN = (((0,), (0,)), ((), ()))
F32 = jnp.float32
BF16 = jnp.bfloat16


def mate(i, q, n):
    j = i + 1 if (i + q) % 2 == 0 else i - 1
    return j if 0 <= j < n else None


def turns(n):
    return [q for q in (0, 1) if any(mate(i, q, n) is not None for i in range(n))]


def swap(x, qz, qx):
    strips, subs = lax.axis_size("strip"), lax.axis_size("sub")
    pairs = []
    for s in range(strips):
        for u in range(subs):
            t = s if qz is None else mate(s, qz, strips)
            v = u if qx is None else mate(u, qx, subs)
            if t is not None and v is not None:
                pairs.append((s * subs + u, t * subs + v))
    return lax.ppermute(x, ("strip", "sub"), pairs)


def plan(rows, cols):
    zs, xs = turns(lax.axis_size("strip")), turns(lax.axis_size("sub"))
    pieces = [(q, r) for q in zs for r in xs]
    pieces += [(q, None) for q in zs]
    pieces += [(None, r) for r in xs]
    base, at = {(None, None): 0}, rows * cols
    for qz, qx in pieces:
        base[qz, qx] = at
        at += (rows if qz is None else H) * (cols if qx is None else H)
    return pieces, base, at


def facing(q, extent, index):
    return jnp.where((index + q) % 2 == 0, extent - H, 0)


def places(target_ids, base, rows, cols):
    total_cols = cols * lax.axis_size("sub")
    strip_at, sub_at = lax.axis_index("strip"), lax.axis_index("sub")

    def split(d, extent, index):
        side = jnp.where(d < 0, -1, jnp.where(d >= extent, 1, 0))
        inner = jnp.where(side < 0, d + H, jnp.where(side > 0, d - extent, d))
        ahead = jnp.where(index % 2 == 0, 1, -1)
        turn = jnp.where(side == 0, -1, jnp.where(side == ahead, 0, 1))
        return turn, inner

    row, col = target_ids // total_cols, target_ids % total_cols
    tz, dr = split(row - strip_at * rows, rows, strip_at)
    tx, dc = split(col - sub_at * cols, cols, sub_at)
    where_to = jnp.full(target_ids.shape, -1, jnp.int32)
    for (qz, qx), start in base.items():
        here = (tz == (-1 if qz is None else qz)) & (tx == (-1 if qx is None else qx))
        width = cols if qx is None else H
        where_to = jnp.where(here, start + dr * width + dc, where_to)
    return where_to, (row % rows) * cols + col % cols


def loop(count, body, most=4):
    step = max(d for d in range(1, most + 1) if count % d == 0) if count else 1

    def run(i, _):
        body(i)
        return 0

    lax.fori_loop(0, count, run, 0, unroll=step)


def widen(dst, at, src_ref, px, pitch):
    def body(i):
        rows = src_ref[pl.ds(pl.multiple_of(i * px, px), px), :]
        dst[pl.ds((at + i) * pitch, px), :] = rows.astype(F32)

    loop(src_ref.shape[0] // px, body)


def clear(dst, at, end, px, pitch):
    def body(i):
        dst[pl.ds((at + i) * pitch, px), :] = jnp.zeros((px, dst.shape[1]), F32)

    loop(end - at, body)


def hot(row, tile=0):
    e = lax.broadcasted_iota(jnp.int32, (LANES, LANES), 0) + tile * LANES
    return (e == row).astype(F32).astype(BF16)


def pick_hot(e_ref, b, slots, tile):
    group, j = divmod(b, LANES // slots)
    lane = lax.broadcasted_iota(jnp.int32, (1, LANES), 1) // slots
    return hot(jnp.where(lane == j, e_ref[group : group + 1, :], -1), tile)


def prep_kernel(px, n, slots, src_ref, tgt_ref, og_ref, w_out_ref, src_t, tgt_t, gh_ref, s32, t32, og):
    pitch = px + 1
    widen(s32, 0, src_ref, px, pitch)
    widen(t32, 0, tgt_ref, px, pitch)

    def turn(p):
        src_t[p] = s32[pl.ds(p, n, stride=pitch), :].astype(BF16)
        tgt_t[p] = t32[pl.ds(p, n, stride=pitch), :].astype(BF16)

    loop(px, turn)
    picks = og_ref.shape[1]
    og[...] = jnp.zeros_like(og)

    for b in range(n):
        og[b, :picks, :] = og_ref[b].astype(F32)
    for g in range(n * slots // LANES):
        per = LANES // slots
        block = og[g * per : (g + 1) * per].reshape(LANES, og.shape[2]).astype(BF16)
        gh_ref[:, g * LANES : (g + 1) * LANES] = lax.dot_general(
            w_out_ref[...], block, NT, preferred_element_type=F32
        )


def corr_kernel(px, n, ext, starts, slots, *refs):
    k = len(starts)
    own_t, src_t, e_ref, tgt_refs = refs[0], refs[1], refs[2], refs[3 : 3 + k]
    costs_ref, tgt_t, t32, corr = refs[3 + k :]
    ext_pad = tgt_t.shape[1]
    pitch = px + 1
    inv_root = 1.0 / math.sqrt(tgt_t.shape[2])
    for start, ref in zip(starts, tgt_refs):
        widen(t32, start - n, ref, px, pitch)
    clear(t32, ext - n, ext_pad - n, px, pitch)

    def per_pixel(p):
        tp = t32[pl.ds(p, ext_pad - n, stride=pitch), :].astype(BF16)
        tp = jnp.concatenate([own_t[p], tp], axis=0)
        tgt_t[p] = tp
        c = lax.dot_general(src_t[p], tp, NT, preferred_element_type=F32) * inv_root
        for t in range(ext_pad // LANES):
            corr[t, pl.ds(p, n, stride=pitch), :] = c[:, t * LANES : (t + 1) * LANES]

    loop(px, per_pixel, 8)
    per = LANES // slots
    for g in range(n // per):
        acc = jnp.zeros((px, LANES), F32)
        for j in range(per):
            b = g * per + j
            for t in range(ext_pad // LANES):
                acc += jnp.dot(
                    corr[t, b * pitch : b * pitch + px, :].astype(BF16),
                    pick_hot(e_ref, b, slots, t),
                    preferred_element_type=F32,
                )
        costs_ref[:, g * LANES : (g + 1) * LANES] = acc.astype(BF16)


def gelu_slope(x):
    c = math.sqrt(2.0 / math.pi)
    x2 = x * x
    th = jnp.tanh(c * (x + 0.044715 * (x2 * x)))
    inner = c * (1.0 + (3.0 * 0.044715) * x2)
    return 0.5 * (1.0 + th) + (0.5 * x) * ((1.0 - th) * (1.0 + th)) * inner


def decoder_kernel(info_ref, mine_ref, other_ref, gh_ref, wt_ref, b_ref, w_ref, gc_ref, whole):
    px = mine_ref.shape[0]
    rep = info_ref[0]
    whole[pl.ds(pl.multiple_of(rep * px, px), px), :] = mine_ref[...]
    whole[pl.ds(pl.multiple_of((1 - rep) * px, px), px), :] = other_ref[...]
    w_half = w_ref[pl.ds(pl.multiple_of(rep * px, px), px), :]
    width = 2 * LANES
    for g in range(mine_ref.shape[1] // width):
        cut = slice(g * width, (g + 1) * width)
        pre = jnp.dot(wt_ref[...], whole[:, cut], preferred_element_type=F32) + b_ref[...]
        grad = (gh_ref[:, cut] * gelu_slope(pre)).astype(BF16)
        gc_ref[:, cut] = jnp.dot(w_half, grad, preferred_element_type=F32).astype(BF16)


def send_kernel(px, rows, cols, slots, pieces, starts, counts, info_ref, gc_ref, e_ref, m_ref, *out_refs):
    per = LANES // slots
    wide = cols // per
    lane = lax.broadcasted_iota(jnp.int32, (1, LANES), 1) // slots
    for (qz, qx), start, count, ref in zip(pieces, starts, counts, out_refs):
        r0 = 0 if qz is None else info_ref[1 + qz]
        c0 = 0 if qx is None else info_ref[3 + qx]
        half, shift = c0 // per, c0 % per
        i = 0
        for r in range(rows if qz is None else H):
            for h in range(wide if qx is None else 1):
                g = (r0 + r) * wide + half + h
                e, m = e_ref[pl.ds(g, 1), :], m_ref[pl.ds(g, 1), :]
                here = (e >= start) & (e < start + count)
                to = jnp.where(here, (lane - shift) * slots + m, -1)
                gc = gc_ref[:, pl.ds(pl.multiple_of(g * LANES, LANES), LANES)]
                ref[:, i * LANES : (i + 1) * LANES] = lax.dot_general(
                    gc, hot(to), NT, preferred_element_type=F32
                ).astype(BF16)
                i += 1


def own_kernel(px, n, slots, gc_ref, e_ref, tgt_t, src_t, sg_ref, own_ref, pw, s32):
    ext_pad = tgt_t.shape[1]
    pitch = px + 1
    inv_root = 1.0 / math.sqrt(tgt_t.shape[2])
    tiles = ext_pad // LANES
    per = LANES // slots
    for b in range(n):
        g = b // per
        gc = gc_ref[:, g * LANES : (g + 1) * LANES]
        for t in range(tiles):
            pw[t, b * pitch : b * pitch + px, :] = lax.dot_general(
                gc, pick_hot(e_ref, b, slots, t), NT, preferred_element_type=F32
            )

    def per_pixel(p):
        tp = tgt_t[p]
        sg = jnp.zeros((n, tp.shape[1]), F32)
        for t in range(tiles):
            w = pw[t, pl.ds(p, n, stride=pitch), :].astype(BF16)
            sg += jnp.dot(w, tp[t * LANES : (t + 1) * LANES, :], preferred_element_type=F32)
            if t == 0:
                own_ref[p] = lax.dot_general(
                    w[:, :n], src_t[p], TN, preferred_element_type=F32
                )
        s32[pl.ds(p, n, stride=pitch), :] = sg * inv_root

    loop(px, per_pixel, 8)

    def narrow(i):
        sg_ref[pl.ds(pl.multiple_of(i * px, px), px), :] = s32[pl.ds(i * pitch, px), :].astype(BF16)

    loop(n, narrow)


def halo_kernel(px, starts, *refs):
    k = len(starts)
    src_refs, out, s32 = refs[:k], refs[k], refs[k + 1]
    pitch = px + 1
    for start, ref in zip(starts, src_refs):
        widen(s32, start, ref, px, pitch)
    last = starts[-1] + src_refs[-1].shape[0] // px
    clear(s32, last, out.shape[1], px, pitch)

    def turn(p):
        out[p] = s32[pl.ds(p, out.shape[1], stride=pitch), :].astype(BF16)

    loop(px, turn)


def total_kernel(px, n, slots, widths, own_ref, halo_t, *refs):
    k = len(widths)
    msg_refs, tg_ref, pw, t32 = refs[:k], refs[k], refs[k + 1], refs[k + 2]
    pitch = px + 1
    inv_root = 1.0 / math.sqrt(own_ref.shape[2])
    at = 0
    for width, ref in zip(widths, msg_refs):
        for g in range(ref.shape[1] // LANES):
            block = ref[:, g * LANES : (g + 1) * LANES].astype(F32)
            for j in range(width):
                turned = block if j == 0 else pltpu.roll(block, LANES - j * slots, 1)
                pw[at * pitch : at * pitch + px, :] = turned
                at += 1
    clear(pw, at, halo_t.shape[1], px, pitch)

    def per_pixel(p):
        w = pw[pl.ds(p, halo_t.shape[1], stride=pitch), :]
        tg = own_ref[p] + lax.dot_general(
            w[:, :n].astype(BF16), halo_t[p], TN, preferred_element_type=F32
        )
        t32[pl.ds(p, n, stride=pitch), :] = tg * inv_root

    loop(px, per_pixel, 8)

    def narrow(i):
        tg_ref[pl.ds(pl.multiple_of(i * px, px), px), :] = t32[pl.ds(i * pitch, px), :].astype(BF16)

    loop(n, narrow)


VM = pl.BlockSpec(memory_space=pltpu.VMEM)
SM = pl.BlockSpec(memory_space=pltpu.SMEM)


def call(name, kernel, outs, scratch, args, scalars=0, us=2.0):
    return pl.pallas_call(
        kernel,
        name=name,
        out_shape=[jax.ShapeDtypeStruct(s, d) for s, d in outs],
        in_specs=[SM] * scalars + [VM] * (len(args) - scalars),
        out_specs=[VM] * len(outs),
        scratch_shapes=[pltpu.VMEM(s, d) for s, d in scratch],
        compiler_params=pltpu.CompilerParams(vmem_limit_bytes=28 * 2**20),
        cost_estimate=pl.CostEstimate(
            flops=0, bytes_accessed=int(us * 3 * 10**6), transcendentals=0
        ),
    )(*args)


def shards(source, target, target_ids, out_grad, w_in, b_in, w_out):
    rows, cols, px, channels = source.shape
    picks = target_ids.shape[2]
    n = rows * cols
    pitch = px + 1
    slots = 1 << (picks - 1).bit_length()
    per = LANES // slots
    groups = n // per
    assert n <= slots and cols % per == 0 and H <= per and groups * per == n
    pieces, base, ext = plan(rows, cols)
    ext_pad = -(-ext // LANES) * LANES
    strip_at, sub_at = lax.axis_index("strip"), lax.axis_index("sub")
    rep = lax.axis_index("rep")

    def boundary(x, qz, qx):
        if qz is not None:
            x = lax.dynamic_slice_in_dim(x, facing(qz, rows, strip_at), H, 0)
        if qx is not None:
            x = lax.dynamic_slice_in_dim(x, facing(qx, cols, sub_at), H, 1)
        return x

    def halo_of(x):
        got = [swap(boundary(x, qz, qx), qz, qx) for qz, qx in pieces]
        return [h.reshape(-1, channels) for h in got]

    tgt_halo = halo_of(target)
    src_halo = halo_of(source)
    starts = [base[q] for q in pieces]
    counts = [h.shape[0] // px for h in tgt_halo]

    def slotted(x):
        return jnp.pad(x, ((0, 0), (0, slots - picks)), constant_values=-1).reshape(groups, LANES)

    e_at, m_at = places(target_ids.reshape(n, picks), base, rows, cols)
    e_ids, m_ids = slotted(e_at), slotted(m_at)
    info = jnp.stack(
        [rep]
        + [facing(q, rows, strip_at) for q in (0, 1)]
        + [facing(q, cols, sub_at) for q in (0, 1)]
    ).astype(jnp.int32)

    src_t, own_t, grad_hidden = call(
        "prep",
        partial(prep_kernel, px, n, slots),
        [((px, n, channels), BF16), ((px, n, channels), BF16), ((w_out.shape[0], n * slots), F32)],
        [((n * pitch, channels), F32)] * 2 + [((n, slots, out_grad.shape[3]), F32)],
        (
            source.reshape(n * px, channels),
            target.reshape(n * px, channels),
            out_grad.reshape(n, picks, out_grad.shape[3]),
            w_out,
        ),
        us=4,
    )
    costs, tgt_t = call(
        "corr",
        partial(corr_kernel, px, n, ext, starts, slots),
        [((px, n * slots), BF16), ((px, ext_pad, channels), BF16)],
        [
            (((ext_pad - n) * pitch, channels), F32),
            ((ext_pad // LANES, n * pitch, LANES), F32),
        ],
        (own_t, src_t, e_ids, *tgt_halo),
        us=3,
    )
    reps = lax.axis_size("rep")
    other = lax.ppermute(costs, "rep", [(i, reps - 1 - i) for i in range(reps)])
    (gc,) = call(
        "decoder",
        decoder_kernel,
        [((px, n * slots), BF16)],
        [((2 * px, n * slots), BF16)],
        (info, costs, other, grad_hidden, w_in.T, b_in[:, None], w_in),
        scalars=1,
        us=3,
    )
    lanes = [
        (rows if qz is None else H) * (cols // per if qx is None else 1) * LANES
        for qz, qx in pieces
    ]
    sent = call(
        "send",
        partial(send_kernel, px, rows, cols, slots, pieces, starts, counts),
        [((px, w), BF16) for w in lanes],
        [],
        (info, gc, e_ids, m_ids),
        scalars=1,
        us=1,
    )
    got = [swap(x, qz, qx) for x, (qz, qx) in zip(sent, pieces)]
    sg, own = call(
        "own",
        partial(own_kernel, px, n, slots),
        [((n * px, channels), BF16), ((px, n, channels), F32)],
        [((ext_pad // LANES, n * pitch, LANES), F32), ((n * pitch, channels), F32)],
        (gc, e_ids, tgt_t, src_t),
        us=4,
    )
    halo_pad = -(-(ext - n) // 16) * 16
    (halo_t,) = call(
        "halo",
        partial(halo_kernel, px, [s - n for s in starts]),
        [((px, halo_pad, channels), BF16)],
        [((halo_pad * pitch, channels), F32)],
        tuple(src_halo),
        us=1,
    )
    (tg,) = call(
        "total",
        partial(total_kernel, px, n, slots, [per if qx is None else H for _, qx in pieces]),
        [((n * px, channels), BF16)],
        [((halo_pad * pitch, LANES), F32), ((n * pitch, channels), F32)],
        (own, halo_t, *got),
        us=3,
    )
    return sg.reshape(source.shape), tg.reshape(source.shape)


def solution(mesh):
    cells = P(("groups", "strip"), "sub", "rep", None)
    placed = (
        cells,
        cells,
        P(("groups", "strip"), "sub", None),
        P(("groups", "strip"), "sub", None, None),
        P(),
        P(),
        P(),
    )
    return jax.shard_map(
        shards, mesh=mesh, in_specs=placed, out_specs=(cells, cells), check_vma=False
    )
```

time: 75.3 us -> 63.6 us (0.84)
  the two profiles are of different devices: /device:TPU:12 before, /device:TPU:0 now
where the time goes in v2:
time: 63.6 us; the launch traced here: 63.1 us
  starting transfers between devices  25.7 us (40%)
  local copies, waits for them, and re-layouts  20.3 us (32%)
  Pallas kernels  14.6 us (23%)
  waiting for transfers between devices  1.41 us (2%)
  between operations  1.01 us (2%)
    ppermute x15, starting transfers between devices, swap(): return lax.ppermute(x, ('strip', 'sub'), pairs)  25.6 us
    pallas_call x7, Pallas kernels, call(): pl.pallas_call(kernel, name=name, out_shape=[jax.ShapeDtypeStruct(s, d) f...  14.6 us
    unnamed x54, local copies, waits for them, and re-layouts  13 us
    dynamic_slice x4, local copies, waits for them, and re-layouts, boundary(): x = lax.dynamic_slice_in_dim(x, facing(qx, cols, sub_at), H, 1)  3.92 us
    dynamic_slice x2, local copies, waits for them, and re-layouts, boundary(): x = lax.dynamic_slice_in_dim(x, facing(qz, rows, strip_at), H, 0)  3.03 us
    ppermute x15, waiting for transfers between devices, swap(): return lax.ppermute(x, ('strip', 'sub'), pairs)  1.41 us
  transfers between devices with their start and end apart: 16, of which 1 were waited for; matrix products, arithmetic and copies ran while one was open for 9% of the time, Pallas kernels for 17%

profile of v2, /device:TPU:0, one launch (start us, length us, event | category | flops | bytes accessed | tf_op | source)
XLA Modules:
  0.0 63.1 jit_solution(10531688610277667488)
XLA Ops:
  0.7 1.7 %constant_dynamic-slice_fusion.8 = (bf16[3,3,64,128]{3,2,1,0:T(8,128)(2,1)S(1)}, bf16[3,3,64,128]{3,2,1,0:T(8,128)(2,1)}) fusion(bf16[4,8,64,128]{3,2,1,0:T(8,128)(2,1)} %param.8, s32[]{:T(128)S(6)} %select_n.214, s32[]{:T(128)S(6)} %select_n.213, s32[]{:T(128)S(6)} %select_n.212), kind=kLoop, calls=%fused_computation.50 | loop fusion | bytes 589836 | tf_op jit(solution)/shard_map/dynamic_slice | solution.py:331
  2.5 4.0 %collective-permute-start = (bf16[3,3,64,128]{3,2,1,0:T(8,128)(2,1)}, bf16[3,3,64,128]{3,2,1,0:T(8,128)(2,1)S(1)}, u32[]{:S(2)}, u32[]{:S(2)}) collective-permute-start(bf16[3,3,64,128]{3,2,1,0:T(8,128)(2,1)} %get-tuple-element.33), channel_id=1, source_target_pairs={{0,6},{2,4},{4,2},{6,0},{8,14},{10,12},{12,10},{14,8},{1,7},{3,5},... | collective-permute-start | bytes 442376 | tf_op jit(solution)/shard_map/ppermute | solution.py:37
  7.1 2.1 %constant_dynamic-slice_fusion.6 = (bf16[3,8,64,128]{3,2,1,0:T(8,128)(2,1)S(1)}, bf16[3,8,64,128]{3,2,1,0:T(8,128)(2,1)}) fusion(bf16[4,8,64,128]{3,2,1,0:T(8,128)(2,1)} %param.8, s32[]{:T(128)} %select_n.185, s32[]{:T(128)} %select_n.183), kind=kLoop, calls=%fused_computation.48 | loop fusion | bytes 1572872 | tf_op jit(solution)/shard_map/dynamic_slice | solution.py:329
  9.2 4.4 %collective-permute-start.2 = (bf16[3,8,64,128]{3,2,1,0:T(8,128)(2,1)}, bf16[3,8,64,128]{3,2,1,0:T(8,128)(2,1)S(1)}, u32[]{:S(2)}, u32[]{:S(2)}) collective-permute-start(bf16[3,8,64,128]{3,2,1,0:T(8,128)(2,1)} %get-tuple-element.31), channel_id=1, source_target_pairs={{0,4},{2,6},{4,0},{6,2},{8,12},{10,14},{12,8},{14,10},{1,5},{3,7},... | collective-permute-start | bytes 1179656 | tf_op jit(solution)/shard_map/ppermute | solution.py:37
  14.2 0.7 %constant_dynamic-slice_fusion.5 = bf16[4,3,64,128]{3,2,1,0:T(8,128)(2,1)} fusion(bf16[4,8,64,128]{3,2,1,0:T(8,128)(2,1)S(1)} %copy-done, s32[]{:T(128)} %select_n.187), kind=kLoop, calls=%fused_computation.47 | loop fusion | bytes 393220 | tf_op jit(solution)/shard_map/dynamic_slice | solution.py:331
  14.9 1.5 %collective-permute-start.4 = (bf16[4,3,64,128]{3,2,1,0:T(8,128)(2,1)}, bf16[4,3,64,128]{3,2,1,0:T(8,128)(2,1)S(1)}, u32[]{:S(2)}, u32[]{:S(2)}) collective-permute-start(bf16[4,3,64,128]{3,2,1,0:T(8,128)(2,1)} %constant_dynamic-slice_fusion.5), channel_id=1, source_target_pairs={{0,2},{2,0},{4,6},{6,4},{8,10},{10,8},{12,14},{14,12},{1,3},{3,1},... | collective-permute-start | bytes 589832 | tf_op jit(solution)/shard_map/ppermute | solution.py:37
  17.4 1.0 %constant_dynamic-slice_fusion.1 = (bf16[3,8,64,128]{3,2,1,0:T(8,128)(2,1)}, bf16[3,8,64,128]{3,2,1,0:T(8,128)(2,1)}) fusion(bf16[4,8,64,128]{3,2,1,0:T(8,128)(2,1)S(1)} %copy-done.1, s32[]{:T(128)} %select_n.185, s32[]{:T(128)} %select_n.183), kind=kLoop, calls=%fused_computation.43 | loop fusion | bytes 1572872 | tf_op jit(solution)/shard_map/dynamic_slice | solution.py:329
  19.0 1.2 %collective-permute-start.8 = (bf16[3,8,64,128]{3,2,1,0:T(8,128)(2,1)}, bf16[3,8,64,128]{3,2,1,0:T(8,128)(2,1)S(1)}, u32[]{:S(2)}, u32[]{:S(2)}) collective-permute-start(bf16[3,8,64,128]{3,2,1,0:T(8,128)(2,1)} %get-tuple-element.27), channel_id=1, source_target_pairs={{0,4},{2,6},{4,0},{6,2},{8,12},{10,14},{12,8},{14,10},{1,5},{3,7},... | collective-permute-start | bytes 1179656 | tf_op jit(solution)/shard_map/ppermute | solution.py:37
  22.3 1.4 %collective-permute-done.2 = bf16[3,8,64,128]{3,2,1,0:T(8,128)(2,1)S(1)} collective-permute-done((bf16[3,8,64,128]{3,2,1,0:T(8,128)(2,1)}, bf16[3,8,64,128]{3,2,1,0:T(8,128)(2,1)S(1)}, u32[]{:S(2)}, u32[]{:S(2)}) %collective-permute-start.2) | collective-permute-done | bytes 393248 | tf_op jit(solution)/shard_map/ppermute | solution.py:37
  23.7 0.7 %copy-done.6 = bf16[3,8,64,128]{3,2,1,0:T(8,128)(2,1)} copy-done((bf16[3,8,64,128]{3,2,1,0:T(8,128)(2,1)}, bf16[3,8,64,128]{3,2,1,0:T(8,128)(2,1)S(1)}, u32[]{:S(2)}) %copy-start.6) | copy-done | bytes 393240
  24.5 0.8 %copy-done.8 = bf16[3,8,64,128]{3,2,1,0:T(8,128)(2,1)} copy-done((bf16[3,8,64,128]{3,2,1,0:T(8,128)(2,1)}, bf16[3,8,64,128]{3,2,1,0:T(8,128)(2,1)S(1)}, u32[]{:S(2)}) %copy-start.8) | copy-done | bytes 393240
  25.2 1.0 %copy-done.7 = bf16[3,8,64,128]{3,2,1,0:T(8,128)(2,1)S(1)} copy-done((bf16[3,8,64,128]{3,2,1,0:T(8,128)(2,1)S(1)}, bf16[3,8,64,128]{3,2,1,0:T(8,128)(2,1)}, u32[]{:S(2)}) %copy-start.7) | copy-done | bytes 393240
  26.2 1.0 %copy-done.9 = bf16[3,8,64,128]{3,2,1,0:T(8,128)(2,1)S(1)} copy-done((bf16[3,8,64,128]{3,2,1,0:T(8,128)(2,1)S(1)}, bf16[3,8,64,128]{3,2,1,0:T(8,128)(2,1)}, u32[]{:S(2)}) %copy-start.9) | copy-done | bytes 393240
  27.2 0.9 %copy-done.13 = bf16[4,3,64,128]{3,2,1,0:T(8,128)(2,1)S(1)} copy-done((bf16[4,3,64,128]{3,2,1,0:T(8,128)(2,1)S(1)}, bf16[4,3,64,128]{3,2,1,0:T(8,128)(2,1)}, u32[]{:S(2)}) %copy-start.13) | copy-done | bytes 196632
  28.1 0.9 %copy-done.15 = bf16[3,3,64,128]{3,2,1,0:T(8,128)(2,1)S(1)} copy-done((bf16[3,3,64,128]{3,2,1,0:T(8,128)(2,1)S(1)}, bf16[3,3,64,128]{3,2,1,0:T(8,128)(2,1)}, u32[]{:S(2)}) %copy-start.15) | copy-done | bytes 147480
  29.1 0.9 %copy-done.17 = bf16[3,3,64,128]{3,2,1,0:T(8,128)(2,1)S(1)} copy-done((bf16[3,3,64,128]{3,2,1,0:T(8,128)(2,1)S(1)}, bf16[3,3,64,128]{3,2,1,0:T(8,128)(2,1)}, u32[]{:S(2)}) %copy-start.17) | copy-done | bytes 147480
  30.0 2.7 %corr.1 = (bf16[64,1024]{1,0:T(8,128)(2,1)S(1)}, bf16[64,128,128]{2,1,0:T(8,128)(2,1)S(1)}) custom-call(bf16[64,32,128]{2,1,0:T(8,128)(2,1)S(1)} %get-tuple-element.14.refs_0_, bf16[64,32,128]{2,1,0:T(8,128)(2,1)S(1)} %get-tuple-element.15.refs_1_.src_t, s32[8,128]{1,0:T(8,128)S(1)} %reshape.62.refs_2_.e_ref, bf16[576,128]{1,0:T(8,128)(2,1)S(1)} %bitcast.67, ...), custom_call_target="tpu_custom_call" | custom-call | bytes 9000000 | tf_op jit(solution)/shard_map/corr/pallas_call | solution.py:299
  33.5 1.5 %collective-permute-start.10 = (bf16[4,3,64,128]{3,2,1,0:T(8,128)(2,1)}, bf16[4,3,64,128]{3,2,1,0:T(8,128)(2,1)}, u32[]{:S(2)}, u32[]{:S(2)}) collective-permute-start(bf16[4,3,64,128]{3,2,1,0:T(8,128)(2,1)} %constant_dynamic-slice_fusion), channel_id=1, source_target_pairs={{0,2},{2,0},{4,6},{6,4},{8,10},{10,8},{12,14},{14,12},{1,3},{3,1},... | collective-permute-start | bytes 589832 | tf_op jit(solution)/shard_map/ppermute | solution.py:37
  35.0 0.8 %constant_dynamic-slice_fusion.3 = (bf16[3,3,64,128]{3,2,1,0:T(8,128)(2,1)}, bf16[3,3,64,128]{3,2,1,0:T(8,128)(2,1)}) fusion(bf16[4,8,64,128]{3,2,1,0:T(8,128)(2,1)S(1)} %copy-done.1, s32[]{:T(128)S(6)} %select_n.214, s32[]{:T(128)S(6)} %select_n.213, s32[]{:T(128)S(6)} %select_n.212), kind=kLoop, calls=%fused_computation.45 | loop fusion | bytes 589836 | tf_op jit(solution)/shard_map/dynamic_slice | solution.py:331
  35.7 2.4 %collective-permute-start.6 = (bf16[3,3,64,128]{3,2,1,0:T(8,128)(2,1)}, bf16[3,3,64,128]{3,2,1,0:T(8,128)(2,1)S(1)}, u32[]{:S(2)}, u32[]{:S(2)}) collective-permute-start(bf16[3,3,64,128]{3,2,1,0:T(8,128)(2,1)} %get-tuple-element.29), channel_id=1, source_target_pairs={{0,6},{2,4},{4,2},{6,0},{8,14},{10,12},{12,10},{14,8},{1,7},{3,5},... | collective-permute-start | bytes 442376 | tf_op jit(solution)/shard_map/ppermute | solution.py:37
  39.9 1.2 %copy-done.5 = f32[256,1024]{1,0:T(8,128)S(1)} copy-done((f32[256,1024]{1,0:T(8,128)S(1)}, f32[256,1024]{1,0:T(8,128)}, u32[]{:S(2)}) %copy-start.5) | copy-done | bytes 1048600
  41.1 0.8 %copy-done.11 = bf16[128,256]{1,0:T(8,128)(2,1)S(1)} copy-done((bf16[128,256]{1,0:T(8,128)(2,1)S(1)}, bf16[128,256]{1,0:T(8,128)(2,1)}, u32[]{:S(2)}) %copy-start.11) | copy-done | bytes 65560
  42.0 0.9 %copy-done.19 = bf16[64,1024]{1,0:T(8,128)(2,1)S(1)} copy-done((bf16[64,1024]{1,0:T(8,128)(2,1)S(1)}, bf16[64,1024]{1,0:T(8,128)(2,1)}, u32[]{:S(2)}) %copy-start.19) | copy-done | bytes 131096
  42.9 0.9 %copy-done.21 = bf16[64,1024]{1,0:T(8,128)(2,1)S(1)} copy-done((bf16[64,1024]{1,0:T(8,128)(2,1)S(1)}, bf16[64,1024]{1,0:T(8,128)(2,1)}, u32[]{:S(2)}) %copy-start.21) | copy-done | bytes 131096
  43.8 1.9 %decoder.1.gc_ref = bf16[64,1024]{1,0:T(8,128)(2,1)S(1)} custom-call(s32[5]{0:T(128)S(1)} %stack.23.info_ref, bf16[64,1024]{1,0:T(8,128)(2,1)S(1)} %copy-done.19, bf16[64,1024]{1,0:T(8,128)(2,1)S(1)} %copy-done.21, f32[256,1024]{1,0:T(8,128)S(1)} %copy-done.5, bf16[256,128]{1,0:T(8,128)(2,1)S(1)} %bitcast.63, f32[256,1]{1,0:T(8,128)S(1)} %copy.13.b_ref, ...), custom_call_target="tpu_custom_call" | custom-call | bytes 9000000 | tf_op jit(solution)/shard_map/decoder/pallas_call | solution.py:299
  45.7 1.1 %send.1 = (bf16[64,384]{1,0:T(8,128)(2,1)S(1)}, bf16[64,384]{1,0:T(8,128)(2,1)S(1)}, bf16[64,768]{1,0:T(8,128)(2,1)S(1)}, bf16[64,768]{1,0:T(8,128)(2,1)S(1)}, bf16[64,512]{1,0:T(8,128)(2,1)S(1)}) custom-call(s32[5]{0:T(128)S(1)} %stack.23.info_ref, bf16[64,1024]{1,0:T(8,128)(2,1)S(1)} %decoder.1.gc_ref, s32[8,128]{1,0:T(8,128)S(1)} %reshape.62.refs_2_.e_ref, ...), custom_call_target="tpu_custom_call" | custom-call | bytes 3000000 | tf_op jit(solution)/shard_map/send/pallas_call | solution.py:299
  46.9 1.9 %collective-permute-start.13 = (bf16[64,768]{1,0:T(8,128)(2,1)S(1)}, bf16[64,768]{1,0:T(8,128)(2,1)S(1)}, u32[]{:S(2)}, u32[]{:S(2)}) collective-permute-start(bf16[64,768]{1,0:T(8,128)(2,1)S(1)} %get-tuple-element.23), channel_id=1, source_target_pairs={{0,4},{2,6},{4,0},{6,2},{8,12},{10,14},{12,8},{14,10},{1,5},{3,7},... | collective-permute-start | bytes 294920 | tf_op jit(solution)/shard_map/ppermute | solution.py:37
  49.5 1.2 %collective-permute-start.15 = (bf16[64,512]{1,0:T(8,128)(2,1)S(1)}, bf16[64,512]{1,0:T(8,128)(2,1)S(1)}, u32[]{:S(2)}, u32[]{:S(2)}) collective-permute-start(bf16[64,512]{1,0:T(8,128)(2,1)S(1)} %get-tuple-element.25), channel_id=1, source_target_pairs={{0,2},{2,0},{4,6},{6,4},{8,10},{10,8},{12,14},{14,12},{1,3},{3,1},... | collective-permute-start | bytes 196616 | tf_op jit(solution)/shard_map/ppermute | solution.py:37
  50.7 3.6 %collective-permute-start.11 = (bf16[64,384]{1,0:T(8,128)(2,1)S(1)}, bf16[64,384]{1,0:T(8,128)(2,1)S(1)}, u32[]{:S(2)}, u32[]{:S(2)}) collective-permute-start(bf16[64,384]{1,0:T(8,128)(2,1)S(1)} %get-tuple-element.21), channel_id=1, source_target_pairs={{0,6},{2,4},{4,2},{6,0},{8,14},{10,12},{12,10},{14,8},{1,7},{3,5},... | collective-permute-start | bytes 147464 | tf_op jit(solution)/shard_map/ppermute | solution.py:37
  54.9 1.4 %halo.1.halo_t = bf16[64,80,128]{2,1,0:T(8,128)(2,1)S(1)} custom-call(bf16[576,128]{1,0:T(8,128)(2,1)S(1)} %bitcast.65, bf16[576,128]{1,0:T(8,128)(2,1)S(1)} %bitcast.66, bf16[1536,128]{1,0:T(8,128)(2,1)S(1)} %bitcast.59, bf16[1536,128]{1,0:T(8,128)(2,1)S(1)} %bitcast.60, bf16[768,128]{1,0:T(8,128)(2,1)} %bitcast.21.refs_4_), custom_call_target="tpu_custom_call" | custom-call | bytes 3000000 | tf_op jit(solution)/shard_map/halo/pallas_call | solution.py:299
  56.3 3.8 %own.1 = (bf16[2048,128]{1,0:T(8,128)(2,1)}, f32[64,32,128]{2,1,0:T(8,128)S(1)}) custom-call(bf16[64,1024]{1,0:T(8,128)(2,1)S(1)} %decoder.1.gc_ref, s32[8,128]{1,0:T(8,128)S(1)} %reshape.62.refs_2_.e_ref, bf16[64,128,128]{2,1,0:T(8,128)(2,1)S(1)} %get-tuple-element.18.tgt_t, bf16[64,32,128]{2,1,0:T(8,128)(2,1)S(1)} %copy-done.3), custom_call_target="tpu_custom_call" | custom-call | bytes 12000000 | tf_op jit(solution)/shard_map/own/pallas_call | solution.py:299
  60.1 2.9 %total.1 = bf16[2048,128]{1,0:T(8,128)(2,1)} custom-call(f32[64,32,128]{2,1,0:T(8,128)S(1)} %get-tuple-element.20.own_ref, bf16[64,80,128]{2,1,0:T(8,128)(2,1)S(1)} %halo.1.halo_t, bf16[64,384]{1,0:T(8,128)(2,1)S(1)} %collective-permute-done.11.refs_0_, bf16[64,384]{1,0:T(8,128)(2,1)S(1)} %collective-permute-done.12.refs_1_, ...), custom_call_target="tpu_custom_call" | custom-call | bytes 9000000 | tf_op jit(solution)/shard_map/total/pallas_call | solution.py:299
  (74 shorter events, 8.8 us)
Async XLA Ops:
  0.6 13.6 %copy-start = (bf16[4,8,64,128]{3,2,1,0:T(8,128)(2,1)S(1)}, bf16[4,8,64,128]{3,2,1,0:T(8,128)(2,1)}, u32[]{:S(2)}) copy-start(bf16[4,8,64,128]{3,2,1,0:T(8,128)(2,1)} %param.8) | copy-start | bytes 1572868
  0.6 15.8 %copy-start.24 = (s32[4,8,25]{2,1,0:T(8,128)S(1)}, s32[4,8,25]{2,1,0:T(8,128)}, u32[]{:S(2)}) copy-start(s32[4,8,25]{2,1,0:T(8,128)} %param.9) | copy-start | bytes 9604
  0.7 15.9 %copy-start.23 = (bf16[4,8,25,128]{3,1,2,0:T(8,128)(2,1)S(1)}, bf16[4,8,25,128]{3,1,2,0:T(8,128)(2,1)}, u32[]{:S(2)}) copy-start(bf16[4,8,25,128]{3,1,2,0:T(8,128)(2,1)} %param.10) | copy-start | bytes 614404
  0.7 16.0 %copy-start.1 = (bf16[4,8,64,128]{3,2,1,0:T(8,128)(2,1)S(1)}, bf16[4,8,64,128]{3,2,1,0:T(8,128)(2,1)}, u32[]{:S(2)}) copy-start(bf16[4,8,64,128]{3,2,1,0:T(8,128)(2,1)} %param.7) | copy-start | bytes 1572868
  0.7 16.0 %copy-start.22 = (bf16[256,128]{1,0:T(8,128)(2,1)S(1)}, bf16[256,128]{1,0:T(8,128)(2,1)}, u32[]{:S(2)}) copy-start(bf16[256,128]{1,0:T(8,128)(2,1)} %w_out_ref.1) | copy-start | bytes 196612
  2.5 15.9 %collective-permute-start = (bf16[3,3,64,128]{3,2,1,0:T(8,128)(2,1)}, bf16[3,3,64,128]{3,2,1,0:T(8,128)(2,1)S(1)}, u32[]{:S(2)}, u32[]{:S(2)}) collective-permute-start(bf16[3,3,64,128]{3,2,1,0:T(8,128)(2,1)} %get-tuple-element.33), channel_id=1, source_target_pairs={{0,6},{2,4},{4,2},{6,0},{8,14},{10,12},{12,10},{14,8},{1,7},{3,5},... | collective-permute-start | bytes 442376 | tf_op jit(solution)/shard_map/ppermute | solution.py:37
  6.5 13.8 %collective-permute-start.1 = (bf16[3,3,64,128]{3,2,1,0:T(8,128)(2,1)S(1)}, bf16[3,3,64,128]{3,2,1,0:T(8,128)(2,1)S(1)}, u32[]{:S(2)}, u32[]{:S(2)}) collective-permute-start(bf16[3,3,64,128]{3,2,1,0:T(8,128)(2,1)S(1)} %get-tuple-element.32), channel_id=1, source_target_pairs={{4,10},{6,8},{8,6},{10,4},{5,11},{7,9},{9,7},{11,5},{20,26},{22,24... | collective-permute-start | bytes 442376 | tf_op jit(solution)/shard_map/ppermute | solution.py:37
  9.2 14.5 %collective-permute-start.2 = (bf16[3,8,64,128]{3,2,1,0:T(8,128)(2,1)}, bf16[3,8,64,128]{3,2,1,0:T(8,128)(2,1)S(1)}, u32[]{:S(2)}, u32[]{:S(2)}) collective-permute-start(bf16[3,8,64,128]{3,2,1,0:T(8,128)(2,1)} %get-tuple-element.31), channel_id=1, source_target_pairs={{0,4},{2,6},{4,0},{6,2},{8,12},{10,14},{12,8},{14,10},{1,5},{3,7},... | collective-permute-start | bytes 1179656 | tf_op jit(solution)/shard_map/ppermute | solution.py:37
  13.5 10.9 %collective-permute-start.3 = (bf16[3,8,64,128]{3,2,1,0:T(8,128)(2,1)S(1)}, bf16[3,8,64,128]{3,2,1,0:T(8,128)(2,1)S(1)}, u32[]{:S(2)}, u32[]{:S(2)}) collective-permute-start(bf16[3,8,64,128]{3,2,1,0:T(8,128)(2,1)S(1)} %get-tuple-element.30), channel_id=1, source_target_pairs={{4,8},{6,10},{8,4},{10,6},{5,9},{7,11},{9,5},{11,7},{20,24},{22,26... | collective-permute-start | bytes 1179656 | tf_op jit(solution)/shard_map/ppermute | solution.py:37
  14.9 6.7 %collective-permute-start.4 = (bf16[4,3,64,128]{3,2,1,0:T(8,128)(2,1)}, bf16[4,3,64,128]{3,2,1,0:T(8,128)(2,1)S(1)}, u32[]{:S(2)}, u32[]{:S(2)}) collective-permute-start(bf16[4,3,64,128]{3,2,1,0:T(8,128)(2,1)} %constant_dynamic-slice_fusion.5), channel_id=1, source_target_pairs={{0,2},{2,0},{4,6},{6,4},{8,10},{10,8},{12,14},{14,12},{1,3},{3,1},... | collective-permute-start | bytes 589832 | tf_op jit(solution)/shard_map/ppermute | solution.py:37
  17.4 7.9 %copy-start.4 = (f32[256,1024]{1,0:T(8,128)}, f32[256,1024]{1,0:T(8,128)S(1)}, u32[]{:S(2)}) copy-start(f32[256,1024]{1,0:T(8,128)S(1)} %get-tuple-element.17.gh_ref) | copy-start | bytes 3145732
  17.4 16.1 %copy-start.2 = (bf16[64,32,128]{2,1,0:T(8,128)(2,1)}, bf16[64,32,128]{2,1,0:T(8,128)(2,1)S(1)}, u32[]{:S(2)}) copy-start(bf16[64,32,128]{2,1,0:T(8,128)(2,1)S(1)} %get-tuple-element.15.refs_1_.src_t) | copy-start | bytes 1572868
  17.4 22.1 %copy-start.10 = (bf16[128,256]{1,0:T(8,128)(2,1)S(1)}, bf16[128,256]{1,0:T(8,128)(2,1)}, u32[]{:S(2)}) copy-start(bf16[128,256]{1,0:T(8,128)(2,1)} %w_ref.1) | copy-start | bytes 196612
  18.4 21.2 %copy-start.25 = (f32[256]{0:T(256)S(1)}, f32[256]{0:T(256)}, u32[]{:S(2)}) copy-start(f32[256]{0:T(256)} %param.12) | copy-start | bytes 3076
  19.0 31.6 %collective-permute-start.8 = (bf16[3,8,64,128]{3,2,1,0:T(8,128)(2,1)}, bf16[3,8,64,128]{3,2,1,0:T(8,128)(2,1)S(1)}, u32[]{:S(2)}, u32[]{:S(2)}) collective-permute-start(bf16[3,8,64,128]{3,2,1,0:T(8,128)(2,1)} %get-tuple-element.27), channel_id=1, source_target_pairs={{0,4},{2,6},{4,0},{6,2},{8,12},{10,14},{12,8},{14,10},{1,5},{3,7},... | collective-permute-start | bytes 1179656 | tf_op jit(solution)/shard_map/ppermute | solution.py:37
  21.0 33.3 %collective-permute-start.9 = (bf16[3,8,64,128]{3,2,1,0:T(8,128)(2,1)}, bf16[3,8,64,128]{3,2,1,0:T(8,128)(2,1)S(1)}, u32[]{:S(2)}, u32[]{:S(2)}) collective-permute-start(bf16[3,8,64,128]{3,2,1,0:T(8,128)(2,1)} %get-tuple-element.26), channel_id=1, source_target_pairs={{4,8},{6,10},{8,4},{10,6},{5,9},{7,11},{9,5},{11,7},{20,24},{22,26... | collective-permute-start | bytes 1179656 | tf_op jit(solution)/shard_map/ppermute | solution.py:37
  25.2 1.0 %copy-start.7 = (bf16[3,8,64,128]{3,2,1,0:T(8,128)(2,1)S(1)}, bf16[3,8,64,128]{3,2,1,0:T(8,128)(2,1)}, u32[]{:S(2)}) copy-start(bf16[3,8,64,128]{3,2,1,0:T(8,128)(2,1)} %copy-done.6) | copy-start | bytes 1179652
  26.2 1.0 %copy-start.9 = (bf16[3,8,64,128]{3,2,1,0:T(8,128)(2,1)S(1)}, bf16[3,8,64,128]{3,2,1,0:T(8,128)(2,1)}, u32[]{:S(2)}) copy-start(bf16[3,8,64,128]{3,2,1,0:T(8,128)(2,1)} %copy-done.8) | copy-start | bytes 1179652
  27.2 0.9 %copy-start.13 = (bf16[4,3,64,128]{3,2,1,0:T(8,128)(2,1)S(1)}, bf16[4,3,64,128]{3,2,1,0:T(8,128)(2,1)}, u32[]{:S(2)}) copy-start(bf16[4,3,64,128]{3,2,1,0:T(8,128)(2,1)} %copy-done.12) | copy-start | bytes 589828
  28.1 0.9 %copy-start.15 = (bf16[3,3,64,128]{3,2,1,0:T(8,128)(2,1)S(1)}, bf16[3,3,64,128]{3,2,1,0:T(8,128)(2,1)}, u32[]{:S(2)}) copy-start(bf16[3,3,64,128]{3,2,1,0:T(8,128)(2,1)} %copy-done.14) | copy-start | bytes 442372
  32.7 5.4 %copy-start.18 = (bf16[64,1024]{1,0:T(8,128)(2,1)}, bf16[64,1024]{1,0:T(8,128)(2,1)S(1)}, u32[]{:S(2)}) copy-start(bf16[64,1024]{1,0:T(8,128)(2,1)S(1)} %get-tuple-element.16.mine_ref) | copy-start | bytes 393220
  32.7 5.4 %collective-permute-start.5 = (bf16[64,1024]{1,0:T(8,128)(2,1)S(1)}, bf16[64,1024]{1,0:T(8,128)(2,1)S(1)}, u32[]{:S(2)}, u32[]{:S(2)}) collective-permute-start(bf16[64,1024]{1,0:T(8,128)(2,1)S(1)} %get-tuple-element.16.mine_ref), channel_id=1, source_target_pairs={{0,1},{1,0},{2,3},{3,2},{4,5},{5,4},{6,7},{7,6},{8,9},{9,8},{10,11... | collective-permute-start | bytes 393224 | tf_op jit(solution)/shard_map/ppermute | solution.py:379
  33.5 16.0 %collective-permute-start.10 = (bf16[4,3,64,128]{3,2,1,0:T(8,128)(2,1)}, bf16[4,3,64,128]{3,2,1,0:T(8,128)(2,1)}, u32[]{:S(2)}, u32[]{:S(2)}) collective-permute-start(bf16[4,3,64,128]{3,2,1,0:T(8,128)(2,1)} %constant_dynamic-slice_fusion), channel_id=1, source_target_pairs={{0,2},{2,0},{4,6},{6,4},{8,10},{10,8},{12,14},{14,12},{1,3},{3,1},... | collective-permute-start | bytes 589832 | tf_op jit(solution)/shard_map/ppermute | solution.py:37
  35.7 11.2 %collective-permute-start.6 = (bf16[3,3,64,128]{3,2,1,0:T(8,128)(2,1)}, bf16[3,3,64,128]{3,2,1,0:T(8,128)(2,1)S(1)}, u32[]{:S(2)}, u32[]{:S(2)}) collective-permute-start(bf16[3,3,64,128]{3,2,1,0:T(8,128)(2,1)} %get-tuple-element.29), channel_id=1, source_target_pairs={{0,6},{2,4},{4,2},{6,0},{8,14},{10,12},{12,10},{14,8},{1,7},{3,5},... | collective-permute-start | bytes 442376 | tf_op jit(solution)/shard_map/ppermute | solution.py:37
  38.8 10.0 %collective-permute-start.7 = (bf16[3,3,64,128]{3,2,1,0:T(8,128)(2,1)}, bf16[3,3,64,128]{3,2,1,0:T(8,128)(2,1)S(1)}, u32[]{:S(2)}, u32[]{:S(2)}) collective-permute-start(bf16[3,3,64,128]{3,2,1,0:T(8,128)(2,1)} %get-tuple-element.28), channel_id=1, source_target_pairs={{4,10},{6,8},{8,6},{10,4},{5,11},{7,9},{9,7},{11,5},{20,26},{22,24... | collective-permute-start | bytes 442376 | tf_op jit(solution)/shard_map/ppermute | solution.py:37
  39.9 1.2 %copy-start.5 = (f32[256,1024]{1,0:T(8,128)S(1)}, f32[256,1024]{1,0:T(8,128)}, u32[]{:S(2)}) copy-start(f32[256,1024]{1,0:T(8,128)} %copy-done.4) | copy-start | bytes 3145732
  43.8 12.5 %copy-start.3 = (bf16[64,32,128]{2,1,0:T(8,128)(2,1)S(1)}, bf16[64,32,128]{2,1,0:T(8,128)(2,1)}, u32[]{:S(2)}) copy-start(bf16[64,32,128]{2,1,0:T(8,128)(2,1)} %copy-done.2) | copy-start | bytes 1572868
  46.9 13.2 %collective-permute-start.13 = (bf16[64,768]{1,0:T(8,128)(2,1)S(1)}, bf16[64,768]{1,0:T(8,128)(2,1)S(1)}, u32[]{:S(2)}, u32[]{:S(2)}) collective-permute-start(bf16[64,768]{1,0:T(8,128)(2,1)S(1)} %get-tuple-element.23), channel_id=1, source_target_pairs={{0,4},{2,6},{4,0},{6,2},{8,12},{10,14},{12,8},{14,10},{1,5},{3,7},... | collective-permute-start | bytes 294920 | tf_op jit(solution)/shard_map/ppermute | solution.py:37
  48.8 11.3 %collective-permute-start.14 = (bf16[64,768]{1,0:T(8,128)(2,1)S(1)}, bf16[64,768]{1,0:T(8,128)(2,1)S(1)}, u32[]{:S(2)}, u32[]{:S(2)}) collective-permute-start(bf16[64,768]{1,0:T(8,128)(2,1)S(1)} %get-tuple-element.24), channel_id=1, source_target_pairs={{4,8},{6,10},{8,4},{10,6},{5,9},{7,11},{9,5},{11,7},{20,24},{22,26... | collective-permute-start | bytes 294920 | tf_op jit(solution)/shard_map/ppermute | solution.py:37
  49.5 10.7 %collective-permute-start.15 = (bf16[64,512]{1,0:T(8,128)(2,1)S(1)}, bf16[64,512]{1,0:T(8,128)(2,1)S(1)}, u32[]{:S(2)}, u32[]{:S(2)}) collective-permute-start(bf16[64,512]{1,0:T(8,128)(2,1)S(1)} %get-tuple-element.25), channel_id=1, source_target_pairs={{0,2},{2,0},{4,6},{6,4},{8,10},{10,8},{12,14},{14,12},{1,3},{3,1},... | collective-permute-start | bytes 196616 | tf_op jit(solution)/shard_map/ppermute | solution.py:37
  50.7 9.5 %collective-permute-start.11 = (bf16[64,384]{1,0:T(8,128)(2,1)S(1)}, bf16[64,384]{1,0:T(8,128)(2,1)S(1)}, u32[]{:S(2)}, u32[]{:S(2)}) collective-permute-start(bf16[64,384]{1,0:T(8,128)(2,1)S(1)} %get-tuple-element.21), channel_id=1, source_target_pairs={{0,6},{2,4},{4,2},{6,0},{8,14},{10,12},{12,10},{14,8},{1,7},{3,5},... | collective-permute-start | bytes 147464 | tf_op jit(solution)/shard_map/ppermute | solution.py:37
  54.3 5.9 %collective-permute-start.12 = (bf16[64,384]{1,0:T(8,128)(2,1)S(1)}, bf16[64,384]{1,0:T(8,128)(2,1)S(1)}, u32[]{:S(2)}, u32[]{:S(2)}) collective-permute-start(bf16[64,384]{1,0:T(8,128)(2,1)S(1)} %get-tuple-element.22), channel_id=1, source_target_pairs={{4,10},{6,8},{8,6},{10,4},{5,11},{7,9},{9,7},{11,5},{20,26},{22,24... | collective-permute-start | bytes 147464 | tf_op jit(solution)/shard_map/ppermute | solution.py:37
  (10 other events, 7.7 us)

commit v3 on v2

--- a/solution.py
+++ b/solution.py
@@ -53,7 +53,12 @@
     return jnp.where((index + q) % 2 == 0, extent - H, 0)
 
 
-def places(target_ids, base, rows, cols):
+def scale_of(n):
+    assert n & (n - 1) == 0
+    return n.bit_length() - 1
+
+
+def places(ids, base, rows, cols):
     total_cols = cols * lax.axis_size("sub")
     strip_at, sub_at = lax.axis_index("strip"), lax.axis_index("sub")
 
@@ -64,15 +69,31 @@
         turn = jnp.where(side == 0, -1, jnp.where(side == ahead, 0, 1))
         return turn, inner
 
-    row, col = target_ids // total_cols, target_ids % total_cols
+    row = lax.shift_right_arithmetic(ids, jnp.int32(scale_of(total_cols)))
+    col = ids & (total_cols - 1)
     tz, dr = split(row - strip_at * rows, rows, strip_at)
     tx, dc = split(col - sub_at * cols, cols, sub_at)
-    where_to = jnp.full(target_ids.shape, -1, jnp.int32)
+    where_to = jnp.full(ids.shape, -1, jnp.int32)
     for (qz, qx), start in base.items():
         here = (tz == (-1 if qz is None else qz)) & (tx == (-1 if qx is None else qx))
         width = cols if qx is None else H
         where_to = jnp.where(here, start + dr * width + dc, where_to)
-    return where_to, (row % rows) * cols + col % cols
+    assert scale_of(rows) + scale_of(cols) >= 0
+    return where_to, (row & (rows - 1)) * cols + (col & (cols - 1))
+
+
+def cut_kernel(pieces, rows, cols, x_ref, *refs):
+    out_refs, sems = refs[:-1], refs[-1]
+    strip_at, sub_at = lax.axis_index("strip"), lax.axis_index("sub")
+    copies = []
+    for i, ((qz, qx), ref) in enumerate(zip(pieces, out_refs)):
+        r = pl.ds(0, rows) if qz is None else pl.ds(facing(qz, rows, strip_at), H)
+        c = pl.ds(0, cols) if qx is None else pl.ds(facing(qx, cols, sub_at), H)
+        copies.append(pltpu.make_async_copy(x_ref.at[r, c], ref, sems.at[i]))
+    for copy in copies:
+        copy.start()
+    for copy in copies:
+        copy.wait()
 
 
 def loop(count, body, most=4):
@@ -111,8 +132,28 @@
     return hot(jnp.where(lane == j, e_ref[group : group + 1, :], -1), tile)
 
 
-def prep_kernel(px, n, slots, src_ref, tgt_ref, og_ref, w_out_ref, src_t, tgt_t, gh_ref, s32, t32, og):
-    pitch = px + 1
+def slotted(x, out_ref, table, slots):
+    n, picks = x.shape
+    per = LANES // slots
+    table[...] = jnp.full(table.shape, -1, jnp.int32)
+    table[:, :picks] = x
+    lane = lax.broadcasted_iota(jnp.int32, (n // per, LANES), 1) // slots
+    acc = jnp.full((n // per, LANES), -1, jnp.int32)
+    for j in range(per):
+        rows = table[pl.ds(j, n // per, stride=per), :]
+        acc = jnp.where(lane == j, rows if j == 0 else pltpu.roll(rows, j * slots, 1), acc)
+    out_ref[...] = acc
+
+
+def prep_kernel(base, rows, cols, slots, src_ref, tgt_ref, og_ref, ids_ref, w_in_ref, b_ref, w_out_ref, *refs):
+    src_t, tgt_t, gh_ref, wt_ref, bt_ref, e_ref, m_ref, s32, t32, og, table = refs
+    px, n, _ = src_t.shape
+    pitch = px + 1
+    e_at, m_at = places(ids_ref[...], base, rows, cols)
+    slotted(e_at, e_ref, table, slots)
+    slotted(m_at, m_ref, table, slots)
+    wt_ref[...] = w_in_ref[...].T
+    bt_ref[...] = jnp.broadcast_to(b_ref[...], (LANES, b_ref.shape[1])).T
     widen(s32, 0, src_ref, px, pitch)
     widen(t32, 0, tgt_ref, px, pitch)
 
@@ -176,28 +217,35 @@
     return 0.5 * (1.0 + th) + (0.5 * x) * ((1.0 - th) * (1.0 + th)) * inner
 
 
-def decoder_kernel(info_ref, mine_ref, other_ref, gh_ref, wt_ref, b_ref, w_ref, gc_ref, whole):
+def decoder_kernel(rows, cols, slots, pieces, starts, counts, *refs):
+    mine_ref, other_ref, gh_ref, wt_ref, bt_ref, w_ref, e_ref, m_ref = refs[:8]
+    gc_ref, out_refs, whole = refs[8], refs[9:-1], refs[-1]
     px = mine_ref.shape[0]
-    rep = info_ref[0]
+    rep = lax.axis_index("rep")
     whole[pl.ds(pl.multiple_of(rep * px, px), px), :] = mine_ref[...]
     whole[pl.ds(pl.multiple_of((1 - rep) * px, px), px), :] = other_ref[...]
     w_half = w_ref[pl.ds(pl.multiple_of(rep * px, px), px), :]
-    width = 2 * LANES
+    wide = 2
+    bias = jnp.concatenate([bt_ref[...]] * wide, axis=1)
+    width = wide * LANES
     for g in range(mine_ref.shape[1] // width):
         cut = slice(g * width, (g + 1) * width)
-        pre = jnp.dot(wt_ref[...], whole[:, cut], preferred_element_type=F32) + b_ref[...]
+        pre = jnp.dot(wt_ref[...], whole[:, cut], preferred_element_type=F32) + bias
         grad = (gh_ref[:, cut] * gelu_slope(pre)).astype(BF16)
         gc_ref[:, cut] = jnp.dot(w_half, grad, preferred_element_type=F32).astype(BF16)
-
-
-def send_kernel(px, rows, cols, slots, pieces, starts, counts, info_ref, gc_ref, e_ref, m_ref, *out_refs):
+    send(rows, cols, slots, pieces, starts, counts, gc_ref, e_ref, m_ref, out_refs)
+
+
+def send(rows, cols, slots, pieces, starts, counts, gc_ref, e_ref, m_ref, out_refs):
     per = LANES // slots
     wide = cols // per
+    strip_at, sub_at = lax.axis_index("strip"), lax.axis_index("sub")
     lane = lax.broadcasted_iota(jnp.int32, (1, LANES), 1) // slots
     for (qz, qx), start, count, ref in zip(pieces, starts, counts, out_refs):
-        r0 = 0 if qz is None else info_ref[1 + qz]
-        c0 = 0 if qx is None else info_ref[3 + qx]
-        half, shift = c0 // per, c0 % per
+        r0 = 0 if qz is None else facing(qz, rows, strip_at)
+        tail = None if qx is None else (sub_at + qx) % 2 == 0
+        half = 0 if qx is None else jnp.where(tail, (cols - H) // per, 0)
+        shift = 0 if qx is None else jnp.where(tail, (cols - H) % per, 0)
         i = 0
         for r in range(rows if qz is None else H):
             for h in range(wide if qx is None else 1):
@@ -205,9 +253,10 @@
                 e, m = e_ref[pl.ds(g, 1), :], m_ref[pl.ds(g, 1), :]
                 here = (e >= start) & (e < start + count)
                 to = jnp.where(here, (lane - shift) * slots + m, -1)
-                gc = gc_ref[:, pl.ds(pl.multiple_of(g * LANES, LANES), LANES)]
+                at = g * LANES
+                at = at if isinstance(at, int) else pl.multiple_of(at, LANES)
                 ref[:, i * LANES : (i + 1) * LANES] = lax.dot_general(
-                    gc, hot(to), NT, preferred_element_type=F32
+                    gc_ref[:, pl.ds(at, LANES)], hot(to), NT, preferred_element_type=F32
                 ).astype(BF16)
                 i += 1
 
@@ -292,18 +341,17 @@
 
 
 VM = pl.BlockSpec(memory_space=pltpu.VMEM)
-SM = pl.BlockSpec(memory_space=pltpu.SMEM)
-
-
-def call(name, kernel, outs, scratch, args, scalars=0, us=2.0):
+
+
+def call(name, kernel, outs, scratch, args, us=2.0):
     return pl.pallas_call(
         kernel,
         name=name,
         out_shape=[jax.ShapeDtypeStruct(s, d) for s, d in outs],
-        in_specs=[SM] * scalars + [VM] * (len(args) - scalars),
+        in_specs=[VM] * len(args),
         out_specs=[VM] * len(outs),
         scratch_shapes=[pltpu.VMEM(s, d) for s, d in scratch],
-        compiler_params=pltpu.CompilerParams(vmem_limit_bytes=28 * 2**20),
+        compiler_params=pltpu.CompilerParams(vmem_limit_bytes=24 * 2**20),
         cost_estimate=pl.CostEstimate(
             flops=0, bytes_accessed=int(us * 3 * 10**6), transcendentals=0
         ),
@@ -321,45 +369,50 @@
     assert n <= slots and cols % per == 0 and H <= per and groups * per == n
     pieces, base, ext = plan(rows, cols)
     ext_pad = -(-ext // LANES) * LANES
-    strip_at, sub_at = lax.axis_index("strip"), lax.axis_index("sub")
-    rep = lax.axis_index("rep")
-
-    def boundary(x, qz, qx):
-        if qz is not None:
-            x = lax.dynamic_slice_in_dim(x, facing(qz, rows, strip_at), H, 0)
-        if qx is not None:
-            x = lax.dynamic_slice_in_dim(x, facing(qx, cols, sub_at), H, 1)
-        return x
-
-    def halo_of(x):
-        got = [swap(boundary(x, qz, qx), qz, qx) for qz, qx in pieces]
+
+    shapes = [
+        (rows if qz is None else H, cols if qx is None else H, px, channels) for qz, qx in pieces
+    ]
+
+    def halo_of(name, x):
+        slabs = pl.pallas_call(
+            partial(cut_kernel, pieces, rows, cols),
+            name=name,
+            out_shape=[jax.ShapeDtypeStruct(s, BF16) for s in shapes],
+            in_specs=[pl.BlockSpec(memory_space=pl.ANY)],
+            out_specs=[VM] * len(pieces),
+            scratch_shapes=[pltpu.SemaphoreType.DMA((len(pieces),))],
+            compiler_params=pltpu.CompilerParams(vmem_limit_bytes=4 * 2**20),
+        )(x)
+        got = [swap(x, qz, qx) for x, (qz, qx) in zip(slabs, pieces)]
         return [h.reshape(-1, channels) for h in got]
 
-    tgt_halo = halo_of(target)
-    src_halo = halo_of(source)
+    tgt_halo = halo_of("cut_target", target)
+    src_halo = halo_of("cut_source", source)
     starts = [base[q] for q in pieces]
     counts = [h.shape[0] // px for h in tgt_halo]
-
-    def slotted(x):
-        return jnp.pad(x, ((0, 0), (0, slots - picks)), constant_values=-1).reshape(groups, LANES)
-
-    e_at, m_at = places(target_ids.reshape(n, picks), base, rows, cols)
-    e_ids, m_ids = slotted(e_at), slotted(m_at)
-    info = jnp.stack(
-        [rep]
-        + [facing(q, rows, strip_at) for q in (0, 1)]
-        + [facing(q, cols, sub_at) for q in (0, 1)]
-    ).astype(jnp.int32)
-
-    src_t, own_t, grad_hidden = call(
+    hidden = w_in.shape[1]
+    src_t, own_t, grad_hidden, w_t, b_t, e_ids, m_ids = call(
         "prep",
-        partial(prep_kernel, px, n, slots),
-        [((px, n, channels), BF16), ((px, n, channels), BF16), ((w_out.shape[0], n * slots), F32)],
-        [((n * pitch, channels), F32)] * 2 + [((n, slots, out_grad.shape[3]), F32)],
+        partial(prep_kernel, base, rows, cols, slots),
+        [
+            ((px, n, channels), BF16),
+            ((px, n, channels), BF16),
+            ((hidden, n * slots), F32),
+            ((hidden, 2 * px), BF16),
+            ((hidden, LANES), F32),
+            ((groups, LANES), jnp.int32),
+            ((groups, LANES), jnp.int32),
+        ],
+        [((n * pitch, channels), F32)] * 2
+        + [((n, slots, out_grad.shape[3]), F32), ((n, LANES), jnp.int32)],
         (
             source.reshape(n * px, channels),
             target.reshape(n * px, channels),
             out_grad.reshape(n, picks, out_grad.shape[3]),
+            target_ids.reshape(n, picks),
+            w_in,
+            b_in.reshape(1, hidden),
             w_out,
         ),
         us=4,
@@ -377,27 +430,17 @@
     )
     reps = lax.axis_size("rep")
     other = lax.ppermute(costs, "rep", [(i, reps - 1 - i) for i in range(reps)])
-    (gc,) = call(
-        "decoder",
-        decoder_kernel,
-        [((px, n * slots), BF16)],
-        [((2 * px, n * slots), BF16)],
-        (info, costs, other, grad_hidden, w_in.T, b_in[:, None], w_in),
-        scalars=1,
-        us=3,
-    )
     lanes = [
         (rows if qz is None else H) * (cols // per if qx is None else 1) * LANES
         for qz, qx in pieces
     ]
-    sent = call(
-        "send",
-        partial(send_kernel, px, rows, cols, slots, pieces, starts, counts),
-        [((px, w), BF16) for w in lanes],
-        [],
-        (info, gc, e_ids, m_ids),
-        scalars=1,
-        us=1,
+    gc, *sent = call(
+        "decoder",
+        partial(decoder_kernel, rows, cols, slots, pieces, starts, counts),
+        [((px, n * slots), BF16)] + [((px, w), BF16) for w in lanes],
+        [((2 * px, n * slots), BF16)],
+        (costs, other, grad_hidden, w_t, b_t, w_in, e_ids, m_ids),
+        us=3,
     )
     got = [swap(x, qz, qx) for x, (qz, qx) in zip(sent, pieces)]
     sg, own = call(

time: 63.6 us -> 60.7 us (0.954)
  local copies, waits for them, and re-layouts: 20.3 us -> 8.21 us
  starting transfers between devices: 25.7 us -> 31 us
  waiting for transfers between devices: 1.41 us -> 6.07 us
  Pallas kernels: 14.6 us -> 13.9 us
    dynamic_slice x6 -> x0, local copies, waits for them, and re-layouts: 6.95 us -> none  [the longest x4 3.92 us: boundary(): x = lax.dynamic_slice_in_dim(x, facing(qx, cols, sub_at), H, 1)]
    ppermute x15, starting transfers between devices: 25.6 us -> 31 us  [swap(): return lax.ppermute(x, ('strip', 'sub'), pairs)]
    unnamed x54 -> x19, local copies, waits for them, and re-layouts: 13 us -> 8.21 us
    ppermute x15, waiting for transfers between devices: 1.41 us -> 6.06 us  [swap(): return lax.ppermute(x, ('strip', 'sub'), pairs)]
    pallas_call x7 -> x6, Pallas kernels: 14.6 us -> 12.7 us  [call(): pl.pallas_call(kernel, name=name, out_shape=[jax.ShapeDtypeStruct(s, d) f...]
    pallas_call x0 -> x2, Pallas kernels: none -> 1.2 us  [halo_of(): pl.pallas_call(partial(cut_kernel, pieces, rows, cols), name=name, out_sh...]
  transfers between devices with their start and end apart: 16 -> 16, of which waited for: 1 -> 2; matrix products, arithmetic and copies ran while one was open for 9% -> 2% of each run, Pallas kernels for 17% -> 17%
where the time goes in v3:
time: 60.7 us; the launch traced here: 60.1 us
  starting transfers between devices  31 us (51%)
  Pallas kernels  13.9 us (23%)
  local copies, waits for them, and re-layouts  8.21 us (14%)
  waiting for transfers between devices  6.07 us (10%)
  between operations  0.81 us (1%)
    ppermute x15, starting transfers between devices, swap(): return lax.ppermute(x, ('strip', 'sub'), pairs)  31 us
    pallas_call x6, Pallas kernels, call(): pl.pallas_call(kernel, name=name, out_shape=[jax.ShapeDtypeStruct(s, d) f...  12.7 us
    unnamed x19, local copies, waits for them, and re-layouts  8.21 us
    ppermute x15, waiting for transfers between devices, swap(): return lax.ppermute(x, ('strip', 'sub'), pairs)  6.06 us
  transfers between devices with their start and end apart: 16, of which 2 were waited for; matrix products, arithmetic and copies ran while one was open for 2% of the time, Pallas kernels for 17%

profile of v3, /device:TPU:0, one launch (start us, length us, event | category | flops | bytes accessed | tf_op | source)
XLA Modules:
  0.0 60.1 jit_solution(10442609896939328132)
XLA Ops:
  0.6 1.0 %copy-done.2 = bf16[4,8,64,128]{3,2,1,0:T(8,128)(2,1)S(1)} copy-done((bf16[4,8,64,128]{3,2,1,0:T(8,128)(2,1)S(1)}, bf16[4,8,64,128]{3,2,1,0:T(8,128)(2,1)}, u32[]{:S(2)}) %copy-start.2) | copy-done | bytes 524312
  1.7 0.6 %cut_target.1 = (bf16[3,3,64,128]{3,2,1,0:T(8,128)(2,1)S(1)}, bf16[3,3,64,128]{3,2,1,0:T(8,128)(2,1)S(1)}, bf16[3,8,64,128]{3,2,1,0:T(8,128)(2,1)S(1)}, bf16[3,8...) custom-call(bf16[4,8,64,128]{3,2,1,0:T(8,128)(2,1)S(1)} %copy-done.2), custom_call_target="tpu_custom_call" | custom-call | tf_op jit(solution)/shard_map/cut_target/pallas_call | solution.py:378
  2.3 3.1 %collective-permute-start.2 = (bf16[3,8,64,128]{3,2,1,0:T(8,128)(2,1)S(1)}, bf16[3,8,64,128]{3,2,1,0:T(8,128)(2,1)S(1)}, u32[]{:S(2)}, u32[]{:S(2)}) collective-permute-start(bf16[3,8,64,128]{3,2,1,0:T(8,128)(2,1)S(1)} %get-tuple-element.34), channel_id=1, source_target_pairs={{0,4},{2,6},{4,0},{6,2},{8,12},{10,14},{12,8},{14,10},{1,5},{3,7},... | collective-permute-start | bytes 1179656 | tf_op jit(solution)/shard_map/ppermute | solution.py:37
  5.4 0.7 %collective-permute-start.3 = (bf16[3,8,64,128]{3,2,1,0:T(8,128)(2,1)S(1)}, bf16[3,8,64,128]{3,2,1,0:T(8,128)(2,1)S(1)}, u32[]{:S(2)}, u32[]{:S(2)}) collective-permute-start(bf16[3,8,64,128]{3,2,1,0:T(8,128)(2,1)S(1)} %get-tuple-element.35), channel_id=1, source_target_pairs={{4,8},{6,10},{8,4},{10,6},{5,9},{7,11},{9,5},{11,7},{20,24},{22,26... | collective-permute-start | bytes 1179656 | tf_op jit(solution)/shard_map/ppermute | solution.py:37
  6.1 5.4 %collective-permute-start = (bf16[3,3,64,128]{3,2,1,0:T(8,128)(2,1)S(1)}, bf16[3,3,64,128]{3,2,1,0:T(8,128)(2,1)S(1)}, u32[]{:S(2)}, u32[]{:S(2)}) collective-permute-start(bf16[3,3,64,128]{3,2,1,0:T(8,128)(2,1)S(1)} %get-tuple-element.32), channel_id=1, source_target_pairs={{0,6},{2,4},{4,2},{6,0},{8,14},{10,12},{12,10},{14,8},{1,7},{3,5},... | collective-permute-start | bytes 442376 | tf_op jit(solution)/shard_map/ppermute | solution.py:37
  11.5 0.7 %collective-permute-start.1 = (bf16[3,3,64,128]{3,2,1,0:T(8,128)(2,1)S(1)}, bf16[3,3,64,128]{3,2,1,0:T(8,128)(2,1)S(1)}, u32[]{:S(2)}, u32[]{:S(2)}) collective-permute-start(bf16[3,3,64,128]{3,2,1,0:T(8,128)(2,1)S(1)} %get-tuple-element.33), channel_id=1, source_target_pairs={{4,10},{6,8},{8,6},{10,4},{5,11},{7,9},{9,7},{11,5},{20,26},{22,24... | collective-permute-start | bytes 442376 | tf_op jit(solution)/shard_map/ppermute | solution.py:37
  12.7 1.0 %copy-done = bf16[4,8,64,128]{3,2,1,0:T(8,128)(2,1)S(1)} copy-done((bf16[4,8,64,128]{3,2,1,0:T(8,128)(2,1)S(1)}, bf16[4,8,64,128]{3,2,1,0:T(8,128)(2,1)}, u32[]{:S(2)}) %copy-start) | copy-done | bytes 524312
  13.8 0.6 %cut_source.1 = (bf16[3,3,64,128]{3,2,1,0:T(8,128)(2,1)S(1)}, bf16[3,3,64,128]{3,2,1,0:T(8,128)(2,1)S(1)}, bf16[3,8,64,128]{3,2,1,0:T(8,128)(2,1)S(1)}, bf16[3,8...) custom-call(bf16[4,8,64,128]{3,2,1,0:T(8,128)(2,1)S(1)} %copy-done), custom_call_target="tpu_custom_call" | custom-call | tf_op jit(solution)/shard_map/cut_source/pallas_call | solution.py:378
  14.4 4.5 %collective-permute-done = bf16[3,3,64,128]{3,2,1,0:T(8,128)(2,1)S(1)} collective-permute-done((bf16[3,3,64,128]{3,2,1,0:T(8,128)(2,1)S(1)}, bf16[3,3,64,128]{3,2,1,0:T(8,128)(2,1)S(1)}, u32[]{:S(2)}, u32[]{:S(2)}) %collective-permute-start) | collective-permute-done | bytes 147488 | tf_op jit(solution)/shard_map/ppermute | solution.py:37
  18.9 2.3 %collective-permute-start.8 = (bf16[3,8,64,128]{3,2,1,0:T(8,128)(2,1)S(1)}, bf16[3,8,64,128]{3,2,1,0:T(8,128)(2,1)S(1)}, u32[]{:S(2)}, u32[]{:S(2)}) collective-permute-start(bf16[3,8,64,128]{3,2,1,0:T(8,128)(2,1)S(1)} %get-tuple-element.48), channel_id=1, source_target_pairs={{0,4},{2,6},{4,0},{6,2},{8,12},{10,14},{12,8},{14,10},{1,5},{3,7},... | collective-permute-start | bytes 1179656 | tf_op jit(solution)/shard_map/ppermute | solution.py:37
  21.2 0.8 %collective-permute-start.9 = (bf16[3,8,64,128]{3,2,1,0:T(8,128)(2,1)S(1)}, bf16[3,8,64,128]{3,2,1,0:T(8,128)(2,1)S(1)}, u32[]{:S(2)}, u32[]{:S(2)}) collective-permute-start(bf16[3,8,64,128]{3,2,1,0:T(8,128)(2,1)S(1)} %get-tuple-element.49), channel_id=1, source_target_pairs={{4,8},{6,10},{8,4},{10,6},{5,9},{7,11},{9,5},{11,7},{20,24},{22,26... | collective-permute-start | bytes 1179656 | tf_op jit(solution)/shard_map/ppermute | solution.py:37
  22.0 1.0 %copy.9 = bf16[4,8,25,128]{3,2,1,0:T(8,128)(2,1)S(1)} copy(bf16[4,8,25,128]{3,1,2,0:T(8,128)(2,1)} %param.10) | data formatting | bytes 409600 | tf_op args[3]
  23.0 1.0 %copy-done.1 = bf16[4,8,64,128]{3,2,1,0:T(8,128)(2,1)S(1)} copy-done((bf16[4,8,64,128]{3,2,1,0:T(8,128)(2,1)S(1)}, bf16[4,8,64,128]{3,2,1,0:T(8,128)(2,1)}, u32[]{:S(2)}) %copy-start.1) | copy-done | bytes 524312
  24.0 1.0 %copy-done.3 = bf16[4,8,64,128]{3,2,1,0:T(8,128)(2,1)S(1)} copy-done((bf16[4,8,64,128]{3,2,1,0:T(8,128)(2,1)S(1)}, bf16[4,8,64,128]{3,2,1,0:T(8,128)(2,1)}, u32[]{:S(2)}) %copy-start.3) | copy-done | bytes 524312
  25.1 0.8 %copy-done.4 = bf16[128,256]{1,0:T(8,128)(2,1)S(1)} copy-done((bf16[128,256]{1,0:T(8,128)(2,1)S(1)}, bf16[128,256]{1,0:T(8,128)(2,1)}, u32[]{:S(2)}) %copy-start.4) | copy-done | bytes 65560
  25.9 0.8 %copy-done.6 = bf16[256,128]{1,0:T(8,128)(2,1)S(1)} copy-done((bf16[256,128]{1,0:T(8,128)(2,1)S(1)}, bf16[256,128]{1,0:T(8,128)(2,1)}, u32[]{:S(2)}) %copy-start.6) | copy-done | bytes 65560
  26.8 0.7 %copy-done.7 = s32[4,8,25]{2,1,0:T(8,128)S(1)} copy-done((s32[4,8,25]{2,1,0:T(8,128)S(1)}, s32[4,8,25]{2,1,0:T(8,128)}, u32[]{:S(2)}) %copy-start.7) | copy-done | bytes 3224
  27.5 0.7 %copy-done.8 = f32[256]{0:T(256)S(1)} copy-done((f32[256]{0:T(256)S(1)}, f32[256]{0:T(256)}, u32[]{:S(2)}) %copy-start.8) | copy-done | bytes 1048
  28.2 0.9 %prep.1 = (bf16[64,32,128]{2,1,0:T(8,128)(2,1)S(1)}, bf16[64,32,128]{2,1,0:T(8,128)(2,1)S(1)}, f32[256,1024]{1,0:T(8,128)S(1)}, bf16[256,128]{1,0:T(8,128)(2,1)S...) custom-call(bf16[2048,128]{1,0:T(8,128)(2,1)S(1)} %bitcast.17, ...), custom_call_target="tpu_custom_call" | custom-call | bytes 12000000 | tf_op jit(solution)/shard_map/prep/pallas_call | solution.py:347
  29.1 2.7 %corr.1 = (bf16[64,1024]{1,0:T(8,128)(2,1)S(1)}, bf16[64,128,128]{2,1,0:T(8,128)(2,1)S(1)}) custom-call(bf16[64,32,128]{2,1,0:T(8,128)(2,1)S(1)} %get-tuple-element.29.refs_0_, bf16[64,32,128]{2,1,0:T(8,128)(2,1)S(1)} %get-tuple-element.30.refs_1_.src_t, s32[8,128]{1,0:T(8,128)S(1)} %get-tuple-element.31.refs_2_.refs_6_.e_ref, ...), custom_call_target="tpu_custom_call" | custom-call | bytes 9000000 | tf_op jit(solution)/shard_map/corr/pallas_call | solution.py:347
  31.9 0.6 %collective-permute-start.10 = (bf16[4,3,64,128]{3,2,1,0:T(8,128)(2,1)S(1)}, bf16[4,3,64,128]{3,2,1,0:T(8,128)(2,1)S(1)}, u32[]{:S(2)}, u32[]{:S(2)}) collective-permute-start(bf16[4,3,64,128]{3,2,1,0:T(8,128)(2,1)S(1)} %get-tuple-element.50), channel_id=1, source_target_pairs={{0,2},{2,0},{4,6},{6,4},{8,10},{10,8},{12,14},{14,12},{1,3},{3,1},... | collective-permute-start | bytes 589832 | tf_op jit(solution)/shard_map/ppermute | solution.py:37
  32.5 6.1 %collective-permute-start.6 = (bf16[3,3,64,128]{3,2,1,0:T(8,128)(2,1)S(1)}, bf16[3,3,64,128]{3,2,1,0:T(8,128)(2,1)S(1)}, u32[]{:S(2)}, u32[]{:S(2)}) collective-permute-start(bf16[3,3,64,128]{3,2,1,0:T(8,128)(2,1)S(1)} %get-tuple-element.46), channel_id=1, source_target_pairs={{0,6},{2,4},{4,2},{6,0},{8,14},{10,12},{12,10},{14,8},{1,7},{3,5},... | collective-permute-start | bytes 442376 | tf_op jit(solution)/shard_map/ppermute | solution.py:37
  38.6 0.7 %collective-permute-start.7 = (bf16[3,3,64,128]{3,2,1,0:T(8,128)(2,1)S(1)}, bf16[3,3,64,128]{3,2,1,0:T(8,128)(2,1)S(1)}, u32[]{:S(2)}, u32[]{:S(2)}) collective-permute-start(bf16[3,3,64,128]{3,2,1,0:T(8,128)(2,1)S(1)} %get-tuple-element.47), channel_id=1, source_target_pairs={{4,10},{6,8},{8,6},{10,4},{5,11},{7,9},{9,7},{11,5},{20,26},{22,24... | collective-permute-start | bytes 442376 | tf_op jit(solution)/shard_map/ppermute | solution.py:37
  39.3 1.9 %decoder.1 = (bf16[64,1024]{1,0:T(8,128)(2,1)S(1)}, bf16[64,384]{1,0:T(8,128)(2,1)S(1)}, bf16[64,384]{1,0:T(8,128)(2,1)S(1)}, bf16[64,768]{1,0:T(8,128)(2,1)S(1)...) custom-call(bf16[64,1024]{1,0:T(8,128)(2,1)S(1)} %get-tuple-element.37.refs_0_, ...), custom_call_target="tpu_custom_call" | custom-call | bytes 9000000 | tf_op jit(solution)/shard_map/decoder/pallas_call | solution.py:347
  41.2 1.5 %collective-permute-done.6 = bf16[3,3,64,128]{3,2,1,0:T(8,128)(2,1)S(1)} collective-permute-done((bf16[3,3,64,128]{3,2,1,0:T(8,128)(2,1)S(1)}, bf16[3,3,64,128]{3,2,1,0:T(8,128)(2,1)S(1)}, u32[]{:S(2)}, u32[]{:S(2)}) %collective-permute-start.6) | collective-permute-done | bytes 147488 | tf_op jit(solution)/shard_map/ppermute | solution.py:37
  42.8 2.4 %collective-permute-start.13 = (bf16[64,768]{1,0:T(8,128)(2,1)S(1)}, bf16[64,768]{1,0:T(8,128)(2,1)S(1)}, u32[]{:S(2)}, u32[]{:S(2)}) collective-permute-start(bf16[64,768]{1,0:T(8,128)(2,1)S(1)} %get-tuple-element.53), channel_id=1, source_target_pairs={{0,4},{2,6},{4,0},{6,2},{8,12},{10,14},{12,8},{14,10},{1,5},{3,7},... | collective-permute-start | bytes 294920 | tf_op jit(solution)/shard_map/ppermute | solution.py:37
  45.2 0.7 %collective-permute-start.14 = (bf16[64,768]{1,0:T(8,128)(2,1)S(1)}, bf16[64,768]{1,0:T(8,128)(2,1)S(1)}, u32[]{:S(2)}, u32[]{:S(2)}) collective-permute-start(bf16[64,768]{1,0:T(8,128)(2,1)S(1)} %get-tuple-element.54), channel_id=1, source_target_pairs={{4,8},{6,10},{8,4},{10,6},{5,9},{7,11},{9,5},{11,7},{20,24},{22,26... | collective-permute-start | bytes 294920 | tf_op jit(solution)/shard_map/ppermute | solution.py:37
  45.9 2.3 %collective-permute-start.15 = (bf16[64,512]{1,0:T(8,128)(2,1)S(1)}, bf16[64,512]{1,0:T(8,128)(2,1)S(1)}, u32[]{:S(2)}, u32[]{:S(2)}) collective-permute-start(bf16[64,512]{1,0:T(8,128)(2,1)S(1)} %get-tuple-element.55), channel_id=1, source_target_pairs={{0,2},{2,0},{4,6},{6,4},{8,10},{10,8},{12,14},{14,12},{1,3},{3,1},... | collective-permute-start | bytes 196616 | tf_op jit(solution)/shard_map/ppermute | solution.py:37
  48.1 4.0 %collective-permute-start.11 = (bf16[64,384]{1,0:T(8,128)(2,1)S(1)}, bf16[64,384]{1,0:T(8,128)(2,1)S(1)}, u32[]{:S(2)}, u32[]{:S(2)}) collective-permute-start(bf16[64,384]{1,0:T(8,128)(2,1)S(1)} %get-tuple-element.51), channel_id=1, source_target_pairs={{0,6},{2,4},{4,2},{6,0},{8,14},{10,12},{12,10},{14,8},{1,7},{3,5},... | collective-permute-start | bytes 147464 | tf_op jit(solution)/shard_map/ppermute | solution.py:37
  52.2 0.7 %collective-permute-start.12 = (bf16[64,384]{1,0:T(8,128)(2,1)S(1)}, bf16[64,384]{1,0:T(8,128)(2,1)S(1)}, u32[]{:S(2)}, u32[]{:S(2)}) collective-permute-start(bf16[64,384]{1,0:T(8,128)(2,1)S(1)} %get-tuple-element.52), channel_id=1, source_target_pairs={{4,10},{6,8},{8,6},{10,4},{5,11},{7,9},{9,7},{11,5},{20,26},{22,24... | collective-permute-start | bytes 147464 | tf_op jit(solution)/shard_map/ppermute | solution.py:37
  53.3 3.8 %own.1 = (bf16[2048,128]{1,0:T(8,128)(2,1)}, f32[64,32,128]{2,1,0:T(8,128)S(1)}) custom-call(bf16[64,1024]{1,0:T(8,128)(2,1)S(1)} %get-tuple-element.42.gc_ref, s32[8,128]{1,0:T(8,128)S(1)} %get-tuple-element.31.refs_2_.refs_6_.e_ref, bf16[64,128,128]{2,1,0:T(8,128)(2,1)S(1)} %get-tuple-element.43.tgt_t, bf16[64,32,128]{2,1,0:T(8,128)(2,1)S(1)} %get-tuple-element.30.refs_1_.src_t), custom_call_target="tpu_custom_call" | custom-call | bytes 12000000 | tf_op jit(solution)/shard_map/own/pallas_call | solution.py:347
  57.1 2.9 %total.1 = bf16[2048,128]{1,0:T(8,128)(2,1)} custom-call(f32[64,32,128]{2,1,0:T(8,128)S(1)} %get-tuple-element.45.own_ref, bf16[64,80,128]{2,1,0:T(8,128)(2,1)S(1)} %halo.1.halo_t, bf16[64,384]{1,0:T(8,128)(2,1)S(1)} %collective-permute-done.11.refs_0_, bf16[64,384]{1,0:T(8,128)(2,1)S(1)} %collective-permute-done.12.refs_1_, ...), custom_call_target="tpu_custom_call" | custom-call | bytes 9000000 | tf_op jit(solution)/shard_map/total/pallas_call | solution.py:347
  (27 shorter events, 1.2 us)
Async XLA Ops:
  0.6 1.0 %copy-start.2 = (bf16[4,8,64,128]{3,2,1,0:T(8,128)(2,1)S(1)}, bf16[4,8,64,128]{3,2,1,0:T(8,128)(2,1)}, u32[]{:S(2)}) copy-start(bf16[4,8,64,128]{3,2,1,0:T(8,128)(2,1)} %x_ref.2) | copy-start | bytes 1572868
  2.3 26.8 %collective-permute-start.2 = (bf16[3,8,64,128]{3,2,1,0:T(8,128)(2,1)S(1)}, bf16[3,8,64,128]{3,2,1,0:T(8,128)(2,1)S(1)}, u32[]{:S(2)}, u32[]{:S(2)}) collective-permute-start(bf16[3,8,64,128]{3,2,1,0:T(8,128)(2,1)S(1)} %get-tuple-element.34), channel_id=1, source_target_pairs={{0,4},{2,6},{4,0},{6,2},{8,12},{10,14},{12,8},{14,10},{1,5},{3,7},... | collective-permute-start | bytes 1179656 | tf_op jit(solution)/shard_map/ppermute | solution.py:37
  5.4 23.7 %collective-permute-start.3 = (bf16[3,8,64,128]{3,2,1,0:T(8,128)(2,1)S(1)}, bf16[3,8,64,128]{3,2,1,0:T(8,128)(2,1)S(1)}, u32[]{:S(2)}, u32[]{:S(2)}) collective-permute-start(bf16[3,8,64,128]{3,2,1,0:T(8,128)(2,1)S(1)} %get-tuple-element.35), channel_id=1, source_target_pairs={{4,8},{6,10},{8,4},{10,6},{5,9},{7,11},{9,5},{11,7},{20,24},{22,26... | collective-permute-start | bytes 1179656 | tf_op jit(solution)/shard_map/ppermute | solution.py:37
  6.1 12.8 %collective-permute-start = (bf16[3,3,64,128]{3,2,1,0:T(8,128)(2,1)S(1)}, bf16[3,3,64,128]{3,2,1,0:T(8,128)(2,1)S(1)}, u32[]{:S(2)}, u32[]{:S(2)}) collective-permute-start(bf16[3,3,64,128]{3,2,1,0:T(8,128)(2,1)S(1)} %get-tuple-element.32), channel_id=1, source_target_pairs={{0,6},{2,4},{4,2},{6,0},{8,14},{10,12},{12,10},{14,8},{1,7},{3,5},... | collective-permute-start | bytes 442376 | tf_op jit(solution)/shard_map/ppermute | solution.py:37
  11.5 9.7 %collective-permute-start.1 = (bf16[3,3,64,128]{3,2,1,0:T(8,128)(2,1)S(1)}, bf16[3,3,64,128]{3,2,1,0:T(8,128)(2,1)S(1)}, u32[]{:S(2)}, u32[]{:S(2)}) collective-permute-start(bf16[3,3,64,128]{3,2,1,0:T(8,128)(2,1)S(1)} %get-tuple-element.33), channel_id=1, source_target_pairs={{4,10},{6,8},{8,6},{10,4},{5,11},{7,9},{9,7},{11,5},{20,26},{22,24... | collective-permute-start | bytes 442376 | tf_op jit(solution)/shard_map/ppermute | solution.py:37
  12.1 16.9 %collective-permute-start.4 = (bf16[4,3,64,128]{3,2,1,0:T(8,128)(2,1)S(1)}, bf16[4,3,64,128]{3,2,1,0:T(8,128)(2,1)S(1)}, u32[]{:S(2)}, u32[]{:S(2)}) collective-permute-start(bf16[4,3,64,128]{3,2,1,0:T(8,128)(2,1)S(1)} %get-tuple-element.36), channel_id=1, source_target_pairs={{0,2},{2,0},{4,6},{6,4},{8,10},{10,8},{12,14},{14,12},{1,3},{3,1},... | collective-permute-start | bytes 589832 | tf_op jit(solution)/shard_map/ppermute | solution.py:37
  12.7 1.0 %copy-start = (bf16[4,8,64,128]{3,2,1,0:T(8,128)(2,1)S(1)}, bf16[4,8,64,128]{3,2,1,0:T(8,128)(2,1)}, u32[]{:S(2)}) copy-start(bf16[4,8,64,128]{3,2,1,0:T(8,128)(2,1)} %x_ref.3) | copy-start | bytes 1572868
  18.9 29.3 %collective-permute-start.8 = (bf16[3,8,64,128]{3,2,1,0:T(8,128)(2,1)S(1)}, bf16[3,8,64,128]{3,2,1,0:T(8,128)(2,1)S(1)}, u32[]{:S(2)}, u32[]{:S(2)}) collective-permute-start(bf16[3,8,64,128]{3,2,1,0:T(8,128)(2,1)S(1)} %get-tuple-element.48), channel_id=1, source_target_pairs={{0,4},{2,6},{4,0},{6,2},{8,12},{10,14},{12,8},{14,10},{1,5},{3,7},... | collective-permute-start | bytes 1179656 | tf_op jit(solution)/shard_map/ppermute | solution.py:37
  21.2 18.1 %copy-start.5 = (bf16[128,256]{1,0:T(8,128)(2,1)S(1)}, bf16[128,256]{1,0:T(8,128)(2,1)}, u32[]{:S(2)}) copy-start(bf16[128,256]{1,0:T(8,128)(2,1)} %refs_5_.1) | copy-start | bytes 196612
  21.2 31.0 %collective-permute-start.9 = (bf16[3,8,64,128]{3,2,1,0:T(8,128)(2,1)S(1)}, bf16[3,8,64,128]{3,2,1,0:T(8,128)(2,1)S(1)}, u32[]{:S(2)}, u32[]{:S(2)}) collective-permute-start(bf16[3,8,64,128]{3,2,1,0:T(8,128)(2,1)S(1)} %get-tuple-element.49), channel_id=1, source_target_pairs={{4,8},{6,10},{8,4},{10,6},{5,9},{7,11},{9,5},{11,7},{20,24},{22,26... | collective-permute-start | bytes 1179656 | tf_op jit(solution)/shard_map/ppermute | solution.py:37
  23.0 1.0 %copy-start.1 = (bf16[4,8,64,128]{3,2,1,0:T(8,128)(2,1)S(1)}, bf16[4,8,64,128]{3,2,1,0:T(8,128)(2,1)}, u32[]{:S(2)}) copy-start(bf16[4,8,64,128]{3,2,1,0:T(8,128)(2,1)} %x_ref.3) | copy-start | bytes 1572868
  24.0 1.0 %copy-start.3 = (bf16[4,8,64,128]{3,2,1,0:T(8,128)(2,1)S(1)}, bf16[4,8,64,128]{3,2,1,0:T(8,128)(2,1)}, u32[]{:S(2)}) copy-start(bf16[4,8,64,128]{3,2,1,0:T(8,128)(2,1)} %x_ref.2) | copy-start | bytes 1572868
  25.1 0.8 %copy-start.4 = (bf16[128,256]{1,0:T(8,128)(2,1)S(1)}, bf16[128,256]{1,0:T(8,128)(2,1)}, u32[]{:S(2)}) copy-start(bf16[128,256]{1,0:T(8,128)(2,1)} %refs_5_.1) | copy-start | bytes 196612
  25.9 0.8 %copy-start.6 = (bf16[256,128]{1,0:T(8,128)(2,1)S(1)}, bf16[256,128]{1,0:T(8,128)(2,1)}, u32[]{:S(2)}) copy-start(bf16[256,128]{1,0:T(8,128)(2,1)} %w_out_ref.1) | copy-start | bytes 196612
  26.8 0.7 %copy-start.7 = (s32[4,8,25]{2,1,0:T(8,128)S(1)}, s32[4,8,25]{2,1,0:T(8,128)}, u32[]{:S(2)}) copy-start(s32[4,8,25]{2,1,0:T(8,128)} %param.9) | copy-start | bytes 9604
  27.5 0.7 %copy-start.8 = (f32[256]{0:T(256)S(1)}, f32[256]{0:T(256)}, u32[]{:S(2)}) copy-start(f32[256]{0:T(256)} %param.12) | copy-start | bytes 3076
  31.8 6.8 %collective-permute-start.5 = (bf16[64,1024]{1,0:T(8,128)(2,1)S(1)}, bf16[64,1024]{1,0:T(8,128)(2,1)S(1)}, u32[]{:S(2)}, u32[]{:S(2)}) collective-permute-start(bf16[64,1024]{1,0:T(8,128)(2,1)S(1)} %get-tuple-element.37.refs_0_), channel_id=1, source_target_pairs={{0,1},{1,0},{2,3},{3,2},{4,5},{5,4},{6,7},{7,6},{8,9},{9,8},{10,11... | collective-permute-start | bytes 393224 | tf_op jit(solution)/shard_map/ppermute | solution.py:432
  31.9 14.0 %collective-permute-start.10 = (bf16[4,3,64,128]{3,2,1,0:T(8,128)(2,1)S(1)}, bf16[4,3,64,128]{3,2,1,0:T(8,128)(2,1)S(1)}, u32[]{:S(2)}, u32[]{:S(2)}) collective-permute-start(bf16[4,3,64,128]{3,2,1,0:T(8,128)(2,1)S(1)} %get-tuple-element.50), channel_id=1, source_target_pairs={{0,2},{2,0},{4,6},{6,4},{8,10},{10,8},{12,14},{14,12},{1,3},{3,1},... | collective-permute-start | bytes 589832 | tf_op jit(solution)/shard_map/ppermute | solution.py:37
  32.5 10.3 %collective-permute-start.6 = (bf16[3,3,64,128]{3,2,1,0:T(8,128)(2,1)S(1)}, bf16[3,3,64,128]{3,2,1,0:T(8,128)(2,1)S(1)}, u32[]{:S(2)}, u32[]{:S(2)}) collective-permute-start(bf16[3,3,64,128]{3,2,1,0:T(8,128)(2,1)S(1)} %get-tuple-element.46), channel_id=1, source_target_pairs={{0,6},{2,4},{4,2},{6,0},{8,14},{10,12},{12,10},{14,8},{1,7},{3,5},... | collective-permute-start | bytes 442376 | tf_op jit(solution)/shard_map/ppermute | solution.py:37
  38.6 6.6 %collective-permute-start.7 = (bf16[3,3,64,128]{3,2,1,0:T(8,128)(2,1)S(1)}, bf16[3,3,64,128]{3,2,1,0:T(8,128)(2,1)S(1)}, u32[]{:S(2)}, u32[]{:S(2)}) collective-permute-start(bf16[3,3,64,128]{3,2,1,0:T(8,128)(2,1)S(1)} %get-tuple-element.47), channel_id=1, source_target_pairs={{4,10},{6,8},{8,6},{10,4},{5,11},{7,9},{9,7},{11,5},{20,26},{22,24... | collective-permute-start | bytes 442376 | tf_op jit(solution)/shard_map/ppermute | solution.py:37
  42.8 14.3 %collective-permute-start.13 = (bf16[64,768]{1,0:T(8,128)(2,1)S(1)}, bf16[64,768]{1,0:T(8,128)(2,1)S(1)}, u32[]{:S(2)}, u32[]{:S(2)}) collective-permute-start(bf16[64,768]{1,0:T(8,128)(2,1)S(1)} %get-tuple-element.53), channel_id=1, source_target_pairs={{0,4},{2,6},{4,0},{6,2},{8,12},{10,14},{12,8},{14,10},{1,5},{3,7},... | collective-permute-start | bytes 294920 | tf_op jit(solution)/shard_map/ppermute | solution.py:37
  45.2 11.9 %collective-permute-start.14 = (bf16[64,768]{1,0:T(8,128)(2,1)S(1)}, bf16[64,768]{1,0:T(8,128)(2,1)S(1)}, u32[]{:S(2)}, u32[]{:S(2)}) collective-permute-start(bf16[64,768]{1,0:T(8,128)(2,1)S(1)} %get-tuple-element.54), channel_id=1, source_target_pairs={{4,8},{6,10},{8,4},{10,6},{5,9},{7,11},{9,5},{11,7},{20,24},{22,26... | collective-permute-start | bytes 294920 | tf_op jit(solution)/shard_map/ppermute | solution.py:37
  45.9 11.3 %collective-permute-start.15 = (bf16[64,512]{1,0:T(8,128)(2,1)S(1)}, bf16[64,512]{1,0:T(8,128)(2,1)S(1)}, u32[]{:S(2)}, u32[]{:S(2)}) collective-permute-start(bf16[64,512]{1,0:T(8,128)(2,1)S(1)} %get-tuple-element.55), channel_id=1, source_target_pairs={{0,2},{2,0},{4,6},{6,4},{8,10},{10,8},{12,14},{14,12},{1,3},{3,1},... | collective-permute-start | bytes 196616 | tf_op jit(solution)/shard_map/ppermute | solution.py:37
  48.1 9.0 %collective-permute-start.11 = (bf16[64,384]{1,0:T(8,128)(2,1)S(1)}, bf16[64,384]{1,0:T(8,128)(2,1)S(1)}, u32[]{:S(2)}, u32[]{:S(2)}) collective-permute-start(bf16[64,384]{1,0:T(8,128)(2,1)S(1)} %get-tuple-element.51), channel_id=1, source_target_pairs={{0,6},{2,4},{4,2},{6,0},{8,14},{10,12},{12,10},{14,8},{1,7},{3,5},... | collective-permute-start | bytes 147464 | tf_op jit(solution)/shard_map/ppermute | solution.py:37
  52.2 4.9 %collective-permute-start.12 = (bf16[64,384]{1,0:T(8,128)(2,1)S(1)}, bf16[64,384]{1,0:T(8,128)(2,1)S(1)}, u32[]{:S(2)}, u32[]{:S(2)}) collective-permute-start(bf16[64,384]{1,0:T(8,128)(2,1)S(1)} %get-tuple-element.52), channel_id=1, source_target_pairs={{4,10},{6,8},{8,6},{10,4},{5,11},{7,9},{9,7},{11,5},{20,26},{22,24... | collective-permute-start | bytes 147464 | tf_op jit(solution)/shard_map/ppermute | solution.py:37

commit v4 on v3

--- a/solution.py
+++ b/solution.py
@@ -82,18 +82,14 @@
     return where_to, (row & (rows - 1)) * cols + (col & (cols - 1))
 
 
-def cut_kernel(pieces, rows, cols, x_ref, *refs):
-    out_refs, sems = refs[:-1], refs[-1]
+def cuts(pieces, rows, cols, x_ref, out_refs, sems, at):
     strip_at, sub_at = lax.axis_index("strip"), lax.axis_index("sub")
     copies = []
     for i, ((qz, qx), ref) in enumerate(zip(pieces, out_refs)):
         r = pl.ds(0, rows) if qz is None else pl.ds(facing(qz, rows, strip_at), H)
         c = pl.ds(0, cols) if qx is None else pl.ds(facing(qx, cols, sub_at), H)
-        copies.append(pltpu.make_async_copy(x_ref.at[r, c], ref, sems.at[i]))
-    for copy in copies:
-        copy.start()
-    for copy in copies:
-        copy.wait()
+        copies.append(pltpu.make_async_copy(x_ref.at[r, c], ref, sems.at[at + i]))
+    return copies
 
 
 def loop(count, body, most=4):
@@ -145,34 +141,60 @@
     out_ref[...] = acc
 
 
-def prep_kernel(base, rows, cols, slots, src_ref, tgt_ref, og_ref, ids_ref, w_in_ref, b_ref, w_out_ref, *refs):
-    src_t, tgt_t, gh_ref, wt_ref, bt_ref, e_ref, m_ref, s32, t32, og, table = refs
+def head_kernel(base, pieces, rows, cols, slots, *refs):
+    k = len(pieces)
+    far, rest = refs[:7], refs[7:]
+    tgt_slabs, src_slabs, outs, rest = rest[:k], rest[k : 2 * k], rest[2 * k : 2 * k + 8], rest[2 * k + 8 :]
+    src_t, tgt_t, gh_ref, wt_ref, wh_ref, bt_ref, e_ref, m_ref = outs
+    (s32, t32, og, table), near, sems = rest[:4], rest[4:-1], rest[-1]
+    src_ref, tgt_ref, og_ref, ids_ref, w_in_ref, b_ref, w_out_ref = near
+    fetches = [pltpu.make_async_copy(f, v, sems.at[i]) for i, (f, v) in enumerate(zip(far, near))]
+    slabs = cuts(pieces, rows, cols, far[1], tgt_slabs, sems, 7)
+    slabs += cuts(pieces, rows, cols, far[0], src_slabs, sems, 7 + k)
+    for copy in fetches[2:] + fetches[:2] + slabs:
+        copy.start()
     px, n, _ = src_t.shape
     pitch = px + 1
+    for fetch in fetches[2:]:
+        fetch.wait()
     e_at, m_at = places(ids_ref[...], base, rows, cols)
     slotted(e_at, e_ref, table, slots)
     slotted(m_at, m_ref, table, slots)
     wt_ref[...] = w_in_ref[...].T
+    rep = lax.axis_index("rep")
+    wh_ref[...] = w_in_ref[pl.ds(pl.multiple_of(rep * px, px), px), :]
     bt_ref[...] = jnp.broadcast_to(b_ref[...], (LANES, b_ref.shape[1])).T
-    widen(s32, 0, src_ref, px, pitch)
-    widen(t32, 0, tgt_ref, px, pitch)
+    picks = og_ref.shape[1]
+    og[...] = jnp.zeros_like(og)
+    for r in range(rows):
+        for pick in range(picks):
+            at = r * cols * (slots + 1) + pick
+            og[pl.ds(at, cols, stride=slots + 1), :] = og_ref[r, pick].astype(F32)
+    per = LANES // slots
+    for g in range(n // per):
+        block = jnp.concatenate(
+            [og[b * (slots + 1) : b * (slots + 1) + slots, :] for b in range(g * per, (g + 1) * per)]
+        ).astype(BF16)
+        gh_ref[:, g * LANES : (g + 1) * LANES] = lax.dot_general(
+            w_out_ref[...], block, NT, preferred_element_type=F32
+        )
+    for fetch in fetches[:2]:
+        fetch.wait()
+    for dst, src in ((s32, src_ref), (t32, tgt_ref)):
+
+        def body(i, dst=dst, src=src):
+            rows_of = src[i // cols, lax.rem(i, cols)]
+            dst[pl.ds(i * pitch, px), :] = rows_of.astype(F32)
+
+        loop(n, body)
 
     def turn(p):
         src_t[p] = s32[pl.ds(p, n, stride=pitch), :].astype(BF16)
         tgt_t[p] = t32[pl.ds(p, n, stride=pitch), :].astype(BF16)
 
     loop(px, turn)
-    picks = og_ref.shape[1]
-    og[...] = jnp.zeros_like(og)
-
-    for b in range(n):
-        og[b, :picks, :] = og_ref[b].astype(F32)
-    for g in range(n * slots // LANES):
-        per = LANES // slots
-        block = og[g * per : (g + 1) * per].reshape(LANES, og.shape[2]).astype(BF16)
-        gh_ref[:, g * LANES : (g + 1) * LANES] = lax.dot_general(
-            w_out_ref[...], block, NT, preferred_element_type=F32
-        )
+    for copy in slabs:
+        copy.wait()
 
 
 def corr_kernel(px, n, ext, starts, slots, *refs):
@@ -224,7 +246,7 @@
     rep = lax.axis_index("rep")
     whole[pl.ds(pl.multiple_of(rep * px, px), px), :] = mine_ref[...]
     whole[pl.ds(pl.multiple_of((1 - rep) * px, px), px), :] = other_ref[...]
-    w_half = w_ref[pl.ds(pl.multiple_of(rep * px, px), px), :]
+    w_half = w_ref[...]
     wide = 2
     bias = jnp.concatenate([bt_ref[...]] * wide, axis=1)
     width = wide * LANES
@@ -341,17 +363,19 @@
 
 
 VM = pl.BlockSpec(memory_space=pltpu.VMEM)
-
-
-def call(name, kernel, outs, scratch, args, us=2.0):
+HB = pl.BlockSpec(memory_space=pltpu.HBM)
+
+
+def call(kernel, outs, scratch, args, us=2.0, far=0, sems=0, limit=24):
     return pl.pallas_call(
         kernel,
-        name=name,
         out_shape=[jax.ShapeDtypeStruct(s, d) for s, d in outs],
-        in_specs=[VM] * len(args),
+        in_specs=[HB] * far + [VM] * (len(args) - far),
         out_specs=[VM] * len(outs),
-        scratch_shapes=[pltpu.VMEM(s, d) for s, d in scratch],
-        compiler_params=pltpu.CompilerParams(vmem_limit_bytes=24 * 2**20),
+        scratch_shapes=[pltpu.VMEM(s, d) for s, d in scratch]
+        + ([pltpu.VMEM(x.shape, x.dtype) for x in args[:far]] if far else [])
+        + ([pltpu.SemaphoreType.DMA((sems,))] if far else []),
+        compiler_params=pltpu.CompilerParams(vmem_limit_bytes=limit * 2**20),
         cost_estimate=pl.CostEstimate(
             flops=0, bytes_accessed=int(us * 3 * 10**6), transcendentals=0
         ),
@@ -374,51 +398,51 @@
         (rows if qz is None else H, cols if qx is None else H, px, channels) for qz, qx in pieces
     ]
 
-    def halo_of(name, x):
-        slabs = pl.pallas_call(
-            partial(cut_kernel, pieces, rows, cols),
-            name=name,
-            out_shape=[jax.ShapeDtypeStruct(s, BF16) for s in shapes],
-            in_specs=[pl.BlockSpec(memory_space=pl.ANY)],
-            out_specs=[VM] * len(pieces),
-            scratch_shapes=[pltpu.SemaphoreType.DMA((len(pieces),))],
-            compiler_params=pltpu.CompilerParams(vmem_limit_bytes=4 * 2**20),
-        )(x)
-        got = [swap(x, qz, qx) for x, (qz, qx) in zip(slabs, pieces)]
-        return [h.reshape(-1, channels) for h in got]
-
-    tgt_halo = halo_of("cut_target", target)
-    src_halo = halo_of("cut_source", source)
+    hidden = w_in.shape[1]
+    outs = [(s, BF16) for s in shapes] * 2 + [
+        ((px, n, channels), BF16),
+        ((px, n, channels), BF16),
+        ((hidden, n * slots), F32),
+        ((hidden, 2 * px), BF16),
+        ((px, hidden), BF16),
+        ((hidden, LANES), F32),
+        ((groups, LANES), jnp.int32),
+        ((groups, LANES), jnp.int32),
+    ]
+    args = (
+        source,
+        target,
+        jnp.swapaxes(out_grad, 1, 2),
+        target_ids.reshape(n, picks),
+        w_in,
+        b_in.reshape(1, hidden),
+        w_out,
+    )
+    args = tuple(pltpu.with_memory_space_constraint(a, pltpu.HBM) for a in args)
+    made = call(
+        partial(head_kernel, base, pieces, rows, cols, slots),
+        outs,
+        [((n * pitch, channels), F32)] * 2
+        + [((n * (slots + 1), out_grad.shape[3]), F32), ((n, LANES), jnp.int32)],
+        args,
+        far=len(args),
+        sems=len(args) + 2 * len(pieces),
+        limit=24,
+    )
+    k = len(pieces)
+    src_t, own_t, grad_hidden, w_t, w_half, b_t, e_ids, m_ids = made[2 * k :]
+
+    def halo_of(slabs):
+        got = []
+        for x, (qz, qx) in zip(slabs, pieces):
+            got.append(swap(x, qz, qx).reshape(-1, channels))
+        return got
+
+    tgt_halo = halo_of(made[:k])
+    src_halo = halo_of(made[k : 2 * k])
     starts = [base[q] for q in pieces]
     counts = [h.shape[0] // px for h in tgt_halo]
-    hidden = w_in.shape[1]
-    src_t, own_t, grad_hidden, w_t, b_t, e_ids, m_ids = call(
-        "prep",
-        partial(prep_kernel, base, rows, cols, slots),
-        [
-            ((px, n, channels), BF16),
-            ((px, n, channels), BF16),
-            ((hidden, n * slots), F32),
-            ((hidden, 2 * px), BF16),
-            ((hidden, LANES), F32),
-            ((groups, LANES), jnp.int32),
-            ((groups, LANES), jnp.int32),
-        ],
-        [((n * pitch, channels), F32)] * 2
-        + [((n, slots, out_grad.shape[3]), F32), ((n, LANES), jnp.int32)],
-        (
-            source.reshape(n * px, channels),
-            target.reshape(n * px, channels),
-            out_grad.reshape(n, picks, out_grad.shape[3]),
-            target_ids.reshape(n, picks),
-            w_in,
-            b_in.reshape(1, hidden),
-            w_out,
-        ),
-        us=4,
-    )
     costs, tgt_t = call(
-        "corr",
         partial(corr_kernel, px, n, ext, starts, slots),
         [((px, n * slots), BF16), ((px, ext_pad, channels), BF16)],
         [
@@ -435,16 +459,16 @@
         for qz, qx in pieces
     ]
     gc, *sent = call(
-        "decoder",
         partial(decoder_kernel, rows, cols, slots, pieces, starts, counts),
         [((px, n * slots), BF16)] + [((px, w), BF16) for w in lanes],
         [((2 * px, n * slots), BF16)],
-        (costs, other, grad_hidden, w_t, b_t, w_in, e_ids, m_ids),
+        (costs, other, grad_hidden, w_t, b_t, w_half, e_ids, m_ids),
         us=3,
     )
-    got = [swap(x, qz, qx) for x, (qz, qx) in zip(sent, pieces)]
+    got = []
+    for x, (qz, qx) in zip(sent, pieces):
+        got.append(swap(x, qz, qx))
     sg, own = call(
-        "own",
         partial(own_kernel, px, n, slots),
         [((n * px, channels), BF16), ((px, n, channels), F32)],
         [((ext_pad // LANES, n * pitch, LANES), F32), ((n * pitch, channels), F32)],
@@ -453,7 +477,6 @@
     )
     halo_pad = -(-(ext - n) // 16) * 16
     (halo_t,) = call(
-        "halo",
         partial(halo_kernel, px, [s - n for s in starts]),
         [((px, halo_pad, channels), BF16)],
         [((halo_pad * pitch, channels), F32)],
@@ -461,7 +484,6 @@
         us=1,
     )
     (tg,) = call(
-        "total",
         partial(total_kernel, px, n, slots, [per if qx is None else H for _, qx in pieces]),
         [((n * px, channels), BF16)],
         [((halo_pad * pitch, LANES), F32), ((n * pitch, channels), F32)],
@@ -482,6 +504,7 @@
         P(),
         P(),
     )
+
     return jax.shard_map(
         shards, mesh=mesh, in_specs=placed, out_specs=(cells, cells), check_vma=False
     )

time: 60.7 us -> 55.5 us (0.914)
  local copies, waits for them, and re-layouts: 8.21 us -> 0 us
  starting transfers between devices: 31 us -> 34.1 us
    unnamed x19 -> x0, local copies, waits for them, and re-layouts: 8.21 us -> none
    ppermute x15, starting transfers between devices: 31 us -> 34.1 us  [swap(): return lax.ppermute(x, ('strip', 'sub'), pairs)]
    pallas_call x8 -> x6, Pallas kernels: 13.9 us -> 14.3 us  [call(): pl.pallas_call(kernel, out_shape=[jax.ShapeDtypeStruct(s, d) for s, d in...]
  transfers between devices with their start and end apart: 16 -> 16, of which waited for: 2 -> 1; matrix products, arithmetic and copies ran while one was open for 2% -> 0% of each run, Pallas kernels for 17% -> 16%
where the time goes in v4:
time: 55.5 us; the launch traced here: 55.3 us
  starting transfers between devices  34.1 us (61%)
  Pallas kernels  14.3 us (26%)
  waiting for transfers between devices  6.05 us (11%)
  between operations  0.78 us (1%)
    ppermute x15, starting transfers between devices, swap(): return lax.ppermute(x, ('strip', 'sub'), pairs)  34.1 us
    pallas_call x6, Pallas kernels, call(): pl.pallas_call(kernel, out_shape=[jax.ShapeDtypeStruct(s, d) for s, d in...  14.3 us
    ppermute x15, waiting for transfers between devices, swap(): return lax.ppermute(x, ('strip', 'sub'), pairs)  6.05 us
  transfers between devices with their start and end apart: 16, of which 1 were waited for; matrix products, arithmetic and copies ran while one was open for 0% of the time, Pallas kernels for 16%

profile of v4, /device:TPU:0, one launch (start us, length us, event | category | flops | bytes accessed | tf_op | source)
XLA Modules:
  0.0 55.3 jit_solution(8532296563338558717)
XLA Ops:
  0.6 2.5 %shard_map.86 = (bf16[3,3,64,128]{3,2,1,0:T(8,128)(2,1)S(1)}, bf16[3,3,64,128]{3,2,1,0:T(8,128)(2,1)S(1)}, bf16[3,8,64,128]{3,2,1,0:T(8,128)(2,1)S(1)}, bf16[3,8...) custom-call(bf16[4,8,64,128]{3,2,1,0:T(8,128)(2,1)} %refs_0_.1, ...), custom_call_target="tpu_custom_call" | custom-call | bytes 6000000 | tf_op jit(solution)/shard_map/pallas_call | solution.py:370
  3.2 3.1 %collective-permute-start.2 = (bf16[3,8,64,128]{3,2,1,0:T(8,128)(2,1)S(1)}, bf16[3,8,64,128]{3,2,1,0:T(8,128)(2,1)S(1)}, u32[]{:S(2)}, u32[]{:S(2)}) collective-permute-start(bf16[3,8,64,128]{3,2,1,0:T(8,128)(2,1)S(1)} %get-tuple-element.35), channel_id=1, source_target_pairs={{0,4},{2,6},{4,0},{6,2},{8,12},{10,14},{12,8},{14,10},{1,5},{3,7},... | collective-permute-start | bytes 1179656 | tf_op jit(solution)/shard_map/ppermute | solution.py:37
  6.3 0.7 %collective-permute-start.3 = (bf16[3,8,64,128]{3,2,1,0:T(8,128)(2,1)S(1)}, bf16[3,8,64,128]{3,2,1,0:T(8,128)(2,1)S(1)}, u32[]{:S(2)}, u32[]{:S(2)}) collective-permute-start(bf16[3,8,64,128]{3,2,1,0:T(8,128)(2,1)S(1)} %get-tuple-element.36), channel_id=1, source_target_pairs={{4,8},{6,10},{8,4},{10,6},{5,9},{7,11},{9,5},{11,7},{20,24},{22,26... | collective-permute-start | bytes 1179656 | tf_op jit(solution)/shard_map/ppermute | solution.py:37
  7.0 5.2 %collective-permute-start = (bf16[3,3,64,128]{3,2,1,0:T(8,128)(2,1)S(1)}, bf16[3,3,64,128]{3,2,1,0:T(8,128)(2,1)S(1)}, u32[]{:S(2)}, u32[]{:S(2)}) collective-permute-start(bf16[3,3,64,128]{3,2,1,0:T(8,128)(2,1)S(1)} %get-tuple-element.33), channel_id=1, source_target_pairs={{0,6},{2,4},{4,2},{6,0},{8,14},{10,12},{12,10},{14,8},{1,7},{3,5},... | collective-permute-start | bytes 442376 | tf_op jit(solution)/shard_map/ppermute | solution.py:37
  12.2 0.7 %collective-permute-start.1 = (bf16[3,3,64,128]{3,2,1,0:T(8,128)(2,1)S(1)}, bf16[3,3,64,128]{3,2,1,0:T(8,128)(2,1)S(1)}, u32[]{:S(2)}, u32[]{:S(2)}) collective-permute-start(bf16[3,3,64,128]{3,2,1,0:T(8,128)(2,1)S(1)} %get-tuple-element.34), channel_id=1, source_target_pairs={{4,10},{6,8},{8,6},{10,4},{5,11},{7,9},{9,7},{11,5},{20,26},{22,24... | collective-permute-start | bytes 442376 | tf_op jit(solution)/shard_map/ppermute | solution.py:37
  12.8 0.7 %collective-permute-start.4 = (bf16[4,3,64,128]{3,2,1,0:T(8,128)(2,1)S(1)}, bf16[4,3,64,128]{3,2,1,0:T(8,128)(2,1)S(1)}, u32[]{:S(2)}, u32[]{:S(2)}) collective-permute-start(bf16[4,3,64,128]{3,2,1,0:T(8,128)(2,1)S(1)} %get-tuple-element.37), channel_id=1, source_target_pairs={{0,2},{2,0},{4,6},{6,4},{8,10},{10,8},{12,14},{14,12},{1,3},{3,1},... | collective-permute-start | bytes 589832 | tf_op jit(solution)/shard_map/ppermute | solution.py:37
  13.6 6.0 %collective-permute-done = bf16[3,3,64,128]{3,2,1,0:T(8,128)(2,1)S(1)} collective-permute-done((bf16[3,3,64,128]{3,2,1,0:T(8,128)(2,1)S(1)}, bf16[3,3,64,128]{3,2,1,0:T(8,128)(2,1)S(1)}, u32[]{:S(2)}, u32[]{:S(2)}) %collective-permute-start) | collective-permute-done | bytes 147488 | tf_op jit(solution)/shard_map/ppermute | solution.py:37
  19.6 2.3 %collective-permute-start.8 = (bf16[3,8,64,128]{3,2,1,0:T(8,128)(2,1)S(1)}, bf16[3,8,64,128]{3,2,1,0:T(8,128)(2,1)S(1)}, u32[]{:S(2)}, u32[]{:S(2)}) collective-permute-start(bf16[3,8,64,128]{3,2,1,0:T(8,128)(2,1)S(1)} %get-tuple-element.50), channel_id=1, source_target_pairs={{0,4},{2,6},{4,0},{6,2},{8,12},{10,14},{12,8},{14,10},{1,5},{3,7},... | collective-permute-start | bytes 1179656 | tf_op jit(solution)/shard_map/ppermute | solution.py:37
  21.9 0.0 collective-permute-done.1
  21.9 0.7 %collective-permute-start.9 = (bf16[3,8,64,128]{3,2,1,0:T(8,128)(2,1)S(1)}, bf16[3,8,64,128]{3,2,1,0:T(8,128)(2,1)S(1)}, u32[]{:S(2)}, u32[]{:S(2)}) collective-permute-start(bf16[3,8,64,128]{3,2,1,0:T(8,128)(2,1)S(1)} %get-tuple-element.51), channel_id=1, source_target_pairs={{4,8},{6,10},{8,4},{10,6},{5,9},{7,11},{9,5},{11,7},{20,24},{22,26... | collective-permute-start | bytes 1179656 | tf_op jit(solution)/shard_map/ppermute | solution.py:37
  22.6 0.0 collective-permute-done.4
  22.6 0.0 collective-permute-done.2
  22.6 0.0 collective-permute-done.3
  22.6 2.7 %shard_map.87 = (bf16[64,1024]{1,0:T(8,128)(2,1)S(1)}, bf16[64,128,128]{2,1,0:T(8,128)(2,1)S(1)}) custom-call(bf16[64,32,128]{2,1,0:T(8,128)(2,1)S(1)} %get-tuple-element.30.refs_0_, bf16[64,32,128]{2,1,0:T(8,128)(2,1)S(1)} %get-tuple-element.31.refs_1_.src_t, s32[8,128]{1,0:T(8,128)S(1)} %get-tuple-element.32.refs_2_.refs_6_.e_ref, ...), custom_call_target="tpu_custom_call" | custom-call | bytes 9000000 | tf_op jit(solution)/shard_map/pallas_call | solution.py:370
  25.4 0.0 collective-permute-start.5
  25.4 0.7 %collective-permute-start.10 = (bf16[4,3,64,128]{3,2,1,0:T(8,128)(2,1)S(1)}, bf16[4,3,64,128]{3,2,1,0:T(8,128)(2,1)S(1)}, u32[]{:S(2)}, u32[]{:S(2)}) collective-permute-start(bf16[4,3,64,128]{3,2,1,0:T(8,128)(2,1)S(1)} %get-tuple-element.52), channel_id=1, source_target_pairs={{0,2},{2,0},{4,6},{6,4},{8,10},{10,8},{12,14},{14,12},{1,3},{3,1},... | collective-permute-start | bytes 589832 | tf_op jit(solution)/shard_map/ppermute | solution.py:37
  26.2 0.7 %collective-permute-start.7 = (bf16[3,3,64,128]{3,2,1,0:T(8,128)(2,1)S(1)}, bf16[3,3,64,128]{3,2,1,0:T(8,128)(2,1)S(1)}, u32[]{:S(2)}, u32[]{:S(2)}) collective-permute-start(bf16[3,3,64,128]{3,2,1,0:T(8,128)(2,1)S(1)} %get-tuple-element.49), channel_id=1, source_target_pairs={{4,10},{6,8},{8,6},{10,4},{5,11},{7,9},{9,7},{11,5},{20,26},{22,24... | collective-permute-start | bytes 442376 | tf_op jit(solution)/shard_map/ppermute | solution.py:37
  26.8 0.0 collective-permute-done.5.refs_1_
  26.9 7.9 %collective-permute-start.6 = (bf16[3,3,64,128]{3,2,1,0:T(8,128)(2,1)S(1)}, bf16[3,3,64,128]{3,2,1,0:T(8,128)(2,1)S(1)}, u32[]{:S(2)}, u32[]{:S(2)}) collective-permute-start(bf16[3,3,64,128]{3,2,1,0:T(8,128)(2,1)S(1)} %get-tuple-element.48), channel_id=1, source_target_pairs={{0,6},{2,4},{4,2},{6,0},{8,14},{10,12},{12,10},{14,8},{1,7},{3,5},... | collective-permute-start | bytes 442376 | tf_op jit(solution)/shard_map/ppermute | solution.py:37
  34.7 1.9 %shard_map.88 = (bf16[64,1024]{1,0:T(8,128)(2,1)S(1)}, bf16[64,384]{1,0:T(8,128)(2,1)S(1)}, bf16[64,384]{1,0:T(8,128)(2,1)S(1)}, bf16[64,768]{1,0:T(8,128)(2,1)S...) custom-call(bf16[64,1024]{1,0:T(8,128)(2,1)S(1)} %get-tuple-element.38.refs_0_, ...), custom_call_target="tpu_custom_call" | custom-call | bytes 9000000 | tf_op jit(solution)/shard_map/pallas_call | solution.py:370
  36.7 0.0 collective-permute-done.7
  36.7 5.6 %collective-permute-start.13 = (bf16[64,768]{1,0:T(8,128)(2,1)S(1)}, bf16[64,768]{1,0:T(8,128)(2,1)S(1)}, u32[]{:S(2)}, u32[]{:S(2)}) collective-permute-start(bf16[64,768]{1,0:T(8,128)(2,1)S(1)} %get-tuple-element.55), channel_id=1, source_target_pairs={{0,4},{2,6},{4,0},{6,2},{8,12},{10,14},{12,8},{14,10},{1,5},{3,7},... | collective-permute-start | bytes 294920 | tf_op jit(solution)/shard_map/ppermute | solution.py:37
  42.3 0.7 %collective-permute-start.14 = (bf16[64,768]{1,0:T(8,128)(2,1)S(1)}, bf16[64,768]{1,0:T(8,128)(2,1)S(1)}, u32[]{:S(2)}, u32[]{:S(2)}) collective-permute-start(bf16[64,768]{1,0:T(8,128)(2,1)S(1)} %get-tuple-element.56), channel_id=1, source_target_pairs={{4,8},{6,10},{8,4},{10,6},{5,9},{7,11},{9,5},{11,7},{20,24},{22,26... | collective-permute-start | bytes 294920 | tf_op jit(solution)/shard_map/ppermute | solution.py:37
  43.0 0.0 collective-permute-done.10
  43.0 2.1 %collective-permute-start.15 = (bf16[64,512]{1,0:T(8,128)(2,1)S(1)}, bf16[64,512]{1,0:T(8,128)(2,1)S(1)}, u32[]{:S(2)}, u32[]{:S(2)}) collective-permute-start(bf16[64,512]{1,0:T(8,128)(2,1)S(1)} %get-tuple-element.57), channel_id=1, source_target_pairs={{0,2},{2,0},{4,6},{6,4},{8,10},{10,8},{12,14},{14,12},{1,3},{3,1},... | collective-permute-start | bytes 196616 | tf_op jit(solution)/shard_map/ppermute | solution.py:37
  45.1 2.3 %collective-permute-start.11 = (bf16[64,384]{1,0:T(8,128)(2,1)S(1)}, bf16[64,384]{1,0:T(8,128)(2,1)S(1)}, u32[]{:S(2)}, u32[]{:S(2)}) collective-permute-start(bf16[64,384]{1,0:T(8,128)(2,1)S(1)} %get-tuple-element.53), channel_id=1, source_target_pairs={{0,6},{2,4},{4,2},{6,0},{8,14},{10,12},{12,10},{14,8},{1,7},{3,5},... | collective-permute-start | bytes 147464 | tf_op jit(solution)/shard_map/ppermute | solution.py:37
  47.4 0.7 %collective-permute-start.12 = (bf16[64,384]{1,0:T(8,128)(2,1)S(1)}, bf16[64,384]{1,0:T(8,128)(2,1)S(1)}, u32[]{:S(2)}, u32[]{:S(2)}) collective-permute-start(bf16[64,384]{1,0:T(8,128)(2,1)S(1)} %get-tuple-element.54), channel_id=1, source_target_pairs={{4,10},{6,8},{8,6},{10,4},{5,11},{7,9},{9,7},{11,5},{20,26},{22,24... | collective-permute-start | bytes 147464 | tf_op jit(solution)/shard_map/ppermute | solution.py:37
  48.1 0.5 shard_map.90.halo_t
  48.5 3.8 %shard_map.89 = (bf16[2048,128]{1,0:T(8,128)(2,1)}, f32[64,32,128]{2,1,0:T(8,128)S(1)}) custom-call(bf16[64,1024]{1,0:T(8,128)(2,1)S(1)} %get-tuple-element.44.gc_ref, s32[8,128]{1,0:T(8,128)S(1)} %get-tuple-element.32.refs_2_.refs_6_.e_ref, bf16[64,128,128]{2,1,0:T(8,128)(2,1)S(1)} %get-tuple-element.45.tgt_t, ...), custom_call_target="tpu_custom_call" | custom-call | bytes 12000000 | tf_op jit(solution)/shard_map/pallas_call | solution.py:370
  52.3 0.0 collective-permute-done.13.refs_2_
  52.4 0.0 collective-permute-done.14.refs_3_
  52.4 2.9 %shard_map.91 = bf16[2048,128]{1,0:T(8,128)(2,1)} custom-call(f32[64,32,128]{2,1,0:T(8,128)S(1)} %get-tuple-element.47.own_ref, bf16[64,80,128]{2,1,0:T(8,128)(2,1)S(1)} %shard_map.90.halo_t, bf16[64,384]{1,0:T(8,128)(2,1)S(1)} %collective-permute-done.11.refs_0_, bf16[64,384]{1,0:T(8,128)(2,1)S(1)} %collective-permute-done.12.refs_1_, ...), custom_call_target="tpu_custom_call" | custom-call | bytes 9000000 | tf_op jit(solution)/shard_map/pallas_call | solution.py:370
  (6 shorter events, 0.0 us)
Async XLA Ops:
  3.2 19.5 %collective-permute-start.2 = (bf16[3,8,64,128]{3,2,1,0:T(8,128)(2,1)S(1)}, bf16[3,8,64,128]{3,2,1,0:T(8,128)(2,1)S(1)}, u32[]{:S(2)}, u32[]{:S(2)}) collective-permute-start(bf16[3,8,64,128]{3,2,1,0:T(8,128)(2,1)S(1)} %get-tuple-element.35), channel_id=1, source_target_pairs={{0,4},{2,6},{4,0},{6,2},{8,12},{10,14},{12,8},{14,10},{1,5},{3,7},... | collective-permute-start | bytes 1179656 | tf_op jit(solution)/shard_map/ppermute | solution.py:37
  6.3 16.4 %collective-permute-start.3 = (bf16[3,8,64,128]{3,2,1,0:T(8,128)(2,1)S(1)}, bf16[3,8,64,128]{3,2,1,0:T(8,128)(2,1)S(1)}, u32[]{:S(2)}, u32[]{:S(2)}) collective-permute-start(bf16[3,8,64,128]{3,2,1,0:T(8,128)(2,1)S(1)} %get-tuple-element.36), channel_id=1, source_target_pairs={{4,8},{6,10},{8,4},{10,6},{5,9},{7,11},{9,5},{11,7},{20,24},{22,26... | collective-permute-start | bytes 1179656 | tf_op jit(solution)/shard_map/ppermute | solution.py:37
  7.0 12.6 %collective-permute-start = (bf16[3,3,64,128]{3,2,1,0:T(8,128)(2,1)S(1)}, bf16[3,3,64,128]{3,2,1,0:T(8,128)(2,1)S(1)}, u32[]{:S(2)}, u32[]{:S(2)}) collective-permute-start(bf16[3,3,64,128]{3,2,1,0:T(8,128)(2,1)S(1)} %get-tuple-element.33), channel_id=1, source_target_pairs={{0,6},{2,4},{4,2},{6,0},{8,14},{10,12},{12,10},{14,8},{1,7},{3,5},... | collective-permute-start | bytes 442376 | tf_op jit(solution)/shard_map/ppermute | solution.py:37
  12.2 9.7 %collective-permute-start.1 = (bf16[3,3,64,128]{3,2,1,0:T(8,128)(2,1)S(1)}, bf16[3,3,64,128]{3,2,1,0:T(8,128)(2,1)S(1)}, u32[]{:S(2)}, u32[]{:S(2)}) collective-permute-start(bf16[3,3,64,128]{3,2,1,0:T(8,128)(2,1)S(1)} %get-tuple-element.34), channel_id=1, source_target_pairs={{4,10},{6,8},{8,6},{10,4},{5,11},{7,9},{9,7},{11,5},{20,26},{22,24... | collective-permute-start | bytes 442376 | tf_op jit(solution)/shard_map/ppermute | solution.py:37
  12.8 9.8 %collective-permute-start.4 = (bf16[4,3,64,128]{3,2,1,0:T(8,128)(2,1)S(1)}, bf16[4,3,64,128]{3,2,1,0:T(8,128)(2,1)S(1)}, u32[]{:S(2)}, u32[]{:S(2)}) collective-permute-start(bf16[4,3,64,128]{3,2,1,0:T(8,128)(2,1)S(1)} %get-tuple-element.37), channel_id=1, source_target_pairs={{0,2},{2,0},{4,6},{6,4},{8,10},{10,8},{12,14},{14,12},{1,3},{3,1},... | collective-permute-start | bytes 589832 | tf_op jit(solution)/shard_map/ppermute | solution.py:37
  19.6 25.5 %collective-permute-start.8 = (bf16[3,8,64,128]{3,2,1,0:T(8,128)(2,1)S(1)}, bf16[3,8,64,128]{3,2,1,0:T(8,128)(2,1)S(1)}, u32[]{:S(2)}, u32[]{:S(2)}) collective-permute-start(bf16[3,8,64,128]{3,2,1,0:T(8,128)(2,1)S(1)} %get-tuple-element.50), channel_id=1, source_target_pairs={{0,4},{2,6},{4,0},{6,2},{8,12},{10,14},{12,8},{14,10},{1,5},{3,7},... | collective-permute-start | bytes 1179656 | tf_op jit(solution)/shard_map/ppermute | solution.py:37
  21.9 25.5 %collective-permute-start.9 = (bf16[3,8,64,128]{3,2,1,0:T(8,128)(2,1)S(1)}, bf16[3,8,64,128]{3,2,1,0:T(8,128)(2,1)S(1)}, u32[]{:S(2)}, u32[]{:S(2)}) collective-permute-start(bf16[3,8,64,128]{3,2,1,0:T(8,128)(2,1)S(1)} %get-tuple-element.51), channel_id=1, source_target_pairs={{4,8},{6,10},{8,4},{10,6},{5,9},{7,11},{9,5},{11,7},{20,24},{22,26... | collective-permute-start | bytes 1179656 | tf_op jit(solution)/shard_map/ppermute | solution.py:37
  25.4 1.5 %collective-permute-start.5 = (bf16[64,1024]{1,0:T(8,128)(2,1)S(1)}, bf16[64,1024]{1,0:T(8,128)(2,1)S(1)}, u32[]{:S(2)}, u32[]{:S(2)}) collective-permute-start(bf16[64,1024]{1,0:T(8,128)(2,1)S(1)} %get-tuple-element.38.refs_0_), channel_id=1, source_target_pairs={{0,1},{1,0},{2,3},{3,2},{4,5},{5,4},{6,7},{7,6},{8,9},{9,8},{10,11... | collective-permute-start | bytes 393224 | tf_op jit(solution)/shard_map/ppermute | solution.py:456
  25.4 17.5 %collective-permute-start.10 = (bf16[4,3,64,128]{3,2,1,0:T(8,128)(2,1)S(1)}, bf16[4,3,64,128]{3,2,1,0:T(8,128)(2,1)S(1)}, u32[]{:S(2)}, u32[]{:S(2)}) collective-permute-start(bf16[4,3,64,128]{3,2,1,0:T(8,128)(2,1)S(1)} %get-tuple-element.52), channel_id=1, source_target_pairs={{0,2},{2,0},{4,6},{6,4},{8,10},{10,8},{12,14},{14,12},{1,3},{3,1},... | collective-permute-start | bytes 589832 | tf_op jit(solution)/shard_map/ppermute | solution.py:37
  26.2 10.5 %collective-permute-start.7 = (bf16[3,3,64,128]{3,2,1,0:T(8,128)(2,1)S(1)}, bf16[3,3,64,128]{3,2,1,0:T(8,128)(2,1)S(1)}, u32[]{:S(2)}, u32[]{:S(2)}) collective-permute-start(bf16[3,3,64,128]{3,2,1,0:T(8,128)(2,1)S(1)} %get-tuple-element.49), channel_id=1, source_target_pairs={{4,10},{6,8},{8,6},{10,4},{5,11},{7,9},{9,7},{11,5},{20,26},{22,24... | collective-permute-start | bytes 442376 | tf_op jit(solution)/shard_map/ppermute | solution.py:37
  26.9 15.4 %collective-permute-start.6 = (bf16[3,3,64,128]{3,2,1,0:T(8,128)(2,1)S(1)}, bf16[3,3,64,128]{3,2,1,0:T(8,128)(2,1)S(1)}, u32[]{:S(2)}, u32[]{:S(2)}) collective-permute-start(bf16[3,3,64,128]{3,2,1,0:T(8,128)(2,1)S(1)} %get-tuple-element.48), channel_id=1, source_target_pairs={{0,6},{2,4},{4,2},{6,0},{8,14},{10,12},{12,10},{14,8},{1,7},{3,5},... | collective-permute-start | bytes 442376 | tf_op jit(solution)/shard_map/ppermute | solution.py:37
  36.7 15.7 %collective-permute-start.13 = (bf16[64,768]{1,0:T(8,128)(2,1)S(1)}, bf16[64,768]{1,0:T(8,128)(2,1)S(1)}, u32[]{:S(2)}, u32[]{:S(2)}) collective-permute-start(bf16[64,768]{1,0:T(8,128)(2,1)S(1)} %get-tuple-element.55), channel_id=1, source_target_pairs={{0,4},{2,6},{4,0},{6,2},{8,12},{10,14},{12,8},{14,10},{1,5},{3,7},... | collective-permute-start | bytes 294920 | tf_op jit(solution)/shard_map/ppermute | solution.py:37
  42.3 10.1 %collective-permute-start.14 = (bf16[64,768]{1,0:T(8,128)(2,1)S(1)}, bf16[64,768]{1,0:T(8,128)(2,1)S(1)}, u32[]{:S(2)}, u32[]{:S(2)}) collective-permute-start(bf16[64,768]{1,0:T(8,128)(2,1)S(1)} %get-tuple-element.56), channel_id=1, source_target_pairs={{4,8},{6,10},{8,4},{10,6},{5,9},{7,11},{9,5},{11,7},{20,24},{22,26... | collective-permute-start | bytes 294920 | tf_op jit(solution)/shard_map/ppermute | solution.py:37
  43.0 9.4 %collective-permute-start.15 = (bf16[64,512]{1,0:T(8,128)(2,1)S(1)}, bf16[64,512]{1,0:T(8,128)(2,1)S(1)}, u32[]{:S(2)}, u32[]{:S(2)}) collective-permute-start(bf16[64,512]{1,0:T(8,128)(2,1)S(1)} %get-tuple-element.57), channel_id=1, source_target_pairs={{0,2},{2,0},{4,6},{6,4},{8,10},{10,8},{12,14},{14,12},{1,3},{3,1},... | collective-permute-start | bytes 196616 | tf_op jit(solution)/shard_map/ppermute | solution.py:37
  45.1 7.3 %collective-permute-start.11 = (bf16[64,384]{1,0:T(8,128)(2,1)S(1)}, bf16[64,384]{1,0:T(8,128)(2,1)S(1)}, u32[]{:S(2)}, u32[]{:S(2)}) collective-permute-start(bf16[64,384]{1,0:T(8,128)(2,1)S(1)} %get-tuple-element.53), channel_id=1, source_target_pairs={{0,6},{2,4},{4,2},{6,0},{8,14},{10,12},{12,10},{14,8},{1,7},{3,5},... | collective-permute-start | bytes 147464 | tf_op jit(solution)/shard_map/ppermute | solution.py:37
  47.4 4.9 %collective-permute-start.12 = (bf16[64,384]{1,0:T(8,128)(2,1)S(1)}, bf16[64,384]{1,0:T(8,128)(2,1)S(1)}, u32[]{:S(2)}, u32[]{:S(2)}) collective-permute-start(bf16[64,384]{1,0:T(8,128)(2,1)S(1)} %get-tuple-element.54), channel_id=1, source_target_pairs={{4,10},{6,8},{8,6},{10,4},{5,11},{7,9},{9,7},{11,5},{20,26},{22,24... | collective-permute-start | bytes 147464 | tf_op jit(solution)/shard_map/ppermute | solution.py:37

commit v5 on v4

--- a/solution.py
+++ b/solution.py
@@ -39,9 +39,9 @@
 
 def plan(rows, cols):
     zs, xs = turns(lax.axis_size("strip")), turns(lax.axis_size("sub"))
-    pieces = [(q, r) for q in zs for r in xs]
-    pieces += [(q, None) for q in zs]
+    pieces = [(q, None) for q in zs]
     pieces += [(None, r) for r in xs]
+    pieces += [(q, r) for q in zs for r in xs]
     base, at = {(None, None): 0}, rows * cols
     for qz, qx in pieces:
         base[qz, qx] = at
@@ -128,6 +128,14 @@
     return hot(jnp.where(lane == j, e_ref[group : group + 1, :], -1), tile)
 
 
+def cut_kernel(pieces, rows, cols, x_ref, *refs):
+    copies = cuts(pieces, rows, cols, x_ref, refs[:-1], refs[-1], 0)
+    for copy in copies:
+        copy.start()
+    for copy in copies:
+        copy.wait()
+
+
 def slotted(x, out_ref, table, slots):
     n, picks = x.shape
     per = LANES // slots
@@ -144,13 +152,12 @@
 def head_kernel(base, pieces, rows, cols, slots, *refs):
     k = len(pieces)
     far, rest = refs[:7], refs[7:]
-    tgt_slabs, src_slabs, outs, rest = rest[:k], rest[k : 2 * k], rest[2 * k : 2 * k + 8], rest[2 * k + 8 :]
+    src_slabs, outs, rest = rest[:k], rest[k : k + 8], rest[k + 8 :]
     src_t, tgt_t, gh_ref, wt_ref, wh_ref, bt_ref, e_ref, m_ref = outs
     (s32, t32, og, table), near, sems = rest[:4], rest[4:-1], rest[-1]
     src_ref, tgt_ref, og_ref, ids_ref, w_in_ref, b_ref, w_out_ref = near
     fetches = [pltpu.make_async_copy(f, v, sems.at[i]) for i, (f, v) in enumerate(zip(far, near))]
-    slabs = cuts(pieces, rows, cols, far[1], tgt_slabs, sems, 7)
-    slabs += cuts(pieces, rows, cols, far[0], src_slabs, sems, 7 + k)
+    slabs = cuts(pieces, rows, cols, far[0], src_slabs, sems, 7)
     for copy in fetches[2:] + fetches[:2] + slabs:
         copy.start()
     px, n, _ = src_t.shape
@@ -399,7 +406,7 @@
     ]
 
     hidden = w_in.shape[1]
-    outs = [(s, BF16) for s in shapes] * 2 + [
+    outs = [(s, BF16) for s in shapes] + [
         ((px, n, channels), BF16),
         ((px, n, channels), BF16),
         ((hidden, n * slots), F32),
@@ -426,11 +433,20 @@
         + [((n * (slots + 1), out_grad.shape[3]), F32), ((n, LANES), jnp.int32)],
         args,
         far=len(args),
-        sems=len(args) + 2 * len(pieces),
+        sems=len(args) + len(pieces),
         limit=24,
     )
     k = len(pieces)
-    src_t, own_t, grad_hidden, w_t, w_half, b_t, e_ids, m_ids = made[2 * k :]
+    src_t, own_t, grad_hidden, w_t, w_half, b_t, e_ids, m_ids = made[k:]
+    cut_t = pl.pallas_call(
+        partial(cut_kernel, pieces, rows, cols),
+        name="cut",
+        out_shape=[jax.ShapeDtypeStruct(s, BF16) for s in shapes],
+        in_specs=[HB],
+        out_specs=[VM] * k,
+        scratch_shapes=[pltpu.SemaphoreType.DMA((k,))],
+        compiler_params=pltpu.CompilerParams(vmem_limit_bytes=4 * 2**20),
+    )(args[1])
 
     def halo_of(slabs):
         got = []
@@ -438,8 +454,8 @@
             got.append(swap(x, qz, qx).reshape(-1, channels))
         return got
 
-    tgt_halo = halo_of(made[:k])
-    src_halo = halo_of(made[k : 2 * k])
+    tgt_halo = halo_of(cut_t)
+    src_halo = halo_of(made[:k])
     starts = [base[q] for q in pieces]
     counts = [h.shape[0] // px for h in tgt_halo]
     costs, tgt_t = call(

time: 55.5 us -> 52.7 us (0.950)
  starting transfers between devices: 34.1 us -> 29.4 us
  Pallas kernels: 14.3 us -> 15.5 us
  waiting for transfers between devices: 6.05 us -> 6.79 us
    ppermute x15, starting transfers between devices: 34.1 us -> 29.3 us  [swap(): return lax.ppermute(x, ('strip', 'sub'), pairs)]
    pallas_call x0 -> x1, Pallas kernels: none -> 1.51 us  [shards(): pl.pallas_call(partial(cut_kernel, pieces, rows, cols), name='cut', out_s...]
    ppermute x15, waiting for transfers between devices: 6.05 us -> 6.79 us  [swap(): return lax.ppermute(x, ('strip', 'sub'), pairs)]
  transfers between devices with their start and end apart: 16 -> 16, of which waited for: 1 -> 3; matrix products, arithmetic and copies ran while one was open for 0% -> 0% of each run, Pallas kernels for 16% -> 21%
where the time goes in v5:
time: 52.7 us; the launch traced here: 52.4 us
  starting transfers between devices  29.4 us (56%)
  Pallas kernels  15.5 us (29%)
  waiting for transfers between devices  6.79 us (13%)
  between operations  0.75 us (1%)
    ppermute x15, starting transfers between devices, swap(): return lax.ppermute(x, ('strip', 'sub'), pairs)  29.3 us
    pallas_call x6, Pallas kernels, call(): pl.pallas_call(kernel, out_shape=[jax.ShapeDtypeStruct(s, d) for s, d in...  14 us
    ppermute x15, waiting for transfers between devices, swap(): return lax.ppermute(x, ('strip', 'sub'), pairs)  6.79 us
    pallas_call x1, Pallas kernels, shards(): pl.pallas_call(partial(cut_kernel, pieces, rows, cols), name='cut', out_s...  1.51 us
  transfers between devices with their start and end apart: 16, of which 3 were waited for; matrix products, arithmetic and copies ran while one was open for 0% of the time, Pallas kernels for 21%

profile of v5, /device:TPU:0, one launch (start us, length us, event | category | flops | bytes accessed | tf_op | source)
XLA Modules:
  0.0 52.4 jit_solution(14978806156805389872)
XLA Ops:
  0.6 1.5 %cut.1 = (bf16[3,8,64,128]{3,2,1,0:T(8,128)(2,1)S(1)}, bf16[3,8,64,128]{3,2,1,0:T(8,128)(2,1)S(1)}, bf16[4,3,64,128]{3,2,1,0:T(8,128)(2,1)S(1)}, bf16[3,3,64,128...) custom-call(bf16[4,8,64,128]{3,2,1,0:T(8,128)(2,1)} %x_ref.1), custom_call_target="tpu_custom_call" | custom-call | tf_op jit(solution)/shard_map/cut/pallas_call | solution.py:441
  2.1 3.1 %collective-permute-start = (bf16[3,8,64,128]{3,2,1,0:T(8,128)(2,1)S(1)}, bf16[3,8,64,128]{3,2,1,0:T(8,128)(2,1)S(1)}, u32[]{:S(2)}, u32[]{:S(2)}) collective-permute-start(bf16[3,8,64,128]{3,2,1,0:T(8,128)(2,1)S(1)} %get-tuple-element.33), channel_id=1, source_target_pairs={{0,4},{2,6},{4,0},{6,2},{8,12},{10,14},{12,8},{14,10},{1,5},{3,7},... | collective-permute-start | bytes 1179656 | tf_op jit(solution)/shard_map/ppermute | solution.py:37
  5.3 0.7 %collective-permute-start.1 = (bf16[3,8,64,128]{3,2,1,0:T(8,128)(2,1)S(1)}, bf16[3,8,64,128]{3,2,1,0:T(8,128)(2,1)S(1)}, u32[]{:S(2)}, u32[]{:S(2)}) collective-permute-start(bf16[3,8,64,128]{3,2,1,0:T(8,128)(2,1)S(1)} %get-tuple-element.34), channel_id=1, source_target_pairs={{4,8},{6,10},{8,4},{10,6},{5,9},{7,11},{9,5},{11,7},{20,24},{22,26... | collective-permute-start | bytes 1179656 | tf_op jit(solution)/shard_map/ppermute | solution.py:37
  5.9 5.4 %collective-permute-start.3 = (bf16[3,3,64,128]{3,2,1,0:T(8,128)(2,1)S(1)}, bf16[3,3,64,128]{3,2,1,0:T(8,128)(2,1)S(1)}, u32[]{:S(2)}, u32[]{:S(2)}) collective-permute-start(bf16[3,3,64,128]{3,2,1,0:T(8,128)(2,1)S(1)} %get-tuple-element.36), channel_id=1, source_target_pairs={{0,6},{2,4},{4,2},{6,0},{8,14},{10,12},{12,10},{14,8},{1,7},{3,5},... | collective-permute-start | bytes 442376 | tf_op jit(solution)/shard_map/ppermute | solution.py:37
  11.4 0.7 %collective-permute-start.4 = (bf16[3,3,64,128]{3,2,1,0:T(8,128)(2,1)S(1)}, bf16[3,3,64,128]{3,2,1,0:T(8,128)(2,1)S(1)}, u32[]{:S(2)}, u32[]{:S(2)}) collective-permute-start(bf16[3,3,64,128]{3,2,1,0:T(8,128)(2,1)S(1)} %get-tuple-element.37), channel_id=1, source_target_pairs={{4,10},{6,8},{8,6},{10,4},{5,11},{7,9},{9,7},{11,5},{20,26},{22,24... | collective-permute-start | bytes 442376 | tf_op jit(solution)/shard_map/ppermute | solution.py:37
  12.0 0.5 %collective-permute-start.2 = (bf16[4,3,64,128]{3,2,1,0:T(8,128)(2,1)S(1)}, bf16[4,3,64,128]{3,2,1,0:T(8,128)(2,1)S(1)}, u32[]{:S(2)}, u32[]{:S(2)}) collective-permute-start(bf16[4,3,64,128]{3,2,1,0:T(8,128)(2,1)S(1)} %get-tuple-element.35), channel_id=1, source_target_pairs={{0,2},{2,0},{4,6},{6,4},{8,10},{10,8},{12,14},{14,12},{1,3},{3,1},... | collective-permute-start | bytes 589832 | tf_op jit(solution)/shard_map/ppermute | solution.py:37
  12.6 2.2 %shard_map.86 = (bf16[3,8,64,128]{3,2,1,0:T(8,128)(2,1)S(1)}, bf16[3,8,64,128]{3,2,1,0:T(8,128)(2,1)S(1)}, bf16[4,3,64,128]{3,2,1,0:T(8,128)(2,1)S(1)}, bf16[3,3...) custom-call(bf16[4,8,64,128]{3,2,1,0:T(8,128)(2,1)} %refs_0_.1, ...), custom_call_target="tpu_custom_call" | custom-call | bytes 6000000 | tf_op jit(solution)/shard_map/pallas_call | solution.py:377
  14.7 4.1 %collective-permute-done.3 = bf16[3,3,64,128]{3,2,1,0:T(8,128)(2,1)S(1)} collective-permute-done((bf16[3,3,64,128]{3,2,1,0:T(8,128)(2,1)S(1)}, bf16[3,3,64,128]{3,2,1,0:T(8,128)(2,1)S(1)}, u32[]{:S(2)}, u32[]{:S(2)}) %collective-permute-start.3) | collective-permute-done | bytes 147488 | tf_op jit(solution)/shard_map/ppermute | solution.py:37
  18.8 0.7 %collective-permute-start.7 = (bf16[3,8,64,128]{3,2,1,0:T(8,128)(2,1)S(1)}, bf16[3,8,64,128]{3,2,1,0:T(8,128)(2,1)S(1)}, u32[]{:S(2)}, u32[]{:S(2)}) collective-permute-start(bf16[3,8,64,128]{3,2,1,0:T(8,128)(2,1)S(1)} %get-tuple-element.49), channel_id=1, source_target_pairs={{4,8},{6,10},{8,4},{10,6},{5,9},{7,11},{9,5},{11,7},{20,24},{22,26... | collective-permute-start | bytes 1179656 | tf_op jit(solution)/shard_map/ppermute | solution.py:37
  19.5 0.0 collective-permute-done.4
  19.5 5.3 %collective-permute-start.6 = (bf16[3,8,64,128]{3,2,1,0:T(8,128)(2,1)S(1)}, bf16[3,8,64,128]{3,2,1,0:T(8,128)(2,1)S(1)}, u32[]{:S(2)}, u32[]{:S(2)}) collective-permute-start(bf16[3,8,64,128]{3,2,1,0:T(8,128)(2,1)S(1)} %get-tuple-element.48), channel_id=1, source_target_pairs={{0,4},{2,6},{4,0},{6,2},{8,12},{10,14},{12,8},{14,10},{1,5},{3,7},... | collective-permute-start | bytes 1179656 | tf_op jit(solution)/shard_map/ppermute | solution.py:37
  24.8 0.0 collective-permute-done.1
  24.8 2.7 %shard_map.87 = (bf16[64,1024]{1,0:T(8,128)(2,1)S(1)}, bf16[64,128,128]{2,1,0:T(8,128)(2,1)S(1)}) custom-call(bf16[64,32,128]{2,1,0:T(8,128)(2,1)S(1)} %get-tuple-element.30.refs_0_, bf16[64,32,128]{2,1,0:T(8,128)(2,1)S(1)} %get-tuple-element.31.refs_1_.src_t, s32[8,128]{1,0:T(8,128)S(1)} %get-tuple-element.32.refs_2_.refs_6_.e_ref, ...), custom_call_target="tpu_custom_call" | custom-call | bytes 9000000 | tf_op jit(solution)/shard_map/pallas_call | solution.py:377
  27.5 0.0 collective-permute-start.5
  27.6 0.5 collective-permute-start.8
  28.1 2.0 %collective-permute-start.9 = (bf16[3,3,64,128]{3,2,1,0:T(8,128)(2,1)S(1)}, bf16[3,3,64,128]{3,2,1,0:T(8,128)(2,1)S(1)}, u32[]{:S(2)}, u32[]{:S(2)}) collective-permute-start(bf16[3,3,64,128]{3,2,1,0:T(8,128)(2,1)S(1)} %get-tuple-element.51), channel_id=1, source_target_pairs={{0,6},{2,4},{4,2},{6,0},{8,14},{10,12},{12,10},{14,8},{1,7},{3,5},... | collective-permute-start | bytes 442376 | tf_op jit(solution)/shard_map/ppermute | solution.py:37
  30.1 0.0 collective-permute-done.5.refs_1_
  30.1 0.7 %collective-permute-start.10 = (bf16[3,3,64,128]{3,2,1,0:T(8,128)(2,1)S(1)}, bf16[3,3,64,128]{3,2,1,0:T(8,128)(2,1)S(1)}, u32[]{:S(2)}, u32[]{:S(2)}) collective-permute-start(bf16[3,3,64,128]{3,2,1,0:T(8,128)(2,1)S(1)} %get-tuple-element.52), channel_id=1, source_target_pairs={{4,10},{6,8},{8,6},{10,4},{5,11},{7,9},{9,7},{11,5},{20,26},{22,24... | collective-permute-start | bytes 442376 | tf_op jit(solution)/shard_map/ppermute | solution.py:37
  30.8 1.9 %shard_map.88 = (bf16[64,1024]{1,0:T(8,128)(2,1)S(1)}, bf16[64,768]{1,0:T(8,128)(2,1)S(1)}, bf16[64,768]{1,0:T(8,128)(2,1)S(1)}, bf16[64,512]{1,0:T(8,128)(2,1)S...) custom-call(bf16[64,1024]{1,0:T(8,128)(2,1)S(1)} %get-tuple-element.38.refs_0_, ...), custom_call_target="tpu_custom_call" | custom-call | bytes 9000000 | tf_op jit(solution)/shard_map/pallas_call | solution.py:377
  32.7 2.3 %collective-permute-done.9 = bf16[3,3,64,128]{3,2,1,0:T(8,128)(2,1)S(1)} collective-permute-done((bf16[3,3,64,128]{3,2,1,0:T(8,128)(2,1)S(1)}, bf16[3,3,64,128]{3,2,1,0:T(8,128)(2,1)S(1)}, u32[]{:S(2)}, u32[]{:S(2)}) %collective-permute-start.9) | collective-permute-done | bytes 147488 | tf_op jit(solution)/shard_map/ppermute | solution.py:37
  35.0 2.0 %collective-permute-start.11 = (bf16[64,768]{1,0:T(8,128)(2,1)S(1)}, bf16[64,768]{1,0:T(8,128)(2,1)S(1)}, u32[]{:S(2)}, u32[]{:S(2)}) collective-permute-start(bf16[64,768]{1,0:T(8,128)(2,1)S(1)} %get-tuple-element.53), channel_id=1, source_target_pairs={{0,4},{2,6},{4,0},{6,2},{8,12},{10,14},{12,8},{14,10},{1,5},{3,7},... | collective-permute-start | bytes 294920 | tf_op jit(solution)/shard_map/ppermute | solution.py:37
  37.0 0.0 collective-permute-done.10
  37.0 0.7 %collective-permute-start.12 = (bf16[64,768]{1,0:T(8,128)(2,1)S(1)}, bf16[64,768]{1,0:T(8,128)(2,1)S(1)}, u32[]{:S(2)}, u32[]{:S(2)}) collective-permute-start(bf16[64,768]{1,0:T(8,128)(2,1)S(1)} %get-tuple-element.54), channel_id=1, source_target_pairs={{4,8},{6,10},{8,4},{10,6},{5,9},{7,11},{9,5},{11,7},{20,24},{22,26... | collective-permute-start | bytes 294920 | tf_op jit(solution)/shard_map/ppermute | solution.py:37
  37.7 0.4 collective-permute-done.8
  38.0 2.4 %collective-permute-start.13 = (bf16[64,512]{1,0:T(8,128)(2,1)S(1)}, bf16[64,512]{1,0:T(8,128)(2,1)S(1)}, u32[]{:S(2)}, u32[]{:S(2)}) collective-permute-start(bf16[64,512]{1,0:T(8,128)(2,1)S(1)} %get-tuple-element.55), channel_id=1, source_target_pairs={{0,2},{2,0},{4,6},{6,4},{8,10},{10,8},{12,14},{14,12},{1,3},{3,1},... | collective-permute-start | bytes 196616 | tf_op jit(solution)/shard_map/ppermute | solution.py:37
  40.4 4.1 %collective-permute-start.14 = (bf16[64,384]{1,0:T(8,128)(2,1)S(1)}, bf16[64,384]{1,0:T(8,128)(2,1)S(1)}, u32[]{:S(2)}, u32[]{:S(2)}) collective-permute-start(bf16[64,384]{1,0:T(8,128)(2,1)S(1)} %get-tuple-element.56), channel_id=1, source_target_pairs={{0,6},{2,4},{4,2},{6,0},{8,14},{10,12},{12,10},{14,8},{1,7},{3,5},... | collective-permute-start | bytes 147464 | tf_op jit(solution)/shard_map/ppermute | solution.py:37
  44.5 0.0 collective-permute-done.6
  44.5 0.7 %collective-permute-start.15 = (bf16[64,384]{1,0:T(8,128)(2,1)S(1)}, bf16[64,384]{1,0:T(8,128)(2,1)S(1)}, u32[]{:S(2)}, u32[]{:S(2)}) collective-permute-start(bf16[64,384]{1,0:T(8,128)(2,1)S(1)} %get-tuple-element.57), channel_id=1, source_target_pairs={{4,10},{6,8},{8,6},{10,4},{5,11},{7,9},{9,7},{11,5},{20,26},{22,24... | collective-permute-start | bytes 147464 | tf_op jit(solution)/shard_map/ppermute | solution.py:37
  45.2 0.5 shard_map.90.halo_t
  45.6 3.8 %shard_map.89 = (bf16[2048,128]{1,0:T(8,128)(2,1)}, f32[64,32,128]{2,1,0:T(8,128)S(1)}) custom-call(bf16[64,1024]{1,0:T(8,128)(2,1)S(1)} %get-tuple-element.44.gc_ref, s32[8,128]{1,0:T(8,128)S(1)} %get-tuple-element.32.refs_2_.refs_6_.e_ref, bf16[64,128,128]{2,1,0:T(8,128)(2,1)S(1)} %get-tuple-element.45.tgt_t, ...), custom_call_target="tpu_custom_call" | custom-call | bytes 12000000 | tf_op jit(solution)/shard_map/pallas_call | solution.py:377
  49.5 0.0 collective-permute-done.11.refs_0_
  49.5 2.9 %shard_map.91 = bf16[2048,128]{1,0:T(8,128)(2,1)} custom-call(f32[64,32,128]{2,1,0:T(8,128)S(1)} %get-tuple-element.47.own_ref, bf16[64,80,128]{2,1,0:T(8,128)(2,1)S(1)} %shard_map.90.halo_t, bf16[64,768]{1,0:T(8,128)(2,1)S(1)} %collective-permute-done.11.refs_0_, bf16[64,768]{1,0:T(8,128)(2,1)S(1)} %collective-permute-done.12.refs_1_, ...), custom_call_target="tpu_custom_call" | custom-call | bytes 9000000 | tf_op jit(solution)/shard_map/pallas_call | solution.py:377
  (7 shorter events, 0.0 us)
Async XLA Ops:
  2.1 22.6 %collective-permute-start = (bf16[3,8,64,128]{3,2,1,0:T(8,128)(2,1)S(1)}, bf16[3,8,64,128]{3,2,1,0:T(8,128)(2,1)S(1)}, u32[]{:S(2)}, u32[]{:S(2)}) collective-permute-start(bf16[3,8,64,128]{3,2,1,0:T(8,128)(2,1)S(1)} %get-tuple-element.33), channel_id=1, source_target_pairs={{0,4},{2,6},{4,0},{6,2},{8,12},{10,14},{12,8},{14,10},{1,5},{3,7},... | collective-permute-start | bytes 1179656 | tf_op jit(solution)/shard_map/ppermute | solution.py:37
  5.3 19.5 %collective-permute-start.1 = (bf16[3,8,64,128]{3,2,1,0:T(8,128)(2,1)S(1)}, bf16[3,8,64,128]{3,2,1,0:T(8,128)(2,1)S(1)}, u32[]{:S(2)}, u32[]{:S(2)}) collective-permute-start(bf16[3,8,64,128]{3,2,1,0:T(8,128)(2,1)S(1)} %get-tuple-element.34), channel_id=1, source_target_pairs={{4,8},{6,10},{8,4},{10,6},{5,9},{7,11},{9,5},{11,7},{20,24},{22,26... | collective-permute-start | bytes 1179656 | tf_op jit(solution)/shard_map/ppermute | solution.py:37
  5.9 12.9 %collective-permute-start.3 = (bf16[3,3,64,128]{3,2,1,0:T(8,128)(2,1)S(1)}, bf16[3,3,64,128]{3,2,1,0:T(8,128)(2,1)S(1)}, u32[]{:S(2)}, u32[]{:S(2)}) collective-permute-start(bf16[3,3,64,128]{3,2,1,0:T(8,128)(2,1)S(1)} %get-tuple-element.36), channel_id=1, source_target_pairs={{0,6},{2,4},{4,2},{6,0},{8,14},{10,12},{12,10},{14,8},{1,7},{3,5},... | collective-permute-start | bytes 442376 | tf_op jit(solution)/shard_map/ppermute | solution.py:37
  11.4 8.1 %collective-permute-start.4 = (bf16[3,3,64,128]{3,2,1,0:T(8,128)(2,1)S(1)}, bf16[3,3,64,128]{3,2,1,0:T(8,128)(2,1)S(1)}, u32[]{:S(2)}, u32[]{:S(2)}) collective-permute-start(bf16[3,3,64,128]{3,2,1,0:T(8,128)(2,1)S(1)} %get-tuple-element.37), channel_id=1, source_target_pairs={{4,10},{6,8},{8,6},{10,4},{5,11},{7,9},{9,7},{11,5},{20,26},{22,24... | collective-permute-start | bytes 442376 | tf_op jit(solution)/shard_map/ppermute | solution.py:37
  12.0 12.7 %collective-permute-start.2 = (bf16[4,3,64,128]{3,2,1,0:T(8,128)(2,1)S(1)}, bf16[4,3,64,128]{3,2,1,0:T(8,128)(2,1)S(1)}, u32[]{:S(2)}, u32[]{:S(2)}) collective-permute-start(bf16[4,3,64,128]{3,2,1,0:T(8,128)(2,1)S(1)} %get-tuple-element.35), channel_id=1, source_target_pairs={{0,2},{2,0},{4,6},{6,4},{8,10},{10,8},{12,14},{14,12},{1,3},{3,1},... | collective-permute-start | bytes 589832 | tf_op jit(solution)/shard_map/ppermute | solution.py:37
  18.8 21.6 %collective-permute-start.7 = (bf16[3,8,64,128]{3,2,1,0:T(8,128)(2,1)S(1)}, bf16[3,8,64,128]{3,2,1,0:T(8,128)(2,1)S(1)}, u32[]{:S(2)}, u32[]{:S(2)}) collective-permute-start(bf16[3,8,64,128]{3,2,1,0:T(8,128)(2,1)S(1)} %get-tuple-element.49), channel_id=1, source_target_pairs={{4,8},{6,10},{8,4},{10,6},{5,9},{7,11},{9,5},{11,7},{20,24},{22,26... | collective-permute-start | bytes 1179656 | tf_op jit(solution)/shard_map/ppermute | solution.py:37
  19.5 25.0 %collective-permute-start.6 = (bf16[3,8,64,128]{3,2,1,0:T(8,128)(2,1)S(1)}, bf16[3,8,64,128]{3,2,1,0:T(8,128)(2,1)S(1)}, u32[]{:S(2)}, u32[]{:S(2)}) collective-permute-start(bf16[3,8,64,128]{3,2,1,0:T(8,128)(2,1)S(1)} %get-tuple-element.48), channel_id=1, source_target_pairs={{0,4},{2,6},{4,0},{6,2},{8,12},{10,14},{12,8},{14,10},{1,5},{3,7},... | collective-permute-start | bytes 1179656 | tf_op jit(solution)/shard_map/ppermute | solution.py:37
  27.5 2.6 %collective-permute-start.5 = (bf16[64,1024]{1,0:T(8,128)(2,1)S(1)}, bf16[64,1024]{1,0:T(8,128)(2,1)S(1)}, u32[]{:S(2)}, u32[]{:S(2)}) collective-permute-start(bf16[64,1024]{1,0:T(8,128)(2,1)S(1)} %get-tuple-element.38.refs_0_), channel_id=1, source_target_pairs={{0,1},{1,0},{2,3},{3,2},{4,5},{5,4},{6,7},{7,6},{8,9},{9,8},{10,11... | collective-permute-start | bytes 393224 | tf_op jit(solution)/shard_map/ppermute | solution.py:472
  27.6 10.5 %collective-permute-start.8 = (bf16[4,3,64,128]{3,2,1,0:T(8,128)(2,1)S(1)}, bf16[4,3,64,128]{3,2,1,0:T(8,128)(2,1)S(1)}, u32[]{:S(2)}, u32[]{:S(2)}) collective-permute-start(bf16[4,3,64,128]{3,2,1,0:T(8,128)(2,1)S(1)} %get-tuple-element.50), channel_id=1, source_target_pairs={{0,2},{2,0},{4,6},{6,4},{8,10},{10,8},{12,14},{14,12},{1,3},{3,1},... | collective-permute-start | bytes 589832 | tf_op jit(solution)/shard_map/ppermute | solution.py:37
  28.1 6.9 %collective-permute-start.9 = (bf16[3,3,64,128]{3,2,1,0:T(8,128)(2,1)S(1)}, bf16[3,3,64,128]{3,2,1,0:T(8,128)(2,1)S(1)}, u32[]{:S(2)}, u32[]{:S(2)}) collective-permute-start(bf16[3,3,64,128]{3,2,1,0:T(8,128)(2,1)S(1)} %get-tuple-element.51), channel_id=1, source_target_pairs={{0,6},{2,4},{4,2},{6,0},{8,14},{10,12},{12,10},{14,8},{1,7},{3,5},... | collective-permute-start | bytes 442376 | tf_op jit(solution)/shard_map/ppermute | solution.py:37
  30.1 6.9 %collective-permute-start.10 = (bf16[3,3,64,128]{3,2,1,0:T(8,128)(2,1)S(1)}, bf16[3,3,64,128]{3,2,1,0:T(8,128)(2,1)S(1)}, u32[]{:S(2)}, u32[]{:S(2)}) collective-permute-start(bf16[3,3,64,128]{3,2,1,0:T(8,128)(2,1)S(1)} %get-tuple-element.52), channel_id=1, source_target_pairs={{4,10},{6,8},{8,6},{10,4},{5,11},{7,9},{9,7},{11,5},{20,26},{22,24... | collective-permute-start | bytes 442376 | tf_op jit(solution)/shard_map/ppermute | solution.py:37
  35.0 14.5 %collective-permute-start.11 = (bf16[64,768]{1,0:T(8,128)(2,1)S(1)}, bf16[64,768]{1,0:T(8,128)(2,1)S(1)}, u32[]{:S(2)}, u32[]{:S(2)}) collective-permute-start(bf16[64,768]{1,0:T(8,128)(2,1)S(1)} %get-tuple-element.53), channel_id=1, source_target_pairs={{0,4},{2,6},{4,0},{6,2},{8,12},{10,14},{12,8},{14,10},{1,5},{3,7},... | collective-permute-start | bytes 294920 | tf_op jit(solution)/shard_map/ppermute | solution.py:37
  37.0 12.5 %collective-permute-start.12 = (bf16[64,768]{1,0:T(8,128)(2,1)S(1)}, bf16[64,768]{1,0:T(8,128)(2,1)S(1)}, u32[]{:S(2)}, u32[]{:S(2)}) collective-permute-start(bf16[64,768]{1,0:T(8,128)(2,1)S(1)} %get-tuple-element.54), channel_id=1, source_target_pairs={{4,8},{6,10},{8,4},{10,6},{5,9},{7,11},{9,5},{11,7},{20,24},{22,26... | collective-permute-start | bytes 294920 | tf_op jit(solution)/shard_map/ppermute | solution.py:37
  38.0 11.4 %collective-permute-start.13 = (bf16[64,512]{1,0:T(8,128)(2,1)S(1)}, bf16[64,512]{1,0:T(8,128)(2,1)S(1)}, u32[]{:S(2)}, u32[]{:S(2)}) collective-permute-start(bf16[64,512]{1,0:T(8,128)(2,1)S(1)} %get-tuple-element.55), channel_id=1, source_target_pairs={{0,2},{2,0},{4,6},{6,4},{8,10},{10,8},{12,14},{14,12},{1,3},{3,1},... | collective-permute-start | bytes 196616 | tf_op jit(solution)/shard_map/ppermute | solution.py:37
  40.4 9.0 %collective-permute-start.14 = (bf16[64,384]{1,0:T(8,128)(2,1)S(1)}, bf16[64,384]{1,0:T(8,128)(2,1)S(1)}, u32[]{:S(2)}, u32[]{:S(2)}) collective-permute-start(bf16[64,384]{1,0:T(8,128)(2,1)S(1)} %get-tuple-element.56), channel_id=1, source_target_pairs={{0,6},{2,4},{4,2},{6,0},{8,14},{10,12},{12,10},{14,8},{1,7},{3,5},... | collective-permute-start | bytes 147464 | tf_op jit(solution)/shard_map/ppermute | solution.py:37
  44.5 4.9 %collective-permute-start.15 = (bf16[64,384]{1,0:T(8,128)(2,1)S(1)}, bf16[64,384]{1,0:T(8,128)(2,1)S(1)}, u32[]{:S(2)}, u32[]{:S(2)}) collective-permute-start(bf16[64,384]{1,0:T(8,128)(2,1)S(1)} %get-tuple-element.57), channel_id=1, source_target_pairs={{4,10},{6,8},{8,6},{10,4},{5,11},{7,9},{9,7},{11,5},{20,26},{22,24... | collective-permute-start | bytes 147464 | tf_op jit(solution)/shard_map/ppermute | solution.py:37

commit v6 on v5

--- a/solution.py
+++ b/solution.py
@@ -193,13 +193,13 @@
             rows_of = src[i // cols, lax.rem(i, cols)]
             dst[pl.ds(i * pitch, px), :] = rows_of.astype(F32)
 
-        loop(n, body)
+        loop(n, body, 8)
 
     def turn(p):
         src_t[p] = s32[pl.ds(p, n, stride=pitch), :].astype(BF16)
         tgt_t[p] = t32[pl.ds(p, n, stride=pitch), :].astype(BF16)
 
-    loop(px, turn)
+    loop(px, turn, 8)
     for copy in slabs:
         copy.wait()
 
@@ -207,8 +207,9 @@
 def corr_kernel(px, n, ext, starts, slots, *refs):
     k = len(starts)
     own_t, src_t, e_ref, tgt_refs = refs[0], refs[1], refs[2], refs[3 : 3 + k]
-    costs_ref, tgt_t, t32, corr = refs[3 + k :]
+    costs_ref, tgt_t, hot_ref, t32, corr = refs[3 + k :]
     ext_pad = tgt_t.shape[1]
+    tiles = ext_pad // LANES
     pitch = px + 1
     inv_root = 1.0 / math.sqrt(tgt_t.shape[2])
     for start, ref in zip(starts, tgt_refs):
@@ -220,30 +221,33 @@
         tp = jnp.concatenate([own_t[p], tp], axis=0)
         tgt_t[p] = tp
         c = lax.dot_general(src_t[p], tp, NT, preferred_element_type=F32) * inv_root
-        for t in range(ext_pad // LANES):
+        for t in range(tiles):
             corr[t, pl.ds(p, n, stride=pitch), :] = c[:, t * LANES : (t + 1) * LANES]
 
-    loop(px, per_pixel, 8)
+    loop(px, per_pixel, px)
     per = LANES // slots
     for g in range(n // per):
-        acc = jnp.zeros((px, LANES), F32)
+        left = []
         for j in range(per):
             b = g * per + j
-            for t in range(ext_pad // LANES):
-                acc += jnp.dot(
-                    corr[t, b * pitch : b * pitch + px, :].astype(BF16),
-                    pick_hot(e_ref, b, slots, t),
-                    preferred_element_type=F32,
-                )
-        costs_ref[:, g * LANES : (g + 1) * LANES] = acc.astype(BF16)
+            for t in range(tiles):
+                at = (b * tiles + t) * LANES
+                hot_ref[at : at + LANES, :] = pick_hot(e_ref, b, slots, t)
+                left.append(corr[t, b * pitch : b * pitch + px, :].astype(BF16))
+        high = per * tiles * LANES
+        costs_ref[:, g * LANES : (g + 1) * LANES] = jnp.dot(
+            jnp.concatenate(left, axis=1),
+            hot_ref[g * high : (g + 1) * high, :],
+            preferred_element_type=F32,
+        ).astype(BF16)
 
 
 def gelu_slope(x):
     c = math.sqrt(2.0 / math.pi)
     x2 = x * x
-    th = jnp.tanh(c * (x + 0.044715 * (x2 * x)))
-    inner = c * (1.0 + (3.0 * 0.044715) * x2)
-    return 0.5 * (1.0 + th) + (0.5 * x) * ((1.0 - th) * (1.0 + th)) * inner
+    th = jnp.tanh(x * (c + (c * 0.044715) * x2))
+    inner = x * (c + (c * 3.0 * 0.044715) * x2)
+    return (0.5 + 0.5 * th) * (1.0 + (1.0 - th) * inner)
 
 
 def decoder_kernel(rows, cols, slots, pieces, starts, counts, *refs):
@@ -290,19 +294,25 @@
                 i += 1
 
 
-def own_kernel(px, n, slots, gc_ref, e_ref, tgt_t, src_t, sg_ref, own_ref, pw, s32):
+def own_kernel(px, n, slots, gc_ref, hot_ref, tgt_t, src_t, sg_ref, own_ref, pw, s32):
     ext_pad = tgt_t.shape[1]
     pitch = px + 1
     inv_root = 1.0 / math.sqrt(tgt_t.shape[2])
     tiles = ext_pad // LANES
     per = LANES // slots
-    for b in range(n):
-        g = b // per
-        gc = gc_ref[:, g * LANES : (g + 1) * LANES]
-        for t in range(tiles):
-            pw[t, b * pitch : b * pitch + px, :] = lax.dot_general(
-                gc, pick_hot(e_ref, b, slots, t), NT, preferred_element_type=F32
-            )
+    high = per * tiles * LANES
+    for g in range(n // per):
+        w = lax.dot_general(
+            gc_ref[:, g * LANES : (g + 1) * LANES],
+            hot_ref[g * high : (g + 1) * high, :],
+            NT,
+            preferred_element_type=F32,
+        )
+        for j in range(per):
+            b = g * per + j
+            for t in range(tiles):
+                at = (j * tiles + t) * LANES
+                pw[t, b * pitch : b * pitch + px, :] = w[:, at : at + LANES]
 
     def per_pixel(p):
         tp = tgt_t[p]
@@ -316,7 +326,7 @@
                 )
         s32[pl.ds(p, n, stride=pitch), :] = sg * inv_root
 
-    loop(px, per_pixel, 8)
+    loop(px, per_pixel, px)
 
     def narrow(i):
         sg_ref[pl.ds(pl.multiple_of(i * px, px), px), :] = s32[pl.ds(i * pitch, px), :].astype(BF16)
@@ -336,7 +346,7 @@
     def turn(p):
         out[p] = s32[pl.ds(p, out.shape[1], stride=pitch), :].astype(BF16)
 
-    loop(px, turn)
+    loop(px, turn, 8)
 
 
 def total_kernel(px, n, slots, widths, own_ref, halo_t, *refs):
@@ -361,7 +371,7 @@
         )
         t32[pl.ds(p, n, stride=pitch), :] = tg * inv_root
 
-    loop(px, per_pixel, 8)
+    loop(px, per_pixel, px // 2)
 
     def narrow(i):
         tg_ref[pl.ds(pl.multiple_of(i * px, px), px), :] = t32[pl.ds(i * pitch, px), :].astype(BF16)
@@ -458,9 +468,13 @@
     src_halo = halo_of(made[:k])
     starts = [base[q] for q in pieces]
     counts = [h.shape[0] // px for h in tgt_halo]
-    costs, tgt_t = call(
+    costs, tgt_t, hots = call(
         partial(corr_kernel, px, n, ext, starts, slots),
-        [((px, n * slots), BF16), ((px, ext_pad, channels), BF16)],
+        [
+            ((px, n * slots), BF16),
+            ((px, ext_pad, channels), BF16),
+            ((n * ext_pad, LANES), BF16),
+        ],
         [
             (((ext_pad - n) * pitch, channels), F32),
             ((ext_pad // LANES, n * pitch, LANES), F32),
@@ -488,7 +502,7 @@
         partial(own_kernel, px, n, slots),
         [((n * px, channels), BF16), ((px, n, channels), F32)],
         [((ext_pad // LANES, n * pitch, LANES), F32), ((n * pitch, channels), F32)],
-        (gc, e_ids, tgt_t, src_t),
+        (gc, hots, tgt_t, src_t),
         us=4,
     )
     halo_pad = -(-(ext - n) // 16) * 16

time: 52.7 us -> 50.5 us (0.958)
  Pallas kernels: 15.5 us -> 11.7 us
  waiting for transfers between devices: 6.79 us -> 7.61 us
    pallas_call x6, Pallas kernels: 14 us -> 10.2 us  [call(): pl.pallas_call(kernel, out_shape=[jax.ShapeDtypeStruct(s, d) for s, d in...]
    ppermute x15, waiting for transfers between devices: 6.79 us -> 7.61 us  [swap(): return lax.ppermute(x, ('strip', 'sub'), pairs)]
  transfers between devices with their start and end apart: 16 -> 16, of which waited for: 3 -> 2; matrix products, arithmetic and copies ran while one was open for 0% -> 0% of each run, Pallas kernels for 21% -> 17%
where the time goes in v6:
time: 50.5 us; the launch traced here: 49.7 us
  starting transfers between devices  29.7 us (59%)
  Pallas kernels  11.7 us (23%)
  waiting for transfers between devices  7.61 us (15%)
  between operations  0.76 us (2%)
    ppermute x15, starting transfers between devices, swap(): return lax.ppermute(x, ('strip', 'sub'), pairs)  29.6 us
    pallas_call x6, Pallas kernels, call(): pl.pallas_call(kernel, out_shape=[jax.ShapeDtypeStruct(s, d) for s, d in...  10.2 us
    ppermute x15, waiting for transfers between devices, swap(): return lax.ppermute(x, ('strip', 'sub'), pairs)  7.61 us
    pallas_call x1, Pallas kernels, shards(): pl.pallas_call(partial(cut_kernel, pieces, rows, cols), name='cut', out_s...  1.51 us
  transfers between devices with their start and end apart: 16, of which 2 were waited for; matrix products, arithmetic and copies ran while one was open for 0% of the time, Pallas kernels for 17%

profile of v6, /device:TPU:0, one launch (start us, length us, event | category | flops | bytes accessed | tf_op | source)
XLA Modules:
  0.0 49.7 jit_solution(18172435919890005020)
XLA Ops:
  0.6 1.5 %cut.1 = (bf16[3,8,64,128]{3,2,1,0:T(8,128)(2,1)S(1)}, bf16[3,8,64,128]{3,2,1,0:T(8,128)(2,1)S(1)}, bf16[4,3,64,128]{3,2,1,0:T(8,128)(2,1)S(1)}, bf16[3,3,64,128...) custom-call(bf16[4,8,64,128]{3,2,1,0:T(8,128)(2,1)} %x_ref.1), custom_call_target="tpu_custom_call" | custom-call | tf_op jit(solution)/shard_map/cut/pallas_call | solution.py:451
  2.1 3.1 %collective-permute-start = (bf16[3,8,64,128]{3,2,1,0:T(8,128)(2,1)S(1)}, bf16[3,8,64,128]{3,2,1,0:T(8,128)(2,1)S(1)}, u32[]{:S(2)}, u32[]{:S(2)}) collective-permute-start(bf16[3,8,64,128]{3,2,1,0:T(8,128)(2,1)S(1)} %get-tuple-element.34), channel_id=1, source_target_pairs={{0,4},{2,6},{4,0},{6,2},{8,12},{10,14},{12,8},{14,10},{1,5},{3,7},... | collective-permute-start | bytes 1179656 | tf_op jit(solution)/shard_map/ppermute | solution.py:37
  5.3 0.7 %collective-permute-start.1 = (bf16[3,8,64,128]{3,2,1,0:T(8,128)(2,1)S(1)}, bf16[3,8,64,128]{3,2,1,0:T(8,128)(2,1)S(1)}, u32[]{:S(2)}, u32[]{:S(2)}) collective-permute-start(bf16[3,8,64,128]{3,2,1,0:T(8,128)(2,1)S(1)} %get-tuple-element.35), channel_id=1, source_target_pairs={{4,8},{6,10},{8,4},{10,6},{5,9},{7,11},{9,5},{11,7},{20,24},{22,26... | collective-permute-start | bytes 1179656 | tf_op jit(solution)/shard_map/ppermute | solution.py:37
  5.9 5.4 %collective-permute-start.3 = (bf16[3,3,64,128]{3,2,1,0:T(8,128)(2,1)S(1)}, bf16[3,3,64,128]{3,2,1,0:T(8,128)(2,1)S(1)}, u32[]{:S(2)}, u32[]{:S(2)}) collective-permute-start(bf16[3,3,64,128]{3,2,1,0:T(8,128)(2,1)S(1)} %get-tuple-element.37), channel_id=1, source_target_pairs={{0,6},{2,4},{4,2},{6,0},{8,14},{10,12},{12,10},{14,8},{1,7},{3,5},... | collective-permute-start | bytes 442376 | tf_op jit(solution)/shard_map/ppermute | solution.py:37
  11.4 0.7 %collective-permute-start.4 = (bf16[3,3,64,128]{3,2,1,0:T(8,128)(2,1)S(1)}, bf16[3,3,64,128]{3,2,1,0:T(8,128)(2,1)S(1)}, u32[]{:S(2)}, u32[]{:S(2)}) collective-permute-start(bf16[3,3,64,128]{3,2,1,0:T(8,128)(2,1)S(1)} %get-tuple-element.38), channel_id=1, source_target_pairs={{4,10},{6,8},{8,6},{10,4},{5,11},{7,9},{9,7},{11,5},{20,26},{22,24... | collective-permute-start | bytes 442376 | tf_op jit(solution)/shard_map/ppermute | solution.py:37
  12.0 0.5 %collective-permute-start.2 = (bf16[4,3,64,128]{3,2,1,0:T(8,128)(2,1)S(1)}, bf16[4,3,64,128]{3,2,1,0:T(8,128)(2,1)S(1)}, u32[]{:S(2)}, u32[]{:S(2)}) collective-permute-start(bf16[4,3,64,128]{3,2,1,0:T(8,128)(2,1)S(1)} %get-tuple-element.36), channel_id=1, source_target_pairs={{0,2},{2,0},{4,6},{6,4},{8,10},{10,8},{12,14},{14,12},{1,3},{3,1},... | collective-permute-start | bytes 589832 | tf_op jit(solution)/shard_map/ppermute | solution.py:37
  12.6 2.1 %shard_map.86 = (bf16[3,8,64,128]{3,2,1,0:T(8,128)(2,1)S(1)}, bf16[3,8,64,128]{3,2,1,0:T(8,128)(2,1)S(1)}, bf16[4,3,64,128]{3,2,1,0:T(8,128)(2,1)S(1)}, bf16[3,3...) custom-call(bf16[4,8,64,128]{3,2,1,0:T(8,128)(2,1)} %refs_0_.1, ...), custom_call_target="tpu_custom_call" | custom-call | bytes 6000000 | tf_op jit(solution)/shard_map/pallas_call | solution.py:387
  14.7 4.1 %collective-permute-done.3 = bf16[3,3,64,128]{3,2,1,0:T(8,128)(2,1)S(1)} collective-permute-done((bf16[3,3,64,128]{3,2,1,0:T(8,128)(2,1)S(1)}, bf16[3,3,64,128]{3,2,1,0:T(8,128)(2,1)S(1)}, u32[]{:S(2)}, u32[]{:S(2)}) %collective-permute-start.3) | collective-permute-done | bytes 147488 | tf_op jit(solution)/shard_map/ppermute | solution.py:37
  18.8 0.7 %collective-permute-start.7 = (bf16[3,8,64,128]{3,2,1,0:T(8,128)(2,1)S(1)}, bf16[3,8,64,128]{3,2,1,0:T(8,128)(2,1)S(1)}, u32[]{:S(2)}, u32[]{:S(2)}) collective-permute-start(bf16[3,8,64,128]{3,2,1,0:T(8,128)(2,1)S(1)} %get-tuple-element.51), channel_id=1, source_target_pairs={{4,8},{6,10},{8,4},{10,6},{5,9},{7,11},{9,5},{11,7},{20,24},{22,26... | collective-permute-start | bytes 1179656 | tf_op jit(solution)/shard_map/ppermute | solution.py:37
  19.5 0.0 collective-permute-done.4
  19.5 5.3 %collective-permute-start.6 = (bf16[3,8,64,128]{3,2,1,0:T(8,128)(2,1)S(1)}, bf16[3,8,64,128]{3,2,1,0:T(8,128)(2,1)S(1)}, u32[]{:S(2)}, u32[]{:S(2)}) collective-permute-start(bf16[3,8,64,128]{3,2,1,0:T(8,128)(2,1)S(1)} %get-tuple-element.50), channel_id=1, source_target_pairs={{0,4},{2,6},{4,0},{6,2},{8,12},{10,14},{12,8},{14,10},{1,5},{3,7},... | collective-permute-start | bytes 1179656 | tf_op jit(solution)/shard_map/ppermute | solution.py:37
  24.8 0.0 collective-permute-done.1
  24.8 1.8 %shard_map.87 = (bf16[64,1024]{1,0:T(8,128)(2,1)S(1)}, bf16[64,128,128]{2,1,0:T(8,128)(2,1)S(1)}, bf16[4096,128]{1,0:T(8,128)(2,1)S(1)}) custom-call(bf16[64,32,128]{2,1,0:T(8,128)(2,1)S(1)} %get-tuple-element.31.refs_0_, bf16[64,32,128]{2,1,0:T(8,128)(2,1)S(1)} %get-tuple-element.32.refs_1_.src_t, s32[8,128]{1,0:T(8,128)S(1)} %get-tuple-element.33.refs_2_.refs_6_, ...), custom_call_target="tpu_custom_call" | custom-call | bytes 9000000 | tf_op jit(solution)/shard_map/pallas_call | solution.py:387
  26.6 0.1 collective-permute-start.5
  26.7 0.5 %collective-permute-start.8 = (bf16[4,3,64,128]{3,2,1,0:T(8,128)(2,1)S(1)}, bf16[4,3,64,128]{3,2,1,0:T(8,128)(2,1)S(1)}, u32[]{:S(2)}, u32[]{:S(2)}) collective-permute-start(bf16[4,3,64,128]{3,2,1,0:T(8,128)(2,1)S(1)} %get-tuple-element.52), channel_id=1, source_target_pairs={{0,2},{2,0},{4,6},{6,4},{8,10},{10,8},{12,14},{14,12},{1,3},{3,1},... | collective-permute-start | bytes 589832 | tf_op jit(solution)/shard_map/ppermute | solution.py:37
  27.2 2.0 %collective-permute-start.9 = (bf16[3,3,64,128]{3,2,1,0:T(8,128)(2,1)S(1)}, bf16[3,3,64,128]{3,2,1,0:T(8,128)(2,1)S(1)}, u32[]{:S(2)}, u32[]{:S(2)}) collective-permute-start(bf16[3,3,64,128]{3,2,1,0:T(8,128)(2,1)S(1)} %get-tuple-element.53), channel_id=1, source_target_pairs={{0,6},{2,4},{4,2},{6,0},{8,14},{10,12},{12,10},{14,8},{1,7},{3,5},... | collective-permute-start | bytes 442376 | tf_op jit(solution)/shard_map/ppermute | solution.py:37
  29.2 0.0 collective-permute-done.5.refs_1_
  29.2 0.7 %collective-permute-start.10 = (bf16[3,3,64,128]{3,2,1,0:T(8,128)(2,1)S(1)}, bf16[3,3,64,128]{3,2,1,0:T(8,128)(2,1)S(1)}, u32[]{:S(2)}, u32[]{:S(2)}) collective-permute-start(bf16[3,3,64,128]{3,2,1,0:T(8,128)(2,1)S(1)} %get-tuple-element.54), channel_id=1, source_target_pairs={{4,10},{6,8},{8,6},{10,4},{5,11},{7,9},{9,7},{11,5},{20,26},{22,24... | collective-permute-start | bytes 442376 | tf_op jit(solution)/shard_map/ppermute | solution.py:37
  29.9 1.8 %shard_map.88 = (bf16[64,1024]{1,0:T(8,128)(2,1)S(1)}, bf16[64,768]{1,0:T(8,128)(2,1)S(1)}, bf16[64,768]{1,0:T(8,128)(2,1)S(1)}, bf16[64,512]{1,0:T(8,128)(2,1)S...) custom-call(bf16[64,1024]{1,0:T(8,128)(2,1)S(1)} %get-tuple-element.39.refs_0_, ...), custom_call_target="tpu_custom_call" | custom-call | bytes 9000000 | tf_op jit(solution)/shard_map/pallas_call | solution.py:387
  31.7 3.4 %collective-permute-done.9 = bf16[3,3,64,128]{3,2,1,0:T(8,128)(2,1)S(1)} collective-permute-done((bf16[3,3,64,128]{3,2,1,0:T(8,128)(2,1)S(1)}, bf16[3,3,64,128]{3,2,1,0:T(8,128)(2,1)S(1)}, u32[]{:S(2)}, u32[]{:S(2)}) %collective-permute-start.9) | collective-permute-done | bytes 147488 | tf_op jit(solution)/shard_map/ppermute | solution.py:37
  35.1 2.7 %collective-permute-start.11 = (bf16[64,768]{1,0:T(8,128)(2,1)S(1)}, bf16[64,768]{1,0:T(8,128)(2,1)S(1)}, u32[]{:S(2)}, u32[]{:S(2)}) collective-permute-start(bf16[64,768]{1,0:T(8,128)(2,1)S(1)} %get-tuple-element.55), channel_id=1, source_target_pairs={{0,4},{2,6},{4,0},{6,2},{8,12},{10,14},{12,8},{14,10},{1,5},{3,7},... | collective-permute-start | bytes 294920 | tf_op jit(solution)/shard_map/ppermute | solution.py:37
  37.8 0.0 collective-permute-done.10
  37.8 0.7 %collective-permute-start.12 = (bf16[64,768]{1,0:T(8,128)(2,1)S(1)}, bf16[64,768]{1,0:T(8,128)(2,1)S(1)}, u32[]{:S(2)}, u32[]{:S(2)}) collective-permute-start(bf16[64,768]{1,0:T(8,128)(2,1)S(1)} %get-tuple-element.56), channel_id=1, source_target_pairs={{4,8},{6,10},{8,4},{10,6},{5,9},{7,11},{9,5},{11,7},{20,24},{22,26... | collective-permute-start | bytes 294920 | tf_op jit(solution)/shard_map/ppermute | solution.py:37
  38.5 0.0 collective-permute-done.8
  38.5 2.3 %collective-permute-start.13 = (bf16[64,512]{1,0:T(8,128)(2,1)S(1)}, bf16[64,512]{1,0:T(8,128)(2,1)S(1)}, u32[]{:S(2)}, u32[]{:S(2)}) collective-permute-start(bf16[64,512]{1,0:T(8,128)(2,1)S(1)} %get-tuple-element.57), channel_id=1, source_target_pairs={{0,2},{2,0},{4,6},{6,4},{8,10},{10,8},{12,14},{14,12},{1,3},{3,1},... | collective-permute-start | bytes 196616 | tf_op jit(solution)/shard_map/ppermute | solution.py:37
  40.8 3.7 %collective-permute-start.14 = (bf16[64,384]{1,0:T(8,128)(2,1)S(1)}, bf16[64,384]{1,0:T(8,128)(2,1)S(1)}, u32[]{:S(2)}, u32[]{:S(2)}) collective-permute-start(bf16[64,384]{1,0:T(8,128)(2,1)S(1)} %get-tuple-element.58), channel_id=1, source_target_pairs={{0,6},{2,4},{4,2},{6,0},{8,14},{10,12},{12,10},{14,8},{1,7},{3,5},... | collective-permute-start | bytes 147464 | tf_op jit(solution)/shard_map/ppermute | solution.py:37
  44.5 0.7 %collective-permute-start.15 = (bf16[64,384]{1,0:T(8,128)(2,1)S(1)}, bf16[64,384]{1,0:T(8,128)(2,1)S(1)}, u32[]{:S(2)}, u32[]{:S(2)}) collective-permute-start(bf16[64,384]{1,0:T(8,128)(2,1)S(1)} %get-tuple-element.59), channel_id=1, source_target_pairs={{4,10},{6,8},{8,6},{10,4},{5,11},{7,9},{9,7},{11,5},{20,26},{22,24... | collective-permute-start | bytes 147464 | tf_op jit(solution)/shard_map/ppermute | solution.py:37
  45.2 0.4 shard_map.90.halo_t
  45.6 2.2 %shard_map.89 = (bf16[2048,128]{1,0:T(8,128)(2,1)}, f32[64,32,128]{2,1,0:T(8,128)S(1)}) custom-call(bf16[64,1024]{1,0:T(8,128)(2,1)S(1)} %get-tuple-element.45.gc_ref, bf16[4096,128]{1,0:T(8,128)(2,1)S(1)} %get-tuple-element.46.hot_ref, bf16[64,128,128]{2,1,0:T(8,128)(2,1)S(1)} %get-tuple-element.47.tgt_t, ...), custom_call_target="tpu_custom_call" | custom-call | bytes 12000000 | tf_op jit(solution)/shard_map/pallas_call | solution.py:387
  47.8 0.0 collective-permute-done.11.refs_0_
  47.9 0.0 collective-permute-done.12.refs_1_
  47.9 1.9 %shard_map.91 = bf16[2048,128]{1,0:T(8,128)(2,1)} custom-call(f32[64,32,128]{2,1,0:T(8,128)S(1)} %get-tuple-element.49.own_ref, bf16[64,80,128]{2,1,0:T(8,128)(2,1)S(1)} %shard_map.90.halo_t, bf16[64,768]{1,0:T(8,128)(2,1)S(1)} %collective-permute-done.11.refs_0_, bf16[64,768]{1,0:T(8,128)(2,1)S(1)} %collective-permute-done.12.refs_1_, ...), custom_call_target="tpu_custom_call" | custom-call | bytes 9000000 | tf_op jit(solution)/shard_map/pallas_call | solution.py:387
  (7 shorter events, 0.0 us)
Async XLA Ops:
  2.1 22.6 %collective-permute-start = (bf16[3,8,64,128]{3,2,1,0:T(8,128)(2,1)S(1)}, bf16[3,8,64,128]{3,2,1,0:T(8,128)(2,1)S(1)}, u32[]{:S(2)}, u32[]{:S(2)}) collective-permute-start(bf16[3,8,64,128]{3,2,1,0:T(8,128)(2,1)S(1)} %get-tuple-element.34), channel_id=1, source_target_pairs={{0,4},{2,6},{4,0},{6,2},{8,12},{10,14},{12,8},{14,10},{1,5},{3,7},... | collective-permute-start | bytes 1179656 | tf_op jit(solution)/shard_map/ppermute | solution.py:37
  5.3 19.5 %collective-permute-start.1 = (bf16[3,8,64,128]{3,2,1,0:T(8,128)(2,1)S(1)}, bf16[3,8,64,128]{3,2,1,0:T(8,128)(2,1)S(1)}, u32[]{:S(2)}, u32[]{:S(2)}) collective-permute-start(bf16[3,8,64,128]{3,2,1,0:T(8,128)(2,1)S(1)} %get-tuple-element.35), channel_id=1, source_target_pairs={{4,8},{6,10},{8,4},{10,6},{5,9},{7,11},{9,5},{11,7},{20,24},{22,26... | collective-permute-start | bytes 1179656 | tf_op jit(solution)/shard_map/ppermute | solution.py:37
  5.9 12.9 %collective-permute-start.3 = (bf16[3,3,64,128]{3,2,1,0:T(8,128)(2,1)S(1)}, bf16[3,3,64,128]{3,2,1,0:T(8,128)(2,1)S(1)}, u32[]{:S(2)}, u32[]{:S(2)}) collective-permute-start(bf16[3,3,64,128]{3,2,1,0:T(8,128)(2,1)S(1)} %get-tuple-element.37), channel_id=1, source_target_pairs={{0,6},{2,4},{4,2},{6,0},{8,14},{10,12},{12,10},{14,8},{1,7},{3,5},... | collective-permute-start | bytes 442376 | tf_op jit(solution)/shard_map/ppermute | solution.py:37
  11.4 8.1 %collective-permute-start.4 = (bf16[3,3,64,128]{3,2,1,0:T(8,128)(2,1)S(1)}, bf16[3,3,64,128]{3,2,1,0:T(8,128)(2,1)S(1)}, u32[]{:S(2)}, u32[]{:S(2)}) collective-permute-start(bf16[3,3,64,128]{3,2,1,0:T(8,128)(2,1)S(1)} %get-tuple-element.38), channel_id=1, source_target_pairs={{4,10},{6,8},{8,6},{10,4},{5,11},{7,9},{9,7},{11,5},{20,26},{22,24... | collective-permute-start | bytes 442376 | tf_op jit(solution)/shard_map/ppermute | solution.py:37
  12.0 12.7 %collective-permute-start.2 = (bf16[4,3,64,128]{3,2,1,0:T(8,128)(2,1)S(1)}, bf16[4,3,64,128]{3,2,1,0:T(8,128)(2,1)S(1)}, u32[]{:S(2)}, u32[]{:S(2)}) collective-permute-start(bf16[4,3,64,128]{3,2,1,0:T(8,128)(2,1)S(1)} %get-tuple-element.36), channel_id=1, source_target_pairs={{0,2},{2,0},{4,6},{6,4},{8,10},{10,8},{12,14},{14,12},{1,3},{3,1},... | collective-permute-start | bytes 589832 | tf_op jit(solution)/shard_map/ppermute | solution.py:37
  18.8 22.0 %collective-permute-start.7 = (bf16[3,8,64,128]{3,2,1,0:T(8,128)(2,1)S(1)}, bf16[3,8,64,128]{3,2,1,0:T(8,128)(2,1)S(1)}, u32[]{:S(2)}, u32[]{:S(2)}) collective-permute-start(bf16[3,8,64,128]{3,2,1,0:T(8,128)(2,1)S(1)} %get-tuple-element.51), channel_id=1, source_target_pairs={{4,8},{6,10},{8,4},{10,6},{5,9},{7,11},{9,5},{11,7},{20,24},{22,26... | collective-permute-start | bytes 1179656 | tf_op jit(solution)/shard_map/ppermute | solution.py:37
  19.5 25.0 %collective-permute-start.6 = (bf16[3,8,64,128]{3,2,1,0:T(8,128)(2,1)S(1)}, bf16[3,8,64,128]{3,2,1,0:T(8,128)(2,1)S(1)}, u32[]{:S(2)}, u32[]{:S(2)}) collective-permute-start(bf16[3,8,64,128]{3,2,1,0:T(8,128)(2,1)S(1)} %get-tuple-element.50), channel_id=1, source_target_pairs={{0,4},{2,6},{4,0},{6,2},{8,12},{10,14},{12,8},{14,10},{1,5},{3,7},... | collective-permute-start | bytes 1179656 | tf_op jit(solution)/shard_map/ppermute | solution.py:37
  26.6 2.6 %collective-permute-start.5 = (bf16[64,1024]{1,0:T(8,128)(2,1)S(1)}, bf16[64,1024]{1,0:T(8,128)(2,1)S(1)}, u32[]{:S(2)}, u32[]{:S(2)}) collective-permute-start(bf16[64,1024]{1,0:T(8,128)(2,1)S(1)} %get-tuple-element.39.refs_0_), channel_id=1, source_target_pairs={{0,1},{1,0},{2,3},{3,2},{4,5},{5,4},{6,7},{7,6},{8,9},{9,8},{10,11... | collective-permute-start | bytes 393224 | tf_op jit(solution)/shard_map/ppermute | solution.py:486
  26.7 11.8 %collective-permute-start.8 = (bf16[4,3,64,128]{3,2,1,0:T(8,128)(2,1)S(1)}, bf16[4,3,64,128]{3,2,1,0:T(8,128)(2,1)S(1)}, u32[]{:S(2)}, u32[]{:S(2)}) collective-permute-start(bf16[4,3,64,128]{3,2,1,0:T(8,128)(2,1)S(1)} %get-tuple-element.52), channel_id=1, source_target_pairs={{0,2},{2,0},{4,6},{6,4},{8,10},{10,8},{12,14},{14,12},{1,3},{3,1},... | collective-permute-start | bytes 589832 | tf_op jit(solution)/shard_map/ppermute | solution.py:37
  27.2 7.9 %collective-permute-start.9 = (bf16[3,3,64,128]{3,2,1,0:T(8,128)(2,1)S(1)}, bf16[3,3,64,128]{3,2,1,0:T(8,128)(2,1)S(1)}, u32[]{:S(2)}, u32[]{:S(2)}) collective-permute-start(bf16[3,3,64,128]{3,2,1,0:T(8,128)(2,1)S(1)} %get-tuple-element.53), channel_id=1, source_target_pairs={{0,6},{2,4},{4,2},{6,0},{8,14},{10,12},{12,10},{14,8},{1,7},{3,5},... | collective-permute-start | bytes 442376 | tf_op jit(solution)/shard_map/ppermute | solution.py:37
  29.2 8.6 %collective-permute-start.10 = (bf16[3,3,64,128]{3,2,1,0:T(8,128)(2,1)S(1)}, bf16[3,3,64,128]{3,2,1,0:T(8,128)(2,1)S(1)}, u32[]{:S(2)}, u32[]{:S(2)}) collective-permute-start(bf16[3,3,64,128]{3,2,1,0:T(8,128)(2,1)S(1)} %get-tuple-element.54), channel_id=1, source_target_pairs={{4,10},{6,8},{8,6},{10,4},{5,11},{7,9},{9,7},{11,5},{20,26},{22,24... | collective-permute-start | bytes 442376 | tf_op jit(solution)/shard_map/ppermute | solution.py:37
  35.1 12.8 %collective-permute-start.11 = (bf16[64,768]{1,0:T(8,128)(2,1)S(1)}, bf16[64,768]{1,0:T(8,128)(2,1)S(1)}, u32[]{:S(2)}, u32[]{:S(2)}) collective-permute-start(bf16[64,768]{1,0:T(8,128)(2,1)S(1)} %get-tuple-element.55), channel_id=1, source_target_pairs={{0,4},{2,6},{4,0},{6,2},{8,12},{10,14},{12,8},{14,10},{1,5},{3,7},... | collective-permute-start | bytes 294920 | tf_op jit(solution)/shard_map/ppermute | solution.py:37
  37.8 10.0 %collective-permute-start.12 = (bf16[64,768]{1,0:T(8,128)(2,1)S(1)}, bf16[64,768]{1,0:T(8,128)(2,1)S(1)}, u32[]{:S(2)}, u32[]{:S(2)}) collective-permute-start(bf16[64,768]{1,0:T(8,128)(2,1)S(1)} %get-tuple-element.56), channel_id=1, source_target_pairs={{4,8},{6,10},{8,4},{10,6},{5,9},{7,11},{9,5},{11,7},{20,24},{22,26... | collective-permute-start | bytes 294920 | tf_op jit(solution)/shard_map/ppermute | solution.py:37
  38.5 9.3 %collective-permute-start.13 = (bf16[64,512]{1,0:T(8,128)(2,1)S(1)}, bf16[64,512]{1,0:T(8,128)(2,1)S(1)}, u32[]{:S(2)}, u32[]{:S(2)}) collective-permute-start(bf16[64,512]{1,0:T(8,128)(2,1)S(1)} %get-tuple-element.57), channel_id=1, source_target_pairs={{0,2},{2,0},{4,6},{6,4},{8,10},{10,8},{12,14},{14,12},{1,3},{3,1},... | collective-permute-start | bytes 196616 | tf_op jit(solution)/shard_map/ppermute | solution.py:37
  40.8 7.0 %collective-permute-start.14 = (bf16[64,384]{1,0:T(8,128)(2,1)S(1)}, bf16[64,384]{1,0:T(8,128)(2,1)S(1)}, u32[]{:S(2)}, u32[]{:S(2)}) collective-permute-start(bf16[64,384]{1,0:T(8,128)(2,1)S(1)} %get-tuple-element.58), channel_id=1, source_target_pairs={{0,6},{2,4},{4,2},{6,0},{8,14},{10,12},{12,10},{14,8},{1,7},{3,5},... | collective-permute-start | bytes 147464 | tf_op jit(solution)/shard_map/ppermute | solution.py:37
  44.5 3.3 %collective-permute-start.15 = (bf16[64,384]{1,0:T(8,128)(2,1)S(1)}, bf16[64,384]{1,0:T(8,128)(2,1)S(1)}, u32[]{:S(2)}, u32[]{:S(2)}) collective-permute-start(bf16[64,384]{1,0:T(8,128)(2,1)S(1)} %get-tuple-element.59), channel_id=1, source_target_pairs={{4,10},{6,8},{8,6},{10,4},{5,11},{7,9},{9,7},{11,5},{20,26},{22,24... | collective-permute-start | bytes 147464 | tf_op jit(solution)/shard_map/ppermute | solution.py:37

commit v7 on v6

--- a/solution.py
+++ b/solution.py
@@ -128,8 +128,12 @@
     return hot(jnp.where(lane == j, e_ref[group : group + 1, :], -1), tile)
 
 
-def cut_kernel(pieces, rows, cols, x_ref, *refs):
-    copies = cuts(pieces, rows, cols, x_ref, refs[:-1], refs[-1], 0)
+def cut_kernel(pieces, rows, cols, *refs):
+    k = len(pieces)
+    far, slabs, near, sems = refs[:7], refs[7 : 7 + k], refs[7 + k : -1], refs[-1]
+    copies = cuts(pieces, rows, cols, far[1], slabs, sems, 0)
+    for i, (f, v) in enumerate(zip(far, near)):
+        copies.append(pltpu.make_async_copy(f, v, sems.at[k + i]))
     for copy in copies:
         copy.start()
     for copy in copies:
@@ -151,19 +155,16 @@
 
 def head_kernel(base, pieces, rows, cols, slots, *refs):
     k = len(pieces)
-    far, rest = refs[:7], refs[7:]
+    far_ref, near, rest = refs[0], refs[1:8], refs[8:]
     src_slabs, outs, rest = rest[:k], rest[k : k + 8], rest[k + 8 :]
     src_t, tgt_t, gh_ref, wt_ref, wh_ref, bt_ref, e_ref, m_ref = outs
-    (s32, t32, og, table), near, sems = rest[:4], rest[4:-1], rest[-1]
+    s32, t32, og, table, sems = rest
     src_ref, tgt_ref, og_ref, ids_ref, w_in_ref, b_ref, w_out_ref = near
-    fetches = [pltpu.make_async_copy(f, v, sems.at[i]) for i, (f, v) in enumerate(zip(far, near))]
-    slabs = cuts(pieces, rows, cols, far[0], src_slabs, sems, 7)
-    for copy in fetches[2:] + fetches[:2] + slabs:
+    slabs = cuts(pieces, rows, cols, far_ref, src_slabs, sems, 0)
+    for copy in slabs:
         copy.start()
     px, n, _ = src_t.shape
     pitch = px + 1
-    for fetch in fetches[2:]:
-        fetch.wait()
     e_at, m_at = places(ids_ref[...], base, rows, cols)
     slotted(e_at, e_ref, table, slots)
     slotted(m_at, m_ref, table, slots)
@@ -185,8 +186,6 @@
         gh_ref[:, g * LANES : (g + 1) * LANES] = lax.dot_general(
             w_out_ref[...], block, NT, preferred_element_type=F32
         )
-    for fetch in fetches[:2]:
-        fetch.wait()
     for dst, src in ((s32, src_ref), (t32, tgt_ref)):
 
         def body(i, dst=dst, src=src):
@@ -390,8 +389,7 @@
         in_specs=[HB] * far + [VM] * (len(args) - far),
         out_specs=[VM] * len(outs),
         scratch_shapes=[pltpu.VMEM(s, d) for s, d in scratch]
-        + ([pltpu.VMEM(x.shape, x.dtype) for x in args[:far]] if far else [])
-        + ([pltpu.SemaphoreType.DMA((sems,))] if far else []),
+        + ([pltpu.SemaphoreType.DMA((sems,))] if sems else []),
         compiler_params=pltpu.CompilerParams(vmem_limit_bytes=limit * 2**20),
         cost_estimate=pl.CostEstimate(
             flops=0, bytes_accessed=int(us * 3 * 10**6), transcendentals=0
@@ -436,27 +434,27 @@
         w_out,
     )
     args = tuple(pltpu.with_memory_space_constraint(a, pltpu.HBM) for a in args)
+    k = len(pieces)
+    cut_t = pl.pallas_call(
+        partial(cut_kernel, pieces, rows, cols),
+        name="cut",
+        out_shape=[jax.ShapeDtypeStruct(s, BF16) for s in shapes]
+        + [jax.ShapeDtypeStruct(x.shape, x.dtype) for x in args],
+        in_specs=[HB] * len(args),
+        out_specs=[VM] * (k + len(args)),
+        scratch_shapes=[pltpu.SemaphoreType.DMA((k + len(args),))],
+        compiler_params=pltpu.CompilerParams(vmem_limit_bytes=8 * 2**20),
+    )(*args)
     made = call(
         partial(head_kernel, base, pieces, rows, cols, slots),
         outs,
         [((n * pitch, channels), F32)] * 2
         + [((n * (slots + 1), out_grad.shape[3]), F32), ((n, LANES), jnp.int32)],
-        args,
-        far=len(args),
-        sems=len(args) + len(pieces),
-        limit=24,
-    )
-    k = len(pieces)
+        (args[0], *cut_t[k:]),
+        far=1,
+        sems=k,
+    )
     src_t, own_t, grad_hidden, w_t, w_half, b_t, e_ids, m_ids = made[k:]
-    cut_t = pl.pallas_call(
-        partial(cut_kernel, pieces, rows, cols),
-        name="cut",
-        out_shape=[jax.ShapeDtypeStruct(s, BF16) for s in shapes],
-        in_specs=[HB],
-        out_specs=[VM] * k,
-        scratch_shapes=[pltpu.SemaphoreType.DMA((k,))],
-        compiler_params=pltpu.CompilerParams(vmem_limit_bytes=4 * 2**20),
-    )(args[1])
 
     def halo_of(slabs):
         got = []
@@ -464,7 +462,7 @@
             got.append(swap(x, qz, qx).reshape(-1, channels))
         return got
 
-    tgt_halo = halo_of(cut_t)
+    tgt_halo = halo_of(cut_t[:k])
     src_halo = halo_of(made[:k])
     starts = [base[q] for q in pieces]
     counts = [h.shape[0] // px for h in tgt_halo]

time: 50.5 us -> 50.1 us (level)
  waiting for transfers between devices: 7.61 us -> 6.17 us
  starting transfers between devices: 29.7 us -> 30.9 us
    ppermute x15, waiting for transfers between devices: 7.61 us -> 6.17 us  [swap(): return lax.ppermute(x, ('strip', 'sub'), pairs)]
    ppermute x15, starting transfers between devices: 29.6 us -> 30.8 us  [swap(): return lax.ppermute(x, ('strip', 'sub'), pairs)]
    pallas_call x1, Pallas kernels: 1.51 us -> 2.18 us  [shards(): pl.pallas_call(partial(cut_kernel, pieces, rows, cols), name='cut', out_s...]
  transfers between devices with their start and end apart: 16 -> 16, of which waited for: 2 -> 2; matrix products, arithmetic and copies ran while one was open for 0% -> 0% of each run, Pallas kernels for 17% -> 16%
where the time goes in v7:
time: 50.1 us; the launch traced here: 49.8 us
  starting transfers between devices  30.9 us (62%)
  Pallas kernels  11.9 us (24%)
  waiting for transfers between devices  6.17 us (12%)
  between operations  0.78 us (2%)
    ppermute x15, starting transfers between devices, swap(): return lax.ppermute(x, ('strip', 'sub'), pairs)  30.8 us
    pallas_call x6, Pallas kernels, call(): pl.pallas_call(kernel, out_shape=[jax.ShapeDtypeStruct(s, d) for s, d in...  9.76 us
    ppermute x15, waiting for transfers between devices, swap(): return lax.ppermute(x, ('strip', 'sub'), pairs)  6.17 us
    pallas_call x1, Pallas kernels, shards(): pl.pallas_call(partial(cut_kernel, pieces, rows, cols), name='cut', out_s...  2.18 us
  transfers between devices with their start and end apart: 16, of which 2 were waited for; matrix products, arithmetic and copies ran while one was open for 0% of the time, Pallas kernels for 16%

profile of v7, /device:TPU:0, one launch (start us, length us, event | category | flops | bytes accessed | tf_op | source)
XLA Modules:
  0.0 49.8 jit_solution(6657450657795555139)
XLA Ops:
  0.6 2.2 %cut.1 = (bf16[3,8,64,128]{3,2,1,0:T(8,128)(2,1)S(1)}, bf16[3,8,64,128]{3,2,1,0:T(8,128)(2,1)S(1)}, bf16[4,3,64,128]{3,2,1,0:T(8,128)(2,1)S(1)}, bf16[3,3,64,128...) custom-call(bf16[4,8,64,128]{3,2,1,0:T(8,128)(2,1)} %refs_0_.3, ...), custom_call_target="tpu_custom_call" | custom-call | tf_op jit(solution)/shard_map/cut/pallas_call | solution.py:438
  2.8 3.1 %collective-permute-start = (bf16[3,8,64,128]{3,2,1,0:T(8,128)(2,1)S(1)}, bf16[3,8,64,128]{3,2,1,0:T(8,128)(2,1)S(1)}, u32[]{:S(2)}, u32[]{:S(2)}) collective-permute-start(bf16[3,8,64,128]{3,2,1,0:T(8,128)(2,1)S(1)} %get-tuple-element.48), channel_id=1, source_target_pairs={{0,4},{2,6},{4,0},{6,2},{8,12},{10,14},{12,8},{14,10},{1,5},{3,7},... | collective-permute-start | bytes 1179656 | tf_op jit(solution)/shard_map/ppermute | solution.py:37
  5.9 0.7 %collective-permute-start.1 = (bf16[3,8,64,128]{3,2,1,0:T(8,128)(2,1)S(1)}, bf16[3,8,64,128]{3,2,1,0:T(8,128)(2,1)S(1)}, u32[]{:S(2)}, u32[]{:S(2)}) collective-permute-start(bf16[3,8,64,128]{3,2,1,0:T(8,128)(2,1)S(1)} %get-tuple-element.49), channel_id=1, source_target_pairs={{4,8},{6,10},{8,4},{10,6},{5,9},{7,11},{9,5},{11,7},{20,24},{22,26... | collective-permute-start | bytes 1179656 | tf_op jit(solution)/shard_map/ppermute | solution.py:37
  6.6 5.3 %collective-permute-start.3 = (bf16[3,3,64,128]{3,2,1,0:T(8,128)(2,1)S(1)}, bf16[3,3,64,128]{3,2,1,0:T(8,128)(2,1)S(1)}, u32[]{:S(2)}, u32[]{:S(2)}) collective-permute-start(bf16[3,3,64,128]{3,2,1,0:T(8,128)(2,1)S(1)} %get-tuple-element.51), channel_id=1, source_target_pairs={{0,6},{2,4},{4,2},{6,0},{8,14},{10,12},{12,10},{14,8},{1,7},{3,5},... | collective-permute-start | bytes 442376 | tf_op jit(solution)/shard_map/ppermute | solution.py:37
  11.9 0.7 %collective-permute-start.4 = (bf16[3,3,64,128]{3,2,1,0:T(8,128)(2,1)S(1)}, bf16[3,3,64,128]{3,2,1,0:T(8,128)(2,1)S(1)}, u32[]{:S(2)}, u32[]{:S(2)}) collective-permute-start(bf16[3,3,64,128]{3,2,1,0:T(8,128)(2,1)S(1)} %get-tuple-element.52), channel_id=1, source_target_pairs={{4,10},{6,8},{8,6},{10,4},{5,11},{7,9},{9,7},{11,5},{20,26},{22,24... | collective-permute-start | bytes 442376 | tf_op jit(solution)/shard_map/ppermute | solution.py:37
  12.6 0.7 %collective-permute-start.2 = (bf16[4,3,64,128]{3,2,1,0:T(8,128)(2,1)S(1)}, bf16[4,3,64,128]{3,2,1,0:T(8,128)(2,1)S(1)}, u32[]{:S(2)}, u32[]{:S(2)}) collective-permute-start(bf16[4,3,64,128]{3,2,1,0:T(8,128)(2,1)S(1)} %get-tuple-element.50), channel_id=1, source_target_pairs={{0,2},{2,0},{4,6},{6,4},{8,10},{10,8},{12,14},{14,12},{1,3},{3,1},... | collective-permute-start | bytes 589832 | tf_op jit(solution)/shard_map/ppermute | solution.py:37
  13.2 1.7 %shard_map.86 = (bf16[3,8,64,128]{3,2,1,0:T(8,128)(2,1)S(1)}, bf16[3,8,64,128]{3,2,1,0:T(8,128)(2,1)S(1)}, bf16[4,3,64,128]{3,2,1,0:T(8,128)(2,1)S(1)}, bf16[3,3...) custom-call(bf16[4,8,64,128]{3,2,1,0:T(8,128)(2,1)} %refs_0_.3, ...), custom_call_target="tpu_custom_call" | custom-call | bytes 6000000 | tf_op jit(solution)/shard_map/pallas_call | solution.py:386
  14.9 4.4 %collective-permute-done.3 = bf16[3,3,64,128]{3,2,1,0:T(8,128)(2,1)S(1)} collective-permute-done((bf16[3,3,64,128]{3,2,1,0:T(8,128)(2,1)S(1)}, bf16[3,3,64,128]{3,2,1,0:T(8,128)(2,1)S(1)}, u32[]{:S(2)}, u32[]{:S(2)}) %collective-permute-start.3) | collective-permute-done | bytes 147488 | tf_op jit(solution)/shard_map/ppermute | solution.py:37
  19.3 2.3 %collective-permute-start.6 = (bf16[3,8,64,128]{3,2,1,0:T(8,128)(2,1)S(1)}, bf16[3,8,64,128]{3,2,1,0:T(8,128)(2,1)S(1)}, u32[]{:S(2)}, u32[]{:S(2)}) collective-permute-start(bf16[3,8,64,128]{3,2,1,0:T(8,128)(2,1)S(1)} %get-tuple-element.64), channel_id=1, source_target_pairs={{0,4},{2,6},{4,0},{6,2},{8,12},{10,14},{12,8},{14,10},{1,5},{3,7},... | collective-permute-start | bytes 1179656 | tf_op jit(solution)/shard_map/ppermute | solution.py:37
  21.7 0.7 %collective-permute-start.7 = (bf16[3,8,64,128]{3,2,1,0:T(8,128)(2,1)S(1)}, bf16[3,8,64,128]{3,2,1,0:T(8,128)(2,1)S(1)}, u32[]{:S(2)}, u32[]{:S(2)}) collective-permute-start(bf16[3,8,64,128]{3,2,1,0:T(8,128)(2,1)S(1)} %get-tuple-element.65), channel_id=1, source_target_pairs={{4,8},{6,10},{8,4},{10,6},{5,9},{7,11},{9,5},{11,7},{20,24},{22,26... | collective-permute-start | bytes 1179656 | tf_op jit(solution)/shard_map/ppermute | solution.py:37
  22.4 0.0 collective-permute-done.2
  22.4 0.0 collective-permute-done
  22.4 1.8 %shard_map.87 = (bf16[64,1024]{1,0:T(8,128)(2,1)S(1)}, bf16[64,128,128]{2,1,0:T(8,128)(2,1)S(1)}, bf16[4096,128]{1,0:T(8,128)(2,1)S(1)}) custom-call(bf16[64,32,128]{2,1,0:T(8,128)(2,1)S(1)} %get-tuple-element.45.refs_0_, bf16[64,32,128]{2,1,0:T(8,128)(2,1)S(1)} %get-tuple-element.46.refs_1_.src_t, s32[8,128]{1,0:T(8,128)S(1)} %get-tuple-element.47.refs_2_.refs_6_, ...), custom_call_target="tpu_custom_call" | custom-call | bytes 9000000 | tf_op jit(solution)/shard_map/pallas_call | solution.py:386
  24.2 0.1 collective-permute-start.5
  24.3 0.7 %collective-permute-start.8 = (bf16[4,3,64,128]{3,2,1,0:T(8,128)(2,1)S(1)}, bf16[4,3,64,128]{3,2,1,0:T(8,128)(2,1)S(1)}, u32[]{:S(2)}, u32[]{:S(2)}) collective-permute-start(bf16[4,3,64,128]{3,2,1,0:T(8,128)(2,1)S(1)} %get-tuple-element.66), channel_id=1, source_target_pairs={{0,2},{2,0},{4,6},{6,4},{8,10},{10,8},{12,14},{14,12},{1,3},{3,1},... | collective-permute-start | bytes 589832 | tf_op jit(solution)/shard_map/ppermute | solution.py:37
  24.9 6.1 %collective-permute-start.9 = (bf16[3,3,64,128]{3,2,1,0:T(8,128)(2,1)S(1)}, bf16[3,3,64,128]{3,2,1,0:T(8,128)(2,1)S(1)}, u32[]{:S(2)}, u32[]{:S(2)}) collective-permute-start(bf16[3,3,64,128]{3,2,1,0:T(8,128)(2,1)S(1)} %get-tuple-element.67), channel_id=1, source_target_pairs={{0,6},{2,4},{4,2},{6,0},{8,14},{10,12},{12,10},{14,8},{1,7},{3,5},... | collective-permute-start | bytes 442376 | tf_op jit(solution)/shard_map/ppermute | solution.py:37
  31.0 0.0 collective-permute-done.5.refs_1_
  31.0 0.7 %collective-permute-start.10 = (bf16[3,3,64,128]{3,2,1,0:T(8,128)(2,1)S(1)}, bf16[3,3,64,128]{3,2,1,0:T(8,128)(2,1)S(1)}, u32[]{:S(2)}, u32[]{:S(2)}) collective-permute-start(bf16[3,3,64,128]{3,2,1,0:T(8,128)(2,1)S(1)} %get-tuple-element.68), channel_id=1, source_target_pairs={{4,10},{6,8},{8,6},{10,4},{5,11},{7,9},{9,7},{11,5},{20,26},{22,24... | collective-permute-start | bytes 442376 | tf_op jit(solution)/shard_map/ppermute | solution.py:37
  31.7 1.8 %shard_map.88 = (bf16[64,1024]{1,0:T(8,128)(2,1)S(1)}, bf16[64,768]{1,0:T(8,128)(2,1)S(1)}, bf16[64,768]{1,0:T(8,128)(2,1)S(1)}, bf16[64,512]{1,0:T(8,128)(2,1)S...) custom-call(bf16[64,1024]{1,0:T(8,128)(2,1)S(1)} %get-tuple-element.53.refs_0_, ...), custom_call_target="tpu_custom_call" | custom-call | bytes 9000000 | tf_op jit(solution)/shard_map/pallas_call | solution.py:386
  33.4 1.7 %collective-permute-done.9 = bf16[3,3,64,128]{3,2,1,0:T(8,128)(2,1)S(1)} collective-permute-done((bf16[3,3,64,128]{3,2,1,0:T(8,128)(2,1)S(1)}, bf16[3,3,64,128]{3,2,1,0:T(8,128)(2,1)S(1)}, u32[]{:S(2)}, u32[]{:S(2)}) %collective-permute-start.9) | collective-permute-done | bytes 147488 | tf_op jit(solution)/shard_map/ppermute | solution.py:37
  35.2 2.6 %collective-permute-start.11 = (bf16[64,768]{1,0:T(8,128)(2,1)S(1)}, bf16[64,768]{1,0:T(8,128)(2,1)S(1)}, u32[]{:S(2)}, u32[]{:S(2)}) collective-permute-start(bf16[64,768]{1,0:T(8,128)(2,1)S(1)} %get-tuple-element.69), channel_id=1, source_target_pairs={{0,4},{2,6},{4,0},{6,2},{8,12},{10,14},{12,8},{14,10},{1,5},{3,7},... | collective-permute-start | bytes 294920 | tf_op jit(solution)/shard_map/ppermute | solution.py:37
  37.7 0.0 collective-permute-done.10
  37.7 0.7 %collective-permute-start.12 = (bf16[64,768]{1,0:T(8,128)(2,1)S(1)}, bf16[64,768]{1,0:T(8,128)(2,1)S(1)}, u32[]{:S(2)}, u32[]{:S(2)}) collective-permute-start(bf16[64,768]{1,0:T(8,128)(2,1)S(1)} %get-tuple-element.70), channel_id=1, source_target_pairs={{4,8},{6,10},{8,4},{10,6},{5,9},{7,11},{9,5},{11,7},{20,24},{22,26... | collective-permute-start | bytes 294920 | tf_op jit(solution)/shard_map/ppermute | solution.py:37
  38.4 2.0 %collective-permute-start.13 = (bf16[64,512]{1,0:T(8,128)(2,1)S(1)}, bf16[64,512]{1,0:T(8,128)(2,1)S(1)}, u32[]{:S(2)}, u32[]{:S(2)}) collective-permute-start(bf16[64,512]{1,0:T(8,128)(2,1)S(1)} %get-tuple-element.71), channel_id=1, source_target_pairs={{0,2},{2,0},{4,6},{6,4},{8,10},{10,8},{12,14},{14,12},{1,3},{3,1},... | collective-permute-start | bytes 196616 | tf_op jit(solution)/shard_map/ppermute | solution.py:37
  40.4 4.2 %collective-permute-start.14 = (bf16[64,384]{1,0:T(8,128)(2,1)S(1)}, bf16[64,384]{1,0:T(8,128)(2,1)S(1)}, u32[]{:S(2)}, u32[]{:S(2)}) collective-permute-start(bf16[64,384]{1,0:T(8,128)(2,1)S(1)} %get-tuple-element.72), channel_id=1, source_target_pairs={{0,6},{2,4},{4,2},{6,0},{8,14},{10,12},{12,10},{14,8},{1,7},{3,5},... | collective-permute-start | bytes 147464 | tf_op jit(solution)/shard_map/ppermute | solution.py:37
  44.6 0.7 %collective-permute-start.15 = (bf16[64,384]{1,0:T(8,128)(2,1)S(1)}, bf16[64,384]{1,0:T(8,128)(2,1)S(1)}, u32[]{:S(2)}, u32[]{:S(2)}) collective-permute-start(bf16[64,384]{1,0:T(8,128)(2,1)S(1)} %get-tuple-element.73), channel_id=1, source_target_pairs={{4,10},{6,8},{8,6},{10,4},{5,11},{7,9},{9,7},{11,5},{20,26},{22,24... | collective-permute-start | bytes 147464 | tf_op jit(solution)/shard_map/ppermute | solution.py:37
  45.2 0.4 shard_map.90.halo_t
  45.7 2.2 %shard_map.89 = (bf16[2048,128]{1,0:T(8,128)(2,1)}, f32[64,32,128]{2,1,0:T(8,128)S(1)}) custom-call(bf16[64,1024]{1,0:T(8,128)(2,1)S(1)} %get-tuple-element.59.gc_ref, bf16[4096,128]{1,0:T(8,128)(2,1)S(1)} %get-tuple-element.60.hot_ref, bf16[64,128,128]{2,1,0:T(8,128)(2,1)S(1)} %get-tuple-element.61.tgt_t, ...), custom_call_target="tpu_custom_call" | custom-call | bytes 12000000 | tf_op jit(solution)/shard_map/pallas_call | solution.py:386
  47.9 0.0 collective-permute-done.14.refs_3_
  47.9 0.0 collective-permute-done.15.refs_4_
  47.9 0.0 collective-permute-done.11.refs_0_
  47.9 1.9 %shard_map.91 = bf16[2048,128]{1,0:T(8,128)(2,1)} custom-call(f32[64,32,128]{2,1,0:T(8,128)S(1)} %get-tuple-element.63.own_ref, bf16[64,80,128]{2,1,0:T(8,128)(2,1)S(1)} %shard_map.90.halo_t, bf16[64,768]{1,0:T(8,128)(2,1)S(1)} %collective-permute-done.11.refs_0_, bf16[64,768]{1,0:T(8,128)(2,1)S(1)} %collective-permute-done.12.refs_1_, ...), custom_call_target="tpu_custom_call" | custom-call | bytes 9000000 | tf_op jit(solution)/shard_map/pallas_call | solution.py:386
  (7 shorter events, 0.0 us)
Async XLA Ops:
  2.8 19.5 %collective-permute-start = (bf16[3,8,64,128]{3,2,1,0:T(8,128)(2,1)S(1)}, bf16[3,8,64,128]{3,2,1,0:T(8,128)(2,1)S(1)}, u32[]{:S(2)}, u32[]{:S(2)}) collective-permute-start(bf16[3,8,64,128]{3,2,1,0:T(8,128)(2,1)S(1)} %get-tuple-element.48), channel_id=1, source_target_pairs={{0,4},{2,6},{4,0},{6,2},{8,12},{10,14},{12,8},{14,10},{1,5},{3,7},... | collective-permute-start | bytes 1179656 | tf_op jit(solution)/shard_map/ppermute | solution.py:37
  5.9 16.4 %collective-permute-start.1 = (bf16[3,8,64,128]{3,2,1,0:T(8,128)(2,1)S(1)}, bf16[3,8,64,128]{3,2,1,0:T(8,128)(2,1)S(1)}, u32[]{:S(2)}, u32[]{:S(2)}) collective-permute-start(bf16[3,8,64,128]{3,2,1,0:T(8,128)(2,1)S(1)} %get-tuple-element.49), channel_id=1, source_target_pairs={{4,8},{6,10},{8,4},{10,6},{5,9},{7,11},{9,5},{11,7},{20,24},{22,26... | collective-permute-start | bytes 1179656 | tf_op jit(solution)/shard_map/ppermute | solution.py:37
  6.6 12.7 %collective-permute-start.3 = (bf16[3,3,64,128]{3,2,1,0:T(8,128)(2,1)S(1)}, bf16[3,3,64,128]{3,2,1,0:T(8,128)(2,1)S(1)}, u32[]{:S(2)}, u32[]{:S(2)}) collective-permute-start(bf16[3,3,64,128]{3,2,1,0:T(8,128)(2,1)S(1)} %get-tuple-element.51), channel_id=1, source_target_pairs={{0,6},{2,4},{4,2},{6,0},{8,14},{10,12},{12,10},{14,8},{1,7},{3,5},... | collective-permute-start | bytes 442376 | tf_op jit(solution)/shard_map/ppermute | solution.py:37
  11.9 9.7 %collective-permute-start.4 = (bf16[3,3,64,128]{3,2,1,0:T(8,128)(2,1)S(1)}, bf16[3,3,64,128]{3,2,1,0:T(8,128)(2,1)S(1)}, u32[]{:S(2)}, u32[]{:S(2)}) collective-permute-start(bf16[3,3,64,128]{3,2,1,0:T(8,128)(2,1)S(1)} %get-tuple-element.52), channel_id=1, source_target_pairs={{4,10},{6,8},{8,6},{10,4},{5,11},{7,9},{9,7},{11,5},{20,26},{22,24... | collective-permute-start | bytes 442376 | tf_op jit(solution)/shard_map/ppermute | solution.py:37
  12.6 9.8 %collective-permute-start.2 = (bf16[4,3,64,128]{3,2,1,0:T(8,128)(2,1)S(1)}, bf16[4,3,64,128]{3,2,1,0:T(8,128)(2,1)S(1)}, u32[]{:S(2)}, u32[]{:S(2)}) collective-permute-start(bf16[4,3,64,128]{3,2,1,0:T(8,128)(2,1)S(1)} %get-tuple-element.50), channel_id=1, source_target_pairs={{0,2},{2,0},{4,6},{6,4},{8,10},{10,8},{12,14},{14,12},{1,3},{3,1},... | collective-permute-start | bytes 589832 | tf_op jit(solution)/shard_map/ppermute | solution.py:37
  19.3 21.0 %collective-permute-start.6 = (bf16[3,8,64,128]{3,2,1,0:T(8,128)(2,1)S(1)}, bf16[3,8,64,128]{3,2,1,0:T(8,128)(2,1)S(1)}, u32[]{:S(2)}, u32[]{:S(2)}) collective-permute-start(bf16[3,8,64,128]{3,2,1,0:T(8,128)(2,1)S(1)} %get-tuple-element.64), channel_id=1, source_target_pairs={{0,4},{2,6},{4,0},{6,2},{8,12},{10,14},{12,8},{14,10},{1,5},{3,7},... | collective-permute-start | bytes 1179656 | tf_op jit(solution)/shard_map/ppermute | solution.py:37
  21.7 22.9 %collective-permute-start.7 = (bf16[3,8,64,128]{3,2,1,0:T(8,128)(2,1)S(1)}, bf16[3,8,64,128]{3,2,1,0:T(8,128)(2,1)S(1)}, u32[]{:S(2)}, u32[]{:S(2)}) collective-permute-start(bf16[3,8,64,128]{3,2,1,0:T(8,128)(2,1)S(1)} %get-tuple-element.65), channel_id=1, source_target_pairs={{4,8},{6,10},{8,4},{10,6},{5,9},{7,11},{9,5},{11,7},{20,24},{22,26... | collective-permute-start | bytes 1179656 | tf_op jit(solution)/shard_map/ppermute | solution.py:37
  24.2 6.8 %collective-permute-start.5 = (bf16[64,1024]{1,0:T(8,128)(2,1)S(1)}, bf16[64,1024]{1,0:T(8,128)(2,1)S(1)}, u32[]{:S(2)}, u32[]{:S(2)}) collective-permute-start(bf16[64,1024]{1,0:T(8,128)(2,1)S(1)} %get-tuple-element.53.refs_0_), channel_id=1, source_target_pairs={{0,1},{1,0},{2,3},{3,2},{4,5},{5,4},{6,7},{7,6},{8,9},{9,8},{10,11... | collective-permute-start | bytes 393224 | tf_op jit(solution)/shard_map/ppermute | solution.py:484
  24.3 14.1 %collective-permute-start.8 = (bf16[4,3,64,128]{3,2,1,0:T(8,128)(2,1)S(1)}, bf16[4,3,64,128]{3,2,1,0:T(8,128)(2,1)S(1)}, u32[]{:S(2)}, u32[]{:S(2)}) collective-permute-start(bf16[4,3,64,128]{3,2,1,0:T(8,128)(2,1)S(1)} %get-tuple-element.66), channel_id=1, source_target_pairs={{0,2},{2,0},{4,6},{6,4},{8,10},{10,8},{12,14},{14,12},{1,3},{3,1},... | collective-permute-start | bytes 589832 | tf_op jit(solution)/shard_map/ppermute | solution.py:37
  24.9 10.2 %collective-permute-start.9 = (bf16[3,3,64,128]{3,2,1,0:T(8,128)(2,1)S(1)}, bf16[3,3,64,128]{3,2,1,0:T(8,128)(2,1)S(1)}, u32[]{:S(2)}, u32[]{:S(2)}) collective-permute-start(bf16[3,3,64,128]{3,2,1,0:T(8,128)(2,1)S(1)} %get-tuple-element.67), channel_id=1, source_target_pairs={{0,6},{2,4},{4,2},{6,0},{8,14},{10,12},{12,10},{14,8},{1,7},{3,5},... | collective-permute-start | bytes 442376 | tf_op jit(solution)/shard_map/ppermute | solution.py:37
  31.0 6.7 %collective-permute-start.10 = (bf16[3,3,64,128]{3,2,1,0:T(8,128)(2,1)S(1)}, bf16[3,3,64,128]{3,2,1,0:T(8,128)(2,1)S(1)}, u32[]{:S(2)}, u32[]{:S(2)}) collective-permute-start(bf16[3,3,64,128]{3,2,1,0:T(8,128)(2,1)S(1)} %get-tuple-element.68), channel_id=1, source_target_pairs={{4,10},{6,8},{8,6},{10,4},{5,11},{7,9},{9,7},{11,5},{20,26},{22,24... | collective-permute-start | bytes 442376 | tf_op jit(solution)/shard_map/ppermute | solution.py:37
  35.2 12.7 %collective-permute-start.11 = (bf16[64,768]{1,0:T(8,128)(2,1)S(1)}, bf16[64,768]{1,0:T(8,128)(2,1)S(1)}, u32[]{:S(2)}, u32[]{:S(2)}) collective-permute-start(bf16[64,768]{1,0:T(8,128)(2,1)S(1)} %get-tuple-element.69), channel_id=1, source_target_pairs={{0,4},{2,6},{4,0},{6,2},{8,12},{10,14},{12,8},{14,10},{1,5},{3,7},... | collective-permute-start | bytes 294920 | tf_op jit(solution)/shard_map/ppermute | solution.py:37
  37.7 10.2 %collective-permute-start.12 = (bf16[64,768]{1,0:T(8,128)(2,1)S(1)}, bf16[64,768]{1,0:T(8,128)(2,1)S(1)}, u32[]{:S(2)}, u32[]{:S(2)}) collective-permute-start(bf16[64,768]{1,0:T(8,128)(2,1)S(1)} %get-tuple-element.70), channel_id=1, source_target_pairs={{4,8},{6,10},{8,4},{10,6},{5,9},{7,11},{9,5},{11,7},{20,24},{22,26... | collective-permute-start | bytes 294920 | tf_op jit(solution)/shard_map/ppermute | solution.py:37
  38.4 9.5 %collective-permute-start.13 = (bf16[64,512]{1,0:T(8,128)(2,1)S(1)}, bf16[64,512]{1,0:T(8,128)(2,1)S(1)}, u32[]{:S(2)}, u32[]{:S(2)}) collective-permute-start(bf16[64,512]{1,0:T(8,128)(2,1)S(1)} %get-tuple-element.71), channel_id=1, source_target_pairs={{0,2},{2,0},{4,6},{6,4},{8,10},{10,8},{12,14},{14,12},{1,3},{3,1},... | collective-permute-start | bytes 196616 | tf_op jit(solution)/shard_map/ppermute | solution.py:37
  40.4 7.5 %collective-permute-start.14 = (bf16[64,384]{1,0:T(8,128)(2,1)S(1)}, bf16[64,384]{1,0:T(8,128)(2,1)S(1)}, u32[]{:S(2)}, u32[]{:S(2)}) collective-permute-start(bf16[64,384]{1,0:T(8,128)(2,1)S(1)} %get-tuple-element.72), channel_id=1, source_target_pairs={{0,6},{2,4},{4,2},{6,0},{8,14},{10,12},{12,10},{14,8},{1,7},{3,5},... | collective-permute-start | bytes 147464 | tf_op jit(solution)/shard_map/ppermute | solution.py:37
  44.6 3.3 %collective-permute-start.15 = (bf16[64,384]{1,0:T(8,128)(2,1)S(1)}, bf16[64,384]{1,0:T(8,128)(2,1)S(1)}, u32[]{:S(2)}, u32[]{:S(2)}) collective-permute-start(bf16[64,384]{1,0:T(8,128)(2,1)S(1)} %get-tuple-element.73), channel_id=1, source_target_pairs={{4,10},{6,8},{8,6},{10,4},{5,11},{7,9},{9,7},{11,5},{20,26},{22,24... | collective-permute-start | bytes 147464 | tf_op jit(solution)/shard_map/ppermute | solution.py:37

commit v8 on v6

--- a/solution.py
+++ b/solution.py
@@ -250,9 +250,9 @@
     return (0.5 + 0.5 * th) * (1.0 + (1.0 - th) * inner)
 
 
-def decoder_kernel(rows, cols, slots, pieces, starts, counts, *refs):
-    mine_ref, other_ref, gh_ref, wt_ref, bt_ref, w_ref, e_ref, m_ref = refs[:8]
-    gc_ref, out_refs, whole = refs[8], refs[9:-1], refs[-1]
+def decoder_kernel(rows, cols, slots, pieces, *refs):
+    mine_ref, other_ref, gh_ref, wt_ref, bt_ref, w_ref, table_ref = refs[:7]
+    gc_ref, out_refs, whole = refs[7], refs[8:-1], refs[-1]
     px = mine_ref.shape[0]
     rep = lax.axis_index("rep")
     whole[pl.ds(pl.multiple_of(rep * px, px), px), :] = mine_ref[...]
@@ -266,32 +266,55 @@
         pre = jnp.dot(wt_ref[...], whole[:, cut], preferred_element_type=F32) + bias
         grad = (gh_ref[:, cut] * gelu_slope(pre)).astype(BF16)
         gc_ref[:, cut] = jnp.dot(w_half, grad, preferred_element_type=F32).astype(BF16)
-    send(rows, cols, slots, pieces, starts, counts, gc_ref, e_ref, m_ref, out_refs)
-
-
-def send(rows, cols, slots, pieces, starts, counts, gc_ref, e_ref, m_ref, out_refs):
-    per = LANES // slots
+    send(rows, cols, slots, pieces, gc_ref, table_ref, out_refs)
+
+
+def picked(rows, cols, per, piece):
+    qz, qx = piece
+    strip_at, sub_at = lax.axis_index("strip"), lax.axis_index("sub")
     wide = cols // per
-    strip_at, sub_at = lax.axis_index("strip"), lax.axis_index("sub")
+    r0 = 0 if qz is None else facing(qz, rows, strip_at)
+    tail = None if qx is None else (sub_at + qx) % 2 == 0
+    half = 0 if qx is None else jnp.where(tail, (cols - H) // per, 0)
+    shift = 0 if qx is None else jnp.where(tail, (cols - H) % per, 0)
+    groups = [
+        (r0 + r) * wide + half + h
+        for r in range(rows if qz is None else H)
+        for h in range(wide if qx is None else 1)
+    ]
+    return groups, shift
+
+
+def table_kernel(rows, cols, slots, pieces, starts, counts, e_ref, m_ref, out_ref):
+    per = LANES // slots
     lane = lax.broadcasted_iota(jnp.int32, (1, LANES), 1) // slots
-    for (qz, qx), start, count, ref in zip(pieces, starts, counts, out_refs):
-        r0 = 0 if qz is None else facing(qz, rows, strip_at)
-        tail = None if qx is None else (sub_at + qx) % 2 == 0
-        half = 0 if qx is None else jnp.where(tail, (cols - H) // per, 0)
-        shift = 0 if qx is None else jnp.where(tail, (cols - H) % per, 0)
-        i = 0
-        for r in range(rows if qz is None else H):
-            for h in range(wide if qx is None else 1):
-                g = (r0 + r) * wide + half + h
-                e, m = e_ref[pl.ds(g, 1), :], m_ref[pl.ds(g, 1), :]
-                here = (e >= start) & (e < start + count)
-                to = jnp.where(here, (lane - shift) * slots + m, -1)
-                at = g * LANES
-                at = at if isinstance(at, int) else pl.multiple_of(at, LANES)
-                ref[:, i * LANES : (i + 1) * LANES] = lax.dot_general(
-                    gc_ref[:, pl.ds(at, LANES)], hot(to), NT, preferred_element_type=F32
-                ).astype(BF16)
-                i += 1
+    i = 0
+    for piece, start, count in zip(pieces, starts, counts):
+        groups, shift = picked(rows, cols, per, piece)
+        for g in groups:
+            e, m = e_ref[pl.ds(g, 1), :], m_ref[pl.ds(g, 1), :]
+            here = (e >= start) & (e < start + count)
+            out_ref[i * LANES : (i + 1) * LANES, :] = hot(
+                jnp.where(here, (lane - shift) * slots + m, -1)
+            )
+            i += 1
+
+
+def send(rows, cols, slots, pieces, gc_ref, table_ref, out_refs):
+    per = LANES // slots
+    i = 0
+    for piece, ref in zip(pieces, out_refs):
+        groups, _ = picked(rows, cols, per, piece)
+        for at, g in enumerate(groups):
+            lane = g * LANES
+            lane = lane if isinstance(lane, int) else pl.multiple_of(lane, LANES)
+            ref[:, at * LANES : (at + 1) * LANES] = lax.dot_general(
+                gc_ref[:, pl.ds(lane, LANES)],
+                table_ref[i * LANES : (i + 1) * LANES, :],
+                NT,
+                preferred_element_type=F32,
+            ).astype(BF16)
+            i += 1
 
 
 def own_kernel(px, n, slots, gc_ref, hot_ref, tgt_t, src_t, sg_ref, own_ref, pw, s32):
@@ -383,10 +406,10 @@
 HB = pl.BlockSpec(memory_space=pltpu.HBM)
 
 
-def call(kernel, outs, scratch, args, us=2.0, far=0, sems=0, limit=24):
+def call(kernel, outs, scratch, args, us=2.0, far=0, sems=0, limit=24, near=False):
     return pl.pallas_call(
         kernel,
-        out_shape=[jax.ShapeDtypeStruct(s, d) for s, d in outs],
+        out_shape=[pltpu.VMEM(s, d) if near else jax.ShapeDtypeStruct(s, d) for s, d in outs],
         in_specs=[HB] * far + [VM] * (len(args) - far),
         out_specs=[VM] * len(outs),
         scratch_shapes=[pltpu.VMEM(s, d) for s, d in scratch]
@@ -488,11 +511,18 @@
         (rows if qz is None else H) * (cols // per if qx is None else 1) * LANES
         for qz, qx in pieces
     ]
+    (tables,) = call(
+        partial(table_kernel, rows, cols, slots, pieces, starts, counts),
+        [((sum(lanes), LANES), BF16)],
+        [],
+        (e_ids, m_ids),
+        us=0.5,
+    )
     gc, *sent = call(
-        partial(decoder_kernel, rows, cols, slots, pieces, starts, counts),
+        partial(decoder_kernel, rows, cols, slots, pieces),
         [((px, n * slots), BF16)] + [((px, w), BF16) for w in lanes],
         [((2 * px, n * slots), BF16)],
-        (costs, other, grad_hidden, w_t, b_t, w_half, e_ids, m_ids),
+        (costs, other, grad_hidden, w_t, b_t, w_half, tables),
         us=3,
     )
     got = []

time: 50.5 us -> 50.5 us (level)
    pallas_call x6 -> x7, Pallas kernels: 10.2 us -> 10.3 us  [call(): pl.pallas_call(kernel, out_shape=[pltpu.VMEM(s, d) if near else jax.Shape...]
where the time goes in v8:
time: 50.5 us; the launch traced here: 49.7 us
  starting transfers between devices  29.7 us (59%)
  Pallas kernels  11.8 us (23%)
  waiting for transfers between devices  7.47 us (15%)
  between operations  0.77 us (2%)
    ppermute x15, starting transfers between devices, swap(): return lax.ppermute(x, ('strip', 'sub'), pairs)  29.6 us
    pallas_call x7, Pallas kernels, call(): pl.pallas_call(kernel, out_shape=[pltpu.VMEM(s, d) if near else jax.Shape...  10.3 us
    ppermute x15, waiting for transfers between devices, swap(): return lax.ppermute(x, ('strip', 'sub'), pairs)  7.47 us
    pallas_call x1, Pallas kernels, shards(): pl.pallas_call(partial(cut_kernel, pieces, rows, cols), name='cut', out_s...  1.51 us
  transfers between devices with their start and end apart: 16, of which 2 were waited for; matrix products, arithmetic and copies ran while one was open for 0% of the time, Pallas kernels for 17%

profile of v8, /device:TPU:0, one launch (start us, length us, event | category | flops | bytes accessed | tf_op | source)
XLA Modules:
  0.0 49.7 jit_solution(1988558910226201801)
XLA Ops:
  0.6 1.5 %cut.1 = (bf16[3,8,64,128]{3,2,1,0:T(8,128)(2,1)S(1)}, bf16[3,8,64,128]{3,2,1,0:T(8,128)(2,1)S(1)}, bf16[4,3,64,128]{3,2,1,0:T(8,128)(2,1)S(1)}, bf16[3,3,64,128...) custom-call(bf16[4,8,64,128]{3,2,1,0:T(8,128)(2,1)} %x_ref.1), custom_call_target="tpu_custom_call" | custom-call | tf_op jit(solution)/shard_map/cut/pallas_call | solution.py:474
  2.1 3.1 %collective-permute-start = (bf16[3,8,64,128]{3,2,1,0:T(8,128)(2,1)S(1)}, bf16[3,8,64,128]{3,2,1,0:T(8,128)(2,1)S(1)}, u32[]{:S(2)}, u32[]{:S(2)}) collective-permute-start(bf16[3,8,64,128]{3,2,1,0:T(8,128)(2,1)S(1)} %get-tuple-element.34), channel_id=1, source_target_pairs={{0,4},{2,6},{4,0},{6,2},{8,12},{10,14},{12,8},{14,10},{1,5},{3,7},... | collective-permute-start | bytes 1179656 | tf_op jit(solution)/shard_map/ppermute | solution.py:37
  5.3 0.7 %collective-permute-start.1 = (bf16[3,8,64,128]{3,2,1,0:T(8,128)(2,1)S(1)}, bf16[3,8,64,128]{3,2,1,0:T(8,128)(2,1)S(1)}, u32[]{:S(2)}, u32[]{:S(2)}) collective-permute-start(bf16[3,8,64,128]{3,2,1,0:T(8,128)(2,1)S(1)} %get-tuple-element.35), channel_id=1, source_target_pairs={{4,8},{6,10},{8,4},{10,6},{5,9},{7,11},{9,5},{11,7},{20,24},{22,26... | collective-permute-start | bytes 1179656 | tf_op jit(solution)/shard_map/ppermute | solution.py:37
  5.9 5.4 %collective-permute-start.3 = (bf16[3,3,64,128]{3,2,1,0:T(8,128)(2,1)S(1)}, bf16[3,3,64,128]{3,2,1,0:T(8,128)(2,1)S(1)}, u32[]{:S(2)}, u32[]{:S(2)}) collective-permute-start(bf16[3,3,64,128]{3,2,1,0:T(8,128)(2,1)S(1)} %get-tuple-element.37), channel_id=1, source_target_pairs={{0,6},{2,4},{4,2},{6,0},{8,14},{10,12},{12,10},{14,8},{1,7},{3,5},... | collective-permute-start | bytes 442376 | tf_op jit(solution)/shard_map/ppermute | solution.py:37
  11.4 0.7 %collective-permute-start.4 = (bf16[3,3,64,128]{3,2,1,0:T(8,128)(2,1)S(1)}, bf16[3,3,64,128]{3,2,1,0:T(8,128)(2,1)S(1)}, u32[]{:S(2)}, u32[]{:S(2)}) collective-permute-start(bf16[3,3,64,128]{3,2,1,0:T(8,128)(2,1)S(1)} %get-tuple-element.38), channel_id=1, source_target_pairs={{4,10},{6,8},{8,6},{10,4},{5,11},{7,9},{9,7},{11,5},{20,26},{22,24... | collective-permute-start | bytes 442376 | tf_op jit(solution)/shard_map/ppermute | solution.py:37
  12.0 0.5 %collective-permute-start.2 = (bf16[4,3,64,128]{3,2,1,0:T(8,128)(2,1)S(1)}, bf16[4,3,64,128]{3,2,1,0:T(8,128)(2,1)S(1)}, u32[]{:S(2)}, u32[]{:S(2)}) collective-permute-start(bf16[4,3,64,128]{3,2,1,0:T(8,128)(2,1)S(1)} %get-tuple-element.36), channel_id=1, source_target_pairs={{0,2},{2,0},{4,6},{6,4},{8,10},{10,8},{12,14},{14,12},{1,3},{3,1},... | collective-permute-start | bytes 589832 | tf_op jit(solution)/shard_map/ppermute | solution.py:37
  12.6 2.1 %shard_map.86 = (bf16[3,8,64,128]{3,2,1,0:T(8,128)(2,1)S(1)}, bf16[3,8,64,128]{3,2,1,0:T(8,128)(2,1)S(1)}, bf16[4,3,64,128]{3,2,1,0:T(8,128)(2,1)S(1)}, bf16[3,3...) custom-call(bf16[4,8,64,128]{3,2,1,0:T(8,128)(2,1)} %refs_0_.1, ...), custom_call_target="tpu_custom_call" | custom-call | bytes 6000000 | tf_op jit(solution)/shard_map/pallas_call | solution.py:410
  14.7 4.1 %collective-permute-done.3 = bf16[3,3,64,128]{3,2,1,0:T(8,128)(2,1)S(1)} collective-permute-done((bf16[3,3,64,128]{3,2,1,0:T(8,128)(2,1)S(1)}, bf16[3,3,64,128]{3,2,1,0:T(8,128)(2,1)S(1)}, u32[]{:S(2)}, u32[]{:S(2)}) %collective-permute-start.3) | collective-permute-done | bytes 147488 | tf_op jit(solution)/shard_map/ppermute | solution.py:37
  18.8 0.7 %collective-permute-start.7 = (bf16[3,8,64,128]{3,2,1,0:T(8,128)(2,1)S(1)}, bf16[3,8,64,128]{3,2,1,0:T(8,128)(2,1)S(1)}, u32[]{:S(2)}, u32[]{:S(2)}) collective-permute-start(bf16[3,8,64,128]{3,2,1,0:T(8,128)(2,1)S(1)} %get-tuple-element.51), channel_id=1, source_target_pairs={{4,8},{6,10},{8,4},{10,6},{5,9},{7,11},{9,5},{11,7},{20,24},{22,26... | collective-permute-start | bytes 1179656 | tf_op jit(solution)/shard_map/ppermute | solution.py:37
  19.5 0.0 collective-permute-done.4
  19.5 5.3 %collective-permute-start.6 = (bf16[3,8,64,128]{3,2,1,0:T(8,128)(2,1)S(1)}, bf16[3,8,64,128]{3,2,1,0:T(8,128)(2,1)S(1)}, u32[]{:S(2)}, u32[]{:S(2)}) collective-permute-start(bf16[3,8,64,128]{3,2,1,0:T(8,128)(2,1)S(1)} %get-tuple-element.50), channel_id=1, source_target_pairs={{0,4},{2,6},{4,0},{6,2},{8,12},{10,14},{12,8},{14,10},{1,5},{3,7},... | collective-permute-start | bytes 1179656 | tf_op jit(solution)/shard_map/ppermute | solution.py:37
  24.8 0.0 collective-permute-done.1
  24.8 1.8 %shard_map.87 = (bf16[64,1024]{1,0:T(8,128)(2,1)S(1)}, bf16[64,128,128]{2,1,0:T(8,128)(2,1)S(1)}, bf16[4096,128]{1,0:T(8,128)(2,1)S(1)}) custom-call(bf16[64,32,128]{2,1,0:T(8,128)(2,1)S(1)} %get-tuple-element.31.refs_0_, bf16[64,32,128]{2,1,0:T(8,128)(2,1)S(1)} %get-tuple-element.32.refs_1_.src_t, s32[8,128]{1,0:T(8,128)S(1)} %get-tuple-element.33.refs_2_.e_ref, ...), custom_call_target="tpu_custom_call" | custom-call | bytes 9000000 | tf_op jit(solution)/shard_map/pallas_call | solution.py:410
  26.6 0.1 collective-permute-start.5
  26.7 0.5 %collective-permute-start.8 = (bf16[4,3,64,128]{3,2,1,0:T(8,128)(2,1)S(1)}, bf16[4,3,64,128]{3,2,1,0:T(8,128)(2,1)S(1)}, u32[]{:S(2)}, u32[]{:S(2)}) collective-permute-start(bf16[4,3,64,128]{3,2,1,0:T(8,128)(2,1)S(1)} %get-tuple-element.52), channel_id=1, source_target_pairs={{0,2},{2,0},{4,6},{6,4},{8,10},{10,8},{12,14},{14,12},{1,3},{3,1},... | collective-permute-start | bytes 589832 | tf_op jit(solution)/shard_map/ppermute | solution.py:37
  27.2 2.0 %collective-permute-start.9 = (bf16[3,3,64,128]{3,2,1,0:T(8,128)(2,1)S(1)}, bf16[3,3,64,128]{3,2,1,0:T(8,128)(2,1)S(1)}, u32[]{:S(2)}, u32[]{:S(2)}) collective-permute-start(bf16[3,3,64,128]{3,2,1,0:T(8,128)(2,1)S(1)} %get-tuple-element.53), channel_id=1, source_target_pairs={{0,6},{2,4},{4,2},{6,0},{8,14},{10,12},{12,10},{14,8},{1,7},{3,5},... | collective-permute-start | bytes 442376 | tf_op jit(solution)/shard_map/ppermute | solution.py:37
  29.2 0.7 %collective-permute-start.10 = (bf16[3,3,64,128]{3,2,1,0:T(8,128)(2,1)S(1)}, bf16[3,3,64,128]{3,2,1,0:T(8,128)(2,1)S(1)}, u32[]{:S(2)}, u32[]{:S(2)}) collective-permute-start(bf16[3,3,64,128]{3,2,1,0:T(8,128)(2,1)S(1)} %get-tuple-element.54), channel_id=1, source_target_pairs={{4,10},{6,8},{8,6},{10,4},{5,11},{7,9},{9,7},{11,5},{20,26},{22,24... | collective-permute-start | bytes 442376 | tf_op jit(solution)/shard_map/ppermute | solution.py:37
  29.9 0.2 shard_map.88.refs_6_
  30.0 1.7 %shard_map.89 = (bf16[64,1024]{1,0:T(8,128)(2,1)S(1)}, bf16[64,768]{1,0:T(8,128)(2,1)S(1)}, bf16[64,768]{1,0:T(8,128)(2,1)S(1)}, bf16[64,512]{1,0:T(8,128)(2,1)S...) custom-call(bf16[64,1024]{1,0:T(8,128)(2,1)S(1)} %get-tuple-element.39.refs_0_, ...), custom_call_target="tpu_custom_call" | custom-call | bytes 9000000 | tf_op jit(solution)/shard_map/pallas_call | solution.py:410
  31.8 3.3 %collective-permute-done.9 = bf16[3,3,64,128]{3,2,1,0:T(8,128)(2,1)S(1)} collective-permute-done((bf16[3,3,64,128]{3,2,1,0:T(8,128)(2,1)S(1)}, bf16[3,3,64,128]{3,2,1,0:T(8,128)(2,1)S(1)}, u32[]{:S(2)}, u32[]{:S(2)}) %collective-permute-start.9) | collective-permute-done | bytes 147488 | tf_op jit(solution)/shard_map/ppermute | solution.py:37
  35.1 2.7 %collective-permute-start.11 = (bf16[64,768]{1,0:T(8,128)(2,1)S(1)}, bf16[64,768]{1,0:T(8,128)(2,1)S(1)}, u32[]{:S(2)}, u32[]{:S(2)}) collective-permute-start(bf16[64,768]{1,0:T(8,128)(2,1)S(1)} %get-tuple-element.55), channel_id=1, source_target_pairs={{0,4},{2,6},{4,0},{6,2},{8,12},{10,14},{12,8},{14,10},{1,5},{3,7},... | collective-permute-start | bytes 294920 | tf_op jit(solution)/shard_map/ppermute | solution.py:37
  37.8 0.0 collective-permute-done.10
  37.8 0.7 %collective-permute-start.12 = (bf16[64,768]{1,0:T(8,128)(2,1)S(1)}, bf16[64,768]{1,0:T(8,128)(2,1)S(1)}, u32[]{:S(2)}, u32[]{:S(2)}) collective-permute-start(bf16[64,768]{1,0:T(8,128)(2,1)S(1)} %get-tuple-element.56), channel_id=1, source_target_pairs={{4,8},{6,10},{8,4},{10,6},{5,9},{7,11},{9,5},{11,7},{20,24},{22,26... | collective-permute-start | bytes 294920 | tf_op jit(solution)/shard_map/ppermute | solution.py:37
  38.5 0.0 collective-permute-done.8
  38.5 2.3 %collective-permute-start.13 = (bf16[64,512]{1,0:T(8,128)(2,1)S(1)}, bf16[64,512]{1,0:T(8,128)(2,1)S(1)}, u32[]{:S(2)}, u32[]{:S(2)}) collective-permute-start(bf16[64,512]{1,0:T(8,128)(2,1)S(1)} %get-tuple-element.57), channel_id=1, source_target_pairs={{0,2},{2,0},{4,6},{6,4},{8,10},{10,8},{12,14},{14,12},{1,3},{3,1},... | collective-permute-start | bytes 196616 | tf_op jit(solution)/shard_map/ppermute | solution.py:37
  40.8 0.0 collective-permute-done.7
  40.8 3.7 %collective-permute-start.14 = (bf16[64,384]{1,0:T(8,128)(2,1)S(1)}, bf16[64,384]{1,0:T(8,128)(2,1)S(1)}, u32[]{:S(2)}, u32[]{:S(2)}) collective-permute-start(bf16[64,384]{1,0:T(8,128)(2,1)S(1)} %get-tuple-element.58), channel_id=1, source_target_pairs={{0,6},{2,4},{4,2},{6,0},{8,14},{10,12},{12,10},{14,8},{1,7},{3,5},... | collective-permute-start | bytes 147464 | tf_op jit(solution)/shard_map/ppermute | solution.py:37
  44.5 0.7 %collective-permute-start.15 = (bf16[64,384]{1,0:T(8,128)(2,1)S(1)}, bf16[64,384]{1,0:T(8,128)(2,1)S(1)}, u32[]{:S(2)}, u32[]{:S(2)}) collective-permute-start(bf16[64,384]{1,0:T(8,128)(2,1)S(1)} %get-tuple-element.59), channel_id=1, source_target_pairs={{4,10},{6,8},{8,6},{10,4},{5,11},{7,9},{9,7},{11,5},{20,26},{22,24... | collective-permute-start | bytes 147464 | tf_op jit(solution)/shard_map/ppermute | solution.py:37
  45.2 0.4 shard_map.91.halo_t
  45.6 2.2 %shard_map.90 = (bf16[2048,128]{1,0:T(8,128)(2,1)}, f32[64,32,128]{2,1,0:T(8,128)S(1)}) custom-call(bf16[64,1024]{1,0:T(8,128)(2,1)S(1)} %get-tuple-element.45.gc_ref, bf16[4096,128]{1,0:T(8,128)(2,1)S(1)} %get-tuple-element.46.hot_ref, bf16[64,128,128]{2,1,0:T(8,128)(2,1)S(1)} %get-tuple-element.47.tgt_t, ...), custom_call_target="tpu_custom_call" | custom-call | bytes 12000000 | tf_op jit(solution)/shard_map/pallas_call | solution.py:410
  47.8 0.0 collective-permute-done.13.refs_2_
  47.8 1.9 %shard_map.92 = bf16[2048,128]{1,0:T(8,128)(2,1)} custom-call(f32[64,32,128]{2,1,0:T(8,128)S(1)} %get-tuple-element.49.own_ref, bf16[64,80,128]{2,1,0:T(8,128)(2,1)S(1)} %shard_map.91.halo_t, bf16[64,768]{1,0:T(8,128)(2,1)S(1)} %collective-permute-done.11.refs_0_, bf16[64,768]{1,0:T(8,128)(2,1)S(1)} %collective-permute-done.12.refs_1_, ...), custom_call_target="tpu_custom_call" | custom-call | bytes 9000000 | tf_op jit(solution)/shard_map/pallas_call | solution.py:410
  (8 shorter events, 0.0 us)
Async XLA Ops:
  2.1 22.6 %collective-permute-start = (bf16[3,8,64,128]{3,2,1,0:T(8,128)(2,1)S(1)}, bf16[3,8,64,128]{3,2,1,0:T(8,128)(2,1)S(1)}, u32[]{:S(2)}, u32[]{:S(2)}) collective-permute-start(bf16[3,8,64,128]{3,2,1,0:T(8,128)(2,1)S(1)} %get-tuple-element.34), channel_id=1, source_target_pairs={{0,4},{2,6},{4,0},{6,2},{8,12},{10,14},{12,8},{14,10},{1,5},{3,7},... | collective-permute-start | bytes 1179656 | tf_op jit(solution)/shard_map/ppermute | solution.py:37
  5.3 19.5 %collective-permute-start.1 = (bf16[3,8,64,128]{3,2,1,0:T(8,128)(2,1)S(1)}, bf16[3,8,64,128]{3,2,1,0:T(8,128)(2,1)S(1)}, u32[]{:S(2)}, u32[]{:S(2)}) collective-permute-start(bf16[3,8,64,128]{3,2,1,0:T(8,128)(2,1)S(1)} %get-tuple-element.35), channel_id=1, source_target_pairs={{4,8},{6,10},{8,4},{10,6},{5,9},{7,11},{9,5},{11,7},{20,24},{22,26... | collective-permute-start | bytes 1179656 | tf_op jit(solution)/shard_map/ppermute | solution.py:37
  5.9 12.9 %collective-permute-start.3 = (bf16[3,3,64,128]{3,2,1,0:T(8,128)(2,1)S(1)}, bf16[3,3,64,128]{3,2,1,0:T(8,128)(2,1)S(1)}, u32[]{:S(2)}, u32[]{:S(2)}) collective-permute-start(bf16[3,3,64,128]{3,2,1,0:T(8,128)(2,1)S(1)} %get-tuple-element.37), channel_id=1, source_target_pairs={{0,6},{2,4},{4,2},{6,0},{8,14},{10,12},{12,10},{14,8},{1,7},{3,5},... | collective-permute-start | bytes 442376 | tf_op jit(solution)/shard_map/ppermute | solution.py:37
  11.4 8.1 %collective-permute-start.4 = (bf16[3,3,64,128]{3,2,1,0:T(8,128)(2,1)S(1)}, bf16[3,3,64,128]{3,2,1,0:T(8,128)(2,1)S(1)}, u32[]{:S(2)}, u32[]{:S(2)}) collective-permute-start(bf16[3,3,64,128]{3,2,1,0:T(8,128)(2,1)S(1)} %get-tuple-element.38), channel_id=1, source_target_pairs={{4,10},{6,8},{8,6},{10,4},{5,11},{7,9},{9,7},{11,5},{20,26},{22,24... | collective-permute-start | bytes 442376 | tf_op jit(solution)/shard_map/ppermute | solution.py:37
  12.0 12.7 %collective-permute-start.2 = (bf16[4,3,64,128]{3,2,1,0:T(8,128)(2,1)S(1)}, bf16[4,3,64,128]{3,2,1,0:T(8,128)(2,1)S(1)}, u32[]{:S(2)}, u32[]{:S(2)}) collective-permute-start(bf16[4,3,64,128]{3,2,1,0:T(8,128)(2,1)S(1)} %get-tuple-element.36), channel_id=1, source_target_pairs={{0,2},{2,0},{4,6},{6,4},{8,10},{10,8},{12,14},{14,12},{1,3},{3,1},... | collective-permute-start | bytes 589832 | tf_op jit(solution)/shard_map/ppermute | solution.py:37
  18.8 22.0 %collective-permute-start.7 = (bf16[3,8,64,128]{3,2,1,0:T(8,128)(2,1)S(1)}, bf16[3,8,64,128]{3,2,1,0:T(8,128)(2,1)S(1)}, u32[]{:S(2)}, u32[]{:S(2)}) collective-permute-start(bf16[3,8,64,128]{3,2,1,0:T(8,128)(2,1)S(1)} %get-tuple-element.51), channel_id=1, source_target_pairs={{4,8},{6,10},{8,4},{10,6},{5,9},{7,11},{9,5},{11,7},{20,24},{22,26... | collective-permute-start | bytes 1179656 | tf_op jit(solution)/shard_map/ppermute | solution.py:37
  19.5 25.0 %collective-permute-start.6 = (bf16[3,8,64,128]{3,2,1,0:T(8,128)(2,1)S(1)}, bf16[3,8,64,128]{3,2,1,0:T(8,128)(2,1)S(1)}, u32[]{:S(2)}, u32[]{:S(2)}) collective-permute-start(bf16[3,8,64,128]{3,2,1,0:T(8,128)(2,1)S(1)} %get-tuple-element.50), channel_id=1, source_target_pairs={{0,4},{2,6},{4,0},{6,2},{8,12},{10,14},{12,8},{14,10},{1,5},{3,7},... | collective-permute-start | bytes 1179656 | tf_op jit(solution)/shard_map/ppermute | solution.py:37
  26.6 2.6 %collective-permute-start.5 = (bf16[64,1024]{1,0:T(8,128)(2,1)S(1)}, bf16[64,1024]{1,0:T(8,128)(2,1)S(1)}, u32[]{:S(2)}, u32[]{:S(2)}) collective-permute-start(bf16[64,1024]{1,0:T(8,128)(2,1)S(1)} %get-tuple-element.39.refs_0_), channel_id=1, source_target_pairs={{0,1},{1,0},{2,3},{3,2},{4,5},{5,4},{6,7},{7,6},{8,9},{9,8},{10,11... | collective-permute-start | bytes 393224 | tf_op jit(solution)/shard_map/ppermute | solution.py:509
  26.7 11.8 %collective-permute-start.8 = (bf16[4,3,64,128]{3,2,1,0:T(8,128)(2,1)S(1)}, bf16[4,3,64,128]{3,2,1,0:T(8,128)(2,1)S(1)}, u32[]{:S(2)}, u32[]{:S(2)}) collective-permute-start(bf16[4,3,64,128]{3,2,1,0:T(8,128)(2,1)S(1)} %get-tuple-element.52), channel_id=1, source_target_pairs={{0,2},{2,0},{4,6},{6,4},{8,10},{10,8},{12,14},{14,12},{1,3},{3,1},... | collective-permute-start | bytes 589832 | tf_op jit(solution)/shard_map/ppermute | solution.py:37
  27.2 7.9 %collective-permute-start.9 = (bf16[3,3,64,128]{3,2,1,0:T(8,128)(2,1)S(1)}, bf16[3,3,64,128]{3,2,1,0:T(8,128)(2,1)S(1)}, u32[]{:S(2)}, u32[]{:S(2)}) collective-permute-start(bf16[3,3,64,128]{3,2,1,0:T(8,128)(2,1)S(1)} %get-tuple-element.53), channel_id=1, source_target_pairs={{0,6},{2,4},{4,2},{6,0},{8,14},{10,12},{12,10},{14,8},{1,7},{3,5},... | collective-permute-start | bytes 442376 | tf_op jit(solution)/shard_map/ppermute | solution.py:37
  29.2 8.6 %collective-permute-start.10 = (bf16[3,3,64,128]{3,2,1,0:T(8,128)(2,1)S(1)}, bf16[3,3,64,128]{3,2,1,0:T(8,128)(2,1)S(1)}, u32[]{:S(2)}, u32[]{:S(2)}) collective-permute-start(bf16[3,3,64,128]{3,2,1,0:T(8,128)(2,1)S(1)} %get-tuple-element.54), channel_id=1, source_target_pairs={{4,10},{6,8},{8,6},{10,4},{5,11},{7,9},{9,7},{11,5},{20,26},{22,24... | collective-permute-start | bytes 442376 | tf_op jit(solution)/shard_map/ppermute | solution.py:37
  35.1 12.7 %collective-permute-start.11 = (bf16[64,768]{1,0:T(8,128)(2,1)S(1)}, bf16[64,768]{1,0:T(8,128)(2,1)S(1)}, u32[]{:S(2)}, u32[]{:S(2)}) collective-permute-start(bf16[64,768]{1,0:T(8,128)(2,1)S(1)} %get-tuple-element.55), channel_id=1, source_target_pairs={{0,4},{2,6},{4,0},{6,2},{8,12},{10,14},{12,8},{14,10},{1,5},{3,7},... | collective-permute-start | bytes 294920 | tf_op jit(solution)/shard_map/ppermute | solution.py:37
  37.8 10.0 %collective-permute-start.12 = (bf16[64,768]{1,0:T(8,128)(2,1)S(1)}, bf16[64,768]{1,0:T(8,128)(2,1)S(1)}, u32[]{:S(2)}, u32[]{:S(2)}) collective-permute-start(bf16[64,768]{1,0:T(8,128)(2,1)S(1)} %get-tuple-element.56), channel_id=1, source_target_pairs={{4,8},{6,10},{8,4},{10,6},{5,9},{7,11},{9,5},{11,7},{20,24},{22,26... | collective-permute-start | bytes 294920 | tf_op jit(solution)/shard_map/ppermute | solution.py:37
  38.5 9.3 %collective-permute-start.13 = (bf16[64,512]{1,0:T(8,128)(2,1)S(1)}, bf16[64,512]{1,0:T(8,128)(2,1)S(1)}, u32[]{:S(2)}, u32[]{:S(2)}) collective-permute-start(bf16[64,512]{1,0:T(8,128)(2,1)S(1)} %get-tuple-element.57), channel_id=1, source_target_pairs={{0,2},{2,0},{4,6},{6,4},{8,10},{10,8},{12,14},{14,12},{1,3},{3,1},... | collective-permute-start | bytes 196616 | tf_op jit(solution)/shard_map/ppermute | solution.py:37
  40.8 7.0 %collective-permute-start.14 = (bf16[64,384]{1,0:T(8,128)(2,1)S(1)}, bf16[64,384]{1,0:T(8,128)(2,1)S(1)}, u32[]{:S(2)}, u32[]{:S(2)}) collective-permute-start(bf16[64,384]{1,0:T(8,128)(2,1)S(1)} %get-tuple-element.58), channel_id=1, source_target_pairs={{0,6},{2,4},{4,2},{6,0},{8,14},{10,12},{12,10},{14,8},{1,7},{3,5},... | collective-permute-start | bytes 147464 | tf_op jit(solution)/shard_map/ppermute | solution.py:37
  44.5 3.3 %collective-permute-start.15 = (bf16[64,384]{1,0:T(8,128)(2,1)S(1)}, bf16[64,384]{1,0:T(8,128)(2,1)S(1)}, u32[]{:S(2)}, u32[]{:S(2)}) collective-permute-start(bf16[64,384]{1,0:T(8,128)(2,1)S(1)} %get-tuple-element.59), channel_id=1, source_target_pairs={{4,10},{6,8},{8,6},{10,4},{5,11},{7,9},{9,7},{11,5},{20,26},{22,24... | collective-permute-start | bytes 147464 | tf_op jit(solution)/shard_map/ppermute | solution.py:37

commit v9 on v8

--- a/solution.py
+++ b/solution.py
@@ -258,14 +258,10 @@
     whole[pl.ds(pl.multiple_of(rep * px, px), px), :] = mine_ref[...]
     whole[pl.ds(pl.multiple_of((1 - rep) * px, px), px), :] = other_ref[...]
     w_half = w_ref[...]
-    wide = 2
-    bias = jnp.concatenate([bt_ref[...]] * wide, axis=1)
-    width = wide * LANES
-    for g in range(mine_ref.shape[1] // width):
-        cut = slice(g * width, (g + 1) * width)
-        pre = jnp.dot(wt_ref[...], whole[:, cut], preferred_element_type=F32) + bias
-        grad = (gh_ref[:, cut] * gelu_slope(pre)).astype(BF16)
-        gc_ref[:, cut] = jnp.dot(w_half, grad, preferred_element_type=F32).astype(BF16)
+    bias = jnp.concatenate([bt_ref[...]] * (mine_ref.shape[1] // LANES), axis=1)
+    pre = jnp.dot(wt_ref[...], whole[...], preferred_element_type=F32) + bias
+    grad = (gh_ref[...] * gelu_slope(pre)).astype(BF16)
+    gc_ref[...] = jnp.dot(w_half, grad, preferred_element_type=F32).astype(BF16)
     send(rows, cols, slots, pieces, gc_ref, table_ref, out_refs)
 
 
@@ -317,7 +313,7 @@
             i += 1
 
 
-def own_kernel(px, n, slots, gc_ref, hot_ref, tgt_t, src_t, sg_ref, own_ref, pw, s32):
+def own_kernel(px, n, slots, gc_ref, hot_ref, tgt_t, sg_ref, pw, s32):
     ext_pad = tgt_t.shape[1]
     pitch = px + 1
     inv_root = 1.0 / math.sqrt(tgt_t.shape[2])
@@ -343,10 +339,6 @@
         for t in range(tiles):
             w = pw[t, pl.ds(p, n, stride=pitch), :].astype(BF16)
             sg += jnp.dot(w, tp[t * LANES : (t + 1) * LANES, :], preferred_element_type=F32)
-            if t == 0:
-                own_ref[p] = lax.dot_general(
-                    w[:, :n], src_t[p], TN, preferred_element_type=F32
-                )
         s32[pl.ds(p, n, stride=pitch), :] = sg * inv_root
 
     loop(px, per_pixel, px)
@@ -372,11 +364,11 @@
     loop(px, turn, 8)
 
 
-def total_kernel(px, n, slots, widths, own_ref, halo_t, *refs):
+def total_kernel(px, n, slots, widths, pw_own, src_t, halo_t, *refs):
     k = len(widths)
     msg_refs, tg_ref, pw, t32 = refs[:k], refs[k], refs[k + 1], refs[k + 2]
     pitch = px + 1
-    inv_root = 1.0 / math.sqrt(own_ref.shape[2])
+    inv_root = 1.0 / math.sqrt(src_t.shape[2])
     at = 0
     for width, ref in zip(widths, msg_refs):
         for g in range(ref.shape[1] // LANES):
@@ -388,10 +380,11 @@
     clear(pw, at, halo_t.shape[1], px, pitch)
 
     def per_pixel(p):
-        w = pw[pl.ds(p, halo_t.shape[1], stride=pitch), :]
-        tg = own_ref[p] + lax.dot_general(
-            w[:, :n].astype(BF16), halo_t[p], TN, preferred_element_type=F32
-        )
+        near = pw_own[0, pl.ds(p, n, stride=pitch), :]
+        far = pw[pl.ds(p, halo_t.shape[1], stride=pitch), :]
+        w = jnp.concatenate([near, far], axis=0)[:, :n].astype(BF16)
+        s = jnp.concatenate([src_t[p], halo_t[p]], axis=0)
+        tg = lax.dot_general(w, s, TN, preferred_element_type=F32)
         t32[pl.ds(p, n, stride=pitch), :] = tg * inv_root
 
     loop(px, per_pixel, px // 2)
@@ -528,11 +521,11 @@
     got = []
     for x, (qz, qx) in zip(sent, pieces):
         got.append(swap(x, qz, qx))
-    sg, own = call(
+    sg, pw_own = call(
         partial(own_kernel, px, n, slots),
-        [((n * px, channels), BF16), ((px, n, channels), F32)],
-        [((ext_pad // LANES, n * pitch, LANES), F32), ((n * pitch, channels), F32)],
-        (gc, hots, tgt_t, src_t),
+        [((n * px, channels), BF16), ((ext_pad // LANES, n * pitch, LANES), F32)],
+        [((n * pitch, channels), F32)],
+        (gc, hots, tgt_t),
         us=4,
     )
     halo_pad = -(-(ext - n) // 16) * 16
@@ -547,7 +540,7 @@
         partial(total_kernel, px, n, slots, [per if qx is None else H for _, qx in pieces]),
         [((n * px, channels), BF16)],
         [((halo_pad * pitch, LANES), F32), ((n * pitch, channels), F32)],
-        (own, halo_t, *got),
+        (pw_own, src_t, halo_t, *got),
         us=3,
     )
     return sg.reshape(source.shape), tg.reshape(source.shape)

time: 50.5 us -> 50.6 us (level)
  transfers between devices with their start and end apart: 16 -> 16, of which waited for: 2 -> 2; matrix products, arithmetic and copies ran while one was open for 0% -> 0% of each run, Pallas kernels for 17% -> 16%
where the time goes in v9:
time: 50.6 us; the launch traced here: 49.7 us
  starting transfers between devices  29.7 us (59%)
  Pallas kernels  11.4 us (23%)
  waiting for transfers between devices  7.8 us (15%)
  between operations  0.77 us (2%)
    ppermute x15, starting transfers between devices, swap(): return lax.ppermute(x, ('strip', 'sub'), pairs)  29.6 us
    pallas_call x7, Pallas kernels, call(): pl.pallas_call(kernel, out_shape=[pltpu.VMEM(s, d) if near else jax.Shape...  9.88 us
    ppermute x15, waiting for transfers between devices, swap(): return lax.ppermute(x, ('strip', 'sub'), pairs)  7.79 us
    pallas_call x1, Pallas kernels, shards(): pl.pallas_call(partial(cut_kernel, pieces, rows, cols), name='cut', out_s...  1.51 us
  transfers between devices with their start and end apart: 16, of which 2 were waited for; matrix products, arithmetic and copies ran while one was open for 0% of the time, Pallas kernels for 16%

profile of v9, /device:TPU:0, one launch (start us, length us, event | category | flops | bytes accessed | tf_op | source)
XLA Modules:
  0.0 49.7 jit_solution(17021634611062022906)
XLA Ops:
  0.6 1.5 %cut.1 = (bf16[3,8,64,128]{3,2,1,0:T(8,128)(2,1)S(1)}, bf16[3,8,64,128]{3,2,1,0:T(8,128)(2,1)S(1)}, bf16[4,3,64,128]{3,2,1,0:T(8,128)(2,1)S(1)}, bf16[3,3,64,128...) custom-call(bf16[4,8,64,128]{3,2,1,0:T(8,128)(2,1)} %x_ref.1), custom_call_target="tpu_custom_call" | custom-call | tf_op jit(solution)/shard_map/cut/pallas_call | solution.py:467
  2.1 3.1 %collective-permute-start = (bf16[3,8,64,128]{3,2,1,0:T(8,128)(2,1)S(1)}, bf16[3,8,64,128]{3,2,1,0:T(8,128)(2,1)S(1)}, u32[]{:S(2)}, u32[]{:S(2)}) collective-permute-start(bf16[3,8,64,128]{3,2,1,0:T(8,128)(2,1)S(1)} %get-tuple-element.34), channel_id=1, source_target_pairs={{0,4},{2,6},{4,0},{6,2},{8,12},{10,14},{12,8},{14,10},{1,5},{3,7},... | collective-permute-start | bytes 1179656 | tf_op jit(solution)/shard_map/ppermute | solution.py:37
  5.3 0.7 %collective-permute-start.1 = (bf16[3,8,64,128]{3,2,1,0:T(8,128)(2,1)S(1)}, bf16[3,8,64,128]{3,2,1,0:T(8,128)(2,1)S(1)}, u32[]{:S(2)}, u32[]{:S(2)}) collective-permute-start(bf16[3,8,64,128]{3,2,1,0:T(8,128)(2,1)S(1)} %get-tuple-element.35), channel_id=1, source_target_pairs={{4,8},{6,10},{8,4},{10,6},{5,9},{7,11},{9,5},{11,7},{20,24},{22,26... | collective-permute-start | bytes 1179656 | tf_op jit(solution)/shard_map/ppermute | solution.py:37
  5.9 5.4 %collective-permute-start.3 = (bf16[3,3,64,128]{3,2,1,0:T(8,128)(2,1)S(1)}, bf16[3,3,64,128]{3,2,1,0:T(8,128)(2,1)S(1)}, u32[]{:S(2)}, u32[]{:S(2)}) collective-permute-start(bf16[3,3,64,128]{3,2,1,0:T(8,128)(2,1)S(1)} %get-tuple-element.37), channel_id=1, source_target_pairs={{0,6},{2,4},{4,2},{6,0},{8,14},{10,12},{12,10},{14,8},{1,7},{3,5},... | collective-permute-start | bytes 442376 | tf_op jit(solution)/shard_map/ppermute | solution.py:37
  11.4 0.7 %collective-permute-start.4 = (bf16[3,3,64,128]{3,2,1,0:T(8,128)(2,1)S(1)}, bf16[3,3,64,128]{3,2,1,0:T(8,128)(2,1)S(1)}, u32[]{:S(2)}, u32[]{:S(2)}) collective-permute-start(bf16[3,3,64,128]{3,2,1,0:T(8,128)(2,1)S(1)} %get-tuple-element.38), channel_id=1, source_target_pairs={{4,10},{6,8},{8,6},{10,4},{5,11},{7,9},{9,7},{11,5},{20,26},{22,24... | collective-permute-start | bytes 442376 | tf_op jit(solution)/shard_map/ppermute | solution.py:37
  12.0 0.5 %collective-permute-start.2 = (bf16[4,3,64,128]{3,2,1,0:T(8,128)(2,1)S(1)}, bf16[4,3,64,128]{3,2,1,0:T(8,128)(2,1)S(1)}, u32[]{:S(2)}, u32[]{:S(2)}) collective-permute-start(bf16[4,3,64,128]{3,2,1,0:T(8,128)(2,1)S(1)} %get-tuple-element.36), channel_id=1, source_target_pairs={{0,2},{2,0},{4,6},{6,4},{8,10},{10,8},{12,14},{14,12},{1,3},{3,1},... | collective-permute-start | bytes 589832 | tf_op jit(solution)/shard_map/ppermute | solution.py:37
  12.6 2.1 %shard_map.86 = (bf16[3,8,64,128]{3,2,1,0:T(8,128)(2,1)S(1)}, bf16[3,8,64,128]{3,2,1,0:T(8,128)(2,1)S(1)}, bf16[4,3,64,128]{3,2,1,0:T(8,128)(2,1)S(1)}, bf16[3,3...) custom-call(bf16[4,8,64,128]{3,2,1,0:T(8,128)(2,1)} %refs_0_.1, ...), custom_call_target="tpu_custom_call" | custom-call | bytes 6000000 | tf_op jit(solution)/shard_map/pallas_call | solution.py:403
  14.7 4.1 %collective-permute-done.3 = bf16[3,3,64,128]{3,2,1,0:T(8,128)(2,1)S(1)} collective-permute-done((bf16[3,3,64,128]{3,2,1,0:T(8,128)(2,1)S(1)}, bf16[3,3,64,128]{3,2,1,0:T(8,128)(2,1)S(1)}, u32[]{:S(2)}, u32[]{:S(2)}) %collective-permute-start.3) | collective-permute-done | bytes 147488 | tf_op jit(solution)/shard_map/ppermute | solution.py:37
  18.8 0.7 %collective-permute-start.7 = (bf16[3,8,64,128]{3,2,1,0:T(8,128)(2,1)S(1)}, bf16[3,8,64,128]{3,2,1,0:T(8,128)(2,1)S(1)}, u32[]{:S(2)}, u32[]{:S(2)}) collective-permute-start(bf16[3,8,64,128]{3,2,1,0:T(8,128)(2,1)S(1)} %get-tuple-element.51), channel_id=1, source_target_pairs={{4,8},{6,10},{8,4},{10,6},{5,9},{7,11},{9,5},{11,7},{20,24},{22,26... | collective-permute-start | bytes 1179656 | tf_op jit(solution)/shard_map/ppermute | solution.py:37
  19.5 0.0 collective-permute-done.4
  19.5 5.3 %collective-permute-start.6 = (bf16[3,8,64,128]{3,2,1,0:T(8,128)(2,1)S(1)}, bf16[3,8,64,128]{3,2,1,0:T(8,128)(2,1)S(1)}, u32[]{:S(2)}, u32[]{:S(2)}) collective-permute-start(bf16[3,8,64,128]{3,2,1,0:T(8,128)(2,1)S(1)} %get-tuple-element.50), channel_id=1, source_target_pairs={{0,4},{2,6},{4,0},{6,2},{8,12},{10,14},{12,8},{14,10},{1,5},{3,7},... | collective-permute-start | bytes 1179656 | tf_op jit(solution)/shard_map/ppermute | solution.py:37
  24.8 0.0 collective-permute-done.1
  24.8 1.8 %shard_map.87 = (bf16[64,1024]{1,0:T(8,128)(2,1)S(1)}, bf16[64,128,128]{2,1,0:T(8,128)(2,1)S(1)}, bf16[4096,128]{1,0:T(8,128)(2,1)S(1)}) custom-call(bf16[64,32,128]{2,1,0:T(8,128)(2,1)S(1)} %get-tuple-element.31.refs_0_, bf16[64,32,128]{2,1,0:T(8,128)(2,1)S(1)} %get-tuple-element.32.refs_1_.src_t, s32[8,128]{1,0:T(8,128)S(1)} %get-tuple-element.33.refs_2_.e_ref, ...), custom_call_target="tpu_custom_call" | custom-call | bytes 9000000 | tf_op jit(solution)/shard_map/pallas_call | solution.py:403
  26.6 0.1 collective-permute-start.5
  26.7 0.5 %collective-permute-start.8 = (bf16[4,3,64,128]{3,2,1,0:T(8,128)(2,1)S(1)}, bf16[4,3,64,128]{3,2,1,0:T(8,128)(2,1)S(1)}, u32[]{:S(2)}, u32[]{:S(2)}) collective-permute-start(bf16[4,3,64,128]{3,2,1,0:T(8,128)(2,1)S(1)} %get-tuple-element.52), channel_id=1, source_target_pairs={{0,2},{2,0},{4,6},{6,4},{8,10},{10,8},{12,14},{14,12},{1,3},{3,1},... | collective-permute-start | bytes 589832 | tf_op jit(solution)/shard_map/ppermute | solution.py:37
  27.2 2.0 %collective-permute-start.9 = (bf16[3,3,64,128]{3,2,1,0:T(8,128)(2,1)S(1)}, bf16[3,3,64,128]{3,2,1,0:T(8,128)(2,1)S(1)}, u32[]{:S(2)}, u32[]{:S(2)}) collective-permute-start(bf16[3,3,64,128]{3,2,1,0:T(8,128)(2,1)S(1)} %get-tuple-element.53), channel_id=1, source_target_pairs={{0,6},{2,4},{4,2},{6,0},{8,14},{10,12},{12,10},{14,8},{1,7},{3,5},... | collective-permute-start | bytes 442376 | tf_op jit(solution)/shard_map/ppermute | solution.py:37
  29.2 0.0 collective-permute-done.5.refs_1_
  29.2 0.7 %collective-permute-start.10 = (bf16[3,3,64,128]{3,2,1,0:T(8,128)(2,1)S(1)}, bf16[3,3,64,128]{3,2,1,0:T(8,128)(2,1)S(1)}, u32[]{:S(2)}, u32[]{:S(2)}) collective-permute-start(bf16[3,3,64,128]{3,2,1,0:T(8,128)(2,1)S(1)} %get-tuple-element.54), channel_id=1, source_target_pairs={{4,10},{6,8},{8,6},{10,4},{5,11},{7,9},{9,7},{11,5},{20,26},{22,24... | collective-permute-start | bytes 442376 | tf_op jit(solution)/shard_map/ppermute | solution.py:37
  29.9 0.2 shard_map.88.refs_6_
  30.0 1.4 %shard_map.89 = (bf16[64,1024]{1,0:T(8,128)(2,1)S(1)}, bf16[64,768]{1,0:T(8,128)(2,1)S(1)}, bf16[64,768]{1,0:T(8,128)(2,1)S(1)}, bf16[64,512]{1,0:T(8,128)(2,1)S...) custom-call(bf16[64,1024]{1,0:T(8,128)(2,1)S(1)} %get-tuple-element.39.refs_0_, ...), custom_call_target="tpu_custom_call" | custom-call | bytes 9000000 | tf_op jit(solution)/shard_map/pallas_call | solution.py:403
  31.5 3.6 %collective-permute-done.9 = bf16[3,3,64,128]{3,2,1,0:T(8,128)(2,1)S(1)} collective-permute-done((bf16[3,3,64,128]{3,2,1,0:T(8,128)(2,1)S(1)}, bf16[3,3,64,128]{3,2,1,0:T(8,128)(2,1)S(1)}, u32[]{:S(2)}, u32[]{:S(2)}) %collective-permute-start.9) | collective-permute-done | bytes 147488 | tf_op jit(solution)/shard_map/ppermute | solution.py:37
  35.1 2.8 %collective-permute-start.11 = (bf16[64,768]{1,0:T(8,128)(2,1)S(1)}, bf16[64,768]{1,0:T(8,128)(2,1)S(1)}, u32[]{:S(2)}, u32[]{:S(2)}) collective-permute-start(bf16[64,768]{1,0:T(8,128)(2,1)S(1)} %get-tuple-element.55), channel_id=1, source_target_pairs={{0,4},{2,6},{4,0},{6,2},{8,12},{10,14},{12,8},{14,10},{1,5},{3,7},... | collective-permute-start | bytes 294920 | tf_op jit(solution)/shard_map/ppermute | solution.py:37
  37.8 0.0 collective-permute-done.10
  37.8 0.7 %collective-permute-start.12 = (bf16[64,768]{1,0:T(8,128)(2,1)S(1)}, bf16[64,768]{1,0:T(8,128)(2,1)S(1)}, u32[]{:S(2)}, u32[]{:S(2)}) collective-permute-start(bf16[64,768]{1,0:T(8,128)(2,1)S(1)} %get-tuple-element.56), channel_id=1, source_target_pairs={{4,8},{6,10},{8,4},{10,6},{5,9},{7,11},{9,5},{11,7},{20,24},{22,26... | collective-permute-start | bytes 294920 | tf_op jit(solution)/shard_map/ppermute | solution.py:37
  38.5 0.0 collective-permute-done.8
  38.5 2.3 %collective-permute-start.13 = (bf16[64,512]{1,0:T(8,128)(2,1)S(1)}, bf16[64,512]{1,0:T(8,128)(2,1)S(1)}, u32[]{:S(2)}, u32[]{:S(2)}) collective-permute-start(bf16[64,512]{1,0:T(8,128)(2,1)S(1)} %get-tuple-element.57), channel_id=1, source_target_pairs={{0,2},{2,0},{4,6},{6,4},{8,10},{10,8},{12,14},{14,12},{1,3},{3,1},... | collective-permute-start | bytes 196616 | tf_op jit(solution)/shard_map/ppermute | solution.py:37
  40.8 0.0 collective-permute-done.7
  40.8 3.7 %collective-permute-start.14 = (bf16[64,384]{1,0:T(8,128)(2,1)S(1)}, bf16[64,384]{1,0:T(8,128)(2,1)S(1)}, u32[]{:S(2)}, u32[]{:S(2)}) collective-permute-start(bf16[64,384]{1,0:T(8,128)(2,1)S(1)} %get-tuple-element.58), channel_id=1, source_target_pairs={{0,6},{2,4},{4,2},{6,0},{8,14},{10,12},{12,10},{14,8},{1,7},{3,5},... | collective-permute-start | bytes 147464 | tf_op jit(solution)/shard_map/ppermute | solution.py:37
  44.5 0.7 %collective-permute-start.15 = (bf16[64,384]{1,0:T(8,128)(2,1)S(1)}, bf16[64,384]{1,0:T(8,128)(2,1)S(1)}, u32[]{:S(2)}, u32[]{:S(2)}) collective-permute-start(bf16[64,384]{1,0:T(8,128)(2,1)S(1)} %get-tuple-element.59), channel_id=1, source_target_pairs={{4,10},{6,8},{8,6},{10,4},{5,11},{7,9},{9,7},{11,5},{20,26},{22,24... | collective-permute-start | bytes 147464 | tf_op jit(solution)/shard_map/ppermute | solution.py:37
  45.2 0.4 shard_map.91.halo_t
  45.6 2.0 %shard_map.90 = (bf16[2048,128]{1,0:T(8,128)(2,1)}, f32[1,2080,128]{2,1,0:T(8,128)S(1)}) custom-call(bf16[64,1024]{1,0:T(8,128)(2,1)S(1)} %get-tuple-element.45.gc_ref, bf16[4096,128]{1,0:T(8,128)(2,1)S(1)} %get-tuple-element.46.hot_ref, bf16[64,128,128]{2,1,0:T(8,128)(2,1)S(1)} %get-tuple-element.47.tgt_t), custom_call_target="tpu_custom_call" | custom-call | bytes 12000000 | tf_op jit(solution)/shard_map/pallas_call | solution.py:403
  47.7 2.0 %shard_map.92 = bf16[2048,128]{1,0:T(8,128)(2,1)} custom-call(f32[1,2080,128]{2,1,0:T(8,128)S(1)} %get-tuple-element.49.pw_own, bf16[64,32,128]{2,1,0:T(8,128)(2,1)S(1)} %get-tuple-element.32.refs_1_.src_t, bf16[64,80,128]{2,1,0:T(8,128)(2,1)S(1)} %shard_map.91.halo_t, bf16[64,768]{1,0:T(8,128)(2,1)S(1)} %collective-permute-done.11.refs_0_, ...), custom_call_target="tpu_custom_call" | custom-call | bytes 9000000 | tf_op jit(solution)/shard_map/pallas_call | solution.py:403
  (8 shorter events, 0.0 us)
Async XLA Ops:
  2.1 22.6 %collective-permute-start = (bf16[3,8,64,128]{3,2,1,0:T(8,128)(2,1)S(1)}, bf16[3,8,64,128]{3,2,1,0:T(8,128)(2,1)S(1)}, u32[]{:S(2)}, u32[]{:S(2)}) collective-permute-start(bf16[3,8,64,128]{3,2,1,0:T(8,128)(2,1)S(1)} %get-tuple-element.34), channel_id=1, source_target_pairs={{0,4},{2,6},{4,0},{6,2},{8,12},{10,14},{12,8},{14,10},{1,5},{3,7},... | collective-permute-start | bytes 1179656 | tf_op jit(solution)/shard_map/ppermute | solution.py:37
  5.3 19.5 %collective-permute-start.1 = (bf16[3,8,64,128]{3,2,1,0:T(8,128)(2,1)S(1)}, bf16[3,8,64,128]{3,2,1,0:T(8,128)(2,1)S(1)}, u32[]{:S(2)}, u32[]{:S(2)}) collective-permute-start(bf16[3,8,64,128]{3,2,1,0:T(8,128)(2,1)S(1)} %get-tuple-element.35), channel_id=1, source_target_pairs={{4,8},{6,10},{8,4},{10,6},{5,9},{7,11},{9,5},{11,7},{20,24},{22,26... | collective-permute-start | bytes 1179656 | tf_op jit(solution)/shard_map/ppermute | solution.py:37
  5.9 12.9 %collective-permute-start.3 = (bf16[3,3,64,128]{3,2,1,0:T(8,128)(2,1)S(1)}, bf16[3,3,64,128]{3,2,1,0:T(8,128)(2,1)S(1)}, u32[]{:S(2)}, u32[]{:S(2)}) collective-permute-start(bf16[3,3,64,128]{3,2,1,0:T(8,128)(2,1)S(1)} %get-tuple-element.37), channel_id=1, source_target_pairs={{0,6},{2,4},{4,2},{6,0},{8,14},{10,12},{12,10},{14,8},{1,7},{3,5},... | collective-permute-start | bytes 442376 | tf_op jit(solution)/shard_map/ppermute | solution.py:37
  11.4 8.1 %collective-permute-start.4 = (bf16[3,3,64,128]{3,2,1,0:T(8,128)(2,1)S(1)}, bf16[3,3,64,128]{3,2,1,0:T(8,128)(2,1)S(1)}, u32[]{:S(2)}, u32[]{:S(2)}) collective-permute-start(bf16[3,3,64,128]{3,2,1,0:T(8,128)(2,1)S(1)} %get-tuple-element.38), channel_id=1, source_target_pairs={{4,10},{6,8},{8,6},{10,4},{5,11},{7,9},{9,7},{11,5},{20,26},{22,24... | collective-permute-start | bytes 442376 | tf_op jit(solution)/shard_map/ppermute | solution.py:37
  12.0 12.7 %collective-permute-start.2 = (bf16[4,3,64,128]{3,2,1,0:T(8,128)(2,1)S(1)}, bf16[4,3,64,128]{3,2,1,0:T(8,128)(2,1)S(1)}, u32[]{:S(2)}, u32[]{:S(2)}) collective-permute-start(bf16[4,3,64,128]{3,2,1,0:T(8,128)(2,1)S(1)} %get-tuple-element.36), channel_id=1, source_target_pairs={{0,2},{2,0},{4,6},{6,4},{8,10},{10,8},{12,14},{14,12},{1,3},{3,1},... | collective-permute-start | bytes 589832 | tf_op jit(solution)/shard_map/ppermute | solution.py:37
  18.8 22.0 %collective-permute-start.7 = (bf16[3,8,64,128]{3,2,1,0:T(8,128)(2,1)S(1)}, bf16[3,8,64,128]{3,2,1,0:T(8,128)(2,1)S(1)}, u32[]{:S(2)}, u32[]{:S(2)}) collective-permute-start(bf16[3,8,64,128]{3,2,1,0:T(8,128)(2,1)S(1)} %get-tuple-element.51), channel_id=1, source_target_pairs={{4,8},{6,10},{8,4},{10,6},{5,9},{7,11},{9,5},{11,7},{20,24},{22,26... | collective-permute-start | bytes 1179656 | tf_op jit(solution)/shard_map/ppermute | solution.py:37
  19.5 25.0 %collective-permute-start.6 = (bf16[3,8,64,128]{3,2,1,0:T(8,128)(2,1)S(1)}, bf16[3,8,64,128]{3,2,1,0:T(8,128)(2,1)S(1)}, u32[]{:S(2)}, u32[]{:S(2)}) collective-permute-start(bf16[3,8,64,128]{3,2,1,0:T(8,128)(2,1)S(1)} %get-tuple-element.50), channel_id=1, source_target_pairs={{0,4},{2,6},{4,0},{6,2},{8,12},{10,14},{12,8},{14,10},{1,5},{3,7},... | collective-permute-start | bytes 1179656 | tf_op jit(solution)/shard_map/ppermute | solution.py:37
  26.6 2.6 %collective-permute-start.5 = (bf16[64,1024]{1,0:T(8,128)(2,1)S(1)}, bf16[64,1024]{1,0:T(8,128)(2,1)S(1)}, u32[]{:S(2)}, u32[]{:S(2)}) collective-permute-start(bf16[64,1024]{1,0:T(8,128)(2,1)S(1)} %get-tuple-element.39.refs_0_), channel_id=1, source_target_pairs={{0,1},{1,0},{2,3},{3,2},{4,5},{5,4},{6,7},{7,6},{8,9},{9,8},{10,11... | collective-permute-start | bytes 393224 | tf_op jit(solution)/shard_map/ppermute | solution.py:502
  26.7 11.8 %collective-permute-start.8 = (bf16[4,3,64,128]{3,2,1,0:T(8,128)(2,1)S(1)}, bf16[4,3,64,128]{3,2,1,0:T(8,128)(2,1)S(1)}, u32[]{:S(2)}, u32[]{:S(2)}) collective-permute-start(bf16[4,3,64,128]{3,2,1,0:T(8,128)(2,1)S(1)} %get-tuple-element.52), channel_id=1, source_target_pairs={{0,2},{2,0},{4,6},{6,4},{8,10},{10,8},{12,14},{14,12},{1,3},{3,1},... | collective-permute-start | bytes 589832 | tf_op jit(solution)/shard_map/ppermute | solution.py:37
  27.2 7.9 %collective-permute-start.9 = (bf16[3,3,64,128]{3,2,1,0:T(8,128)(2,1)S(1)}, bf16[3,3,64,128]{3,2,1,0:T(8,128)(2,1)S(1)}, u32[]{:S(2)}, u32[]{:S(2)}) collective-permute-start(bf16[3,3,64,128]{3,2,1,0:T(8,128)(2,1)S(1)} %get-tuple-element.53), channel_id=1, source_target_pairs={{0,6},{2,4},{4,2},{6,0},{8,14},{10,12},{12,10},{14,8},{1,7},{3,5},... | collective-permute-start | bytes 442376 | tf_op jit(solution)/shard_map/ppermute | solution.py:37
  29.2 8.6 %collective-permute-start.10 = (bf16[3,3,64,128]{3,2,1,0:T(8,128)(2,1)S(1)}, bf16[3,3,64,128]{3,2,1,0:T(8,128)(2,1)S(1)}, u32[]{:S(2)}, u32[]{:S(2)}) collective-permute-start(bf16[3,3,64,128]{3,2,1,0:T(8,128)(2,1)S(1)} %get-tuple-element.54), channel_id=1, source_target_pairs={{4,10},{6,8},{8,6},{10,4},{5,11},{7,9},{9,7},{11,5},{20,26},{22,24... | collective-permute-start | bytes 442376 | tf_op jit(solution)/shard_map/ppermute | solution.py:37
  35.1 12.6 %collective-permute-start.11 = (bf16[64,768]{1,0:T(8,128)(2,1)S(1)}, bf16[64,768]{1,0:T(8,128)(2,1)S(1)}, u32[]{:S(2)}, u32[]{:S(2)}) collective-permute-start(bf16[64,768]{1,0:T(8,128)(2,1)S(1)} %get-tuple-element.55), channel_id=1, source_target_pairs={{0,4},{2,6},{4,0},{6,2},{8,12},{10,14},{12,8},{14,10},{1,5},{3,7},... | collective-permute-start | bytes 294920 | tf_op jit(solution)/shard_map/ppermute | solution.py:37
  37.8 9.8 %collective-permute-start.12 = (bf16[64,768]{1,0:T(8,128)(2,1)S(1)}, bf16[64,768]{1,0:T(8,128)(2,1)S(1)}, u32[]{:S(2)}, u32[]{:S(2)}) collective-permute-start(bf16[64,768]{1,0:T(8,128)(2,1)S(1)} %get-tuple-element.56), channel_id=1, source_target_pairs={{4,8},{6,10},{8,4},{10,6},{5,9},{7,11},{9,5},{11,7},{20,24},{22,26... | collective-permute-start | bytes 294920 | tf_op jit(solution)/shard_map/ppermute | solution.py:37
  38.5 9.1 %collective-permute-start.13 = (bf16[64,512]{1,0:T(8,128)(2,1)S(1)}, bf16[64,512]{1,0:T(8,128)(2,1)S(1)}, u32[]{:S(2)}, u32[]{:S(2)}) collective-permute-start(bf16[64,512]{1,0:T(8,128)(2,1)S(1)} %get-tuple-element.57), channel_id=1, source_target_pairs={{0,2},{2,0},{4,6},{6,4},{8,10},{10,8},{12,14},{14,12},{1,3},{3,1},... | collective-permute-start | bytes 196616 | tf_op jit(solution)/shard_map/ppermute | solution.py:37
  40.8 6.9 %collective-permute-start.14 = (bf16[64,384]{1,0:T(8,128)(2,1)S(1)}, bf16[64,384]{1,0:T(8,128)(2,1)S(1)}, u32[]{:S(2)}, u32[]{:S(2)}) collective-permute-start(bf16[64,384]{1,0:T(8,128)(2,1)S(1)} %get-tuple-element.58), channel_id=1, source_target_pairs={{0,6},{2,4},{4,2},{6,0},{8,14},{10,12},{12,10},{14,8},{1,7},{3,5},... | collective-permute-start | bytes 147464 | tf_op jit(solution)/shard_map/ppermute | solution.py:37
  44.5 3.1 %collective-permute-start.15 = (bf16[64,384]{1,0:T(8,128)(2,1)S(1)}, bf16[64,384]{1,0:T(8,128)(2,1)S(1)}, u32[]{:S(2)}, u32[]{:S(2)}) collective-permute-start(bf16[64,384]{1,0:T(8,128)(2,1)S(1)} %get-tuple-element.59), channel_id=1, source_target_pairs={{4,10},{6,8},{8,6},{10,4},{5,11},{7,9},{9,7},{11,5},{20,26},{22,24... | collective-permute-start | bytes 147464 | tf_op jit(solution)/shard_map/ppermute | solution.py:37

commit v10 on v9

--- a/solution.py
+++ b/solution.py
@@ -47,6 +47,10 @@
         base[qz, qx] = at
         at += (rows if qz is None else H) * (cols if qx is None else H)
     return pieces, base, at
+
+
+def joined(piece):
+    return piece[0] == 1 and piece[1] is not None
 
 
 def facing(q, extent, index):
@@ -102,12 +106,12 @@
     lax.fori_loop(0, count, run, 0, unroll=step)
 
 
-def widen(dst, at, src_ref, px, pitch):
+def widen(dst, at, src_ref, px, pitch, count):
     def body(i):
         rows = src_ref[pl.ds(pl.multiple_of(i * px, px), px), :]
         dst[pl.ds((at + i) * pitch, px), :] = rows.astype(F32)
 
-    loop(src_ref.shape[0] // px, body)
+    loop(count, body)
 
 
 def clear(dst, at, end, px, pitch):
@@ -213,7 +217,7 @@
     pitch = px + 1
     inv_root = 1.0 / math.sqrt(tgt_t.shape[2])
     for start, ref in zip(starts, tgt_refs):
-        widen(t32, start - n, ref, px, pitch)
+        widen(t32, start - n, ref, px, pitch, ref.shape[0] // px)
     clear(t32, ext - n, ext_pad - n, px, pitch)
 
     def per_pixel(p):
@@ -251,8 +255,14 @@
 
 
 def decoder_kernel(rows, cols, slots, pieces, *refs):
+    both = sum(joined(piece) for piece in pieces)
     mine_ref, other_ref, gh_ref, wt_ref, bt_ref, w_ref, table_ref = refs[:7]
-    gc_ref, out_refs, whole = refs[7], refs[8:-1], refs[-1]
+    slab_refs, rest = refs[7 : 7 + both], refs[7 + both :]
+    gc_ref, out_refs, whole = rest[0], rest[1:-1], rest[-1]
+    for piece, ref in zip(pieces, out_refs):
+        if joined(piece):
+            slab, slab_refs = slab_refs[0], slab_refs[1:]
+            ref[: slab.shape[0], :] = slab[...]
     px = mine_ref.shape[0]
     rep = lax.axis_index("rep")
     whole[pl.ds(pl.multiple_of(rep * px, px), px), :] = mine_ref[...]
@@ -298,13 +308,15 @@
 
 def send(rows, cols, slots, pieces, gc_ref, table_ref, out_refs):
     per = LANES // slots
+    px = gc_ref.shape[0]
     i = 0
     for piece, ref in zip(pieces, out_refs):
         groups, _ = picked(rows, cols, per, piece)
-        for at, g in enumerate(groups):
+        first = ref.shape[0] // px - len(groups)
+        for at, g in enumerate(groups, first):
             lane = g * LANES
             lane = lane if isinstance(lane, int) else pl.multiple_of(lane, LANES)
-            ref[:, at * LANES : (at + 1) * LANES] = lax.dot_general(
+            ref[at * px : (at + 1) * px, :] = lax.dot_general(
                 gc_ref[:, pl.ds(lane, LANES)],
                 table_ref[i * LANES : (i + 1) * LANES, :],
                 NT,
@@ -349,13 +361,13 @@
     loop(n, narrow)
 
 
-def halo_kernel(px, starts, *refs):
+def halo_kernel(px, starts, counts, *refs):
     k = len(starts)
     src_refs, out, s32 = refs[:k], refs[k], refs[k + 1]
     pitch = px + 1
-    for start, ref in zip(starts, src_refs):
-        widen(s32, start, ref, px, pitch)
-    last = starts[-1] + src_refs[-1].shape[0] // px
+    for start, count, ref in zip(starts, counts, src_refs):
+        widen(s32, start, ref, px, pitch, count)
+    last = starts[-1] + counts[-1]
     clear(s32, last, out.shape[1], px, pitch)
 
     def turn(p):
@@ -364,15 +376,15 @@
     loop(px, turn, 8)
 
 
-def total_kernel(px, n, slots, widths, pw_own, src_t, halo_t, *refs):
+def total_kernel(px, n, slots, firsts, widths, pw_own, src_t, halo_t, *refs):
     k = len(widths)
     msg_refs, tg_ref, pw, t32 = refs[:k], refs[k], refs[k + 1], refs[k + 2]
     pitch = px + 1
     inv_root = 1.0 / math.sqrt(src_t.shape[2])
     at = 0
-    for width, ref in zip(widths, msg_refs):
-        for g in range(ref.shape[1] // LANES):
-            block = ref[:, g * LANES : (g + 1) * LANES].astype(F32)
+    for first, width, ref in zip(firsts, widths, msg_refs):
+        for g in range(first, ref.shape[0] // px):
+            block = ref[g * px : (g + 1) * px, :].astype(F32)
             for j in range(width):
                 turned = block if j == 0 else pltpu.roll(block, LANES - j * slots, 1)
                 pw[at * pitch : at * pitch + px, :] = turned
@@ -474,14 +486,19 @@
         compiler_params=pltpu.CompilerParams(vmem_limit_bytes=4 * 2**20),
     )(args[1])
 
-    def halo_of(slabs):
+    def sent_to(arrays, there=lambda piece: True):
         got = []
-        for x, (qz, qx) in zip(slabs, pieces):
-            got.append(swap(x, qz, qx).reshape(-1, channels))
+        for x, (qz, qx) in zip(arrays, pieces):
+            if there((qz, qx)):
+                got.append(swap(x, qz, qx).reshape(-1, channels))
+            else:
+                got.append(None)
         return got
 
-    tgt_halo = halo_of(cut_t)
-    src_halo = halo_of(made[:k])
+    assert channels == LANES
+    slabs = made[:k]
+    tgt_halo = sent_to(cut_t)
+    src_halo = sent_to(slabs, lambda piece: not joined(piece))
     starts = [base[q] for q in pieces]
     counts = [h.shape[0] // px for h in tgt_halo]
     costs, tgt_t, hots = call(
@@ -504,6 +521,7 @@
         (rows if qz is None else H) * (cols // per if qx is None else 1) * LANES
         for qz, qx in pieces
     ]
+    firsts = [c if joined(piece) else 0 for c, piece in zip(counts, pieces)]
     (tables,) = call(
         partial(table_kernel, rows, cols, slots, pieces, starts, counts),
         [((sum(lanes), LANES), BF16)],
@@ -513,14 +531,17 @@
     )
     gc, *sent = call(
         partial(decoder_kernel, rows, cols, slots, pieces),
-        [((px, n * slots), BF16)] + [((px, w), BF16) for w in lanes],
+        [((px, n * slots), BF16)]
+        + [((f * px + w // LANES * px, LANES), BF16) for f, w in zip(firsts, lanes)],
         [((2 * px, n * slots), BF16)],
-        (costs, other, grad_hidden, w_t, b_t, w_half, tables),
+        (
+            *(costs, other, grad_hidden, w_t, b_t, w_half, tables),
+            *(x.reshape(-1, LANES) for x, piece in zip(slabs, pieces) if joined(piece)),
+        ),
         us=3,
     )
-    got = []
-    for x, (qz, qx) in zip(sent, pieces):
-        got.append(swap(x, qz, qx))
+    got = sent_to(sent)
+    src_halo = [m if h is None else h for h, m in zip(src_halo, got)]
     sg, pw_own = call(
         partial(own_kernel, px, n, slots),
         [((n * px, channels), BF16), ((ext_pad // LANES, n * pitch, LANES), F32)],
@@ -530,14 +551,14 @@
     )
     halo_pad = -(-(ext - n) // 16) * 16
     (halo_t,) = call(
-        partial(halo_kernel, px, [s - n for s in starts]),
+        partial(halo_kernel, px, [s - n for s in starts], counts),
         [((px, halo_pad, channels), BF16)],
         [((halo_pad * pitch, channels), F32)],
         tuple(src_halo),
         us=1,
     )
     (tg,) = call(
-        partial(total_kernel, px, n, slots, [per if qx is None else H for _, qx in pieces]),
+        partial(total_kernel, px, n, slots, firsts, [per if qx is None else H for _, qx in pieces]),
         [((n * px, channels), BF16)],
         [((halo_pad * pitch, LANES), F32), ((n * pitch, channels), F32)],
         (pw_own, src_t, halo_t, *got),

time: 50.6 us -> 52.3 us (1.034); the launches traced: 49.7 us -> 52.1 us
  starting transfers between devices: 29.7 us -> 33.8 us
  waiting for transfers between devices: 7.8 us -> 6.08 us
    ppermute x15 -> x14, starting transfers between devices: 29.6 us -> 33.7 us  [swap(): return lax.ppermute(x, ('strip', 'sub'), pairs)]
    ppermute x15 -> x14, waiting for transfers between devices: 7.79 us -> 6.07 us  [swap(): return lax.ppermute(x, ('strip', 'sub'), pairs)]
  transfers between devices with their start and end apart: 16 -> 15, of which waited for: 2 -> 2; matrix products, arithmetic and copies ran while one was open for 0% -> 0% of each run, Pallas kernels for 16% -> 15%
where the time goes in v10:
time: 52.3 us; the launch traced here: 52.1 us
  starting transfers between devices  33.8 us (65%)
  Pallas kernels  11.4 us (22%)
  waiting for transfers between devices  6.08 us (12%)
  between operations  0.79 us (2%)
    ppermute x14, starting transfers between devices, swap(): return lax.ppermute(x, ('strip', 'sub'), pairs)  33.7 us
    pallas_call x7, Pallas kernels, call(): pl.pallas_call(kernel, out_shape=[pltpu.VMEM(s, d) if near else jax.Shape...  9.9 us
    ppermute x14, waiting for transfers between devices, swap(): return lax.ppermute(x, ('strip', 'sub'), pairs)  6.07 us
    pallas_call x1, Pallas kernels, shards(): pl.pallas_call(partial(cut_kernel, pieces, rows, cols), name='cut', out_s...  1.51 us
  transfers between devices with their start and end apart: 15, of which 2 were waited for; matrix products, arithmetic and copies ran while one was open for 0% of the time, Pallas kernels for 15%

profile of v10, /device:TPU:0, one launch (start us, length us, event | category | flops | bytes accessed | tf_op | source)
XLA Modules:
  0.0 52.1 jit_solution(12404561339796582100)
XLA Ops:
  0.6 1.5 %cut.1 = (bf16[3,8,64,128]{3,2,1,0:T(8,128)(2,1)S(1)}, bf16[3,8,64,128]{3,2,1,0:T(8,128)(2,1)S(1)}, bf16[4,3,64,128]{3,2,1,0:T(8,128)(2,1)S(1)}, bf16[3,3,64,128...) custom-call(bf16[4,8,64,128]{3,2,1,0:T(8,128)(2,1)} %x_ref.1), custom_call_target="tpu_custom_call" | custom-call | tf_op jit(solution)/shard_map/cut/pallas_call | solution.py:479
  2.1 3.1 %collective-permute-start = (bf16[3,8,64,128]{3,2,1,0:T(8,128)(2,1)S(1)}, bf16[3,8,64,128]{3,2,1,0:T(8,128)(2,1)S(1)}, u32[]{:S(2)}, u32[]{:S(2)}) collective-permute-start(bf16[3,8,64,128]{3,2,1,0:T(8,128)(2,1)S(1)} %get-tuple-element.34), channel_id=1, source_target_pairs={{0,4},{2,6},{4,0},{6,2},{8,12},{10,14},{12,8},{14,10},{1,5},{3,7},... | collective-permute-start | bytes 1179656 | tf_op jit(solution)/shard_map/ppermute | solution.py:37
  5.3 0.7 %collective-permute-start.1 = (bf16[3,8,64,128]{3,2,1,0:T(8,128)(2,1)S(1)}, bf16[3,8,64,128]{3,2,1,0:T(8,128)(2,1)S(1)}, u32[]{:S(2)}, u32[]{:S(2)}) collective-permute-start(bf16[3,8,64,128]{3,2,1,0:T(8,128)(2,1)S(1)} %get-tuple-element.35), channel_id=1, source_target_pairs={{4,8},{6,10},{8,4},{10,6},{5,9},{7,11},{9,5},{11,7},{20,24},{22,26... | collective-permute-start | bytes 1179656 | tf_op jit(solution)/shard_map/ppermute | solution.py:37
  5.9 5.4 %collective-permute-start.3 = (bf16[3,3,64,128]{3,2,1,0:T(8,128)(2,1)S(1)}, bf16[3,3,64,128]{3,2,1,0:T(8,128)(2,1)S(1)}, u32[]{:S(2)}, u32[]{:S(2)}) collective-permute-start(bf16[3,3,64,128]{3,2,1,0:T(8,128)(2,1)S(1)} %get-tuple-element.37), channel_id=1, source_target_pairs={{0,6},{2,4},{4,2},{6,0},{8,14},{10,12},{12,10},{14,8},{1,7},{3,5},... | collective-permute-start | bytes 442376 | tf_op jit(solution)/shard_map/ppermute | solution.py:37
  11.4 0.7 %collective-permute-start.4 = (bf16[3,3,64,128]{3,2,1,0:T(8,128)(2,1)S(1)}, bf16[3,3,64,128]{3,2,1,0:T(8,128)(2,1)S(1)}, u32[]{:S(2)}, u32[]{:S(2)}) collective-permute-start(bf16[3,3,64,128]{3,2,1,0:T(8,128)(2,1)S(1)} %get-tuple-element.38), channel_id=1, source_target_pairs={{4,10},{6,8},{8,6},{10,4},{5,11},{7,9},{9,7},{11,5},{20,26},{22,24... | collective-permute-start | bytes 442376 | tf_op jit(solution)/shard_map/ppermute | solution.py:37
  12.0 0.5 %collective-permute-start.2 = (bf16[4,3,64,128]{3,2,1,0:T(8,128)(2,1)S(1)}, bf16[4,3,64,128]{3,2,1,0:T(8,128)(2,1)S(1)}, u32[]{:S(2)}, u32[]{:S(2)}) collective-permute-start(bf16[4,3,64,128]{3,2,1,0:T(8,128)(2,1)S(1)} %get-tuple-element.36), channel_id=1, source_target_pairs={{0,2},{2,0},{4,6},{6,4},{8,10},{10,8},{12,14},{14,12},{1,3},{3,1},... | collective-permute-start | bytes 589832 | tf_op jit(solution)/shard_map/ppermute | solution.py:37
  12.6 2.1 %shard_map.86 = (bf16[3,8,64,128]{3,2,1,0:T(8,128)(2,1)S(1)}, bf16[3,8,64,128]{3,2,1,0:T(8,128)(2,1)S(1)}, bf16[4,3,64,128]{3,2,1,0:T(8,128)(2,1)S(1)}, bf16[3,3...) custom-call(bf16[4,8,64,128]{3,2,1,0:T(8,128)(2,1)} %refs_0_.1, ...), custom_call_target="tpu_custom_call" | custom-call | bytes 6000000 | tf_op jit(solution)/shard_map/pallas_call | solution.py:415
  14.7 4.1 %collective-permute-done.3 = bf16[3,3,64,128]{3,2,1,0:T(8,128)(2,1)S(1)} collective-permute-done((bf16[3,3,64,128]{3,2,1,0:T(8,128)(2,1)S(1)}, bf16[3,3,64,128]{3,2,1,0:T(8,128)(2,1)S(1)}, u32[]{:S(2)}, u32[]{:S(2)}) %collective-permute-start.3) | collective-permute-done | bytes 147488 | tf_op jit(solution)/shard_map/ppermute | solution.py:37
  18.8 2.3 %collective-permute-start.6 = (bf16[3,8,64,128]{3,2,1,0:T(8,128)(2,1)S(1)}, bf16[3,8,64,128]{3,2,1,0:T(8,128)(2,1)S(1)}, u32[]{:S(2)}, u32[]{:S(2)}) collective-permute-start(bf16[3,8,64,128]{3,2,1,0:T(8,128)(2,1)S(1)} %get-tuple-element.51), channel_id=1, source_target_pairs={{0,4},{2,6},{4,0},{6,2},{8,12},{10,14},{12,8},{14,10},{1,5},{3,7},... | collective-permute-start | bytes 1179656 | tf_op jit(solution)/shard_map/ppermute | solution.py:37
  21.1 0.7 %collective-permute-start.7 = (bf16[3,8,64,128]{3,2,1,0:T(8,128)(2,1)S(1)}, bf16[3,8,64,128]{3,2,1,0:T(8,128)(2,1)S(1)}, u32[]{:S(2)}, u32[]{:S(2)}) collective-permute-start(bf16[3,8,64,128]{3,2,1,0:T(8,128)(2,1)S(1)} %get-tuple-element.52), channel_id=1, source_target_pairs={{4,8},{6,10},{8,4},{10,6},{5,9},{7,11},{9,5},{11,7},{20,24},{22,26... | collective-permute-start | bytes 1179656 | tf_op jit(solution)/shard_map/ppermute | solution.py:37
  21.8 0.0 collective-permute-done.2
  21.8 0.0 collective-permute-done.1
  21.8 1.8 %shard_map.87 = (bf16[64,1024]{1,0:T(8,128)(2,1)S(1)}, bf16[64,128,128]{2,1,0:T(8,128)(2,1)S(1)}, bf16[4096,128]{1,0:T(8,128)(2,1)S(1)}) custom-call(bf16[64,32,128]{2,1,0:T(8,128)(2,1)S(1)} %get-tuple-element.31.refs_0_, bf16[64,32,128]{2,1,0:T(8,128)(2,1)S(1)} %get-tuple-element.32.refs_1_.src_t, s32[8,128]{1,0:T(8,128)S(1)} %get-tuple-element.33.refs_2_.e_ref, ...), custom_call_target="tpu_custom_call" | custom-call | bytes 9000000 | tf_op jit(solution)/shard_map/pallas_call | solution.py:415
  23.7 0.1 collective-permute-start.5
  23.7 0.5 %collective-permute-start.8 = (bf16[4,3,64,128]{3,2,1,0:T(8,128)(2,1)S(1)}, bf16[4,3,64,128]{3,2,1,0:T(8,128)(2,1)S(1)}, u32[]{:S(2)}, u32[]{:S(2)}) collective-permute-start(bf16[4,3,64,128]{3,2,1,0:T(8,128)(2,1)S(1)} %get-tuple-element.53), channel_id=1, source_target_pairs={{0,2},{2,0},{4,6},{6,4},{8,10},{10,8},{12,14},{14,12},{1,3},{3,1},... | collective-permute-start | bytes 589832 | tf_op jit(solution)/shard_map/ppermute | solution.py:37
  24.3 6.2 %collective-permute-start.9 = (bf16[3,3,64,128]{3,2,1,0:T(8,128)(2,1)S(1)}, bf16[3,3,64,128]{3,2,1,0:T(8,128)(2,1)S(1)}, u32[]{:S(2)}, u32[]{:S(2)}) collective-permute-start(bf16[3,3,64,128]{3,2,1,0:T(8,128)(2,1)S(1)} %get-tuple-element.54), channel_id=1, source_target_pairs={{0,6},{2,4},{4,2},{6,0},{8,14},{10,12},{12,10},{14,8},{1,7},{3,5},... | collective-permute-start | bytes 442376 | tf_op jit(solution)/shard_map/ppermute | solution.py:37
  30.5 0.1 shard_map.88.refs_6_
  30.6 0.0 collective-permute-done.5.refs_1_
  30.6 1.4 %shard_map.89 = (bf16[64,1024]{1,0:T(8,128)(2,1)S(1)}, bf16[384,128]{1,0:T(8,128)(2,1)S(1)}, bf16[384,128]{1,0:T(8,128)(2,1)S(1)}, bf16[256,128]{1,0:T(8,128)(2,...) custom-call(bf16[64,1024]{1,0:T(8,128)(2,1)S(1)} %get-tuple-element.39.refs_0_, ...), custom_call_target="tpu_custom_call" | custom-call | bytes 9000000 | tf_op jit(solution)/shard_map/pallas_call | solution.py:415
  32.1 0.7 %collective-permute-start.10 = (bf16[768,128]{1,0:T(8,128)(2,1)S(1)}, bf16[768,128]{1,0:T(8,128)(2,1)S(1)}, u32[]{:S(2)}, u32[]{:S(2)}) collective-permute-start(bf16[768,128]{1,0:T(8,128)(2,1)S(1)} %get-tuple-element.55), channel_id=1, source_target_pairs={{4,10},{6,8},{8,6},{10,4},{5,11},{7,9},{9,7},{11,5},{20,26},{22,24... | collective-permute-start | bytes 589832 | tf_op jit(solution)/shard_map/ppermute | solution.py:37
  32.7 1.9 %collective-permute-done.9 = bf16[3,3,64,128]{3,2,1,0:T(8,128)(2,1)S(1)} collective-permute-done((bf16[3,3,64,128]{3,2,1,0:T(8,128)(2,1)S(1)}, bf16[3,3,64,128]{3,2,1,0:T(8,128)(2,1)S(1)}, u32[]{:S(2)}, u32[]{:S(2)}) %collective-permute-start.9) | collective-permute-done | bytes 147488 | tf_op jit(solution)/shard_map/ppermute | solution.py:37
  34.6 1.7 %collective-permute-start.11 = (bf16[384,128]{1,0:T(8,128)(2,1)S(1)}, bf16[384,128]{1,0:T(8,128)(2,1)S(1)}, u32[]{:S(2)}, u32[]{:S(2)}) collective-permute-start(bf16[384,128]{1,0:T(8,128)(2,1)S(1)} %get-tuple-element.56), channel_id=1, source_target_pairs={{0,4},{2,6},{4,0},{6,2},{8,12},{10,14},{12,8},{14,10},{1,5},{3,7},... | collective-permute-start | bytes 294920 | tf_op jit(solution)/shard_map/ppermute | solution.py:37
  36.4 0.0 collective-permute-done.8
  36.4 0.7 %collective-permute-start.12 = (bf16[384,128]{1,0:T(8,128)(2,1)S(1)}, bf16[384,128]{1,0:T(8,128)(2,1)S(1)}, u32[]{:S(2)}, u32[]{:S(2)}) collective-permute-start(bf16[384,128]{1,0:T(8,128)(2,1)S(1)} %get-tuple-element.57), channel_id=1, source_target_pairs={{4,8},{6,10},{8,4},{10,6},{5,9},{7,11},{9,5},{11,7},{20,24},{22,26... | collective-permute-start | bytes 294920 | tf_op jit(solution)/shard_map/ppermute | solution.py:37
  37.0 0.0 collective-permute-done.6
  37.1 1.6 %collective-permute-start.13 = (bf16[256,128]{1,0:T(8,128)(2,1)S(1)}, bf16[256,128]{1,0:T(8,128)(2,1)S(1)}, u32[]{:S(2)}, u32[]{:S(2)}) collective-permute-start(bf16[256,128]{1,0:T(8,128)(2,1)S(1)} %get-tuple-element.58), channel_id=1, source_target_pairs={{0,2},{2,0},{4,6},{6,4},{8,10},{10,8},{12,14},{14,12},{1,3},{3,1},... | collective-permute-start | bytes 196616 | tf_op jit(solution)/shard_map/ppermute | solution.py:37
  38.7 8.9 %collective-permute-start.14 = (bf16[192,128]{1,0:T(8,128)(2,1)S(1)}, bf16[192,128]{1,0:T(8,128)(2,1)S(1)}, u32[]{:S(2)}, u32[]{:S(2)}) collective-permute-start(bf16[192,128]{1,0:T(8,128)(2,1)S(1)} %get-tuple-element.59), channel_id=1, source_target_pairs={{0,6},{2,4},{4,2},{6,0},{8,14},{10,12},{12,10},{14,8},{1,7},{3,5},... | collective-permute-start | bytes 147464 | tf_op jit(solution)/shard_map/ppermute | solution.py:37
  47.5 2.0 %shard_map.90 = (bf16[2048,128]{1,0:T(8,128)(2,1)}, f32[1,2080,128]{2,1,0:T(8,128)S(1)}) custom-call(bf16[64,1024]{1,0:T(8,128)(2,1)S(1)} %get-tuple-element.46.gc_ref, bf16[4096,128]{1,0:T(8,128)(2,1)S(1)} %get-tuple-element.47.hot_ref, bf16[64,128,128]{2,1,0:T(8,128)(2,1)S(1)} %get-tuple-element.48.tgt_t), custom_call_target="tpu_custom_call" | custom-call | bytes 12000000 | tf_op jit(solution)/shard_map/pallas_call | solution.py:415
  49.6 0.4 shard_map.91.halo_t
  50.0 0.0 collective-permute-done.14.refs_3_
  50.0 0.0 collective-permute-done.13.refs_2_
  50.0 2.0 %shard_map.92 = bf16[2048,128]{1,0:T(8,128)(2,1)} custom-call(f32[1,2080,128]{2,1,0:T(8,128)S(1)} %get-tuple-element.50.pw_own, bf16[64,32,128]{2,1,0:T(8,128)(2,1)S(1)} %get-tuple-element.32.refs_1_.src_t, bf16[64,80,128]{2,1,0:T(8,128)(2,1)S(1)} %shard_map.91.halo_t, bf16[384,128]{1,0:T(8,128)(2,1)S(1)} %collective-permute-done.11.refs_0_, ...), custom_call_target="tpu_custom_call" | custom-call | bytes 9000000 | tf_op jit(solution)/shard_map/pallas_call | solution.py:415
  (6 shorter events, 0.0 us)
Async XLA Ops:
  2.1 19.7 %collective-permute-start = (bf16[3,8,64,128]{3,2,1,0:T(8,128)(2,1)S(1)}, bf16[3,8,64,128]{3,2,1,0:T(8,128)(2,1)S(1)}, u32[]{:S(2)}, u32[]{:S(2)}) collective-permute-start(bf16[3,8,64,128]{3,2,1,0:T(8,128)(2,1)S(1)} %get-tuple-element.34), channel_id=1, source_target_pairs={{0,4},{2,6},{4,0},{6,2},{8,12},{10,14},{12,8},{14,10},{1,5},{3,7},... | collective-permute-start | bytes 1179656 | tf_op jit(solution)/shard_map/ppermute | solution.py:37
  5.3 16.6 %collective-permute-start.1 = (bf16[3,8,64,128]{3,2,1,0:T(8,128)(2,1)S(1)}, bf16[3,8,64,128]{3,2,1,0:T(8,128)(2,1)S(1)}, u32[]{:S(2)}, u32[]{:S(2)}) collective-permute-start(bf16[3,8,64,128]{3,2,1,0:T(8,128)(2,1)S(1)} %get-tuple-element.35), channel_id=1, source_target_pairs={{4,8},{6,10},{8,4},{10,6},{5,9},{7,11},{9,5},{11,7},{20,24},{22,26... | collective-permute-start | bytes 1179656 | tf_op jit(solution)/shard_map/ppermute | solution.py:37
  5.9 12.9 %collective-permute-start.3 = (bf16[3,3,64,128]{3,2,1,0:T(8,128)(2,1)S(1)}, bf16[3,3,64,128]{3,2,1,0:T(8,128)(2,1)S(1)}, u32[]{:S(2)}, u32[]{:S(2)}) collective-permute-start(bf16[3,3,64,128]{3,2,1,0:T(8,128)(2,1)S(1)} %get-tuple-element.37), channel_id=1, source_target_pairs={{0,6},{2,4},{4,2},{6,0},{8,14},{10,12},{12,10},{14,8},{1,7},{3,5},... | collective-permute-start | bytes 442376 | tf_op jit(solution)/shard_map/ppermute | solution.py:37
  11.4 9.7 %collective-permute-start.4 = (bf16[3,3,64,128]{3,2,1,0:T(8,128)(2,1)S(1)}, bf16[3,3,64,128]{3,2,1,0:T(8,128)(2,1)S(1)}, u32[]{:S(2)}, u32[]{:S(2)}) collective-permute-start(bf16[3,3,64,128]{3,2,1,0:T(8,128)(2,1)S(1)} %get-tuple-element.38), channel_id=1, source_target_pairs={{4,10},{6,8},{8,6},{10,4},{5,11},{7,9},{9,7},{11,5},{20,26},{22,24... | collective-permute-start | bytes 442376 | tf_op jit(solution)/shard_map/ppermute | solution.py:37
  12.0 9.8 %collective-permute-start.2 = (bf16[4,3,64,128]{3,2,1,0:T(8,128)(2,1)S(1)}, bf16[4,3,64,128]{3,2,1,0:T(8,128)(2,1)S(1)}, u32[]{:S(2)}, u32[]{:S(2)}) collective-permute-start(bf16[4,3,64,128]{3,2,1,0:T(8,128)(2,1)S(1)} %get-tuple-element.36), channel_id=1, source_target_pairs={{0,2},{2,0},{4,6},{6,4},{8,10},{10,8},{12,14},{14,12},{1,3},{3,1},... | collective-permute-start | bytes 589832 | tf_op jit(solution)/shard_map/ppermute | solution.py:37
  18.8 18.2 %collective-permute-start.6 = (bf16[3,8,64,128]{3,2,1,0:T(8,128)(2,1)S(1)}, bf16[3,8,64,128]{3,2,1,0:T(8,128)(2,1)S(1)}, u32[]{:S(2)}, u32[]{:S(2)}) collective-permute-start(bf16[3,8,64,128]{3,2,1,0:T(8,128)(2,1)S(1)} %get-tuple-element.51), channel_id=1, source_target_pairs={{0,4},{2,6},{4,0},{6,2},{8,12},{10,14},{12,8},{14,10},{1,5},{3,7},... | collective-permute-start | bytes 1179656 | tf_op jit(solution)/shard_map/ppermute | solution.py:37
  21.1 17.6 %collective-permute-start.7 = (bf16[3,8,64,128]{3,2,1,0:T(8,128)(2,1)S(1)}, bf16[3,8,64,128]{3,2,1,0:T(8,128)(2,1)S(1)}, u32[]{:S(2)}, u32[]{:S(2)}) collective-permute-start(bf16[3,8,64,128]{3,2,1,0:T(8,128)(2,1)S(1)} %get-tuple-element.52), channel_id=1, source_target_pairs={{4,8},{6,10},{8,4},{10,6},{5,9},{7,11},{9,5},{11,7},{20,24},{22,26... | collective-permute-start | bytes 1179656 | tf_op jit(solution)/shard_map/ppermute | solution.py:37
  23.7 7.0 %collective-permute-start.5 = (bf16[64,1024]{1,0:T(8,128)(2,1)S(1)}, bf16[64,1024]{1,0:T(8,128)(2,1)S(1)}, u32[]{:S(2)}, u32[]{:S(2)}) collective-permute-start(bf16[64,1024]{1,0:T(8,128)(2,1)S(1)} %get-tuple-element.39.refs_0_), channel_id=1, source_target_pairs={{0,1},{1,0},{2,3},{3,2},{4,5},{5,4},{6,7},{7,6},{8,9},{9,8},{10,11... | collective-permute-start | bytes 393224 | tf_op jit(solution)/shard_map/ppermute | solution.py:519
  23.7 12.6 %collective-permute-start.8 = (bf16[4,3,64,128]{3,2,1,0:T(8,128)(2,1)S(1)}, bf16[4,3,64,128]{3,2,1,0:T(8,128)(2,1)S(1)}, u32[]{:S(2)}, u32[]{:S(2)}) collective-permute-start(bf16[4,3,64,128]{3,2,1,0:T(8,128)(2,1)S(1)} %get-tuple-element.53), channel_id=1, source_target_pairs={{0,2},{2,0},{4,6},{6,4},{8,10},{10,8},{12,14},{14,12},{1,3},{3,1},... | collective-permute-start | bytes 589832 | tf_op jit(solution)/shard_map/ppermute | solution.py:37
  24.3 10.4 %collective-permute-start.9 = (bf16[3,3,64,128]{3,2,1,0:T(8,128)(2,1)S(1)}, bf16[3,3,64,128]{3,2,1,0:T(8,128)(2,1)S(1)}, u32[]{:S(2)}, u32[]{:S(2)}) collective-permute-start(bf16[3,3,64,128]{3,2,1,0:T(8,128)(2,1)S(1)} %get-tuple-element.54), channel_id=1, source_target_pairs={{0,6},{2,4},{4,2},{6,0},{8,14},{10,12},{12,10},{14,8},{1,7},{3,5},... | collective-permute-start | bytes 442376 | tf_op jit(solution)/shard_map/ppermute | solution.py:37
  32.1 17.5 %collective-permute-start.10 = (bf16[768,128]{1,0:T(8,128)(2,1)S(1)}, bf16[768,128]{1,0:T(8,128)(2,1)S(1)}, u32[]{:S(2)}, u32[]{:S(2)}) collective-permute-start(bf16[768,128]{1,0:T(8,128)(2,1)S(1)} %get-tuple-element.55), channel_id=1, source_target_pairs={{4,10},{6,8},{8,6},{10,4},{5,11},{7,9},{9,7},{11,5},{20,26},{22,24... | collective-permute-start | bytes 589832 | tf_op jit(solution)/shard_map/ppermute | solution.py:37
  34.6 15.4 %collective-permute-start.11 = (bf16[384,128]{1,0:T(8,128)(2,1)S(1)}, bf16[384,128]{1,0:T(8,128)(2,1)S(1)}, u32[]{:S(2)}, u32[]{:S(2)}) collective-permute-start(bf16[384,128]{1,0:T(8,128)(2,1)S(1)} %get-tuple-element.56), channel_id=1, source_target_pairs={{0,4},{2,6},{4,0},{6,2},{8,12},{10,14},{12,8},{14,10},{1,5},{3,7},... | collective-permute-start | bytes 294920 | tf_op jit(solution)/shard_map/ppermute | solution.py:37
  36.4 13.7 %collective-permute-start.12 = (bf16[384,128]{1,0:T(8,128)(2,1)S(1)}, bf16[384,128]{1,0:T(8,128)(2,1)S(1)}, u32[]{:S(2)}, u32[]{:S(2)}) collective-permute-start(bf16[384,128]{1,0:T(8,128)(2,1)S(1)} %get-tuple-element.57), channel_id=1, source_target_pairs={{4,8},{6,10},{8,4},{10,6},{5,9},{7,11},{9,5},{11,7},{20,24},{22,26... | collective-permute-start | bytes 294920 | tf_op jit(solution)/shard_map/ppermute | solution.py:37
  37.1 13.0 %collective-permute-start.13 = (bf16[256,128]{1,0:T(8,128)(2,1)S(1)}, bf16[256,128]{1,0:T(8,128)(2,1)S(1)}, u32[]{:S(2)}, u32[]{:S(2)}) collective-permute-start(bf16[256,128]{1,0:T(8,128)(2,1)S(1)} %get-tuple-element.58), channel_id=1, source_target_pairs={{0,2},{2,0},{4,6},{6,4},{8,10},{10,8},{12,14},{14,12},{1,3},{3,1},... | collective-permute-start | bytes 196616 | tf_op jit(solution)/shard_map/ppermute | solution.py:37
  38.7 11.3 %collective-permute-start.14 = (bf16[192,128]{1,0:T(8,128)(2,1)S(1)}, bf16[192,128]{1,0:T(8,128)(2,1)S(1)}, u32[]{:S(2)}, u32[]{:S(2)}) collective-permute-start(bf16[192,128]{1,0:T(8,128)(2,1)S(1)} %get-tuple-element.59), channel_id=1, source_target_pairs={{0,6},{2,4},{4,2},{6,0},{8,14},{10,12},{12,10},{14,8},{1,7},{3,5},... | collective-permute-start | bytes 147464 | tf_op jit(solution)/shard_map/ppermute | solution.py:37

commit v11 on v9

--- a/solution.py
+++ b/solution.py
@@ -128,8 +128,12 @@
     return hot(jnp.where(lane == j, e_ref[group : group + 1, :], -1), tile)
 
 
-def cut_kernel(pieces, rows, cols, x_ref, *refs):
-    copies = cuts(pieces, rows, cols, x_ref, refs[:-1], refs[-1], 0)
+def cut_kernel(pieces, rows, cols, *refs):
+    k = len(pieces)
+    x_ref, small, slabs, near, sems = refs[0], refs[1:6], refs[6 : 6 + k], refs[6 + k : -1], refs[-1]
+    copies = cuts(pieces, rows, cols, x_ref, slabs, sems, 0)
+    for i, (f, v) in enumerate(zip(small, near)):
+        copies.append(pltpu.make_async_copy(f, v, sems.at[k + i]))
     for copy in copies:
         copy.start()
     for copy in copies:
@@ -151,19 +155,18 @@
 
 def head_kernel(base, pieces, rows, cols, slots, *refs):
     k = len(pieces)
-    far, rest = refs[:7], refs[7:]
+    far, small, rest = refs[:2], refs[2:7], refs[7:]
     src_slabs, outs, rest = rest[:k], rest[k : k + 8], rest[k + 8 :]
     src_t, tgt_t, gh_ref, wt_ref, wh_ref, bt_ref, e_ref, m_ref = outs
     (s32, t32, og, table), near, sems = rest[:4], rest[4:-1], rest[-1]
-    src_ref, tgt_ref, og_ref, ids_ref, w_in_ref, b_ref, w_out_ref = near
+    src_ref, tgt_ref = near
+    og_ref, ids_ref, w_in_ref, b_ref, w_out_ref = small
     fetches = [pltpu.make_async_copy(f, v, sems.at[i]) for i, (f, v) in enumerate(zip(far, near))]
-    slabs = cuts(pieces, rows, cols, far[0], src_slabs, sems, 7)
-    for copy in fetches[2:] + fetches[:2] + slabs:
+    slabs = cuts(pieces, rows, cols, far[0], src_slabs, sems, 2)
+    for copy in fetches + slabs:
         copy.start()
     px, n, _ = src_t.shape
     pitch = px + 1
-    for fetch in fetches[2:]:
-        fetch.wait()
     e_at, m_at = places(ids_ref[...], base, rows, cols)
     slotted(e_at, e_ref, table, slots)
     slotted(m_at, m_ref, table, slots)
@@ -185,7 +188,7 @@
         gh_ref[:, g * LANES : (g + 1) * LANES] = lax.dot_general(
             w_out_ref[...], block, NT, preferred_element_type=F32
         )
-    for fetch in fetches[:2]:
+    for fetch in fetches:
         fetch.wait()
     for dst, src in ((s32, src_ref), (t32, tgt_ref)):
 
@@ -452,27 +455,28 @@
         w_out,
     )
     args = tuple(pltpu.with_memory_space_constraint(a, pltpu.HBM) for a in args)
+    k = len(pieces)
+    small = args[2:]
+    cut_t = pl.pallas_call(
+        partial(cut_kernel, pieces, rows, cols),
+        name="cut",
+        out_shape=[jax.ShapeDtypeStruct(s, BF16) for s in shapes]
+        + [jax.ShapeDtypeStruct(x.shape, x.dtype) for x in small],
+        in_specs=[HB] * (1 + len(small)),
+        out_specs=[VM] * (k + len(small)),
+        scratch_shapes=[pltpu.SemaphoreType.DMA((k + len(small),))],
+        compiler_params=pltpu.CompilerParams(vmem_limit_bytes=6 * 2**20),
+    )(args[1], *small)
     made = call(
         partial(head_kernel, base, pieces, rows, cols, slots),
         outs,
         [((n * pitch, channels), F32)] * 2
         + [((n * (slots + 1), out_grad.shape[3]), F32), ((n, LANES), jnp.int32)],
-        args,
-        far=len(args),
-        sems=len(args) + len(pieces),
-        limit=24,
-    )
-    k = len(pieces)
+        (*args[:2], *cut_t[k:]),
+        far=2,
+        sems=2 + k,
+    )
     src_t, own_t, grad_hidden, w_t, w_half, b_t, e_ids, m_ids = made[k:]
-    cut_t = pl.pallas_call(
-        partial(cut_kernel, pieces, rows, cols),
-        name="cut",
-        out_shape=[jax.ShapeDtypeStruct(s, BF16) for s in shapes],
-        in_specs=[HB],
-        out_specs=[VM] * k,
-        scratch_shapes=[pltpu.SemaphoreType.DMA((k,))],
-        compiler_params=pltpu.CompilerParams(vmem_limit_bytes=4 * 2**20),
-    )(args[1])
 
     def halo_of(slabs):
         got = []
@@ -480,7 +484,7 @@
             got.append(swap(x, qz, qx).reshape(-1, channels))
         return got
 
-    tgt_halo = halo_of(cut_t)
+    tgt_halo = halo_of(cut_t[:k])
     src_halo = halo_of(made[:k])
     starts = [base[q] for q in pieces]
     counts = [h.shape[0] // px for h in tgt_halo]

time: 50.6 us -> 49.8 us (0.984)
  waiting for transfers between devices: 7.8 us -> 5.93 us
  starting transfers between devices: 29.7 us -> 30.9 us
    ppermute x15, waiting for transfers between devices: 7.79 us -> 5.93 us  [swap(): return lax.ppermute(x, ('strip', 'sub'), pairs)]
    ppermute x15, starting transfers between devices: 29.6 us -> 30.8 us  [swap(): return lax.ppermute(x, ('strip', 'sub'), pairs)]
where the time goes in v11:
time: 49.8 us; the launch traced here: 49.2 us
  starting transfers between devices  30.9 us (62%)
  Pallas kernels  11.6 us (23%)
  waiting for transfers between devices  5.93 us (12%)
  between operations  0.78 us (2%)
    ppermute x15, starting transfers between devices, swap(): return lax.ppermute(x, ('strip', 'sub'), pairs)  30.8 us
    pallas_call x7, Pallas kernels, call(): pl.pallas_call(kernel, out_shape=[pltpu.VMEM(s, d) if near else jax.Shape...  9.86 us
    ppermute x15, waiting for transfers between devices, swap(): return lax.ppermute(x, ('strip', 'sub'), pairs)  5.93 us
    pallas_call x1, Pallas kernels, shards(): pl.pallas_call(partial(cut_kernel, pieces, rows, cols), name='cut', out_s...  1.73 us
  transfers between devices with their start and end apart: 16, of which 2 were waited for; matrix products, arithmetic and copies ran while one was open for 0% of the time, Pallas kernels for 16%

profile of v11, /device:TPU:0, one launch (start us, length us, event | category | flops | bytes accessed | tf_op | source)
XLA Modules:
  0.0 49.2 jit_solution(13063163477587336091)
XLA Ops:
  0.6 1.7 %cut.1 = (bf16[3,8,64,128]{3,2,1,0:T(8,128)(2,1)S(1)}, bf16[3,8,64,128]{3,2,1,0:T(8,128)(2,1)S(1)}, bf16[4,3,64,128]{3,2,1,0:T(8,128)(2,1)S(1)}, bf16[3,3,64,128...) custom-call(bf16[4,8,64,128]{3,2,1,0:T(8,128)(2,1)} %refs_1_.1, ...), custom_call_target="tpu_custom_call" | custom-call | tf_op jit(solution)/shard_map/cut/pallas_call | solution.py:460
  2.4 3.1 %collective-permute-start = (bf16[3,8,64,128]{3,2,1,0:T(8,128)(2,1)S(1)}, bf16[3,8,64,128]{3,2,1,0:T(8,128)(2,1)S(1)}, u32[]{:S(2)}, u32[]{:S(2)}) collective-permute-start(bf16[3,8,64,128]{3,2,1,0:T(8,128)(2,1)S(1)} %get-tuple-element.44), channel_id=1, source_target_pairs={{0,4},{2,6},{4,0},{6,2},{8,12},{10,14},{12,8},{14,10},{1,5},{3,7},... | collective-permute-start | bytes 1179656 | tf_op jit(solution)/shard_map/ppermute | solution.py:37
  5.5 0.7 %collective-permute-start.1 = (bf16[3,8,64,128]{3,2,1,0:T(8,128)(2,1)S(1)}, bf16[3,8,64,128]{3,2,1,0:T(8,128)(2,1)S(1)}, u32[]{:S(2)}, u32[]{:S(2)}) collective-permute-start(bf16[3,8,64,128]{3,2,1,0:T(8,128)(2,1)S(1)} %get-tuple-element.45), channel_id=1, source_target_pairs={{4,8},{6,10},{8,4},{10,6},{5,9},{7,11},{9,5},{11,7},{20,24},{22,26... | collective-permute-start | bytes 1179656 | tf_op jit(solution)/shard_map/ppermute | solution.py:37
  6.2 5.3 %collective-permute-start.3 = (bf16[3,3,64,128]{3,2,1,0:T(8,128)(2,1)S(1)}, bf16[3,3,64,128]{3,2,1,0:T(8,128)(2,1)S(1)}, u32[]{:S(2)}, u32[]{:S(2)}) collective-permute-start(bf16[3,3,64,128]{3,2,1,0:T(8,128)(2,1)S(1)} %get-tuple-element.47), channel_id=1, source_target_pairs={{0,6},{2,4},{4,2},{6,0},{8,14},{10,12},{12,10},{14,8},{1,7},{3,5},... | collective-permute-start | bytes 442376 | tf_op jit(solution)/shard_map/ppermute | solution.py:37
  11.4 0.7 %collective-permute-start.4 = (bf16[3,3,64,128]{3,2,1,0:T(8,128)(2,1)S(1)}, bf16[3,3,64,128]{3,2,1,0:T(8,128)(2,1)S(1)}, u32[]{:S(2)}, u32[]{:S(2)}) collective-permute-start(bf16[3,3,64,128]{3,2,1,0:T(8,128)(2,1)S(1)} %get-tuple-element.48), channel_id=1, source_target_pairs={{4,10},{6,8},{8,6},{10,4},{5,11},{7,9},{9,7},{11,5},{20,26},{22,24... | collective-permute-start | bytes 442376 | tf_op jit(solution)/shard_map/ppermute | solution.py:37
  12.1 0.7 %collective-permute-start.2 = (bf16[4,3,64,128]{3,2,1,0:T(8,128)(2,1)S(1)}, bf16[4,3,64,128]{3,2,1,0:T(8,128)(2,1)S(1)}, u32[]{:S(2)}, u32[]{:S(2)}) collective-permute-start(bf16[4,3,64,128]{3,2,1,0:T(8,128)(2,1)S(1)} %get-tuple-element.46), channel_id=1, source_target_pairs={{0,2},{2,0},{4,6},{6,4},{8,10},{10,8},{12,14},{14,12},{1,3},{3,1},... | collective-permute-start | bytes 589832 | tf_op jit(solution)/shard_map/ppermute | solution.py:37
  12.8 2.1 %shard_map.86 = (bf16[3,8,64,128]{3,2,1,0:T(8,128)(2,1)S(1)}, bf16[3,8,64,128]{3,2,1,0:T(8,128)(2,1)S(1)}, bf16[4,3,64,128]{3,2,1,0:T(8,128)(2,1)S(1)}, bf16[3,3...) custom-call(bf16[4,8,64,128]{3,2,1,0:T(8,128)(2,1)} %refs_0_.3, ...), custom_call_target="tpu_custom_call" | custom-call | bytes 6000000 | tf_op jit(solution)/shard_map/pallas_call | solution.py:406
  14.9 4.0 %collective-permute-done.3 = bf16[3,3,64,128]{3,2,1,0:T(8,128)(2,1)S(1)} collective-permute-done((bf16[3,3,64,128]{3,2,1,0:T(8,128)(2,1)S(1)}, bf16[3,3,64,128]{3,2,1,0:T(8,128)(2,1)S(1)}, u32[]{:S(2)}, u32[]{:S(2)}) %collective-permute-start.3) | collective-permute-done | bytes 147488 | tf_op jit(solution)/shard_map/ppermute | solution.py:37
  18.9 2.3 %collective-permute-start.6 = (bf16[3,8,64,128]{3,2,1,0:T(8,128)(2,1)S(1)}, bf16[3,8,64,128]{3,2,1,0:T(8,128)(2,1)S(1)}, u32[]{:S(2)}, u32[]{:S(2)}) collective-permute-start(bf16[3,8,64,128]{3,2,1,0:T(8,128)(2,1)S(1)} %get-tuple-element.60), channel_id=1, source_target_pairs={{0,4},{2,6},{4,0},{6,2},{8,12},{10,14},{12,8},{14,10},{1,5},{3,7},... | collective-permute-start | bytes 1179656 | tf_op jit(solution)/shard_map/ppermute | solution.py:37
  21.2 0.0 collective-permute-done.4
  21.2 0.7 %collective-permute-start.7 = (bf16[3,8,64,128]{3,2,1,0:T(8,128)(2,1)S(1)}, bf16[3,8,64,128]{3,2,1,0:T(8,128)(2,1)S(1)}, u32[]{:S(2)}, u32[]{:S(2)}) collective-permute-start(bf16[3,8,64,128]{3,2,1,0:T(8,128)(2,1)S(1)} %get-tuple-element.61), channel_id=1, source_target_pairs={{4,8},{6,10},{8,4},{10,6},{5,9},{7,11},{9,5},{11,7},{20,24},{22,26... | collective-permute-start | bytes 1179656 | tf_op jit(solution)/shard_map/ppermute | solution.py:37
  21.9 0.0 collective-permute-done.2
  21.9 0.0 collective-permute-done.1
  21.9 1.8 %shard_map.87 = (bf16[64,1024]{1,0:T(8,128)(2,1)S(1)}, bf16[64,128,128]{2,1,0:T(8,128)(2,1)S(1)}, bf16[4096,128]{1,0:T(8,128)(2,1)S(1)}) custom-call(bf16[64,32,128]{2,1,0:T(8,128)(2,1)S(1)} %get-tuple-element.41.refs_0_, bf16[64,32,128]{2,1,0:T(8,128)(2,1)S(1)} %get-tuple-element.42.refs_1_.src_t, s32[8,128]{1,0:T(8,128)S(1)} %get-tuple-element.43.refs_2_.e_ref, ...), custom_call_target="tpu_custom_call" | custom-call | bytes 9000000 | tf_op jit(solution)/shard_map/pallas_call | solution.py:406
  23.7 0.1 collective-permute-start.5
  23.8 0.7 %collective-permute-start.8 = (bf16[4,3,64,128]{3,2,1,0:T(8,128)(2,1)S(1)}, bf16[4,3,64,128]{3,2,1,0:T(8,128)(2,1)S(1)}, u32[]{:S(2)}, u32[]{:S(2)}) collective-permute-start(bf16[4,3,64,128]{3,2,1,0:T(8,128)(2,1)S(1)} %get-tuple-element.62), channel_id=1, source_target_pairs={{0,2},{2,0},{4,6},{6,4},{8,10},{10,8},{12,14},{14,12},{1,3},{3,1},... | collective-permute-start | bytes 589832 | tf_op jit(solution)/shard_map/ppermute | solution.py:37
  24.5 6.0 %collective-permute-start.9 = (bf16[3,3,64,128]{3,2,1,0:T(8,128)(2,1)S(1)}, bf16[3,3,64,128]{3,2,1,0:T(8,128)(2,1)S(1)}, u32[]{:S(2)}, u32[]{:S(2)}) collective-permute-start(bf16[3,3,64,128]{3,2,1,0:T(8,128)(2,1)S(1)} %get-tuple-element.63), channel_id=1, source_target_pairs={{0,6},{2,4},{4,2},{6,0},{8,14},{10,12},{12,10},{14,8},{1,7},{3,5},... | collective-permute-start | bytes 442376 | tf_op jit(solution)/shard_map/ppermute | solution.py:37
  30.5 0.0 collective-permute-done.5.refs_1_
  30.5 0.7 %collective-permute-start.10 = (bf16[3,3,64,128]{3,2,1,0:T(8,128)(2,1)S(1)}, bf16[3,3,64,128]{3,2,1,0:T(8,128)(2,1)S(1)}, u32[]{:S(2)}, u32[]{:S(2)}) collective-permute-start(bf16[3,3,64,128]{3,2,1,0:T(8,128)(2,1)S(1)} %get-tuple-element.64), channel_id=1, source_target_pairs={{4,10},{6,8},{8,6},{10,4},{5,11},{7,9},{9,7},{11,5},{20,26},{22,24... | collective-permute-start | bytes 442376 | tf_op jit(solution)/shard_map/ppermute | solution.py:37
  31.2 0.2 shard_map.88.refs_6_
  31.4 1.4 %shard_map.89 = (bf16[64,1024]{1,0:T(8,128)(2,1)S(1)}, bf16[64,768]{1,0:T(8,128)(2,1)S(1)}, bf16[64,768]{1,0:T(8,128)(2,1)S(1)}, bf16[64,512]{1,0:T(8,128)(2,1)S...) custom-call(bf16[64,1024]{1,0:T(8,128)(2,1)S(1)} %get-tuple-element.49.refs_0_, ...), custom_call_target="tpu_custom_call" | custom-call | bytes 9000000 | tf_op jit(solution)/shard_map/pallas_call | solution.py:406
  32.8 1.9 %collective-permute-done.9 = bf16[3,3,64,128]{3,2,1,0:T(8,128)(2,1)S(1)} collective-permute-done((bf16[3,3,64,128]{3,2,1,0:T(8,128)(2,1)S(1)}, bf16[3,3,64,128]{3,2,1,0:T(8,128)(2,1)S(1)}, u32[]{:S(2)}, u32[]{:S(2)}) %collective-permute-start.9) | collective-permute-done | bytes 147488 | tf_op jit(solution)/shard_map/ppermute | solution.py:37
  34.7 2.6 %collective-permute-start.11 = (bf16[64,768]{1,0:T(8,128)(2,1)S(1)}, bf16[64,768]{1,0:T(8,128)(2,1)S(1)}, u32[]{:S(2)}, u32[]{:S(2)}) collective-permute-start(bf16[64,768]{1,0:T(8,128)(2,1)S(1)} %get-tuple-element.65), channel_id=1, source_target_pairs={{0,4},{2,6},{4,0},{6,2},{8,12},{10,14},{12,8},{14,10},{1,5},{3,7},... | collective-permute-start | bytes 294920 | tf_op jit(solution)/shard_map/ppermute | solution.py:37
  37.3 0.7 %collective-permute-start.12 = (bf16[64,768]{1,0:T(8,128)(2,1)S(1)}, bf16[64,768]{1,0:T(8,128)(2,1)S(1)}, u32[]{:S(2)}, u32[]{:S(2)}) collective-permute-start(bf16[64,768]{1,0:T(8,128)(2,1)S(1)} %get-tuple-element.66), channel_id=1, source_target_pairs={{4,8},{6,10},{8,4},{10,6},{5,9},{7,11},{9,5},{11,7},{20,24},{22,26... | collective-permute-start | bytes 294920 | tf_op jit(solution)/shard_map/ppermute | solution.py:37
  38.0 1.9 %collective-permute-start.13 = (bf16[64,512]{1,0:T(8,128)(2,1)S(1)}, bf16[64,512]{1,0:T(8,128)(2,1)S(1)}, u32[]{:S(2)}, u32[]{:S(2)}) collective-permute-start(bf16[64,512]{1,0:T(8,128)(2,1)S(1)} %get-tuple-element.67), channel_id=1, source_target_pairs={{0,2},{2,0},{4,6},{6,4},{8,10},{10,8},{12,14},{14,12},{1,3},{3,1},... | collective-permute-start | bytes 196616 | tf_op jit(solution)/shard_map/ppermute | solution.py:37
  39.9 4.2 %collective-permute-start.14 = (bf16[64,384]{1,0:T(8,128)(2,1)S(1)}, bf16[64,384]{1,0:T(8,128)(2,1)S(1)}, u32[]{:S(2)}, u32[]{:S(2)}) collective-permute-start(bf16[64,384]{1,0:T(8,128)(2,1)S(1)} %get-tuple-element.68), channel_id=1, source_target_pairs={{0,6},{2,4},{4,2},{6,0},{8,14},{10,12},{12,10},{14,8},{1,7},{3,5},... | collective-permute-start | bytes 147464 | tf_op jit(solution)/shard_map/ppermute | solution.py:37
  44.1 0.7 %collective-permute-start.15 = (bf16[64,384]{1,0:T(8,128)(2,1)S(1)}, bf16[64,384]{1,0:T(8,128)(2,1)S(1)}, u32[]{:S(2)}, u32[]{:S(2)}) collective-permute-start(bf16[64,384]{1,0:T(8,128)(2,1)S(1)} %get-tuple-element.69), channel_id=1, source_target_pairs={{4,10},{6,8},{8,6},{10,4},{5,11},{7,9},{9,7},{11,5},{20,26},{22,24... | collective-permute-start | bytes 147464 | tf_op jit(solution)/shard_map/ppermute | solution.py:37
  44.8 0.4 shard_map.91.halo_t
  45.2 2.0 %shard_map.90 = (bf16[2048,128]{1,0:T(8,128)(2,1)}, f32[1,2080,128]{2,1,0:T(8,128)S(1)}) custom-call(bf16[64,1024]{1,0:T(8,128)(2,1)S(1)} %get-tuple-element.55.gc_ref, bf16[4096,128]{1,0:T(8,128)(2,1)S(1)} %get-tuple-element.56.hot_ref, bf16[64,128,128]{2,1,0:T(8,128)(2,1)S(1)} %get-tuple-element.57.tgt_t), custom_call_target="tpu_custom_call" | custom-call | bytes 12000000 | tf_op jit(solution)/shard_map/pallas_call | solution.py:406
  47.2 0.0 collective-permute-done.11.refs_0_
  47.2 0.0 collective-permute-done.12.refs_1_
  47.2 2.0 %shard_map.92 = bf16[2048,128]{1,0:T(8,128)(2,1)} custom-call(f32[1,2080,128]{2,1,0:T(8,128)S(1)} %get-tuple-element.59.pw_own, bf16[64,32,128]{2,1,0:T(8,128)(2,1)S(1)} %get-tuple-element.42.refs_1_.src_t, bf16[64,80,128]{2,1,0:T(8,128)(2,1)S(1)} %shard_map.91.halo_t, bf16[64,768]{1,0:T(8,128)(2,1)S(1)} %collective-permute-done.11.refs_0_, ...), custom_call_target="tpu_custom_call" | custom-call | bytes 9000000 | tf_op jit(solution)/shard_map/pallas_call | solution.py:406
  (8 shorter events, 0.0 us)
Async XLA Ops:
  2.4 19.5 %collective-permute-start = (bf16[3,8,64,128]{3,2,1,0:T(8,128)(2,1)S(1)}, bf16[3,8,64,128]{3,2,1,0:T(8,128)(2,1)S(1)}, u32[]{:S(2)}, u32[]{:S(2)}) collective-permute-start(bf16[3,8,64,128]{3,2,1,0:T(8,128)(2,1)S(1)} %get-tuple-element.44), channel_id=1, source_target_pairs={{0,4},{2,6},{4,0},{6,2},{8,12},{10,14},{12,8},{14,10},{1,5},{3,7},... | collective-permute-start | bytes 1179656 | tf_op jit(solution)/shard_map/ppermute | solution.py:37
  5.5 16.4 %collective-permute-start.1 = (bf16[3,8,64,128]{3,2,1,0:T(8,128)(2,1)S(1)}, bf16[3,8,64,128]{3,2,1,0:T(8,128)(2,1)S(1)}, u32[]{:S(2)}, u32[]{:S(2)}) collective-permute-start(bf16[3,8,64,128]{3,2,1,0:T(8,128)(2,1)S(1)} %get-tuple-element.45), channel_id=1, source_target_pairs={{4,8},{6,10},{8,4},{10,6},{5,9},{7,11},{9,5},{11,7},{20,24},{22,26... | collective-permute-start | bytes 1179656 | tf_op jit(solution)/shard_map/ppermute | solution.py:37
  6.2 12.7 %collective-permute-start.3 = (bf16[3,3,64,128]{3,2,1,0:T(8,128)(2,1)S(1)}, bf16[3,3,64,128]{3,2,1,0:T(8,128)(2,1)S(1)}, u32[]{:S(2)}, u32[]{:S(2)}) collective-permute-start(bf16[3,3,64,128]{3,2,1,0:T(8,128)(2,1)S(1)} %get-tuple-element.47), channel_id=1, source_target_pairs={{0,6},{2,4},{4,2},{6,0},{8,14},{10,12},{12,10},{14,8},{1,7},{3,5},... | collective-permute-start | bytes 442376 | tf_op jit(solution)/shard_map/ppermute | solution.py:37
  11.4 9.7 %collective-permute-start.4 = (bf16[3,3,64,128]{3,2,1,0:T(8,128)(2,1)S(1)}, bf16[3,3,64,128]{3,2,1,0:T(8,128)(2,1)S(1)}, u32[]{:S(2)}, u32[]{:S(2)}) collective-permute-start(bf16[3,3,64,128]{3,2,1,0:T(8,128)(2,1)S(1)} %get-tuple-element.48), channel_id=1, source_target_pairs={{4,10},{6,8},{8,6},{10,4},{5,11},{7,9},{9,7},{11,5},{20,26},{22,24... | collective-permute-start | bytes 442376 | tf_op jit(solution)/shard_map/ppermute | solution.py:37
  12.1 9.8 %collective-permute-start.2 = (bf16[4,3,64,128]{3,2,1,0:T(8,128)(2,1)S(1)}, bf16[4,3,64,128]{3,2,1,0:T(8,128)(2,1)S(1)}, u32[]{:S(2)}, u32[]{:S(2)}) collective-permute-start(bf16[4,3,64,128]{3,2,1,0:T(8,128)(2,1)S(1)} %get-tuple-element.46), channel_id=1, source_target_pairs={{0,2},{2,0},{4,6},{6,4},{8,10},{10,8},{12,14},{14,12},{1,3},{3,1},... | collective-permute-start | bytes 589832 | tf_op jit(solution)/shard_map/ppermute | solution.py:37
  18.9 21.0 %collective-permute-start.6 = (bf16[3,8,64,128]{3,2,1,0:T(8,128)(2,1)S(1)}, bf16[3,8,64,128]{3,2,1,0:T(8,128)(2,1)S(1)}, u32[]{:S(2)}, u32[]{:S(2)}) collective-permute-start(bf16[3,8,64,128]{3,2,1,0:T(8,128)(2,1)S(1)} %get-tuple-element.60), channel_id=1, source_target_pairs={{0,4},{2,6},{4,0},{6,2},{8,12},{10,14},{12,8},{14,10},{1,5},{3,7},... | collective-permute-start | bytes 1179656 | tf_op jit(solution)/shard_map/ppermute | solution.py:37
  21.2 22.9 %collective-permute-start.7 = (bf16[3,8,64,128]{3,2,1,0:T(8,128)(2,1)S(1)}, bf16[3,8,64,128]{3,2,1,0:T(8,128)(2,1)S(1)}, u32[]{:S(2)}, u32[]{:S(2)}) collective-permute-start(bf16[3,8,64,128]{3,2,1,0:T(8,128)(2,1)S(1)} %get-tuple-element.61), channel_id=1, source_target_pairs={{4,8},{6,10},{8,4},{10,6},{5,9},{7,11},{9,5},{11,7},{20,24},{22,26... | collective-permute-start | bytes 1179656 | tf_op jit(solution)/shard_map/ppermute | solution.py:37
  23.7 6.8 %collective-permute-start.5 = (bf16[64,1024]{1,0:T(8,128)(2,1)S(1)}, bf16[64,1024]{1,0:T(8,128)(2,1)S(1)}, u32[]{:S(2)}, u32[]{:S(2)}) collective-permute-start(bf16[64,1024]{1,0:T(8,128)(2,1)S(1)} %get-tuple-element.49.refs_0_), channel_id=1, source_target_pairs={{0,1},{1,0},{2,3},{3,2},{4,5},{5,4},{6,7},{7,6},{8,9},{9,8},{10,11... | collective-permute-start | bytes 393224 | tf_op jit(solution)/shard_map/ppermute | solution.py:506
  23.8 14.2 %collective-permute-start.8 = (bf16[4,3,64,128]{3,2,1,0:T(8,128)(2,1)S(1)}, bf16[4,3,64,128]{3,2,1,0:T(8,128)(2,1)S(1)}, u32[]{:S(2)}, u32[]{:S(2)}) collective-permute-start(bf16[4,3,64,128]{3,2,1,0:T(8,128)(2,1)S(1)} %get-tuple-element.62), channel_id=1, source_target_pairs={{0,2},{2,0},{4,6},{6,4},{8,10},{10,8},{12,14},{14,12},{1,3},{3,1},... | collective-permute-start | bytes 589832 | tf_op jit(solution)/shard_map/ppermute | solution.py:37
  24.5 10.2 %collective-permute-start.9 = (bf16[3,3,64,128]{3,2,1,0:T(8,128)(2,1)S(1)}, bf16[3,3,64,128]{3,2,1,0:T(8,128)(2,1)S(1)}, u32[]{:S(2)}, u32[]{:S(2)}) collective-permute-start(bf16[3,3,64,128]{3,2,1,0:T(8,128)(2,1)S(1)} %get-tuple-element.63), channel_id=1, source_target_pairs={{0,6},{2,4},{4,2},{6,0},{8,14},{10,12},{12,10},{14,8},{1,7},{3,5},... | collective-permute-start | bytes 442376 | tf_op jit(solution)/shard_map/ppermute | solution.py:37
  30.5 6.8 %collective-permute-start.10 = (bf16[3,3,64,128]{3,2,1,0:T(8,128)(2,1)S(1)}, bf16[3,3,64,128]{3,2,1,0:T(8,128)(2,1)S(1)}, u32[]{:S(2)}, u32[]{:S(2)}) collective-permute-start(bf16[3,3,64,128]{3,2,1,0:T(8,128)(2,1)S(1)} %get-tuple-element.64), channel_id=1, source_target_pairs={{4,10},{6,8},{8,6},{10,4},{5,11},{7,9},{9,7},{11,5},{20,26},{22,24... | collective-permute-start | bytes 442376 | tf_op jit(solution)/shard_map/ppermute | solution.py:37
  34.7 12.5 %collective-permute-start.11 = (bf16[64,768]{1,0:T(8,128)(2,1)S(1)}, bf16[64,768]{1,0:T(8,128)(2,1)S(1)}, u32[]{:S(2)}, u32[]{:S(2)}) collective-permute-start(bf16[64,768]{1,0:T(8,128)(2,1)S(1)} %get-tuple-element.65), channel_id=1, source_target_pairs={{0,4},{2,6},{4,0},{6,2},{8,12},{10,14},{12,8},{14,10},{1,5},{3,7},... | collective-permute-start | bytes 294920 | tf_op jit(solution)/shard_map/ppermute | solution.py:37
  37.3 9.9 %collective-permute-start.12 = (bf16[64,768]{1,0:T(8,128)(2,1)S(1)}, bf16[64,768]{1,0:T(8,128)(2,1)S(1)}, u32[]{:S(2)}, u32[]{:S(2)}) collective-permute-start(bf16[64,768]{1,0:T(8,128)(2,1)S(1)} %get-tuple-element.66), channel_id=1, source_target_pairs={{4,8},{6,10},{8,4},{10,6},{5,9},{7,11},{9,5},{11,7},{20,24},{22,26... | collective-permute-start | bytes 294920 | tf_op jit(solution)/shard_map/ppermute | solution.py:37
  38.0 9.2 %collective-permute-start.13 = (bf16[64,512]{1,0:T(8,128)(2,1)S(1)}, bf16[64,512]{1,0:T(8,128)(2,1)S(1)}, u32[]{:S(2)}, u32[]{:S(2)}) collective-permute-start(bf16[64,512]{1,0:T(8,128)(2,1)S(1)} %get-tuple-element.67), channel_id=1, source_target_pairs={{0,2},{2,0},{4,6},{6,4},{8,10},{10,8},{12,14},{14,12},{1,3},{3,1},... | collective-permute-start | bytes 196616 | tf_op jit(solution)/shard_map/ppermute | solution.py:37
  39.9 7.3 %collective-permute-start.14 = (bf16[64,384]{1,0:T(8,128)(2,1)S(1)}, bf16[64,384]{1,0:T(8,128)(2,1)S(1)}, u32[]{:S(2)}, u32[]{:S(2)}) collective-permute-start(bf16[64,384]{1,0:T(8,128)(2,1)S(1)} %get-tuple-element.68), channel_id=1, source_target_pairs={{0,6},{2,4},{4,2},{6,0},{8,14},{10,12},{12,10},{14,8},{1,7},{3,5},... | collective-permute-start | bytes 147464 | tf_op jit(solution)/shard_map/ppermute | solution.py:37
  44.1 3.1 %collective-permute-start.15 = (bf16[64,384]{1,0:T(8,128)(2,1)S(1)}, bf16[64,384]{1,0:T(8,128)(2,1)S(1)}, u32[]{:S(2)}, u32[]{:S(2)}) collective-permute-start(bf16[64,384]{1,0:T(8,128)(2,1)S(1)} %get-tuple-element.69), channel_id=1, source_target_pairs={{4,10},{6,8},{8,6},{10,4},{5,11},{7,9},{9,7},{11,5},{20,26},{22,24... | collective-permute-start | bytes 147464 | tf_op jit(solution)/shard_map/ppermute | solution.py:37

commit v12 on v9

--- a/solution.py
+++ b/solution.py
@@ -157,8 +157,8 @@
     (s32, t32, og, table), near, sems = rest[:4], rest[4:-1], rest[-1]
     src_ref, tgt_ref, og_ref, ids_ref, w_in_ref, b_ref, w_out_ref = near
     fetches = [pltpu.make_async_copy(f, v, sems.at[i]) for i, (f, v) in enumerate(zip(far, near))]
-    slabs = cuts(pieces, rows, cols, far[0], src_slabs, sems, 7)
-    for copy in fetches[2:] + fetches[:2] + slabs:
+    slabs = cuts(pieces, rows, cols, src_ref, src_slabs, sems, 7)
+    for copy in fetches[2:] + fetches[:2]:
         copy.start()
     px, n, _ = src_t.shape
     pitch = px + 1
@@ -187,6 +187,8 @@
         )
     for fetch in fetches[:2]:
         fetch.wait()
+    for copy in slabs:
+        copy.start()
     for dst, src in ((s32, src_ref), (t32, tgt_ref)):
 
         def body(i, dst=dst, src=src):

time: 50.6 us -> 50.6 us (level)
  Pallas kernels: 11.4 us -> 12.1 us
  waiting for transfers between devices: 7.8 us -> 7.11 us
    ppermute x15, waiting for transfers between devices: 7.79 us -> 7.11 us  [swap(): return lax.ppermute(x, ('strip', 'sub'), pairs)]
    pallas_call x7, Pallas kernels: 9.88 us -> 10.6 us  [call(): pl.pallas_call(kernel, out_shape=[pltpu.VMEM(s, d) if near else jax.Shape...]
  transfers between devices with their start and end apart: 16 -> 16, of which waited for: 2 -> 2; matrix products, arithmetic and copies ran while one was open for 0% -> 0% of each run, Pallas kernels for 16% -> 17%
where the time goes in v12:
time: 50.6 us; the launch traced here: 49.7 us
  starting transfers between devices  29.7 us (59%)
  Pallas kernels  12.1 us (24%)
  waiting for transfers between devices  7.11 us (14%)
  between operations  0.77 us (2%)
    ppermute x15, starting transfers between devices, swap(): return lax.ppermute(x, ('strip', 'sub'), pairs)  29.6 us
    pallas_call x7, Pallas kernels, call(): pl.pallas_call(kernel, out_shape=[pltpu.VMEM(s, d) if near else jax.Shape...  10.6 us
    ppermute x15, waiting for transfers between devices, swap(): return lax.ppermute(x, ('strip', 'sub'), pairs)  7.11 us
    pallas_call x1, Pallas kernels, shards(): pl.pallas_call(partial(cut_kernel, pieces, rows, cols), name='cut', out_s...  1.51 us
  transfers between devices with their start and end apart: 16, of which 2 were waited for; matrix products, arithmetic and copies ran while one was open for 0% of the time, Pallas kernels for 17%

profile of v12, /device:TPU:0, one launch (start us, length us, event | category | flops | bytes accessed | tf_op | source)
XLA Modules:
  0.0 49.7 jit_solution(9353875909782227377)
XLA Ops:
  0.6 1.5 %cut.1 = (bf16[3,8,64,128]{3,2,1,0:T(8,128)(2,1)S(1)}, bf16[3,8,64,128]{3,2,1,0:T(8,128)(2,1)S(1)}, bf16[4,3,64,128]{3,2,1,0:T(8,128)(2,1)S(1)}, bf16[3,3,64,128...) custom-call(bf16[4,8,64,128]{3,2,1,0:T(8,128)(2,1)} %x_ref.1), custom_call_target="tpu_custom_call" | custom-call | tf_op jit(solution)/shard_map/cut/pallas_call | solution.py:469
  2.1 3.1 %collective-permute-start = (bf16[3,8,64,128]{3,2,1,0:T(8,128)(2,1)S(1)}, bf16[3,8,64,128]{3,2,1,0:T(8,128)(2,1)S(1)}, u32[]{:S(2)}, u32[]{:S(2)}) collective-permute-start(bf16[3,8,64,128]{3,2,1,0:T(8,128)(2,1)S(1)} %get-tuple-element.34), channel_id=1, source_target_pairs={{0,4},{2,6},{4,0},{6,2},{8,12},{10,14},{12,8},{14,10},{1,5},{3,7},... | collective-permute-start | bytes 1179656 | tf_op jit(solution)/shard_map/ppermute | solution.py:37
  5.3 0.7 %collective-permute-start.1 = (bf16[3,8,64,128]{3,2,1,0:T(8,128)(2,1)S(1)}, bf16[3,8,64,128]{3,2,1,0:T(8,128)(2,1)S(1)}, u32[]{:S(2)}, u32[]{:S(2)}) collective-permute-start(bf16[3,8,64,128]{3,2,1,0:T(8,128)(2,1)S(1)} %get-tuple-element.35), channel_id=1, source_target_pairs={{4,8},{6,10},{8,4},{10,6},{5,9},{7,11},{9,5},{11,7},{20,24},{22,26... | collective-permute-start | bytes 1179656 | tf_op jit(solution)/shard_map/ppermute | solution.py:37
  5.9 5.4 %collective-permute-start.3 = (bf16[3,3,64,128]{3,2,1,0:T(8,128)(2,1)S(1)}, bf16[3,3,64,128]{3,2,1,0:T(8,128)(2,1)S(1)}, u32[]{:S(2)}, u32[]{:S(2)}) collective-permute-start(bf16[3,3,64,128]{3,2,1,0:T(8,128)(2,1)S(1)} %get-tuple-element.37), channel_id=1, source_target_pairs={{0,6},{2,4},{4,2},{6,0},{8,14},{10,12},{12,10},{14,8},{1,7},{3,5},... | collective-permute-start | bytes 442376 | tf_op jit(solution)/shard_map/ppermute | solution.py:37
  11.4 0.7 %collective-permute-start.4 = (bf16[3,3,64,128]{3,2,1,0:T(8,128)(2,1)S(1)}, bf16[3,3,64,128]{3,2,1,0:T(8,128)(2,1)S(1)}, u32[]{:S(2)}, u32[]{:S(2)}) collective-permute-start(bf16[3,3,64,128]{3,2,1,0:T(8,128)(2,1)S(1)} %get-tuple-element.38), channel_id=1, source_target_pairs={{4,10},{6,8},{8,6},{10,4},{5,11},{7,9},{9,7},{11,5},{20,26},{22,24... | collective-permute-start | bytes 442376 | tf_op jit(solution)/shard_map/ppermute | solution.py:37
  12.0 0.5 %collective-permute-start.2 = (bf16[4,3,64,128]{3,2,1,0:T(8,128)(2,1)S(1)}, bf16[4,3,64,128]{3,2,1,0:T(8,128)(2,1)S(1)}, u32[]{:S(2)}, u32[]{:S(2)}) collective-permute-start(bf16[4,3,64,128]{3,2,1,0:T(8,128)(2,1)S(1)} %get-tuple-element.36), channel_id=1, source_target_pairs={{0,2},{2,0},{4,6},{6,4},{8,10},{10,8},{12,14},{14,12},{1,3},{3,1},... | collective-permute-start | bytes 589832 | tf_op jit(solution)/shard_map/ppermute | solution.py:37
  12.6 2.7 %shard_map.86 = (bf16[3,8,64,128]{3,2,1,0:T(8,128)(2,1)S(1)}, bf16[3,8,64,128]{3,2,1,0:T(8,128)(2,1)S(1)}, bf16[4,3,64,128]{3,2,1,0:T(8,128)(2,1)S(1)}, bf16[3,3...) custom-call(bf16[4,8,64,128]{3,2,1,0:T(8,128)(2,1)} %refs_0_.1, ...), custom_call_target="tpu_custom_call" | custom-call | bytes 6000000 | tf_op jit(solution)/shard_map/pallas_call | solution.py:405
  15.3 3.5 %collective-permute-done.3 = bf16[3,3,64,128]{3,2,1,0:T(8,128)(2,1)S(1)} collective-permute-done((bf16[3,3,64,128]{3,2,1,0:T(8,128)(2,1)S(1)}, bf16[3,3,64,128]{3,2,1,0:T(8,128)(2,1)S(1)}, u32[]{:S(2)}, u32[]{:S(2)}) %collective-permute-start.3) | collective-permute-done | bytes 147488 | tf_op jit(solution)/shard_map/ppermute | solution.py:37
  18.8 0.7 %collective-permute-start.7 = (bf16[3,8,64,128]{3,2,1,0:T(8,128)(2,1)S(1)}, bf16[3,8,64,128]{3,2,1,0:T(8,128)(2,1)S(1)}, u32[]{:S(2)}, u32[]{:S(2)}) collective-permute-start(bf16[3,8,64,128]{3,2,1,0:T(8,128)(2,1)S(1)} %get-tuple-element.51), channel_id=1, source_target_pairs={{4,8},{6,10},{8,4},{10,6},{5,9},{7,11},{9,5},{11,7},{20,24},{22,26... | collective-permute-start | bytes 1179656 | tf_op jit(solution)/shard_map/ppermute | solution.py:37
  19.5 0.0 collective-permute-done.4
  19.5 5.3 %collective-permute-start.6 = (bf16[3,8,64,128]{3,2,1,0:T(8,128)(2,1)S(1)}, bf16[3,8,64,128]{3,2,1,0:T(8,128)(2,1)S(1)}, u32[]{:S(2)}, u32[]{:S(2)}) collective-permute-start(bf16[3,8,64,128]{3,2,1,0:T(8,128)(2,1)S(1)} %get-tuple-element.50), channel_id=1, source_target_pairs={{0,4},{2,6},{4,0},{6,2},{8,12},{10,14},{12,8},{14,10},{1,5},{3,7},... | collective-permute-start | bytes 1179656 | tf_op jit(solution)/shard_map/ppermute | solution.py:37
  24.8 0.0 collective-permute-done.1
  24.8 1.8 %shard_map.87 = (bf16[64,1024]{1,0:T(8,128)(2,1)S(1)}, bf16[64,128,128]{2,1,0:T(8,128)(2,1)S(1)}, bf16[4096,128]{1,0:T(8,128)(2,1)S(1)}) custom-call(bf16[64,32,128]{2,1,0:T(8,128)(2,1)S(1)} %get-tuple-element.31.refs_0_, bf16[64,32,128]{2,1,0:T(8,128)(2,1)S(1)} %get-tuple-element.32.refs_1_.src_t, s32[8,128]{1,0:T(8,128)S(1)} %get-tuple-element.33.refs_2_.e_ref, ...), custom_call_target="tpu_custom_call" | custom-call | bytes 9000000 | tf_op jit(solution)/shard_map/pallas_call | solution.py:405
  26.6 0.1 collective-permute-start.5
  26.7 0.5 %collective-permute-start.8 = (bf16[4,3,64,128]{3,2,1,0:T(8,128)(2,1)S(1)}, bf16[4,3,64,128]{3,2,1,0:T(8,128)(2,1)S(1)}, u32[]{:S(2)}, u32[]{:S(2)}) collective-permute-start(bf16[4,3,64,128]{3,2,1,0:T(8,128)(2,1)S(1)} %get-tuple-element.52), channel_id=1, source_target_pairs={{0,2},{2,0},{4,6},{6,4},{8,10},{10,8},{12,14},{14,12},{1,3},{3,1},... | collective-permute-start | bytes 589832 | tf_op jit(solution)/shard_map/ppermute | solution.py:37
  27.2 2.0 %collective-permute-start.9 = (bf16[3,3,64,128]{3,2,1,0:T(8,128)(2,1)S(1)}, bf16[3,3,64,128]{3,2,1,0:T(8,128)(2,1)S(1)}, u32[]{:S(2)}, u32[]{:S(2)}) collective-permute-start(bf16[3,3,64,128]{3,2,1,0:T(8,128)(2,1)S(1)} %get-tuple-element.53), channel_id=1, source_target_pairs={{0,6},{2,4},{4,2},{6,0},{8,14},{10,12},{12,10},{14,8},{1,7},{3,5},... | collective-permute-start | bytes 442376 | tf_op jit(solution)/shard_map/ppermute | solution.py:37
  29.2 0.0 collective-permute-done.5.refs_1_
  29.2 0.7 %collective-permute-start.10 = (bf16[3,3,64,128]{3,2,1,0:T(8,128)(2,1)S(1)}, bf16[3,3,64,128]{3,2,1,0:T(8,128)(2,1)S(1)}, u32[]{:S(2)}, u32[]{:S(2)}) collective-permute-start(bf16[3,3,64,128]{3,2,1,0:T(8,128)(2,1)S(1)} %get-tuple-element.54), channel_id=1, source_target_pairs={{4,10},{6,8},{8,6},{10,4},{5,11},{7,9},{9,7},{11,5},{20,26},{22,24... | collective-permute-start | bytes 442376 | tf_op jit(solution)/shard_map/ppermute | solution.py:37
  29.9 0.2 shard_map.88.refs_6_
  30.0 1.4 %shard_map.89 = (bf16[64,1024]{1,0:T(8,128)(2,1)S(1)}, bf16[64,768]{1,0:T(8,128)(2,1)S(1)}, bf16[64,768]{1,0:T(8,128)(2,1)S(1)}, bf16[64,512]{1,0:T(8,128)(2,1)S...) custom-call(bf16[64,1024]{1,0:T(8,128)(2,1)S(1)} %get-tuple-element.39.refs_0_, ...), custom_call_target="tpu_custom_call" | custom-call | bytes 9000000 | tf_op jit(solution)/shard_map/pallas_call | solution.py:405
  31.5 3.6 %collective-permute-done.9 = bf16[3,3,64,128]{3,2,1,0:T(8,128)(2,1)S(1)} collective-permute-done((bf16[3,3,64,128]{3,2,1,0:T(8,128)(2,1)S(1)}, bf16[3,3,64,128]{3,2,1,0:T(8,128)(2,1)S(1)}, u32[]{:S(2)}, u32[]{:S(2)}) %collective-permute-start.9) | collective-permute-done | bytes 147488 | tf_op jit(solution)/shard_map/ppermute | solution.py:37
  35.1 2.8 %collective-permute-start.11 = (bf16[64,768]{1,0:T(8,128)(2,1)S(1)}, bf16[64,768]{1,0:T(8,128)(2,1)S(1)}, u32[]{:S(2)}, u32[]{:S(2)}) collective-permute-start(bf16[64,768]{1,0:T(8,128)(2,1)S(1)} %get-tuple-element.55), channel_id=1, source_target_pairs={{0,4},{2,6},{4,0},{6,2},{8,12},{10,14},{12,8},{14,10},{1,5},{3,7},... | collective-permute-start | bytes 294920 | tf_op jit(solution)/shard_map/ppermute | solution.py:37
  37.8 0.0 collective-permute-done.10
  37.8 0.7 %collective-permute-start.12 = (bf16[64,768]{1,0:T(8,128)(2,1)S(1)}, bf16[64,768]{1,0:T(8,128)(2,1)S(1)}, u32[]{:S(2)}, u32[]{:S(2)}) collective-permute-start(bf16[64,768]{1,0:T(8,128)(2,1)S(1)} %get-tuple-element.56), channel_id=1, source_target_pairs={{4,8},{6,10},{8,4},{10,6},{5,9},{7,11},{9,5},{11,7},{20,24},{22,26... | collective-permute-start | bytes 294920 | tf_op jit(solution)/shard_map/ppermute | solution.py:37
  38.5 0.0 collective-permute-done.8
  38.5 2.3 %collective-permute-start.13 = (bf16[64,512]{1,0:T(8,128)(2,1)S(1)}, bf16[64,512]{1,0:T(8,128)(2,1)S(1)}, u32[]{:S(2)}, u32[]{:S(2)}) collective-permute-start(bf16[64,512]{1,0:T(8,128)(2,1)S(1)} %get-tuple-element.57), channel_id=1, source_target_pairs={{0,2},{2,0},{4,6},{6,4},{8,10},{10,8},{12,14},{14,12},{1,3},{3,1},... | collective-permute-start | bytes 196616 | tf_op jit(solution)/shard_map/ppermute | solution.py:37
  40.8 0.0 collective-permute-done.7
  40.8 3.7 %collective-permute-start.14 = (bf16[64,384]{1,0:T(8,128)(2,1)S(1)}, bf16[64,384]{1,0:T(8,128)(2,1)S(1)}, u32[]{:S(2)}, u32[]{:S(2)}) collective-permute-start(bf16[64,384]{1,0:T(8,128)(2,1)S(1)} %get-tuple-element.58), channel_id=1, source_target_pairs={{0,6},{2,4},{4,2},{6,0},{8,14},{10,12},{12,10},{14,8},{1,7},{3,5},... | collective-permute-start | bytes 147464 | tf_op jit(solution)/shard_map/ppermute | solution.py:37
  44.5 0.7 %collective-permute-start.15 = (bf16[64,384]{1,0:T(8,128)(2,1)S(1)}, bf16[64,384]{1,0:T(8,128)(2,1)S(1)}, u32[]{:S(2)}, u32[]{:S(2)}) collective-permute-start(bf16[64,384]{1,0:T(8,128)(2,1)S(1)} %get-tuple-element.59), channel_id=1, source_target_pairs={{4,10},{6,8},{8,6},{10,4},{5,11},{7,9},{9,7},{11,5},{20,26},{22,24... | collective-permute-start | bytes 147464 | tf_op jit(solution)/shard_map/ppermute | solution.py:37
  45.2 0.4 shard_map.91.halo_t
  45.6 2.0 %shard_map.90 = (bf16[2048,128]{1,0:T(8,128)(2,1)}, f32[1,2080,128]{2,1,0:T(8,128)S(1)}) custom-call(bf16[64,1024]{1,0:T(8,128)(2,1)S(1)} %get-tuple-element.45.gc_ref, bf16[4096,128]{1,0:T(8,128)(2,1)S(1)} %get-tuple-element.46.hot_ref, bf16[64,128,128]{2,1,0:T(8,128)(2,1)S(1)} %get-tuple-element.47.tgt_t), custom_call_target="tpu_custom_call" | custom-call | bytes 12000000 | tf_op jit(solution)/shard_map/pallas_call | solution.py:405
  47.7 2.0 %shard_map.92 = bf16[2048,128]{1,0:T(8,128)(2,1)} custom-call(f32[1,2080,128]{2,1,0:T(8,128)S(1)} %get-tuple-element.49.pw_own, bf16[64,32,128]{2,1,0:T(8,128)(2,1)S(1)} %get-tuple-element.32.refs_1_.src_t, bf16[64,80,128]{2,1,0:T(8,128)(2,1)S(1)} %shard_map.91.halo_t, bf16[64,768]{1,0:T(8,128)(2,1)S(1)} %collective-permute-done.11.refs_0_, ...), custom_call_target="tpu_custom_call" | custom-call | bytes 9000000 | tf_op jit(solution)/shard_map/pallas_call | solution.py:405
  (8 shorter events, 0.0 us)
Async XLA Ops:
  2.1 22.6 %collective-permute-start = (bf16[3,8,64,128]{3,2,1,0:T(8,128)(2,1)S(1)}, bf16[3,8,64,128]{3,2,1,0:T(8,128)(2,1)S(1)}, u32[]{:S(2)}, u32[]{:S(2)}) collective-permute-start(bf16[3,8,64,128]{3,2,1,0:T(8,128)(2,1)S(1)} %get-tuple-element.34), channel_id=1, source_target_pairs={{0,4},{2,6},{4,0},{6,2},{8,12},{10,14},{12,8},{14,10},{1,5},{3,7},... | collective-permute-start | bytes 1179656 | tf_op jit(solution)/shard_map/ppermute | solution.py:37
  5.3 19.5 %collective-permute-start.1 = (bf16[3,8,64,128]{3,2,1,0:T(8,128)(2,1)S(1)}, bf16[3,8,64,128]{3,2,1,0:T(8,128)(2,1)S(1)}, u32[]{:S(2)}, u32[]{:S(2)}) collective-permute-start(bf16[3,8,64,128]{3,2,1,0:T(8,128)(2,1)S(1)} %get-tuple-element.35), channel_id=1, source_target_pairs={{4,8},{6,10},{8,4},{10,6},{5,9},{7,11},{9,5},{11,7},{20,24},{22,26... | collective-permute-start | bytes 1179656 | tf_op jit(solution)/shard_map/ppermute | solution.py:37
  5.9 12.9 %collective-permute-start.3 = (bf16[3,3,64,128]{3,2,1,0:T(8,128)(2,1)S(1)}, bf16[3,3,64,128]{3,2,1,0:T(8,128)(2,1)S(1)}, u32[]{:S(2)}, u32[]{:S(2)}) collective-permute-start(bf16[3,3,64,128]{3,2,1,0:T(8,128)(2,1)S(1)} %get-tuple-element.37), channel_id=1, source_target_pairs={{0,6},{2,4},{4,2},{6,0},{8,14},{10,12},{12,10},{14,8},{1,7},{3,5},... | collective-permute-start | bytes 442376 | tf_op jit(solution)/shard_map/ppermute | solution.py:37
  11.4 8.1 %collective-permute-start.4 = (bf16[3,3,64,128]{3,2,1,0:T(8,128)(2,1)S(1)}, bf16[3,3,64,128]{3,2,1,0:T(8,128)(2,1)S(1)}, u32[]{:S(2)}, u32[]{:S(2)}) collective-permute-start(bf16[3,3,64,128]{3,2,1,0:T(8,128)(2,1)S(1)} %get-tuple-element.38), channel_id=1, source_target_pairs={{4,10},{6,8},{8,6},{10,4},{5,11},{7,9},{9,7},{11,5},{20,26},{22,24... | collective-permute-start | bytes 442376 | tf_op jit(solution)/shard_map/ppermute | solution.py:37
  12.0 12.7 %collective-permute-start.2 = (bf16[4,3,64,128]{3,2,1,0:T(8,128)(2,1)S(1)}, bf16[4,3,64,128]{3,2,1,0:T(8,128)(2,1)S(1)}, u32[]{:S(2)}, u32[]{:S(2)}) collective-permute-start(bf16[4,3,64,128]{3,2,1,0:T(8,128)(2,1)S(1)} %get-tuple-element.36), channel_id=1, source_target_pairs={{0,2},{2,0},{4,6},{6,4},{8,10},{10,8},{12,14},{14,12},{1,3},{3,1},... | collective-permute-start | bytes 589832 | tf_op jit(solution)/shard_map/ppermute | solution.py:37
  18.8 22.0 %collective-permute-start.7 = (bf16[3,8,64,128]{3,2,1,0:T(8,128)(2,1)S(1)}, bf16[3,8,64,128]{3,2,1,0:T(8,128)(2,1)S(1)}, u32[]{:S(2)}, u32[]{:S(2)}) collective-permute-start(bf16[3,8,64,128]{3,2,1,0:T(8,128)(2,1)S(1)} %get-tuple-element.51), channel_id=1, source_target_pairs={{4,8},{6,10},{8,4},{10,6},{5,9},{7,11},{9,5},{11,7},{20,24},{22,26... | collective-permute-start | bytes 1179656 | tf_op jit(solution)/shard_map/ppermute | solution.py:37
  19.5 25.0 %collective-permute-start.6 = (bf16[3,8,64,128]{3,2,1,0:T(8,128)(2,1)S(1)}, bf16[3,8,64,128]{3,2,1,0:T(8,128)(2,1)S(1)}, u32[]{:S(2)}, u32[]{:S(2)}) collective-permute-start(bf16[3,8,64,128]{3,2,1,0:T(8,128)(2,1)S(1)} %get-tuple-element.50), channel_id=1, source_target_pairs={{0,4},{2,6},{4,0},{6,2},{8,12},{10,14},{12,8},{14,10},{1,5},{3,7},... | collective-permute-start | bytes 1179656 | tf_op jit(solution)/shard_map/ppermute | solution.py:37
  26.6 2.6 %collective-permute-start.5 = (bf16[64,1024]{1,0:T(8,128)(2,1)S(1)}, bf16[64,1024]{1,0:T(8,128)(2,1)S(1)}, u32[]{:S(2)}, u32[]{:S(2)}) collective-permute-start(bf16[64,1024]{1,0:T(8,128)(2,1)S(1)} %get-tuple-element.39.refs_0_), channel_id=1, source_target_pairs={{0,1},{1,0},{2,3},{3,2},{4,5},{5,4},{6,7},{7,6},{8,9},{9,8},{10,11... | collective-permute-start | bytes 393224 | tf_op jit(solution)/shard_map/ppermute | solution.py:504
  26.7 11.8 %collective-permute-start.8 = (bf16[4,3,64,128]{3,2,1,0:T(8,128)(2,1)S(1)}, bf16[4,3,64,128]{3,2,1,0:T(8,128)(2,1)S(1)}, u32[]{:S(2)}, u32[]{:S(2)}) collective-permute-start(bf16[4,3,64,128]{3,2,1,0:T(8,128)(2,1)S(1)} %get-tuple-element.52), channel_id=1, source_target_pairs={{0,2},{2,0},{4,6},{6,4},{8,10},{10,8},{12,14},{14,12},{1,3},{3,1},... | collective-permute-start | bytes 589832 | tf_op jit(solution)/shard_map/ppermute | solution.py:37
  27.2 7.9 %collective-permute-start.9 = (bf16[3,3,64,128]{3,2,1,0:T(8,128)(2,1)S(1)}, bf16[3,3,64,128]{3,2,1,0:T(8,128)(2,1)S(1)}, u32[]{:S(2)}, u32[]{:S(2)}) collective-permute-start(bf16[3,3,64,128]{3,2,1,0:T(8,128)(2,1)S(1)} %get-tuple-element.53), channel_id=1, source_target_pairs={{0,6},{2,4},{4,2},{6,0},{8,14},{10,12},{12,10},{14,8},{1,7},{3,5},... | collective-permute-start | bytes 442376 | tf_op jit(solution)/shard_map/ppermute | solution.py:37
  29.2 8.6 %collective-permute-start.10 = (bf16[3,3,64,128]{3,2,1,0:T(8,128)(2,1)S(1)}, bf16[3,3,64,128]{3,2,1,0:T(8,128)(2,1)S(1)}, u32[]{:S(2)}, u32[]{:S(2)}) collective-permute-start(bf16[3,3,64,128]{3,2,1,0:T(8,128)(2,1)S(1)} %get-tuple-element.54), channel_id=1, source_target_pairs={{4,10},{6,8},{8,6},{10,4},{5,11},{7,9},{9,7},{11,5},{20,26},{22,24... | collective-permute-start | bytes 442376 | tf_op jit(solution)/shard_map/ppermute | solution.py:37
  35.1 12.6 %collective-permute-start.11 = (bf16[64,768]{1,0:T(8,128)(2,1)S(1)}, bf16[64,768]{1,0:T(8,128)(2,1)S(1)}, u32[]{:S(2)}, u32[]{:S(2)}) collective-permute-start(bf16[64,768]{1,0:T(8,128)(2,1)S(1)} %get-tuple-element.55), channel_id=1, source_target_pairs={{0,4},{2,6},{4,0},{6,2},{8,12},{10,14},{12,8},{14,10},{1,5},{3,7},... | collective-permute-start | bytes 294920 | tf_op jit(solution)/shard_map/ppermute | solution.py:37
  37.8 9.8 %collective-permute-start.12 = (bf16[64,768]{1,0:T(8,128)(2,1)S(1)}, bf16[64,768]{1,0:T(8,128)(2,1)S(1)}, u32[]{:S(2)}, u32[]{:S(2)}) collective-permute-start(bf16[64,768]{1,0:T(8,128)(2,1)S(1)} %get-tuple-element.56), channel_id=1, source_target_pairs={{4,8},{6,10},{8,4},{10,6},{5,9},{7,11},{9,5},{11,7},{20,24},{22,26... | collective-permute-start | bytes 294920 | tf_op jit(solution)/shard_map/ppermute | solution.py:37
  38.5 9.1 %collective-permute-start.13 = (bf16[64,512]{1,0:T(8,128)(2,1)S(1)}, bf16[64,512]{1,0:T(8,128)(2,1)S(1)}, u32[]{:S(2)}, u32[]{:S(2)}) collective-permute-start(bf16[64,512]{1,0:T(8,128)(2,1)S(1)} %get-tuple-element.57), channel_id=1, source_target_pairs={{0,2},{2,0},{4,6},{6,4},{8,10},{10,8},{12,14},{14,12},{1,3},{3,1},... | collective-permute-start | bytes 196616 | tf_op jit(solution)/shard_map/ppermute | solution.py:37
  40.8 6.9 %collective-permute-start.14 = (bf16[64,384]{1,0:T(8,128)(2,1)S(1)}, bf16[64,384]{1,0:T(8,128)(2,1)S(1)}, u32[]{:S(2)}, u32[]{:S(2)}) collective-permute-start(bf16[64,384]{1,0:T(8,128)(2,1)S(1)} %get-tuple-element.58), channel_id=1, source_target_pairs={{0,6},{2,4},{4,2},{6,0},{8,14},{10,12},{12,10},{14,8},{1,7},{3,5},... | collective-permute-start | bytes 147464 | tf_op jit(solution)/shard_map/ppermute | solution.py:37
  44.5 3.1 %collective-permute-start.15 = (bf16[64,384]{1,0:T(8,128)(2,1)S(1)}, bf16[64,384]{1,0:T(8,128)(2,1)S(1)}, u32[]{:S(2)}, u32[]{:S(2)}) collective-permute-start(bf16[64,384]{1,0:T(8,128)(2,1)S(1)} %get-tuple-element.59), channel_id=1, source_target_pairs={{4,10},{6,8},{8,6},{10,4},{5,11},{7,9},{9,7},{11,5},{20,26},{22,24... | collective-permute-start | bytes 147464 | tf_op jit(solution)/shard_map/ppermute | solution.py:37

commit v13 on v9

--- a/solution.py
+++ b/solution.py
@@ -92,7 +92,7 @@
     return copies
 
 
-def loop(count, body, most=4):
+def loop(count, body, most=12):
     step = max(d for d in range(1, most + 1) if count % d == 0) if count else 1
 
     def run(i, _):
@@ -193,13 +193,13 @@
             rows_of = src[i // cols, lax.rem(i, cols)]
             dst[pl.ds(i * pitch, px), :] = rows_of.astype(F32)
 
-        loop(n, body, 8)
+        loop(n, body, n)
 
     def turn(p):
         src_t[p] = s32[pl.ds(p, n, stride=pitch), :].astype(BF16)
         tgt_t[p] = t32[pl.ds(p, n, stride=pitch), :].astype(BF16)
 
-    loop(px, turn, 8)
+    loop(px, turn, px)
     for copy in slabs:
         copy.wait()
 
@@ -346,7 +346,7 @@
     def narrow(i):
         sg_ref[pl.ds(pl.multiple_of(i * px, px), px), :] = s32[pl.ds(i * pitch, px), :].astype(BF16)
 
-    loop(n, narrow)
+    loop(n, narrow, n)
 
 
 def halo_kernel(px, starts, *refs):
@@ -361,7 +361,7 @@
     def turn(p):
         out[p] = s32[pl.ds(p, out.shape[1], stride=pitch), :].astype(BF16)
 
-    loop(px, turn, 8)
+    loop(px, turn, px)
 
 
 def total_kernel(px, n, slots, widths, pw_own, src_t, halo_t, *refs):
@@ -392,7 +392,7 @@
     def narrow(i):
         tg_ref[pl.ds(pl.multiple_of(i * px, px), px), :] = t32[pl.ds(i * pitch, px), :].astype(BF16)
 
-    loop(n, narrow)
+    loop(n, narrow, n)
 
 
 VM = pl.BlockSpec(memory_space=pltpu.VMEM)

time: 50.6 us -> 50.5 us (level)
  the two profiles are of different devices: /device:TPU:0 before, /device:TPU:12 now
where the time goes in v13:
time: 50.5 us; the launch traced here: 50.2 us
  starting transfers between devices  25.1 us (50%)
  waiting for transfers between devices  13.4 us (27%)
  Pallas kernels  11 us (22%)
  between operations  0.77 us (2%)
    ppermute x15, starting transfers between devices, swap(): return lax.ppermute(x, ('strip', 'sub'), pairs)  25 us
    ppermute x15, waiting for transfers between devices, swap(): return lax.ppermute(x, ('strip', 'sub'), pairs)  13.4 us
    pallas_call x7, Pallas kernels, call(): pl.pallas_call(kernel, out_shape=[pltpu.VMEM(s, d) if near else jax.Shape...  9.46 us
    pallas_call x1, Pallas kernels, shards(): pl.pallas_call(partial(cut_kernel, pieces, rows, cols), name='cut', out_s...  1.51 us
  transfers between devices with their start and end apart: 16, of which 5 were waited for; matrix products, arithmetic and copies ran while one was open for 0% of the time, Pallas kernels for 15%

profile of v13, /device:TPU:12, one launch (start us, length us, event | category | flops | bytes accessed | tf_op | source)
XLA Modules:
  0.0 50.2 jit_solution(11167468646078782107)
XLA Ops:
  0.6 1.5 %cut.1 = (bf16[3,8,64,128]{3,2,1,0:T(8,128)(2,1)S(1)}, bf16[3,8,64,128]{3,2,1,0:T(8,128)(2,1)S(1)}, bf16[4,3,64,128]{3,2,1,0:T(8,128)(2,1)S(1)}, bf16[3,3,64,128...) custom-call(bf16[4,8,64,128]{3,2,1,0:T(8,128)(2,1)} %x_ref.1), custom_call_target="tpu_custom_call" | custom-call | tf_op jit(solution)/shard_map/cut/pallas_call | solution.py:467
  2.1 0.5 %collective-permute-start = (bf16[3,8,64,128]{3,2,1,0:T(8,128)(2,1)S(1)}, bf16[3,8,64,128]{3,2,1,0:T(8,128)(2,1)S(1)}, u32[]{:S(2)}, u32[]{:S(2)}) collective-permute-start(bf16[3,8,64,128]{3,2,1,0:T(8,128)(2,1)S(1)} %get-tuple-element.34), channel_id=1, source_target_pairs={{0,4},{2,6},{4,0},{6,2},{8,12},{10,14},{12,8},{14,10},{1,5},{3,7},... | collective-permute-start | bytes 1179656 | tf_op jit(solution)/shard_map/ppermute | solution.py:37
  2.7 4.6 %collective-permute-start.1 = (bf16[3,8,64,128]{3,2,1,0:T(8,128)(2,1)S(1)}, bf16[3,8,64,128]{3,2,1,0:T(8,128)(2,1)S(1)}, u32[]{:S(2)}, u32[]{:S(2)}) collective-permute-start(bf16[3,8,64,128]{3,2,1,0:T(8,128)(2,1)S(1)} %get-tuple-element.35), channel_id=1, source_target_pairs={{4,8},{6,10},{8,4},{10,6},{5,9},{7,11},{9,5},{11,7},{20,24},{22,26... | collective-permute-start | bytes 1179656 | tf_op jit(solution)/shard_map/ppermute | solution.py:37
  7.3 0.1 collective-permute-start.3
  7.3 2.9 %collective-permute-start.4 = (bf16[3,3,64,128]{3,2,1,0:T(8,128)(2,1)S(1)}, bf16[3,3,64,128]{3,2,1,0:T(8,128)(2,1)S(1)}, u32[]{:S(2)}, u32[]{:S(2)}) collective-permute-start(bf16[3,3,64,128]{3,2,1,0:T(8,128)(2,1)S(1)} %get-tuple-element.38), channel_id=1, source_target_pairs={{4,10},{6,8},{8,6},{10,4},{5,11},{7,9},{9,7},{11,5},{20,26},{22,24... | collective-permute-start | bytes 442376 | tf_op jit(solution)/shard_map/ppermute | solution.py:37
  10.3 0.7 %collective-permute-start.2 = (bf16[4,3,64,128]{3,2,1,0:T(8,128)(2,1)S(1)}, bf16[4,3,64,128]{3,2,1,0:T(8,128)(2,1)S(1)}, u32[]{:S(2)}, u32[]{:S(2)}) collective-permute-start(bf16[4,3,64,128]{3,2,1,0:T(8,128)(2,1)S(1)} %get-tuple-element.36), channel_id=1, source_target_pairs={{0,2},{2,0},{4,6},{6,4},{8,10},{10,8},{12,14},{14,12},{1,3},{3,1},... | collective-permute-start | bytes 589832 | tf_op jit(solution)/shard_map/ppermute | solution.py:37
  11.0 1.9 %shard_map.86 = (bf16[3,8,64,128]{3,2,1,0:T(8,128)(2,1)S(1)}, bf16[3,8,64,128]{3,2,1,0:T(8,128)(2,1)S(1)}, bf16[4,3,64,128]{3,2,1,0:T(8,128)(2,1)S(1)}, bf16[3,3...) custom-call(bf16[4,8,64,128]{3,2,1,0:T(8,128)(2,1)} %refs_0_.1, ...), custom_call_target="tpu_custom_call" | custom-call | bytes 6000000 | tf_op jit(solution)/shard_map/pallas_call | solution.py:403
  12.9 5.1 %collective-permute-done.3 = bf16[3,3,64,128]{3,2,1,0:T(8,128)(2,1)S(1)} collective-permute-done((bf16[3,3,64,128]{3,2,1,0:T(8,128)(2,1)S(1)}, bf16[3,3,64,128]{3,2,1,0:T(8,128)(2,1)S(1)}, u32[]{:S(2)}, u32[]{:S(2)}) %collective-permute-start.3) | collective-permute-done | bytes 147488 | tf_op jit(solution)/shard_map/ppermute | solution.py:37
  18.1 3.6 %collective-permute-start.7 = (bf16[3,8,64,128]{3,2,1,0:T(8,128)(2,1)S(1)}, bf16[3,8,64,128]{3,2,1,0:T(8,128)(2,1)S(1)}, u32[]{:S(2)}, u32[]{:S(2)}) collective-permute-start(bf16[3,8,64,128]{3,2,1,0:T(8,128)(2,1)S(1)} %get-tuple-element.51), channel_id=1, source_target_pairs={{4,8},{6,10},{8,4},{10,6},{5,9},{7,11},{9,5},{11,7},{20,24},{22,26... | collective-permute-start | bytes 1179656 | tf_op jit(solution)/shard_map/ppermute | solution.py:37
  21.7 0.1 collective-permute-start.6
  21.7 1.0 %collective-permute-done.2 = bf16[4,3,64,128]{3,2,1,0:T(8,128)(2,1)S(1)} collective-permute-done((bf16[4,3,64,128]{3,2,1,0:T(8,128)(2,1)S(1)}, bf16[4,3,64,128]{3,2,1,0:T(8,128)(2,1)S(1)}, u32[]{:S(2)}, u32[]{:S(2)}) %collective-permute-start.2) | collective-permute-done | bytes 196640 | tf_op jit(solution)/shard_map/ppermute | solution.py:37
  22.7 0.0 collective-permute-done
  22.7 0.0 collective-permute-done.1
  22.7 1.7 %shard_map.87 = (bf16[64,1024]{1,0:T(8,128)(2,1)S(1)}, bf16[64,128,128]{2,1,0:T(8,128)(2,1)S(1)}, bf16[4096,128]{1,0:T(8,128)(2,1)S(1)}) custom-call(bf16[64,32,128]{2,1,0:T(8,128)(2,1)S(1)} %get-tuple-element.31.refs_0_, bf16[64,32,128]{2,1,0:T(8,128)(2,1)S(1)} %get-tuple-element.32.refs_1_.src_t, s32[8,128]{1,0:T(8,128)S(1)} %get-tuple-element.33.refs_2_.e_ref, ...), custom_call_target="tpu_custom_call" | custom-call | bytes 9000000 | tf_op jit(solution)/shard_map/pallas_call | solution.py:403
  24.5 0.1 collective-permute-start.5
  24.6 0.6 %collective-permute-start.8 = (bf16[4,3,64,128]{3,2,1,0:T(8,128)(2,1)S(1)}, bf16[4,3,64,128]{3,2,1,0:T(8,128)(2,1)S(1)}, u32[]{:S(2)}, u32[]{:S(2)}) collective-permute-start(bf16[4,3,64,128]{3,2,1,0:T(8,128)(2,1)S(1)} %get-tuple-element.52), channel_id=1, source_target_pairs={{0,2},{2,0},{4,6},{6,4},{8,10},{10,8},{12,14},{14,12},{1,3},{3,1},... | collective-permute-start | bytes 589832 | tf_op jit(solution)/shard_map/ppermute | solution.py:37
  25.2 1.9 %collective-permute-start.9 = (bf16[3,3,64,128]{3,2,1,0:T(8,128)(2,1)S(1)}, bf16[3,3,64,128]{3,2,1,0:T(8,128)(2,1)S(1)}, u32[]{:S(2)}, u32[]{:S(2)}) collective-permute-start(bf16[3,3,64,128]{3,2,1,0:T(8,128)(2,1)S(1)} %get-tuple-element.53), channel_id=1, source_target_pairs={{0,6},{2,4},{4,2},{6,0},{8,14},{10,12},{12,10},{14,8},{1,7},{3,5},... | collective-permute-start | bytes 442376 | tf_op jit(solution)/shard_map/ppermute | solution.py:37
  27.1 0.0 collective-permute-done.5.refs_1_
  27.1 2.6 %collective-permute-start.10 = (bf16[3,3,64,128]{3,2,1,0:T(8,128)(2,1)S(1)}, bf16[3,3,64,128]{3,2,1,0:T(8,128)(2,1)S(1)}, u32[]{:S(2)}, u32[]{:S(2)}) collective-permute-start(bf16[3,3,64,128]{3,2,1,0:T(8,128)(2,1)S(1)} %get-tuple-element.54), channel_id=1, source_target_pairs={{4,10},{6,8},{8,6},{10,4},{5,11},{7,9},{9,7},{11,5},{20,26},{22,24... | collective-permute-start | bytes 442376 | tf_op jit(solution)/shard_map/ppermute | solution.py:37
  29.7 0.2 shard_map.88.refs_6_
  29.9 1.4 %shard_map.89 = (bf16[64,1024]{1,0:T(8,128)(2,1)S(1)}, bf16[64,768]{1,0:T(8,128)(2,1)S(1)}, bf16[64,768]{1,0:T(8,128)(2,1)S(1)}, bf16[64,512]{1,0:T(8,128)(2,1)S...) custom-call(bf16[64,1024]{1,0:T(8,128)(2,1)S(1)} %get-tuple-element.39.refs_0_, ...), custom_call_target="tpu_custom_call" | custom-call | bytes 9000000 | tf_op jit(solution)/shard_map/pallas_call | solution.py:403
  31.3 3.5 %collective-permute-done.9 = bf16[3,3,64,128]{3,2,1,0:T(8,128)(2,1)S(1)} collective-permute-done((bf16[3,3,64,128]{3,2,1,0:T(8,128)(2,1)S(1)}, bf16[3,3,64,128]{3,2,1,0:T(8,128)(2,1)S(1)}, u32[]{:S(2)}, u32[]{:S(2)}) %collective-permute-start.9) | collective-permute-done | bytes 147488 | tf_op jit(solution)/shard_map/ppermute | solution.py:37
  34.9 2.0 %collective-permute-done.10 = bf16[3,3,64,128]{3,2,1,0:T(8,128)(2,1)S(1)} collective-permute-done((bf16[3,3,64,128]{3,2,1,0:T(8,128)(2,1)S(1)}, bf16[3,3,64,128]{3,2,1,0:T(8,128)(2,1)S(1)}, u32[]{:S(2)}, u32[]{:S(2)}) %collective-permute-start.10) | collective-permute-done | bytes 147488 | tf_op jit(solution)/shard_map/ppermute | solution.py:37
  36.8 3.1 %collective-permute-start.12 = (bf16[64,768]{1,0:T(8,128)(2,1)S(1)}, bf16[64,768]{1,0:T(8,128)(2,1)S(1)}, u32[]{:S(2)}, u32[]{:S(2)}) collective-permute-start(bf16[64,768]{1,0:T(8,128)(2,1)S(1)} %get-tuple-element.56), channel_id=1, source_target_pairs={{4,8},{6,10},{8,4},{10,6},{5,9},{7,11},{9,5},{11,7},{20,24},{22,26... | collective-permute-start | bytes 294920 | tf_op jit(solution)/shard_map/ppermute | solution.py:37
  39.9 1.4 %collective-permute-start.13 = (bf16[64,512]{1,0:T(8,128)(2,1)S(1)}, bf16[64,512]{1,0:T(8,128)(2,1)S(1)}, u32[]{:S(2)}, u32[]{:S(2)}) collective-permute-start(bf16[64,512]{1,0:T(8,128)(2,1)S(1)} %get-tuple-element.57), channel_id=1, source_target_pairs={{0,2},{2,0},{4,6},{6,4},{8,10},{10,8},{12,14},{14,12},{1,3},{3,1},... | collective-permute-start | bytes 196616 | tf_op jit(solution)/shard_map/ppermute | solution.py:37
  41.4 0.0 collective-permute-done.7
  41.4 0.0 collective-permute-start.14
  41.4 2.8 %collective-permute-start.15 = (bf16[64,384]{1,0:T(8,128)(2,1)S(1)}, bf16[64,384]{1,0:T(8,128)(2,1)S(1)}, u32[]{:S(2)}, u32[]{:S(2)}) collective-permute-start(bf16[64,384]{1,0:T(8,128)(2,1)S(1)} %get-tuple-element.59), channel_id=1, source_target_pairs={{4,10},{6,8},{8,6},{10,4},{5,11},{7,9},{9,7},{11,5},{20,26},{22,24... | collective-permute-start | bytes 147464 | tf_op jit(solution)/shard_map/ppermute | solution.py:37
  44.2 0.3 shard_map.91.halo_t
  44.5 2.0 %shard_map.90 = (bf16[2048,128]{1,0:T(8,128)(2,1)}, f32[1,2080,128]{2,1,0:T(8,128)S(1)}) custom-call(bf16[64,1024]{1,0:T(8,128)(2,1)S(1)} %get-tuple-element.45.gc_ref, bf16[4096,128]{1,0:T(8,128)(2,1)S(1)} %get-tuple-element.46.hot_ref, bf16[64,128,128]{2,1,0:T(8,128)(2,1)S(1)} %get-tuple-element.47.tgt_t), custom_call_target="tpu_custom_call" | custom-call | bytes 12000000 | tf_op jit(solution)/shard_map/pallas_call | solution.py:403
  46.5 1.8 %collective-permute-done.15.refs_4_ = bf16[64,384]{1,0:T(8,128)(2,1)S(1)} collective-permute-done((bf16[64,384]{1,0:T(8,128)(2,1)S(1)}, bf16[64,384]{1,0:T(8,128)(2,1)S(1)}, u32[]{:S(2)}, u32[]{:S(2)}) %collective-permute-start.15) | collective-permute-done | bytes 49184 | tf_op jit(solution)/shard_map/ppermute | solution.py:37
  48.3 2.0 %shard_map.92 = bf16[2048,128]{1,0:T(8,128)(2,1)} custom-call(f32[1,2080,128]{2,1,0:T(8,128)S(1)} %get-tuple-element.49.pw_own, bf16[64,32,128]{2,1,0:T(8,128)(2,1)S(1)} %get-tuple-element.32.refs_1_.src_t, bf16[64,80,128]{2,1,0:T(8,128)(2,1)S(1)} %shard_map.91.halo_t, bf16[64,768]{1,0:T(8,128)(2,1)S(1)} %collective-permute-done.11.refs_0_, ...), custom_call_target="tpu_custom_call" | custom-call | bytes 9000000 | tf_op jit(solution)/shard_map/pallas_call | solution.py:403
  (8 shorter events, 0.0 us)
Async XLA Ops:
  2.1 20.6 %collective-permute-start = (bf16[3,8,64,128]{3,2,1,0:T(8,128)(2,1)S(1)}, bf16[3,8,64,128]{3,2,1,0:T(8,128)(2,1)S(1)}, u32[]{:S(2)}, u32[]{:S(2)}) collective-permute-start(bf16[3,8,64,128]{3,2,1,0:T(8,128)(2,1)S(1)} %get-tuple-element.34), channel_id=1, source_target_pairs={{0,4},{2,6},{4,0},{6,2},{8,12},{10,14},{12,8},{14,10},{1,5},{3,7},... | collective-permute-start | bytes 1179656 | tf_op jit(solution)/shard_map/ppermute | solution.py:37
  2.7 20.1 %collective-permute-start.1 = (bf16[3,8,64,128]{3,2,1,0:T(8,128)(2,1)S(1)}, bf16[3,8,64,128]{3,2,1,0:T(8,128)(2,1)S(1)}, u32[]{:S(2)}, u32[]{:S(2)}) collective-permute-start(bf16[3,8,64,128]{3,2,1,0:T(8,128)(2,1)S(1)} %get-tuple-element.35), channel_id=1, source_target_pairs={{4,8},{6,10},{8,4},{10,6},{5,9},{7,11},{9,5},{11,7},{20,24},{22,26... | collective-permute-start | bytes 1179656 | tf_op jit(solution)/shard_map/ppermute | solution.py:37
  7.3 10.8 %collective-permute-start.3 = (bf16[3,3,64,128]{3,2,1,0:T(8,128)(2,1)S(1)}, bf16[3,3,64,128]{3,2,1,0:T(8,128)(2,1)S(1)}, u32[]{:S(2)}, u32[]{:S(2)}) collective-permute-start(bf16[3,3,64,128]{3,2,1,0:T(8,128)(2,1)S(1)} %get-tuple-element.37), channel_id=1, source_target_pairs={{0,6},{2,4},{4,2},{6,0},{8,14},{10,12},{12,10},{14,8},{1,7},{3,5},... | collective-permute-start | bytes 442376 | tf_op jit(solution)/shard_map/ppermute | solution.py:37
  7.3 14.3 %collective-permute-start.4 = (bf16[3,3,64,128]{3,2,1,0:T(8,128)(2,1)S(1)}, bf16[3,3,64,128]{3,2,1,0:T(8,128)(2,1)S(1)}, u32[]{:S(2)}, u32[]{:S(2)}) collective-permute-start(bf16[3,3,64,128]{3,2,1,0:T(8,128)(2,1)S(1)} %get-tuple-element.38), channel_id=1, source_target_pairs={{4,10},{6,8},{8,6},{10,4},{5,11},{7,9},{9,7},{11,5},{20,26},{22,24... | collective-permute-start | bytes 442376 | tf_op jit(solution)/shard_map/ppermute | solution.py:37
  10.3 12.5 %collective-permute-start.2 = (bf16[4,3,64,128]{3,2,1,0:T(8,128)(2,1)S(1)}, bf16[4,3,64,128]{3,2,1,0:T(8,128)(2,1)S(1)}, u32[]{:S(2)}, u32[]{:S(2)}) collective-permute-start(bf16[4,3,64,128]{3,2,1,0:T(8,128)(2,1)S(1)} %get-tuple-element.36), channel_id=1, source_target_pairs={{0,2},{2,0},{4,6},{6,4},{8,10},{10,8},{12,14},{14,12},{1,3},{3,1},... | collective-permute-start | bytes 589832 | tf_op jit(solution)/shard_map/ppermute | solution.py:37
  18.1 23.3 %collective-permute-start.7 = (bf16[3,8,64,128]{3,2,1,0:T(8,128)(2,1)S(1)}, bf16[3,8,64,128]{3,2,1,0:T(8,128)(2,1)S(1)}, u32[]{:S(2)}, u32[]{:S(2)}) collective-permute-start(bf16[3,8,64,128]{3,2,1,0:T(8,128)(2,1)S(1)} %get-tuple-element.51), channel_id=1, source_target_pairs={{4,8},{6,10},{8,4},{10,6},{5,9},{7,11},{9,5},{11,7},{20,24},{22,26... | collective-permute-start | bytes 1179656 | tf_op jit(solution)/shard_map/ppermute | solution.py:37
  21.7 19.7 %collective-permute-start.6 = (bf16[3,8,64,128]{3,2,1,0:T(8,128)(2,1)S(1)}, bf16[3,8,64,128]{3,2,1,0:T(8,128)(2,1)S(1)}, u32[]{:S(2)}, u32[]{:S(2)}) collective-permute-start(bf16[3,8,64,128]{3,2,1,0:T(8,128)(2,1)S(1)} %get-tuple-element.50), channel_id=1, source_target_pairs={{0,4},{2,6},{4,0},{6,2},{8,12},{10,14},{12,8},{14,10},{1,5},{3,7},... | collective-permute-start | bytes 1179656 | tf_op jit(solution)/shard_map/ppermute | solution.py:37
  24.5 2.6 %collective-permute-start.5 = (bf16[64,1024]{1,0:T(8,128)(2,1)S(1)}, bf16[64,1024]{1,0:T(8,128)(2,1)S(1)}, u32[]{:S(2)}, u32[]{:S(2)}) collective-permute-start(bf16[64,1024]{1,0:T(8,128)(2,1)S(1)} %get-tuple-element.39.refs_0_), channel_id=1, source_target_pairs={{0,1},{1,0},{2,3},{3,2},{4,5},{5,4},{6,7},{7,6},{8,9},{9,8},{10,11... | collective-permute-start | bytes 393224 | tf_op jit(solution)/shard_map/ppermute | solution.py:502
  24.6 15.4 %collective-permute-start.8 = (bf16[4,3,64,128]{3,2,1,0:T(8,128)(2,1)S(1)}, bf16[4,3,64,128]{3,2,1,0:T(8,128)(2,1)S(1)}, u32[]{:S(2)}, u32[]{:S(2)}) collective-permute-start(bf16[4,3,64,128]{3,2,1,0:T(8,128)(2,1)S(1)} %get-tuple-element.52), channel_id=1, source_target_pairs={{0,2},{2,0},{4,6},{6,4},{8,10},{10,8},{12,14},{14,12},{1,3},{3,1},... | collective-permute-start | bytes 589832 | tf_op jit(solution)/shard_map/ppermute | solution.py:37
  25.2 9.7 %collective-permute-start.9 = (bf16[3,3,64,128]{3,2,1,0:T(8,128)(2,1)S(1)}, bf16[3,3,64,128]{3,2,1,0:T(8,128)(2,1)S(1)}, u32[]{:S(2)}, u32[]{:S(2)}) collective-permute-start(bf16[3,3,64,128]{3,2,1,0:T(8,128)(2,1)S(1)} %get-tuple-element.53), channel_id=1, source_target_pairs={{0,6},{2,4},{4,2},{6,0},{8,14},{10,12},{12,10},{14,8},{1,7},{3,5},... | collective-permute-start | bytes 442376 | tf_op jit(solution)/shard_map/ppermute | solution.py:37
  27.1 9.7 %collective-permute-start.10 = (bf16[3,3,64,128]{3,2,1,0:T(8,128)(2,1)S(1)}, bf16[3,3,64,128]{3,2,1,0:T(8,128)(2,1)S(1)}, u32[]{:S(2)}, u32[]{:S(2)}) collective-permute-start(bf16[3,3,64,128]{3,2,1,0:T(8,128)(2,1)S(1)} %get-tuple-element.54), channel_id=1, source_target_pairs={{4,10},{6,8},{8,6},{10,4},{5,11},{7,9},{9,7},{11,5},{20,26},{22,24... | collective-permute-start | bytes 442376 | tf_op jit(solution)/shard_map/ppermute | solution.py:37
  34.9 13.4 %collective-permute-start.11 = (bf16[64,768]{1,0:T(8,128)(2,1)S(1)}, bf16[64,768]{1,0:T(8,128)(2,1)S(1)}, u32[]{:S(2)}, u32[]{:S(2)}) collective-permute-start(bf16[64,768]{1,0:T(8,128)(2,1)S(1)} %get-tuple-element.55), channel_id=1, source_target_pairs={{0,4},{2,6},{4,0},{6,2},{8,12},{10,14},{12,8},{14,10},{1,5},{3,7},... | collective-permute-start | bytes 294920 | tf_op jit(solution)/shard_map/ppermute | solution.py:37
  36.8 11.5 %collective-permute-start.12 = (bf16[64,768]{1,0:T(8,128)(2,1)S(1)}, bf16[64,768]{1,0:T(8,128)(2,1)S(1)}, u32[]{:S(2)}, u32[]{:S(2)}) collective-permute-start(bf16[64,768]{1,0:T(8,128)(2,1)S(1)} %get-tuple-element.56), channel_id=1, source_target_pairs={{4,8},{6,10},{8,4},{10,6},{5,9},{7,11},{9,5},{11,7},{20,24},{22,26... | collective-permute-start | bytes 294920 | tf_op jit(solution)/shard_map/ppermute | solution.py:37
  39.9 8.3 %collective-permute-start.13 = (bf16[64,512]{1,0:T(8,128)(2,1)S(1)}, bf16[64,512]{1,0:T(8,128)(2,1)S(1)}, u32[]{:S(2)}, u32[]{:S(2)}) collective-permute-start(bf16[64,512]{1,0:T(8,128)(2,1)S(1)} %get-tuple-element.57), channel_id=1, source_target_pairs={{0,2},{2,0},{4,6},{6,4},{8,10},{10,8},{12,14},{14,12},{1,3},{3,1},... | collective-permute-start | bytes 196616 | tf_op jit(solution)/shard_map/ppermute | solution.py:37
  41.4 5.1 %collective-permute-start.14 = (bf16[64,384]{1,0:T(8,128)(2,1)S(1)}, bf16[64,384]{1,0:T(8,128)(2,1)S(1)}, u32[]{:S(2)}, u32[]{:S(2)}) collective-permute-start(bf16[64,384]{1,0:T(8,128)(2,1)S(1)} %get-tuple-element.58), channel_id=1, source_target_pairs={{0,6},{2,4},{4,2},{6,0},{8,14},{10,12},{12,10},{14,8},{1,7},{3,5},... | collective-permute-start | bytes 147464 | tf_op jit(solution)/shard_map/ppermute | solution.py:37
  41.4 6.9 %collective-permute-start.15 = (bf16[64,384]{1,0:T(8,128)(2,1)S(1)}, bf16[64,384]{1,0:T(8,128)(2,1)S(1)}, u32[]{:S(2)}, u32[]{:S(2)}) collective-permute-start(bf16[64,384]{1,0:T(8,128)(2,1)S(1)} %get-tuple-element.59), channel_id=1, source_target_pairs={{4,10},{6,8},{8,6},{10,4},{5,11},{7,9},{9,7},{11,5},{20,26},{22,24... | collective-permute-start | bytes 147464 | tf_op jit(solution)/shard_map/ppermute | solution.py:37
